TPU v7x, 128 devices: a whole 4x4x4 slice. The times are simulated.
128 devices in a mesh: dp: 4 (over x), seq: 8 (over z, core), tensor: 4 (over y).
Axes of the slice: x: 4, y: 4, z: 4, core: 2. Of those that a mesh axis runs over, the one named last changes fastest.
Arguments:
- block_input: bfloat16 [2048, 4, 1024], P('seq', 'dp', 'tensor'), may hold values from -6 to 6
- attn_gain: bfloat16 [1024], P(('dp', 'seq')), may hold values from 0.099609375 to 1.8984375
- ffn_gain: bfloat16 [1024], P(('dp', 'seq')), may hold values from 0.099609375 to 1.8984375
- query_gain: bfloat16 [64], replicated, may hold values from 0.5 to 2.5
- key_gain: bfloat16 [64], replicated, may hold values from 0.5 to 2.5
- query_weight: bfloat16 [1024, 1024], P(('dp', 'seq'), 'tensor'), may hold values from -0.1875 to 0.1875
- key_weight: bfloat16 [1024, 512], P(('dp', 'seq'), 'tensor'), may hold values from -0.1875 to 0.1875
- value_weight: bfloat16 [1024, 512], P(('dp', 'seq'), 'tensor'), may hold values from -0.1875 to 0.1875
- out_weight: bfloat16 [1024, 1024], P(('dp', 'seq'), 'tensor'), may hold values from -2 to 2
- gate_weight: bfloat16 [1024, 4608], P(('dp', 'seq'), 'tensor'), may hold values from -0.1875 to 0.1875
- up_weight: bfloat16 [1024, 4608], P(('dp', 'seq'), 'tensor'), may hold values from -0.1875 to 0.1875
- down_weight: bfloat16 [1024, 4608], P(('dp', 'seq'), 'tensor'), may hold values from -0.09375 to 0.09375
- cotangent: bfloat16 [2048, 4, 1024], P('seq', 'dp', 'tensor'), may hold values from -6 to 6
Outputs:
- block_output: bfloat16 [2048, 4, 1024], P('seq', 'dp', 'tensor')
- input_grad: bfloat16 [2048, 4, 1024], P('seq', 'dp', 'tensor')
- attn_gain_grad: float32 [1024], P(('dp', 'seq'))
- ffn_gain_grad: float32 [1024], P(('dp', 'seq'))
- query_gain_grad: float32 [64], replicated
- key_gain_grad: float32 [64], replicated
- query_grad: float32 [1024, 1024], P(('dp', 'seq'), 'tensor')
- key_grad: float32 [1024, 512], P(('dp', 'seq'), 'tensor')
- value_grad: float32 [1024, 512], P(('dp', 'seq'), 'tensor')
- out_grad: float32 [1024, 1024], P(('dp', 'seq'), 'tensor')
- gate_grad: float32 [1024, 4608], P(('dp', 'seq'), 'tensor')
- up_grad: float32 [1024, 4608], P(('dp', 'seq'), 'tensor')
- down_grad: float32 [1024, 4608], P(('dp', 'seq'), 'tensor')
All inputs are finite; a program needn't handle non-finite values.
Results may differ from a plain program's by a relative error of at most 0.03.
Values may be sent and summed in bfloat16 or wider, within the bound.
No kernel may reach another device: no remote copies, remote signals or barrier semaphores. Data moves between devices by JAX's collectives and lax.ppermute only.
A program may use at most 64 MiB of HBM per device.

v0:
```python
import functools

import numpy as np
import jax
import jax.numpy as jnp
from jax import lax
from jax.experimental import pallas as pl
from jax.experimental.pallas import tpu as pltpu
from jax.sharding import Mesh, PartitionSpec as P

HD = 64
HALF = HD // 2
EPS = 1e-05
ROPE_BASE = 1000000.0
SCALE = HD ** (-0.5)
PAD = 128
bf16 = jnp.bfloat16
f32 = jnp.float32
NN = (((1,), (0,)), ((), ()))
NT = (((1,), (1,)), ((), ()))


def dot(a, b, dims=NN):
    return lax.dot_general(a, b, dims, preferred_element_type=f32)


def rot_index(a, k, n):
    return lax.rem(a + k, n)


def ds(start, size):
    return pl.ds(pl.multiple_of(start * size, size), size)


def shift(x, axis, k):
    n = lax.axis_size(axis)
    return lax.ppermute(x, axis, [(i, (i + k) % n) for i in range(n)])


def gathered(x, axis):
    return [x] + [shift(x, axis, k) for k in range(1, lax.axis_size(axis))]


def summed(pieces, axis):
    total = pieces[0].astype(f32)
    for k in range(1, lax.axis_size(axis)):
        total = total + shift(pieces[k], axis, k).astype(f32)
    return total


def call(kernel, outs, ins, scratch=(), grid=None, in_specs=None, out_specs=None, flops=0):
    vm = pl.BlockSpec(memory_space=pltpu.VMEM)
    nbytes = sum(x.size * x.dtype.itemsize for x in list(ins) + list(outs))
    kwargs = {} if grid is None else {"grid": grid}
    return pl.pallas_call(
        kernel,
        out_shape=outs,
        in_specs=in_specs or [pl.BlockSpec(memory_space=pltpu.SMEM)] + [vm] * (len(ins) - 1),
        out_specs=out_specs or [vm] * len(outs),
        scratch_shapes=list(scratch),
        cost_estimate=pl.CostEstimate(flops=flops, bytes_accessed=nbytes, transcendentals=0),
        **kwargs,
    )(*ins)


def sds(shape, dtype):
    return jax.ShapeDtypeStruct(shape, dtype)


def store_relative(dims, idx, dst, src, own):
    nx, nz, nc, _ = dims
    x, z, c = idx[0], idx[1], idx[2]
    at = 0
    for other in range(nc):
        core = c if other == 0 else 1 - c
        for xr in range(nx):
            for zr in range(nz):
                row = (rot_index(x, xr, nx) * nz + rot_index(z, zr, nz)) * nc + core
                dst[at * own : (at + 1) * own, :] = src[ds(row, own), :]
                at += 1


def assemble(idx, n, pieces, dst, first=0):
    part = dst.shape[1] // n
    for k in range(n):
        dst[:, ds(rot_index(idx[3], n - k, n), part)] = pieces[k][:, first : first + part]


def cot_kernel(dims, own, idx, *refs):
    n = dims[3]
    pieces, (full, rel, turned) = refs[:n], refs[n:]
    assemble(idx, n, pieces, full, full.shape[1] // n)
    turned[...] = full[...].T
    store_relative(dims, idx, rel, turned, own)


def turn_heads(raw, gain, cosine, sine, heads):
    outs = []
    for h in range(heads):
        v = raw[h * HD : (h + 1) * HD]
        v = v * lax.rsqrt(jnp.mean(v * v, axis=0, keepdims=True) + EPS) * gain
        a, b = v[:HALF], v[HALF:]
        outs += [a * cosine - b * sine, b * cosine + a * sine]
    return jnp.concatenate(outs, axis=0)


def turn_heads_back(raw, grad, gain, cosine, sine, heads):
    outs, gain_grad = [], jnp.zeros((HD, 1), f32)
    for h in range(heads):
        v = raw[h * HD : (h + 1) * HD]
        g = grad[h * HD : (h + 1) * HD]
        ga, gb = g[:HALF], g[HALF:]
        g = jnp.concatenate([ga * cosine + gb * sine, gb * cosine - ga * sine], axis=0)
        r = lax.rsqrt(jnp.mean(v * v, axis=0, keepdims=True) + EPS)
        n = v * r
        gain_grad = gain_grad + jnp.sum(g * n, axis=1, keepdims=True)
        g = g * gain
        outs.append(r * (g - n * jnp.mean(g * n, axis=0, keepdims=True)))
    return jnp.concatenate(outs, axis=0), gain_grad


def qkv_kernel(dims, own, qc, kc, oc, idx, *refs):
    nx, nz, nc, n = dims
    pieces = refs[:n]
    w_own, w_partner, gq, gk, cosine, sine = refs[n : n + 6]
    w, base, gains, q_t, raw_t, kv, rel, turned = refs[n + 6 :]
    assemble(idx, n, pieces, base)
    for other, src in enumerate((w_own, w_partner)):
        core = idx[2] if other == 0 else 1 - idx[2]
        for zr in range(nz):
            for xr in range(nx):
                row = (rot_index(idx[0], nx - xr, nx) * nz + rot_index(idx[1], nz - zr, nz)) * nc + core
                at = xr * nz + zr
                w[ds(row, own), :] = src[at * own : (at + 1) * own, :]
    qkv = qc + 2 * kc
    gains[...] = w[:, qkv:].astype(f32).T[:8]
    b = base[...].astype(f32)
    normed = b * lax.rsqrt(jnp.mean(b * b, axis=1, keepdims=True) + EPS) * gains[0:1, :]
    normed = normed.astype(bf16)
    raw = dot(normed, w[:, :qkv])
    turned[...] = normed.T
    store_relative(dims, idx, rel, turned, own)
    kv[:, kc:] = raw[:, qc + kc :].astype(bf16)
    rt = raw[:, : qc + kc].T
    raw_t[...] = rt
    co, si = cosine[...], sine[...]
    q_t[...] = turn_heads(rt[:qc], gq[...], co, si, qc // HD).astype(bf16)
    kv[:, :kc] = turn_heads(rt[qc:], gk[...], co, si, kc // HD).T.astype(bf16)


def attend_kernel(dims, qc, kc, oc, idx, q_t, kv_own, kv_partner, w_low, w_high, *refs):
    nx, nz, nc, n = dims
    kv, attn_t, attn_b, log_total = refs[:4]
    pieces = refs[4 : 4 + n]
    acc, tot = refs[4 + n :]
    span = q_t.shape[1]
    me = idx[1] * nc + idx[2]
    for other, src in enumerate((kv_own, kv_partner)):
        core = idx[2] if other == 0 else 1 - idx[2]
        for zr in range(nz):
            block = rot_index(idx[1], nz - zr, nz) * nc + core
            kv[ds(block, span), :] = src[zr * span : (zr + 1) * span, :]
    heads, kv_heads = qc // HD, kc // HD
    group = heads // kv_heads
    acc[...] = jnp.zeros_like(acc)
    tot[...] = jnp.zeros_like(tot)
    keys_at = lax.broadcasted_iota(jnp.int32, (span, span), 0)
    query_at = lax.broadcasted_iota(jnp.int32, (span, span), 1)

    def step(j, carry):
        kb = kv[ds(j, span), :kc]
        vt = kv[ds(j, span), kc:].T
        allowed = keys_at + j * span <= query_at + me * span
        for h in range(heads):
            g = h // group
            s = dot(kb[:, g * HD : (g + 1) * HD], q_t[h * HD : (h + 1) * HD, :])
            e = jnp.where(allowed, jnp.exp(s * SCALE), 0.0)
            tot[h : h + 1, :] += jnp.sum(e, axis=0, keepdims=True)
            acc[h * HD : (h + 1) * HD, :] += dot(vt[g * HD : (g + 1) * HD], e.astype(bf16))
        return carry

    lax.fori_loop(0, me + 1, step, 0)
    for h in range(heads):
        rows = slice(h * HD, (h + 1) * HD)
        attn_t[rows, :] = acc[rows, :] / tot[h : h + 1, :]
    log_total[...] = jnp.log(jnp.maximum(tot[...], 1e-30))
    attn = attn_t[...].T.astype(bf16)
    attn_b[...] = attn
    part = w_low.shape[0] // n
    for k in range(n):
        rows = ds(rot_index(idx[3], k, n), part)
        out = dot(attn[:, :PAD], w_low[rows, :], NT) + dot(attn[:, PAD:], w_high[rows, :], NT)
        pieces[k][...] = out.astype(bf16)


def ffn_kernel(dims, own, idx, base, gains, cot, *refs):
    n = dims[3]
    sums = refs[:n]
    wg, wu, wd = refs[n : n + 3]
    middle, normed, big = refs[n + 3 : n + 6]
    pieces = refs[n + 6 : n + 6 + n]
    acc = refs[n + 6 + n]
    j = pl.program_id(0)
    part = sums[0].shape[1]

    @pl.when(j == 0)
    def _():
        for k in range(n):
            at = ds(rot_index(idx[3], n - k, n), part)
            middle[:, at] = base[:, at].astype(f32) + sums[k][...].astype(f32)
        m = middle[...]
        v = m * lax.rsqrt(jnp.mean(m * m, axis=1, keepdims=True) + EPS) * gains[1:2, :]
        v = v.astype(bf16)
        normed[...] = v
        acc[...] = jnp.zeros_like(acc)

    v = normed[...]
    block = wg.shape[1]
    ff = big.shape[1] // 3
    gate = dot(v, wg[...])
    up = dot(v, wu[...])
    hg = dot(cot[...], wd[...])
    sig = 1.0 / (1.0 + jnp.exp(-gate))
    act = gate * sig
    hidden = (act * up).astype(bf16)
    gate_gb = (hg * up * (sig + act * (1.0 - sig))).astype(bf16)
    up_gb = (hg * act).astype(bf16)
    big[:, pl.ds(pl.multiple_of(j * block, block), block)] = gate_gb
    big[:, pl.ds(pl.multiple_of(ff + j * block, PAD), block)] = up_gb
    big[:, pl.ds(pl.multiple_of(2 * ff + j * block, PAD), block)] = hidden
    acc[...] += dot(gate_gb, wg[...], NT) + dot(up_gb, wu[...], NT)

    @pl.when(j == pl.num_programs(0) - 1)
    def _():
        for k in range(n):
            pieces[k][...] = acc[:, ds(rot_index(idx[3], k, n), part)].astype(bf16)


def down_kernel(dims, idx, hidden, wd, *refs):
    n = dims[3]
    part = wd.shape[0] // n
    for k in range(n):
        rows = ds(rot_index(idx[3], k, n), part)
        refs[k][...] = dot(hidden[...], wd[rows, :], NT).astype(bf16)


def ffn_grad_kernel(dims, own, idx, normed, cot_rel, big, keep, send, normed_rel, turned):
    j = pl.program_id(0)

    @pl.when(j == 0)
    def _():
        turned[...] = normed[...].T
        store_relative(dims, idx, normed_rel, turned, own)

    half = keep.shape[0]
    of_down = j * 3 >= pl.num_programs(0) * 2

    def write(left):
        out = dot(left[...], big[...]).astype(bf16)
        keep[...] = out[:half]
        send[...] = out[half:]

    pl.when(jnp.logical_not(of_down))(lambda: write(normed_rel))
    pl.when(of_down)(lambda: write(cot_rel))


def attend_back_kernel(dims, own, qc, kc, oc, idx, middle, gains, cot, *refs):
    nx, nz, nc, n = dims
    grads = refs[:n]
    w_low, w_high, attn_t, q_t, raw_t, kv, log_total, gq, cosine, sine = refs[n : n + 10]
    mine, rel, gain_two, q_gb, gq_grad, kv_keep, kv_send = refs[n + 10 : n + 17]
    full, turned, dq, do_t, delta, mid_grad = refs[n + 17 :]
    span = q_t.shape[1]
    me = idx[1] * nc + idx[2]
    heads, kv_heads = qc // HD, kc // HD
    group = heads // kv_heads
    assemble(idx, n, grads, full)
    m = middle[...]
    r = lax.rsqrt(jnp.mean(m * m, axis=1, keepdims=True) + EPS)
    unit = m * r
    ng = full[...].astype(f32)
    gain_two[...] = jnp.broadcast_to(jnp.sum(ng * unit, axis=0, keepdims=True), gain_two.shape)
    gg = ng * gains[1:2, :]
    mg = cot[...].astype(f32) + r * (gg - unit * jnp.mean(gg * unit, axis=1, keepdims=True))
    mid_grad[...] = mg
    part = grads[0].shape[1]
    mine[...] = mid_grad[:, ds(idx[3], part)]
    mgb = mg.astype(bf16)
    turned[...] = mgb.T
    store_relative(dims, idx, rel, turned, own)
    ag = jnp.concatenate([dot(mgb, w_low[...]), dot(mgb, w_high[...])], axis=1)
    do = ag.astype(bf16)
    ag_t = ag.T
    do_t[...] = ag_t.astype(bf16)
    prod = ag_t * attn_t[...]
    for h in range(heads):
        delta[h : h + 1, :] = jnp.sum(prod[h * HD : (h + 1) * HD], axis=0, keepdims=True)
    q = q_t[...].T
    dq[...] = jnp.zeros_like(dq)
    keys_at = lax.broadcasted_iota(jnp.int32, (span, span), 0)
    query_at = lax.broadcasted_iota(jnp.int32, (span, span), 1)
    for other, out in enumerate((kv_keep, kv_send)):
        core = idx[2] if other == 0 else 1 - idx[2]

        def step(zr, carry, out=out, core=core):
            j = rot_index(idx[1], zr, nz) * nc + core
            at = ds(zr, span)

            @pl.when(j > me)
            def _():
                out[at, :] = jnp.zeros((span, 2 * kc), bf16)

            @pl.when(j <= me)
            def _():
                kb = kv[ds(j, span), :kc]
                vb = kv[ds(j, span), kc:]
                kt = kb.T
                allowed = keys_at + j * span <= query_at + me * span
                for g in range(kv_heads):
                    cols = slice(g * HD, (g + 1) * HD)
                    dk = jnp.zeros((span, HD), f32)
                    dv = jnp.zeros((span, HD), f32)
                    for h in range(g * group, (g + 1) * group):
                        rows = slice(h * HD, (h + 1) * HD)
                        s = dot(kb[:, cols], q_t[rows, :])
                        p = jnp.where(allowed, jnp.exp(s * SCALE - log_total[h : h + 1, :]), 0.0)
                        dp = dot(vb[:, cols], do_t[rows, :])
                        sg = (p * (dp - delta[h : h + 1, :])).astype(bf16)
                        dq[rows, :] += dot(kt[cols], sg)
                        dk = dk + dot(sg, q[:, rows])
                        dv = dv + dot(p.astype(bf16), do[:, rows])
                    out[at, g * HD : (g + 1) * HD] = (dk * SCALE).astype(bf16)
                    out[at, kc + g * HD : kc + (g + 1) * HD] = dv.astype(bf16)

            return carry

        lax.fori_loop(0, nz, step, 0)
    raw_grad, gain_grad = turn_heads_back(
        raw_t[:qc, :], dq[...] * SCALE, gq[...], cosine[...], sine[...], heads
    )
    gq_grad[...] = gain_grad
    q_gb[...] = raw_grad.T.astype(bf16)


def input_grad_kernel(dims, qc, kc, idx, *refs):
    n, nz = dims[3], dims[1]
    kv_parts = refs[:nz]
    raw_t, gk, cosine, sine, q_gb, w, base, gains = refs[nz : nz + 8]
    qkv_gb, gain_one, gk_grad = refs[nz + 8 : nz + 11]
    pieces = refs[nz + 11 : nz + 11 + n]
    acc = refs[nz + 11 + n]
    total = kv_parts[0][...].astype(f32)
    for k in range(1, nz):
        total = total + kv_parts[k][...].astype(f32)
    raw_grad, gain_grad = turn_heads_back(
        raw_t[qc:, :], total[:, :kc].T, gk[...], cosine[...], sine[...], kc // HD
    )
    gk_grad[...] = gain_grad
    qkv_gb[:, :qc] = q_gb[...]
    qkv_gb[:, qc : qc + kc] = raw_grad.T.astype(bf16)
    qkv_gb[:, qc + kc :] = total[:, kc:].astype(bf16)
    ng = dot(qkv_gb[...], w[:, : qc + 2 * kc], NT)
    acc[...] = ng
    b = base[...].astype(f32)
    unit = b * lax.rsqrt(jnp.mean(b * b, axis=1, keepdims=True) + EPS)
    prod = ng * unit
    gain_one[...] = jnp.broadcast_to(jnp.sum(prod, axis=0, keepdims=True), gain_one.shape)
    along = jnp.sum(prod * gains[0:1, :], axis=1, keepdims=True)
    along = jnp.broadcast_to(along, (along.shape[0], PAD)).T[:16]
    high = along.astype(bf16)
    low = (along - high.astype(f32)).astype(bf16)
    row = lax.broadcasted_iota(jnp.int32, along.shape, 0)
    tail = jnp.where(row == 0, high.astype(f32), low.astype(f32)).astype(bf16)
    part = acc.shape[1] // n
    for k in range(n):
        pieces[k][: along.shape[1], :] = acc[:, ds(rot_index(idx[3], k, n), part)].astype(bf16)
        pieces[k][along.shape[1] :, :] = tail


def attn_grad_kernel(dims, own, qc, kc, oc, idx, one_rel, mid_rel, qkv_gb, attn_b, gain_one, gain_two, gq_grad, gk_grad, keep, send, extra, extra_rel):
    half = keep.shape[0]
    qkv = qc + 2 * kc
    width = one_rel.shape[0]

    def halves(v):
        high = v.astype(bf16).astype(f32)
        return high, v - high

    rows = lax.broadcasted_iota(jnp.int32, (PAD, width), 0)
    lines = jnp.zeros((PAD, width), f32)
    values = halves(gain_one[0:1, :]) + halves(gain_two[0:1, :])
    for i, v in enumerate(values):
        lines = lines + jnp.where(rows == i, v, 0.0)
    cols = lines.T
    heads = jnp.concatenate([gq_grad[...], gk_grad[...]], axis=0)
    high, low = halves(heads)
    lane = lax.broadcasted_iota(jnp.int32, (own, PAD), 1)
    tile = jnp.zeros((own, PAD), f32)
    count = 2 * HD // own
    for i in range(count):
        at = slice(i * own, (i + 1) * own)
        tile = tile + jnp.where(lane == 4 + i, high[at], 0.0)
        tile = tile + jnp.where(lane == 4 + count + i, low[at], 0.0)
    for i in range(width // own):
        extra[i * own : (i + 1) * own, :] = (cols[i * own : (i + 1) * own] + tile).astype(bf16)
    store_relative(dims, idx, extra_rel, extra, own)
    a = dot(one_rel[...], qkv_gb[...]).astype(bf16)
    b = dot(mid_rel[...], attn_b[...]).astype(bf16)
    for out, at in ((keep, slice(0, half)), (send, slice(half, 2 * half))):
        out[:, :qkv] = a[at]
        out[:, qkv : qkv + oc] = b[at]
        out[:, qkv + oc :] = extra_rel[at, :]


def core_sum(keep, send, n):
    got = shift(send, "core", 1)
    step = keep.shape[0] // n
    return [
        (keep[k * step : (k + 1) * step].astype(f32) + got[k * step : (k + 1) * step].astype(f32)).astype(bf16)
        for k in range(n)
    ]


def row_sum(x, axis):
    step = x.shape[0] // lax.axis_size(axis)
    return summed([x[k * step : (k + 1) * step] for k in range(lax.axis_size(axis))], axis)


def after(values, others):
    return lax.optimization_barrier((list(values), others))[0]


def body(
    block_input,
    attn_gain,
    ffn_gain,
    query_gain,
    key_gain,
    query_weight,
    key_weight,
    value_weight,
    out_weight,
    gate_weight,
    up_weight,
    down_weight,
    cotangent,
):
    span, seq_local, part = block_input.shape
    axes = ("dp", "z", "core", "tensor")
    dims = tuple(lax.axis_size(a) for a in axes)
    nx, nz, nc, n = dims
    idx = jnp.stack([lax.axis_index(a) for a in axes]).astype(jnp.int32)
    width = part * n
    own = query_weight.shape[0]
    qc, kc, oc, ff = (w.shape[1] for w in (query_weight, key_weight, out_weight, gate_weight))
    qkv = qc + 2 * kc
    aw = qkv + oc + PAD

    ffn_local = jnp.concatenate([gate_weight, up_weight, down_weight, out_weight], axis=1)
    ffn_w = lax.all_gather(ffn_local, ("dp", "z", "core"), axis=0, tiled=True)

    gains_local = jnp.pad(jnp.stack([attn_gain, ffn_gain], axis=1), ((0, 0), (0, PAD - 2)))
    attn_local = jnp.concatenate([query_weight, key_weight, value_weight, gains_local], axis=1)
    by_z = jnp.concatenate(gathered(attn_local, "z"), axis=0)
    both = jnp.concatenate([block_input.reshape(span, part), cotangent.reshape(span, part)], axis=1)
    both_parts = gathered(both, "tensor")
    w_own = jnp.concatenate(gathered(by_z, "dp"), axis=0)
    cot, cot_rel = call(
        functools.partial(cot_kernel, dims, own),
        [sds((span, width), bf16), sds((width, span), bf16)],
        [idx] + both_parts,
        [pltpu.VMEM((width, span), bf16)],
    )
    w_own, (cot, cot_rel) = lax.optimization_barrier((w_own, (cot, cot_rel)))
    w_partner = shift(w_own, "core", 1)

    my_first = (idx[1] * nc + idx[2]) * span
    positions = (my_first + jnp.arange(span, dtype=jnp.int32)).astype(f32)
    frequency = jnp.power(ROPE_BASE, -2.0 * jnp.arange(HALF, dtype=f32) / HD)
    angle = frequency[:, None] * positions[None, :]
    cosine, sine = jnp.cos(angle), jnp.sin(angle)
    gq = query_gain.astype(f32)[:, None]
    gk = key_gain.astype(f32)[:, None]

    w, base, gains, q_t, raw_t, kv, one_rel = call(
        functools.partial(qkv_kernel, dims, own, qc, kc, oc),
        [
            sds((width, qkv + PAD), bf16),
            sds((span, width), bf16),
            sds((8, width), f32),
            sds((qc, span), bf16),
            sds((qc + kc, span), f32),
            sds((span, 2 * kc), bf16),
            sds((width, span), bf16),
        ],
        [idx] + both_parts + [w_own, w_partner, gq, gk, cosine, sine],
        [pltpu.VMEM((width, span), bf16)],
        flops=2 * span * width * qkv,
    )
    kv_own = jnp.concatenate(gathered(kv, "z"), axis=0)
    kv_partner = shift(kv_own, "core", 1)

    length = span * nz * nc
    block = 384
    const = lambda s: pl.BlockSpec(s, lambda j: (0, 0))
    steps = ff // block
    out_blocks = [pl.BlockSpec((width, PAD), lambda j, o=o: (0, o)) for o in (3 * ff // PAD, 3 * ff // PAD + 1)]
    res = call(
        functools.partial(attend_kernel, dims, qc, kc, oc),
        [
            sds((length, 2 * kc), bf16),
            sds((qc, span), f32),
            sds((span, qc), bf16),
            sds((8, span), f32),
        ]
        + [sds((span, part), bf16)] * n,
        [idx, q_t, kv_own, kv_partner, ffn_w, ffn_w],
        [pltpu.VMEM((qc, span), f32), pltpu.VMEM((8, span), f32)],
        grid=(1,),
        in_specs=[pl.BlockSpec(memory_space=pltpu.SMEM), const((qc, span)), const((length // 2, 2 * kc)), const((length // 2, 2 * kc))]
        + out_blocks,
        out_specs=[const((length, 2 * kc)), const((qc, span)), const((span, qc)), const((8, span))]
        + [const((span, part))] * n,
        flops=4 * span * length * qc,
    )
    kv_full, attn_t, attn_b, log_total = res[:4]
    attn_mine = summed(res[4:], "tensor").astype(bf16)
    attn_parts = gathered(attn_mine, "tensor")

    res = call(
        functools.partial(ffn_kernel, dims, own),
        [sds((span, width), f32), sds((span, width), bf16), sds((span, 3 * ff), bf16)]
        + [sds((span, part), bf16)] * n,
        [idx, base, gains, cot] + attn_parts + [ffn_w] * 3,
        [pltpu.VMEM((span, width), f32)],
        grid=(steps,),
        in_specs=[pl.BlockSpec(memory_space=pltpu.SMEM)]
        + [const((span, width)), const((8, width)), const((span, width))]
        + [const((span, part))] * n
        + [pl.BlockSpec((width, block), lambda j, o=o: (0, o + j)) for o in (0, steps, 2 * steps)],
        out_specs=[const((span, width)), const((span, width)), const((span, 3 * ff))]
        + [const((span, part))] * n,
        flops=10 * span * width * ff,
    )
    middle, normed_two, big = res[:3]
    grad_mine = summed(res[3:], "tensor").astype(bf16)
    grad_parts = gathered(grad_mine, "tensor")

    ffn_keep, ffn_send = call(
        functools.partial(ffn_grad_kernel, dims, own),
        [sds((width // 2, 3 * ff), bf16)] * 2,
        [idx, normed_two, cot_rel, big],
        [pltpu.VMEM((width, span), bf16)] * 2,
        grid=(3 * steps,),
        in_specs=[pl.BlockSpec(memory_space=pltpu.SMEM), const((span, width)), const((width, span)), pl.BlockSpec((span, block), lambda j: (0, j))],
        out_specs=[pl.BlockSpec((width // 2, block), lambda j: (0, j))] * 2,
        flops=6 * span * width * ff,
    )
    ffn_pieces = core_sum(ffn_keep, ffn_send, nx)
    ffn_x = summed(ffn_pieces, "dp").astype(bf16)

    down_parts = call(
        functools.partial(down_kernel, dims),
        [sds((span, part), bf16)] * n,
        [idx, big, ffn_w],
        grid=(1,),
        in_specs=[
            pl.BlockSpec(memory_space=pltpu.SMEM),
            pl.BlockSpec((span, ff), lambda j: (0, 2)),
            pl.BlockSpec((width, ff), lambda j: (0, 2)),
        ],
        out_specs=[const((span, part))] * n,
        flops=2 * span * width * ff,
    )
    me_t = idx[3]
    middle_mine = lax.dynamic_slice_in_dim(middle, me_t * part, part, 1)
    block_output = (middle_mine + summed(down_parts, "tensor")).astype(bf16)

    mine, mid_rel, gain_two, q_gb, gq_grad, kv_keep, kv_send = call(
        functools.partial(attend_back_kernel, dims, own, qc, kc, oc),
        [
            sds((span, part), f32),
            sds((width, span), bf16),
            sds((8, width), f32),
            sds((span, qc), bf16),
            sds((HD, 1), f32),
            sds((length // 2, 2 * kc), bf16),
            sds((length // 2, 2 * kc), bf16),
        ],
        [idx, middle, gains, cot] + grad_parts + [ffn_w, ffn_w, attn_t, q_t, raw_t, kv_full, log_total, gq, cosine, sine],
        [
            pltpu.VMEM((span, width), bf16),
            pltpu.VMEM((width, span), bf16),
            pltpu.VMEM((qc, span), f32),
            pltpu.VMEM((qc, span), bf16),
            pltpu.VMEM((8, span), f32),
            pltpu.VMEM((span, width), f32),
        ],
        grid=(1,),
        in_specs=[pl.BlockSpec(memory_space=pltpu.SMEM), const((span, width)), const((8, width)), const((span, width))]
        + [const((span, part))] * n
        + out_blocks
        + [const(v.shape) for v in (attn_t, q_t, raw_t, kv_full, log_total, gq, cosine, sine)],
        out_specs=[
            const((span, part)),
            const((width, span)),
            const((8, width)),
            const((span, qc)),
            const((HD, 1)),
            const((length // 2, 2 * kc)),
            const((length // 2, 2 * kc)),
        ],
        flops=10 * span * length * qc,
    )
    kv_pieces = core_sum(kv_keep, kv_send, nz)
    kv_parts = [kv_pieces[0]] + [shift(kv_pieces[k], "z", k) for k in range(1, nz)]
    kv_parts, ffn_x = lax.optimization_barrier((kv_parts, ffn_x))

    res = call(
        functools.partial(input_grad_kernel, dims, qc, kc),
        [sds((span, qkv), bf16), sds((8, width), f32), sds((HD, 1), f32)]
        + [sds((span + 16, part), bf16)] * n,
        [idx] + kv_parts + [raw_t, gk, cosine, sine, q_gb, w, base, gains],
        [pltpu.VMEM((span, width), f32)],
        flops=2 * span * width * qkv,
    )
    qkv_gb, gain_one, gk_grad = res[:3]
    norm_mine = summed(res[3:], "tensor")
    along = (norm_mine[span] + norm_mine[span + 1])[:, None] * (1.0 / width)
    base_f = base.astype(f32)
    scale_one = lax.rsqrt(jnp.mean(base_f * base_f, axis=1, keepdims=True) + EPS)
    unit_mine = block_input.reshape(span, part).astype(f32) * scale_one
    gain_mine = lax.dynamic_slice_in_dim(gains, me_t * part, part, 1)[0:1]
    input_grad = (mine + scale_one * (norm_mine[:span] * gain_mine - unit_mine * along)).astype(bf16)

    keep, send = call(
        functools.partial(attn_grad_kernel, dims, own, qc, kc, oc),
        [sds((width // 2, aw), bf16)] * 2,
        [idx, one_rel, mid_rel, qkv_gb, attn_b, gain_one, gain_two, gq_grad, gk_grad],
        [pltpu.VMEM((width, PAD), bf16), pltpu.VMEM((width, PAD), bf16)],
        flops=2 * span * width * (qkv + oc),
    )
    (keep, send), ffn_x = lax.optimization_barrier(((keep, send), ffn_x))
    ffn_sum = row_sum(ffn_x, "z")
    attn_x = summed(core_sum(keep, send, nx), "dp").astype(bf16)
    attn_sum = row_sum(attn_x, "z")
    small = attn_sum[:, qkv + oc :]
    small_all = sum(gathered(small, "tensor"))
    count = 2 * HD // own
    head_sum = (small_all[:, 4 : 4 + count] + small_all[:, 4 + count : 4 + 2 * count]).T.reshape(-1)
    return (
        block_output.reshape(span, seq_local, part),
        input_grad.reshape(span, seq_local, part),
        small_all[:, 0] + small_all[:, 1],
        small[:, 2] + small[:, 3],
        head_sum[:HD],
        head_sum[HD:],
        attn_sum[:, :qc],
        attn_sum[:, qc : qc + kc],
        attn_sum[:, qc + kc : qkv],
        attn_sum[:, qkv : qkv + oc],
        ffn_sum[:, :ff],
        ffn_sum[:, ff : 2 * ff],
        ffn_sum[:, 2 * ff :],
    )


def solution(mesh):
    dp, seq, tensor = (mesh.shape[a] for a in ("dp", "seq", "tensor"))
    grid = Mesh(
        np.asarray(mesh.devices).reshape(dp, seq // 2, 2, tensor), ("dp", "z", "core", "tensor")
    )
    tokens = P(("z", "core"), "dp", "tensor")
    rows = P(("dp", "z", "core"))
    weight = P(("dp", "z", "core"), "tensor")
    return jax.shard_map(
        body,
        mesh=grid,
        in_specs=(tokens, rows, rows, P(), P()) + (weight,) * 7 + (tokens,),
        out_specs=(tokens, tokens, rows, rows, P(), P()) + (weight,) * 7,
        check_vma=False,
    )
```

profile of v0, /device:TPU:0, one launch (start us, length us, event | category | flops | bytes accessed | tf_op | source)
XLA Modules:
  0.0 250.3 jit_solution(5687585464046041462)
XLA Ops:
  7.2 1.7 pad_maximum_fusion.1
  9.9 3.2 %collective-permute-start.2 = (bf16[256,512]{1,0:T(8,128)(2,1)S(1)}, bf16[256,512]{1,0:T(8,128)(2,1)S(1)}, u32[]{:S(2)}, u32[]{:S(2)}) collective-permute-start(bf16[256,512]{1,0:T(8,128)(2,1)S(1)} %pad_maximum_fusion.refs_0_), channel_id=1, source_target_pairs={{0,3},{1,0},{2,1},{3,2},{4,7},{5,4},{6,5},{7,6},{8,11},{9,8},{10,9... | collective-permute-start | bytes 786440 | tf_op jit(solution)/shard_map/ppermute | solution.py:37
  15.3 4.0 %collective-permute-start.4 = (bf16[32,640]{1,0:T(8,128)(2,1)S(1)}, bf16[32,640]{1,0:T(8,128)(2,1)S(1)}, u32[]{:S(2)}, u32[]{:S(2)}) collective-permute-start(bf16[32,640]{1,0:T(8,128)(2,1)S(1)} %get-tuple-element.151), channel_id=1, source_target_pairs={{0,16},{8,24},{16,0},{24,8},{1,17},{9,25},{17,1},{25,9},{2,18},{10... | collective-permute-start | bytes 122888 | tf_op jit(solution)/shard_map/ppermute | solution.py:37
  20.3 2.2 collective-permute-start.5
  26.2 3.1 %collective-permute-start.7 = (bf16[128,640]{1,0:T(8,128)(2,1)S(1)}, bf16[128,640]{1,0:T(8,128)(2,1)S(1)}, u32[]{:S(2)}, u32[]{:S(2)}) collective-permute-start(bf16[128,640]{1,0:T(8,128)(2,1)S(1)} %pad_maximum_fusion.2), channel_id=1, source_target_pairs={{0,64},{32,96},{64,0},{96,32},{1,65},{33,97},{65,1},{97,33},{2,66}... | collective-permute-start | bytes 491528 | tf_op jit(solution)/shard_map/ppermute | solution.py:37
  29.9 8.4 %collective-permute-done.6 = bf16[128,640]{1,0:T(8,128)(2,1)S(1)} collective-permute-done((bf16[128,640]{1,0:T(8,128)(2,1)S(1)}, bf16[128,640]{1,0:T(8,128)(2,1)S(1)}, u32[]{:S(2)}, u32[]{:S(2)}) %collective-permute-start.6) | collective-permute-done | bytes 163872 | tf_op jit(solution)/shard_map/ppermute | solution.py:37
  38.6 5.3 %collective-permute-done.8 = bf16[128,640]{1,0:T(8,128)(2,1)S(1)} collective-permute-done((bf16[128,640]{1,0:T(8,128)(2,1)S(1)}, bf16[128,640]{1,0:T(8,128)(2,1)S(1)}, u32[]{:S(2)}, u32[]{:S(2)}) %collective-permute-start.8) | collective-permute-done | bytes 163872 | tf_op jit(solution)/shard_map/ppermute | solution.py:37
  45.5 2.3 shard_map.228
  50.7 4.1 %shard_map.229 = (bf16[1024,640]{1,0:T(8,128)(2,1)}, bf16[256,1024]{1,0:T(8,128)(2,1)}, f32[8,1024]{1,0:T(8,128)}, bf16[256,256]{1,0:T(8,128)(2,1)}, f32[384,256...) custom-call(s32[4]{0:T(128)} %pad_add_fusion.idx, bf16[256,512]{1,0:T(8,128)(2,1)} %copy-done.3, ...), custom_call_target="tpu_custom_call" | custom-call | flops 268435456 | bytes 5472784 | tf_op jit(solution)/shard_map/pallas_call | solution.py:55
  54.8 1.3 collective-permute-start.10
  56.1 1.9 collective-permute-start.12
  59.8 5.4 %collective-permute-done.10 = bf16[256,256]{1,0:T(8,128)(2,1)S(1)} collective-permute-done((bf16[256,256]{1,0:T(8,128)(2,1)}, bf16[256,256]{1,0:T(8,128)(2,1)S(1)}, u32[]{:S(2)}, u32[]{:S(2)}) %collective-permute-start.10) | collective-permute-done | bytes 131104 | tf_op jit(solution)/shard_map/ppermute | solution.py:37
  65.2 4.5 %collective-permute-done.11 = bf16[256,256]{1,0:T(8,128)(2,1)S(1)} collective-permute-done((bf16[256,256]{1,0:T(8,128)(2,1)}, bf16[256,256]{1,0:T(8,128)(2,1)S(1)}, u32[]{:S(2)}, u32[]{:S(2)}) %collective-permute-start.11) | collective-permute-done | bytes 131104 | tf_op jit(solution)/shard_map/ppermute | solution.py:37
  69.9 1.9 collective-permute-done.13.kv_partner
  72.6 3.8 %shard_map.230 = (bf16[2048,256]{1,0:T(8,128)(2,1)}, f32[256,256]{1,0:T(8,128)}, bf16[256,256]{1,0:T(8,128)(2,1)}, f32[8,256]{1,0:T(8,128)}, bf16[256,256]{1,0:T...) custom-call(s32[4]{0:T(128)} %pad_add_fusion.idx, ...), custom_call_target="tpu_custom_call" | custom-call | flops 536870912 | bytes 18358288 | tf_op jit(solution)/shard_map/pallas_call | solution.py:55
  76.3 1.5 collective-permute-start.14
  77.8 2.7 %collective-permute-start.15 = (bf16[256,256]{1,0:T(8,128)(2,1)}, bf16[256,256]{1,0:T(8,128)(2,1)S(1)}, u32[]{:S(2)}, u32[]{:S(2)}) collective-permute-start(bf16[256,256]{1,0:T(8,128)(2,1)} %get-tuple-element.80), channel_id=1, source_target_pairs={{0,2},{1,3},{2,0},{3,1},{4,6},{5,7},{6,4},{7,5},{8,10},{9,11},{10,... | collective-permute-start | bytes 393224 | tf_op jit(solution)/shard_map/ppermute | solution.py:37
  80.5 1.4 collective-permute-start.16
  82.0 2.0 collective-permute-done.14
  84.0 3.8 %collective-permute-done.15 = bf16[256,256]{1,0:T(8,128)(2,1)S(1)} collective-permute-done((bf16[256,256]{1,0:T(8,128)(2,1)}, bf16[256,256]{1,0:T(8,128)(2,1)S(1)}, u32[]{:S(2)}, u32[]{:S(2)}) %collective-permute-start.15) | collective-permute-done | bytes 131104 | tf_op jit(solution)/shard_map/ppermute | solution.py:37
  88.8 2.6 %collective-permute-start.19 = (bf16[256,256]{1,0:T(8,128)(2,1)S(1)}, bf16[256,256]{1,0:T(8,128)(2,1)S(1)}, u32[]{:S(2)}, u32[]{:S(2)}) collective-permute-start(bf16[256,256]{1,0:T(8,128)(2,1)S(1)} %add_convert_fusion.16.refs_0_), channel_id=1, source_target_pairs={{0,3},{1,0},{2,1},{3,2},{4,7},{5,4},{6,5},{7,6},{8,11},{9,8},{10,9... | collective-permute-start | bytes 393224 | tf_op jit(solution)/shard_map/ppermute | solution.py:37
  93.2 4.0 %collective-permute-done.19.refs_3_ = bf16[256,256]{1,0:T(8,128)(2,1)S(1)} collective-permute-done((bf16[256,256]{1,0:T(8,128)(2,1)S(1)}, bf16[256,256]{1,0:T(8,128)(2,1)S(1)}, u32[]{:S(2)}, u32[]{:S(2)}) %collective-permute-start.19) | collective-permute-done | bytes 131104 | tf_op jit(solution)/shard_map/ppermute | solution.py:37
  97.2 2.1 collective-permute-done.18.refs_2_
  99.3 1.6 collective-permute-done.17.refs_1_
  101.5 9.8 %shard_map.231 = (f32[256,1024]{1,0:T(8,128)}, bf16[256,1024]{1,0:T(8,128)(2,1)}, bf16[256,3456]{1,0:T(8,128)(2,1)}, bf16[256,256]{1,0:T(8,128)(2,1)}, bf16[256,...) custom-call(s32[4]{0:T(128)} %pad_add_fusion.idx, ...), custom_call_target="tpu_custom_call" | custom-call | flops 3019898880 | bytes 28278800 | tf_op jit(solution)/shard_map/pallas_call | solution.py:55
  111.4 9.7 %shard_map.234 = (bf16[512,3456]{1,0:T(8,128)(2,1)}, bf16[512,3456]{1,0:T(8,128)(2,1)}) custom-call(s32[4]{0:T(128)} %pad_add_fusion.idx, bf16[256,1024]{1,0:T(8,128)(2,1)} %get-tuple-element.99.normed, bf16[1024,256]{1,0:T(8,128)(2,1)} %get-tuple-element.100.cot_rel, bf16[256,3456]{1,0:T(8,128)(2,1)} %get-tuple-element.83.hidden.big), custom_call_target="tpu_custom_call" | custom-call | flops 1811939328 | bytes 9895952 | tf_op jit(solution)/shard_map/pallas_call | solution.py:55
  121.1 2.0 collective-permute-start.24
  123.1 1.4 collective-permute-start.25
  124.8 3.6 %shard_map.232 = (bf16[256,256]{1,0:T(8,128)(2,1)}, bf16[256,256]{1,0:T(8,128)(2,1)}, bf16[256,256]{1,0:T(8,128)(2,1)}, bf16[256,256]{1,0:T(8,128)(2,1)}) custom-call(s32[4]{0:T(128)} %pad_add_fusion.idx, bf16[256,3456]{1,0:T(8,128)(2,1)} %get-tuple-element.83.hidden.big, bf16[1024,3712]{1,0:T(8,128)(2,1)} %all-gather.2.cloned.1.call-done.w_low.w_high.refs_4_.refs_5_.refs_6_.wd), custom_call_target="tpu_custom_call" | custom-call | flops 603979776 | bytes 9895952 | tf_op jit(solution)/shard_map/pallas_call | solution.py:55
  129.0 2.3 collective-permute-done.23
  133.1 2.4 collective-permute-start.28
  136.2 1.3 collective-permute-start.26
  137.5 3.6 %add_convert_fusion.3 = (bf16[128,3456]{1,0:T(8,128)(2,1)}, bf16[128,3456]{1,0:T(8,128)(2,1)}, bf16[128,3456]{1,0:T(8,128)(2,1)}) fusion(bf16[512,3456]{1,0:T(8,128)(2,1)} %collective-permute-done.33, bf16[512,3456]{1,0:T(8,128)(2,1)S(1)} %copy-done.1), kind=kLoop, calls=%fused_computation.3 | loop fusion | flops 5308416 | bytes 7962624 | tf_op jit(solution)/shard_map/convert_element_type | solution.py:419
  141.1 1.5 collective-permute-start.34
  143.3 2.7 %collective-permute-start.36 = (bf16[128,3456]{1,0:T(8,128)(2,1)}, bf16[128,3456]{1,0:T(8,128)(2,1)}, u32[]{:S(2)}, u32[]{:S(2)}) collective-permute-start(bf16[128,3456]{1,0:T(8,128)(2,1)} %get-tuple-element.128), channel_id=1, source_target_pairs={{0,96},{32,0},{64,32},{96,64},{1,97},{33,1},{65,33},{97,65},{2,98}... | collective-permute-start | bytes 2654216 | tf_op jit(solution)/shard_map/ppermute | solution.py:37
  146.0 2.1 collective-permute-start.35
  148.1 6.5 %shard_map.233 = (f32[256,256]{1,0:T(8,128)}, bf16[1024,256]{1,0:T(8,128)(2,1)}, f32[8,1024]{1,0:T(8,128)}, bf16[256,256]{1,0:T(8,128)(2,1)}, f32[64,1]{1,0:T(8,...) custom-call(s32[4]{0:T(128)} %pad_add_fusion.idx, f32[256,1024]{1,0:T(8,128)} %get-tuple-element.82.middle, ...), custom_call_target="tpu_custom_call" | custom-call | flops 1342177280 | bytes 21242384 | tf_op jit(solution)/shard_map/pallas_call | solution.py:55
  154.6 2.1 collective-permute-start.22
  157.4 3.6 %collective-permute-done.22 = bf16[256,256]{1,0:T(8,128)(2,1)S(1)} collective-permute-done((bf16[256,256]{1,0:T(8,128)(2,1)}, bf16[256,256]{1,0:T(8,128)(2,1)S(1)}, u32[]{:S(2)}, u32[]{:S(2)}) %collective-permute-start.22) | collective-permute-done | bytes 131104 | tf_op jit(solution)/shard_map/ppermute | solution.py:37
  161.1 1.9 fusion.4
  162.9 1.9 add_convert_fusion.10
  164.8 14.7 %collective-permute-start.32 = (bf16[256,256]{1,0:T(8,128)(2,1)S(1)}, bf16[256,256]{1,0:T(8,128)(2,1)S(1)}, u32[]{:S(2)}, u32[]{:S(2)}) collective-permute-start(bf16[256,256]{1,0:T(8,128)(2,1)S(1)} %get-tuple-element.133), channel_id=1, source_target_pairs={{0,24},{8,0},{16,8},{24,16},{1,25},{9,1},{17,9},{25,17},{2,26},{10... | collective-permute-start | bytes 393224 | tf_op jit(solution)/shard_map/ppermute | solution.py:37
  181.5 1.2 collective-permute-done.35
  182.7 3.4 %add_convert_fusion = bf16[128,3456]{1,0:T(8,128)(2,1)} fusion(bf16[128,3456]{1,0:T(8,128)(2,1)} %collective-permute-done.36, bf16[128,3456]{1,0:T(8,128)(2,1)} %collective-permute-done.35, bf16[128,3456]{1,0:T(8,128)(2,1)} %collective-permute-done.34, bf16[512,3456]{1,0:T(8,128)(2,1)} %collective-permute-done.33, bf16[512,3456]{1,0:T(8,128)(2,1)S(1)} %copy-done.1), kind=kLoop, calls=%fused_computation | loop fusion | flops 5308416 | bytes 5308416 | tf_op jit(solution)/shard_map/convert_element_type | solution.py:560
  186.1 1.2 collective-permute-done.31.refs_2_
  187.4 1.3 collective-permute-done.30.refs_1_
  189.4 3.6 %shard_map.235 = (bf16[256,512]{1,0:T(8,128)(2,1)}, f32[8,1024]{1,0:T(8,128)}, f32[64,1]{1,0:T(8,128)}, bf16[272,256]{1,0:T(8,128)(2,1)}, bf16[272,256]{1,0:T(8,...) custom-call(s32[4]{0:T(128)} %pad_add_fusion.idx, bf16[256,256]{1,0:T(8,128)(2,1)} %get-tuple-element.103.refs_0_, ...), custom_call_target="tpu_custom_call" | custom-call | flops 268435456 | bytes 3834384 | tf_op jit(solution)/shard_map/pallas_call | solution.py:55
  193.1 1.9 collective-permute-start.38
  194.9 1.4 collective-permute-start.39
  196.3 3.2 %shard_map.236 = (bf16[512,896]{1,0:T(8,128)(2,1)}, bf16[512,896]{1,0:T(8,128)(2,1)}) custom-call(s32[4]{0:T(128)} %pad_add_fusion.idx, bf16[1024,256]{1,0:T(8,128)(2,1)} %get-tuple-element.113.one_rel, bf16[1024,256]{1,0:T(8,128)(2,1)} %get-tuple-element.114.mid_rel, bf16[256,512]{1,0:T(8,128)(2,1)} %get-tuple-element.115.qkv_gb, ...), custom_call_target="tpu_custom_call" | custom-call | flops 402653184 | bytes 3342864 | tf_op jit(solution)/shard_map/pallas_call | solution.py:55
  199.6 1.8 collective-permute-start.50
  201.4 1.3 collective-permute-done.37
  202.7 3.1 %collective-permute-start.52 = (bf16[32,3456]{1,0:T(8,128)(2,1)S(1)}, bf16[32,3456]{1,0:T(8,128)(2,1)S(1)}, u32[]{:S(2)}, u32[]{:S(2)}) collective-permute-start(bf16[32,3456]{1,0:T(8,128)(2,1)S(1)} %get-tuple-element.138), channel_id=1, source_target_pairs={{0,24},{8,0},{16,8},{24,16},{1,25},{9,1},{17,9},{25,17},{2,26},{10... | collective-permute-start | bytes 663560 | tf_op jit(solution)/shard_map/ppermute | solution.py:37
  205.8 1.5 collective-permute-start.51
  208.4 1.2 collective-permute-start.41
  209.6 2.1 collective-permute-start.43
  212.7 3.3 %collective-permute-done.52 = bf16[32,3456]{1,0:T(8,128)(2,1)S(1)} collective-permute-done((bf16[32,3456]{1,0:T(8,128)(2,1)S(1)}, bf16[32,3456]{1,0:T(8,128)(2,1)S(1)}, u32[]{:S(2)}, u32[]{:S(2)}) %collective-permute-start.52) | collective-permute-done | bytes 221216 | tf_op jit(solution)/shard_map/ppermute | solution.py:37
  215.9 1.8 collective-permute-done.51
  217.9 3.4 %collective-permute-done.43 = bf16[128,896]{1,0:T(8,128)(2,1)S(1)} collective-permute-done((bf16[128,896]{1,0:T(8,128)(2,1)S(1)}, bf16[128,896]{1,0:T(8,128)(2,1)S(1)}, u32[]{:S(2)}, u32[]{:S(2)}) %collective-permute-start.43) | collective-permute-done | bytes 229408 | tf_op jit(solution)/shard_map/ppermute | solution.py:37
  223.6 2.2 collective-permute-start.46
  228.1 3.3 %collective-permute-done.45 = bf16[32,896]{1,0:T(8,128)(2,1)S(1)} collective-permute-done((bf16[32,896]{1,0:T(8,128)(2,1)S(1)}, bf16[32,896]{1,0:T(8,128)(2,1)S(1)}, u32[]{:S(2)}, u32[]{:S(2)}) %collective-permute-start.45) | collective-permute-done | bytes 57376 | tf_op jit(solution)/shard_map/ppermute | solution.py:37
  231.5 1.8 collective-permute-start.48
  233.2 2.4 collective-permute-start.49
  237.1 3.5 %collective-permute-done.47 = f32[32,128]{1,0:T(8,128)S(1)} collective-permute-done((f32[32,128]{1,0:T(8,128)S(1)}, f32[32,128]{1,0:T(8,128)S(1)}, u32[]{:S(2)}, u32[]{:S(2)}) %collective-permute-start.47) | collective-permute-done | bytes 16416 | tf_op jit(solution)/shard_map/ppermute | solution.py:37
  (163 shorter events, 37.9 us)
Async XLA Ops:
  7.2 64.6 %all-gather.2.cloned.1.call-start = ((), (), s32[]{:S(2)}) async-start(), calls=%async_computation | async-start | bytes 7839744 | tf_op jit(solution)/shard_map/all_gather | solution.py:460
  8.9 38.9 %copy-start.26 = (bf16[64]{0:T(256)(128)(2,1)S(1)}, bf16[64]{0:T(256)(128)(2,1)}, u32[]{:S(2)}) copy-start(bf16[64]{0:T(256)(128)(2,1)} %param.16) | copy-start | bytes 388
  9.9 34.0 %copy-start.3 = (bf16[256,512]{1,0:T(8,128)(2,1)}, bf16[256,512]{1,0:T(8,128)(2,1)S(1)}, u32[]{:S(2)}) copy-start(bf16[256,512]{1,0:T(8,128)(2,1)S(1)} %pad_maximum_fusion.refs_0_) | copy-start | bytes 786436
  9.9 33.9 %collective-permute-start.2 = (bf16[256,512]{1,0:T(8,128)(2,1)S(1)}, bf16[256,512]{1,0:T(8,128)(2,1)S(1)}, u32[]{:S(2)}, u32[]{:S(2)}) collective-permute-start(bf16[256,512]{1,0:T(8,128)(2,1)S(1)} %pad_maximum_fusion.refs_0_), channel_id=1, source_target_pairs={{0,3},{1,0},{2,1},{3,2},{4,7},{5,4},{6,5},{7,6},{8,11},{9,8},{10,9... | collective-permute-start | bytes 786440 | tf_op jit(solution)/shard_map/ppermute | solution.py:37
  13.1 30.8 %collective-permute-start.1 = (bf16[256,512]{1,0:T(8,128)(2,1)S(1)}, bf16[256,512]{1,0:T(8,128)(2,1)S(1)}, u32[]{:S(2)}, u32[]{:S(2)}) collective-permute-start(bf16[256,512]{1,0:T(8,128)(2,1)S(1)} %pad_maximum_fusion.refs_0_), channel_id=1, source_target_pairs={{0,2},{1,3},{2,0},{3,1},{4,6},{5,7},{6,4},{7,5},{8,10},{9,11},{10,... | collective-permute-start | bytes 786440 | tf_op jit(solution)/shard_map/ppermute | solution.py:37
  15.3 9.1 %collective-permute-start.4 = (bf16[32,640]{1,0:T(8,128)(2,1)S(1)}, bf16[32,640]{1,0:T(8,128)(2,1)S(1)}, u32[]{:S(2)}, u32[]{:S(2)}) collective-permute-start(bf16[32,640]{1,0:T(8,128)(2,1)S(1)} %get-tuple-element.151), channel_id=1, source_target_pairs={{0,16},{8,24},{16,0},{24,8},{1,17},{9,25},{17,1},{25,9},{2,18},{10... | collective-permute-start | bytes 122888 | tf_op jit(solution)/shard_map/ppermute | solution.py:37
  19.2 6.2 %collective-permute-start.3 = (bf16[32,640]{1,0:T(8,128)(2,1)S(1)}, bf16[32,640]{1,0:T(8,128)(2,1)S(1)}, u32[]{:S(2)}, u32[]{:S(2)}) collective-permute-start(bf16[32,640]{1,0:T(8,128)(2,1)S(1)} %get-tuple-element.151), channel_id=1, source_target_pairs={{0,8},{8,16},{16,24},{24,0},{1,9},{9,17},{17,25},{25,1},{2,10},{10... | collective-permute-start | bytes 122888 | tf_op jit(solution)/shard_map/ppermute | solution.py:37
  20.3 5.2 %collective-permute-start.5 = (bf16[32,640]{1,0:T(8,128)(2,1)S(1)}, bf16[32,640]{1,0:T(8,128)(2,1)S(1)}, u32[]{:S(2)}, u32[]{:S(2)}) collective-permute-start(bf16[32,640]{1,0:T(8,128)(2,1)S(1)} %get-tuple-element.151), channel_id=1, source_target_pairs={{0,24},{8,0},{16,8},{24,16},{1,25},{9,1},{17,9},{25,17},{2,26},{10... | collective-permute-start | bytes 122888 | tf_op jit(solution)/shard_map/ppermute | solution.py:37
  24.4 19.5 %collective-permute-start = (bf16[256,512]{1,0:T(8,128)(2,1)S(1)}, bf16[256,512]{1,0:T(8,128)(2,1)S(1)}, u32[]{:S(2)}, u32[]{:S(2)}) collective-permute-start(bf16[256,512]{1,0:T(8,128)(2,1)S(1)} %pad_maximum_fusion.refs_0_), channel_id=1, source_target_pairs={{0,1},{1,2},{2,3},{3,0},{4,5},{5,6},{6,7},{7,4},{8,9},{9,10},{10,1... | collective-permute-start | bytes 786440 | tf_op jit(solution)/shard_map/ppermute | solution.py:37
  26.2 12.3 %collective-permute-start.7 = (bf16[128,640]{1,0:T(8,128)(2,1)S(1)}, bf16[128,640]{1,0:T(8,128)(2,1)S(1)}, u32[]{:S(2)}, u32[]{:S(2)}) collective-permute-start(bf16[128,640]{1,0:T(8,128)(2,1)S(1)} %pad_maximum_fusion.2), channel_id=1, source_target_pairs={{0,64},{32,96},{64,0},{96,32},{1,65},{33,97},{65,1},{97,33},{2,66}... | collective-permute-start | bytes 491528 | tf_op jit(solution)/shard_map/ppermute | solution.py:37
  29.3 9.0 %collective-permute-start.6 = (bf16[128,640]{1,0:T(8,128)(2,1)S(1)}, bf16[128,640]{1,0:T(8,128)(2,1)S(1)}, u32[]{:S(2)}, u32[]{:S(2)}) collective-permute-start(bf16[128,640]{1,0:T(8,128)(2,1)S(1)} %pad_maximum_fusion.2), channel_id=1, source_target_pairs={{0,32},{32,64},{64,96},{96,0},{1,33},{33,65},{65,97},{97,1},{2,34}... | collective-permute-start | bytes 491528 | tf_op jit(solution)/shard_map/ppermute | solution.py:37
  38.3 5.5 %collective-permute-start.8 = (bf16[128,640]{1,0:T(8,128)(2,1)S(1)}, bf16[128,640]{1,0:T(8,128)(2,1)S(1)}, u32[]{:S(2)}, u32[]{:S(2)}) collective-permute-start(bf16[128,640]{1,0:T(8,128)(2,1)S(1)} %pad_maximum_fusion.2), channel_id=1, source_target_pairs={{0,96},{32,0},{64,32},{96,64},{1,97},{33,1},{65,33},{97,65},{2,98}... | collective-permute-start | bytes 491528 | tf_op jit(solution)/shard_map/ppermute | solution.py:37
  47.8 2.1 collective-permute-start.9
  54.8 10.4 %collective-permute-start.10 = (bf16[256,256]{1,0:T(8,128)(2,1)}, bf16[256,256]{1,0:T(8,128)(2,1)S(1)}, u32[]{:S(2)}, u32[]{:S(2)}) collective-permute-start(bf16[256,256]{1,0:T(8,128)(2,1)} %get-tuple-element.77), channel_id=1, source_target_pairs={{0,8},{8,16},{16,24},{24,0},{1,9},{9,17},{17,25},{25,1},{2,10},{10... | collective-permute-start | bytes 393224 | tf_op jit(solution)/shard_map/ppermute | solution.py:37
  56.1 13.6 %collective-permute-start.12 = (bf16[256,256]{1,0:T(8,128)(2,1)}, bf16[256,256]{1,0:T(8,128)(2,1)S(1)}, u32[]{:S(2)}, u32[]{:S(2)}) collective-permute-start(bf16[256,256]{1,0:T(8,128)(2,1)} %get-tuple-element.77), channel_id=1, source_target_pairs={{0,24},{8,0},{16,8},{24,16},{1,25},{9,1},{17,9},{25,17},{2,26},{10... | collective-permute-start | bytes 393224 | tf_op jit(solution)/shard_map/ppermute | solution.py:37
  58.0 11.7 %collective-permute-start.11 = (bf16[256,256]{1,0:T(8,128)(2,1)}, bf16[256,256]{1,0:T(8,128)(2,1)S(1)}, u32[]{:S(2)}, u32[]{:S(2)}) collective-permute-start(bf16[256,256]{1,0:T(8,128)(2,1)} %get-tuple-element.77), channel_id=1, source_target_pairs={{0,16},{8,24},{16,0},{24,8},{1,17},{9,25},{17,1},{25,9},{2,18},{10... | collective-permute-start | bytes 393224 | tf_op jit(solution)/shard_map/ppermute | solution.py:37
  69.8 2.0 collective-permute-start.13
  76.3 7.7 %collective-permute-start.14 = (bf16[256,256]{1,0:T(8,128)(2,1)}, bf16[256,256]{1,0:T(8,128)(2,1)S(1)}, u32[]{:S(2)}, u32[]{:S(2)}) collective-permute-start(bf16[256,256]{1,0:T(8,128)(2,1)} %get-tuple-element.79), channel_id=1, source_target_pairs={{0,1},{1,2},{2,3},{3,0},{4,5},{5,6},{6,7},{7,4},{8,9},{9,10},{10,1... | collective-permute-start | bytes 393224 | tf_op jit(solution)/shard_map/ppermute | solution.py:37
  77.8 9.9 %collective-permute-start.15 = (bf16[256,256]{1,0:T(8,128)(2,1)}, bf16[256,256]{1,0:T(8,128)(2,1)S(1)}, u32[]{:S(2)}, u32[]{:S(2)}) collective-permute-start(bf16[256,256]{1,0:T(8,128)(2,1)} %get-tuple-element.80), channel_id=1, source_target_pairs={{0,2},{1,3},{2,0},{3,1},{4,6},{5,7},{6,4},{7,5},{8,10},{9,11},{10,... | collective-permute-start | bytes 393224 | tf_op jit(solution)/shard_map/ppermute | solution.py:37
  80.5 7.2 %collective-permute-start.16 = (bf16[256,256]{1,0:T(8,128)(2,1)}, bf16[256,256]{1,0:T(8,128)(2,1)S(1)}, u32[]{:S(2)}, u32[]{:S(2)}) collective-permute-start(bf16[256,256]{1,0:T(8,128)(2,1)} %get-tuple-element.81), channel_id=1, source_target_pairs={{0,3},{1,0},{2,1},{3,2},{4,7},{5,4},{6,5},{7,6},{8,11},{9,8},{10,9... | collective-permute-start | bytes 393224 | tf_op jit(solution)/shard_map/ppermute | solution.py:37
  88.7 12.1 %copy-start.12 = (bf16[256,256]{1,0:T(8,128)(2,1)}, bf16[256,256]{1,0:T(8,128)(2,1)S(1)}, u32[]{:S(2)}) copy-start(bf16[256,256]{1,0:T(8,128)(2,1)S(1)} %add_convert_fusion.16.refs_0_) | copy-start | bytes 393220
  88.8 8.5 %collective-permute-start.19 = (bf16[256,256]{1,0:T(8,128)(2,1)S(1)}, bf16[256,256]{1,0:T(8,128)(2,1)S(1)}, u32[]{:S(2)}, u32[]{:S(2)}) collective-permute-start(bf16[256,256]{1,0:T(8,128)(2,1)S(1)} %add_convert_fusion.16.refs_0_), channel_id=1, source_target_pairs={{0,3},{1,0},{2,1},{3,2},{4,7},{5,4},{6,5},{7,6},{8,11},{9,8},{10,9... | collective-permute-start | bytes 393224 | tf_op jit(solution)/shard_map/ppermute | solution.py:37
  91.4 7.9 %collective-permute-start.18 = (bf16[256,256]{1,0:T(8,128)(2,1)S(1)}, bf16[256,256]{1,0:T(8,128)(2,1)S(1)}, u32[]{:S(2)}, u32[]{:S(2)}) collective-permute-start(bf16[256,256]{1,0:T(8,128)(2,1)S(1)} %add_convert_fusion.16.refs_0_), channel_id=1, source_target_pairs={{0,2},{1,3},{2,0},{3,1},{4,6},{5,7},{6,4},{7,5},{8,10},{9,11},{10,... | collective-permute-start | bytes 393224 | tf_op jit(solution)/shard_map/ppermute | solution.py:37
  92.5 8.4 %collective-permute-start.17 = (bf16[256,256]{1,0:T(8,128)(2,1)S(1)}, bf16[256,256]{1,0:T(8,128)(2,1)S(1)}, u32[]{:S(2)}, u32[]{:S(2)}) collective-permute-start(bf16[256,256]{1,0:T(8,128)(2,1)S(1)} %add_convert_fusion.16.refs_0_), channel_id=1, source_target_pairs={{0,1},{1,2},{2,3},{3,0},{4,5},{5,6},{6,7},{7,4},{8,9},{9,10},{10,1... | collective-permute-start | bytes 393224 | tf_op jit(solution)/shard_map/ppermute | solution.py:37
  111.3 13.2 %copy-start = (bf16[256,1024]{1,0:T(8,128)(2,1)S(1)}, bf16[256,1024]{1,0:T(8,128)(2,1)}, u32[]{:S(2)}) copy-start(bf16[256,1024]{1,0:T(8,128)(2,1)} %get-tuple-element.73.base.refs_10_) | copy-start | bytes 1572868
  121.1 15.1 %collective-permute-start.33 = (bf16[512,3456]{1,0:T(8,128)(2,1)}, bf16[512,3456]{1,0:T(8,128)(2,1)}, u32[]{:S(2)}, u32[]{:S(2)}) collective-permute-start(bf16[512,3456]{1,0:T(8,128)(2,1)} %get-tuple-element.102), channel_id=1, source_target_pairs={{0,4},{4,0},{1,5},{5,1},{2,6},{6,2},{3,7},{7,3},{8,12},{12,8},{9,1... | collective-permute-start | bytes 10616840 | tf_op jit(solution)/shard_map/ppermute | solution.py:37
  121.1 10.2 %collective-permute-start.23 = (bf16[256,256]{1,0:T(8,128)(2,1)}, bf16[256,256]{1,0:T(8,128)(2,1)}, u32[]{:S(2)}, u32[]{:S(2)}) collective-permute-start(bf16[256,256]{1,0:T(8,128)(2,1)} %get-tuple-element.89), channel_id=1, source_target_pairs={{0,1},{1,2},{2,3},{3,0},{4,5},{5,6},{6,7},{7,4},{8,9},{9,10},{10,1... | collective-permute-start | bytes 393224 | tf_op jit(solution)/shard_map/ppermute | solution.py:37
  121.1 10.2 %collective-permute-start.24 = (bf16[256,256]{1,0:T(8,128)(2,1)}, bf16[256,256]{1,0:T(8,128)(2,1)}, u32[]{:S(2)}, u32[]{:S(2)}) collective-permute-start(bf16[256,256]{1,0:T(8,128)(2,1)} %get-tuple-element.90), channel_id=1, source_target_pairs={{0,2},{1,3},{2,0},{3,1},{4,6},{5,7},{6,4},{7,5},{8,10},{9,11},{10,... | collective-permute-start | bytes 393224 | tf_op jit(solution)/shard_map/ppermute | solution.py:37
  123.1 8.8 %collective-permute-start.25 = (bf16[256,256]{1,0:T(8,128)(2,1)}, bf16[256,256]{1,0:T(8,128)(2,1)}, u32[]{:S(2)}, u32[]{:S(2)}) collective-permute-start(bf16[256,256]{1,0:T(8,128)(2,1)} %get-tuple-element.91), channel_id=1, source_target_pairs={{0,3},{1,0},{2,1},{3,2},{4,7},{5,4},{6,5},{7,6},{8,11},{9,8},{10,9... | collective-permute-start | bytes 393224 | tf_op jit(solution)/shard_map/ppermute | solution.py:37
  124.8 12.8 %copy-start.1 = (bf16[512,3456]{1,0:T(8,128)(2,1)S(1)}, bf16[512,3456]{1,0:T(8,128)(2,1)}, u32[]{:S(2)}) copy-start(bf16[512,3456]{1,0:T(8,128)(2,1)} %get-tuple-element.101) | copy-start | bytes 10616836
  128.4 26.2 %collective-permute-start.20 = (bf16[256,256]{1,0:T(8,128)(2,1)}, bf16[256,256]{1,0:T(8,128)(2,1)}, u32[]{:S(2)}, u32[]{:S(2)}) collective-permute-start(bf16[256,256]{1,0:T(8,128)(2,1)} %get-tuple-element.85), channel_id=1, source_target_pairs={{0,1},{1,2},{2,3},{3,0},{4,5},{5,6},{6,7},{7,4},{8,9},{9,10},{10,1... | collective-permute-start | bytes 393224 | tf_op jit(solution)/shard_map/ppermute | solution.py:37
  131.3 25.4 %collective-permute-start.21 = (bf16[256,256]{1,0:T(8,128)(2,1)}, bf16[256,256]{1,0:T(8,128)(2,1)}, u32[]{:S(2)}, u32[]{:S(2)}) collective-permute-start(bf16[256,256]{1,0:T(8,128)(2,1)} %get-tuple-element.86), channel_id=1, source_target_pairs={{0,2},{1,3},{2,0},{3,1},{4,6},{5,7},{6,4},{7,5},{8,10},{9,11},{10,... | collective-permute-start | bytes 393224 | tf_op jit(solution)/shard_map/ppermute | solution.py:37
  133.1 8.0 %collective-permute-start.28 = (bf16[256,256]{1,0:T(8,128)(2,1)S(1)}, bf16[256,256]{1,0:T(8,128)(2,1)S(1)}, u32[]{:S(2)}, u32[]{:S(2)}) collective-permute-start(bf16[256,256]{1,0:T(8,128)(2,1)S(1)} %add_convert_fusion.14.refs_0_), channel_id=1, source_target_pairs={{0,3},{1,0},{2,1},{3,2},{4,7},{5,4},{6,5},{7,6},{8,11},{9,8},{10,9... | collective-permute-start | bytes 393224 | tf_op jit(solution)/shard_map/ppermute | solution.py:37
  135.5 7.8 %collective-permute-start.27 = (bf16[256,256]{1,0:T(8,128)(2,1)S(1)}, bf16[256,256]{1,0:T(8,128)(2,1)S(1)}, u32[]{:S(2)}, u32[]{:S(2)}) collective-permute-start(bf16[256,256]{1,0:T(8,128)(2,1)S(1)} %add_convert_fusion.14.refs_0_), channel_id=1, source_target_pairs={{0,2},{1,3},{2,0},{3,1},{4,6},{5,7},{6,4},{7,5},{8,10},{9,11},{10,... | collective-permute-start | bytes 393224 | tf_op jit(solution)/shard_map/ppermute | solution.py:37
  136.2 9.8 %collective-permute-start.26 = (bf16[256,256]{1,0:T(8,128)(2,1)S(1)}, bf16[256,256]{1,0:T(8,128)(2,1)S(1)}, u32[]{:S(2)}, u32[]{:S(2)}) collective-permute-start(bf16[256,256]{1,0:T(8,128)(2,1)S(1)} %add_convert_fusion.14.refs_0_), channel_id=1, source_target_pairs={{0,1},{1,2},{2,3},{3,0},{4,5},{5,6},{6,7},{7,4},{8,9},{9,10},{10,1... | collective-permute-start | bytes 393224 | tf_op jit(solution)/shard_map/ppermute | solution.py:37
  141.1 38.4 %collective-permute-start.34 = (bf16[128,3456]{1,0:T(8,128)(2,1)}, bf16[128,3456]{1,0:T(8,128)(2,1)}, u32[]{:S(2)}, u32[]{:S(2)}) collective-permute-start(bf16[128,3456]{1,0:T(8,128)(2,1)} %get-tuple-element.127), channel_id=1, source_target_pairs={{0,32},{32,64},{64,96},{96,0},{1,33},{33,65},{65,97},{97,1},{2,34}... | collective-permute-start | bytes 2654216 | tf_op jit(solution)/shard_map/ppermute | solution.py:37
  143.3 38.2 %collective-permute-start.36 = (bf16[128,3456]{1,0:T(8,128)(2,1)}, bf16[128,3456]{1,0:T(8,128)(2,1)}, u32[]{:S(2)}, u32[]{:S(2)}) collective-permute-start(bf16[128,3456]{1,0:T(8,128)(2,1)} %get-tuple-element.128), channel_id=1, source_target_pairs={{0,96},{32,0},{64,32},{96,64},{1,97},{33,1},{65,33},{97,65},{2,98}... | collective-permute-start | bytes 2654216 | tf_op jit(solution)/shard_map/ppermute | solution.py:37
  146.0 36.7 %collective-permute-start.35 = (bf16[128,3456]{1,0:T(8,128)(2,1)}, bf16[128,3456]{1,0:T(8,128)(2,1)}, u32[]{:S(2)}, u32[]{:S(2)}) collective-permute-start(bf16[128,3456]{1,0:T(8,128)(2,1)} %get-tuple-element.129), channel_id=1, source_target_pairs={{0,64},{32,96},{64,0},{96,32},{1,65},{33,97},{65,1},{97,33},{2,66}... | collective-permute-start | bytes 2654216 | tf_op jit(solution)/shard_map/ppermute | solution.py:37
  154.6 6.5 %collective-permute-start.22 = (bf16[256,256]{1,0:T(8,128)(2,1)}, bf16[256,256]{1,0:T(8,128)(2,1)S(1)}, u32[]{:S(2)}, u32[]{:S(2)}) collective-permute-start(bf16[256,256]{1,0:T(8,128)(2,1)} %get-tuple-element.87), channel_id=1, source_target_pairs={{0,3},{1,0},{2,1},{3,2},{4,7},{5,4},{6,5},{7,6},{8,11},{9,8},{10,9... | collective-permute-start | bytes 393224 | tf_op jit(solution)/shard_map/ppermute | solution.py:37
  156.7 6.3 %collective-permute-start.29 = (bf16[1024,256]{1,0:T(8,128)(2,1)}, bf16[1024,256]{1,0:T(8,128)(2,1)S(1)}, u32[]{:S(2)}, u32[]{:S(2)}) collective-permute-start(bf16[1024,256]{1,0:T(8,128)(2,1)} %get-tuple-element.98), channel_id=1, source_target_pairs={{0,4},{4,0},{1,5},{5,1},{2,6},{6,2},{3,7},{7,3},{8,12},{12,8},{9,1... | collective-permute-start | bytes 1572872 | tf_op jit(solution)/shard_map/ppermute | solution.py:37
  164.8 21.3 %collective-permute-start.32 = (bf16[256,256]{1,0:T(8,128)(2,1)S(1)}, bf16[256,256]{1,0:T(8,128)(2,1)S(1)}, u32[]{:S(2)}, u32[]{:S(2)}) collective-permute-start(bf16[256,256]{1,0:T(8,128)(2,1)S(1)} %get-tuple-element.133), channel_id=1, source_target_pairs={{0,24},{8,0},{16,8},{24,16},{1,25},{9,1},{17,9},{25,17},{2,26},{10... | collective-permute-start | bytes 393224 | tf_op jit(solution)/shard_map/ppermute | solution.py:37
  179.5 7.9 %collective-permute-start.31 = (bf16[256,256]{1,0:T(8,128)(2,1)S(1)}, bf16[256,256]{1,0:T(8,128)(2,1)S(1)}, u32[]{:S(2)}, u32[]{:S(2)}) collective-permute-start(bf16[256,256]{1,0:T(8,128)(2,1)S(1)} %get-tuple-element.134), channel_id=1, source_target_pairs={{0,16},{8,24},{16,0},{24,8},{1,17},{9,25},{17,1},{25,9},{2,18},{10... | collective-permute-start | bytes 393224 | tf_op jit(solution)/shard_map/ppermute | solution.py:37
  179.5 9.2 %collective-permute-start.30 = (bf16[256,256]{1,0:T(8,128)(2,1)S(1)}, bf16[256,256]{1,0:T(8,128)(2,1)S(1)}, u32[]{:S(2)}, u32[]{:S(2)}) collective-permute-start(bf16[256,256]{1,0:T(8,128)(2,1)S(1)} %get-tuple-element.135), channel_id=1, source_target_pairs={{0,8},{8,16},{16,24},{24,0},{1,9},{9,17},{17,25},{25,1},{2,10},{10... | collective-permute-start | bytes 393224 | tf_op jit(solution)/shard_map/ppermute | solution.py:37
  189.4 10.2 %copy-start.2 = (bf16[128,3456]{1,0:T(8,128)(2,1)S(1)}, bf16[128,3456]{1,0:T(8,128)(2,1)}, u32[]{:S(2)}) copy-start(bf16[128,3456]{1,0:T(8,128)(2,1)} %add_convert_fusion) | copy-start | bytes 2654212
  193.0 14.3 %copy-start.16 = (bf16[272,256]{1,0:T(8,128)(2,1)S(1)}, bf16[272,256]{1,0:T(8,128)(2,1)}, u32[]{:S(2)}) copy-start(bf16[272,256]{1,0:T(8,128)(2,1)} %get-tuple-element.109) | copy-start | bytes 417796
  193.0 9.7 %collective-permute-start.37 = (bf16[272,256]{1,0:T(8,128)(2,1)}, bf16[272,256]{1,0:T(8,128)(2,1)S(1)}, u32[]{:S(2)}, u32[]{:S(2)}) collective-permute-start(bf16[272,256]{1,0:T(8,128)(2,1)} %get-tuple-element.110), channel_id=1, source_target_pairs={{0,1},{1,2},{2,3},{3,0},{4,5},{5,6},{6,7},{7,4},{8,9},{9,10},{10,1... | collective-permute-start | bytes 417800 | tf_op jit(solution)/shard_map/ppermute | solution.py:37
  193.1 12.8 %collective-permute-start.38 = (bf16[272,256]{1,0:T(8,128)(2,1)}, bf16[272,256]{1,0:T(8,128)(2,1)S(1)}, u32[]{:S(2)}, u32[]{:S(2)}) collective-permute-start(bf16[272,256]{1,0:T(8,128)(2,1)} %get-tuple-element.111), channel_id=1, source_target_pairs={{0,2},{1,3},{2,0},{3,1},{4,6},{5,7},{6,4},{7,5},{8,10},{9,11},{10,... | collective-permute-start | bytes 417800 | tf_op jit(solution)/shard_map/ppermute | solution.py:37
  194.9 12.4 %collective-permute-start.39 = (bf16[272,256]{1,0:T(8,128)(2,1)}, bf16[272,256]{1,0:T(8,128)(2,1)S(1)}, u32[]{:S(2)}, u32[]{:S(2)}) collective-permute-start(bf16[272,256]{1,0:T(8,128)(2,1)} %get-tuple-element.112), channel_id=1, source_target_pairs={{0,3},{1,0},{2,1},{3,2},{4,7},{5,4},{6,5},{7,6},{8,11},{9,8},{10,9... | collective-permute-start | bytes 417800 | tf_op jit(solution)/shard_map/ppermute | solution.py:37
  196.3 11.1 %copy-start.14 = (bf16[256,1,256]{2,0,1:T(8,128)(2,1)S(1)}, bf16[256,1,256]{2,0,1:T(8,128)(2,1)}, u32[]{:S(2)}) copy-start(bf16[256,1,256]{2,0,1:T(8,128)(2,1)} %param.13) | copy-start | bytes 393220
  196.3 11.1 %copy-start.15 = (f32[256,256]{1,0:T(8,128)S(1)}, f32[256,256]{1,0:T(8,128)}, u32[]{:S(2)}) copy-start(f32[256,256]{1,0:T(8,128)} %get-tuple-element.96) | copy-start | bytes 786436
  199.5 8.7 %copy-start.7 = (bf16[512,896]{1,0:T(8,128)(2,1)S(1)}, bf16[512,896]{1,0:T(8,128)(2,1)}, u32[]{:S(2)}) copy-start(bf16[512,896]{1,0:T(8,128)(2,1)} %get-tuple-element.124) | copy-start | bytes 2752516
  199.5 8.7 %collective-permute-start.40 = (bf16[512,896]{1,0:T(8,128)(2,1)}, bf16[512,896]{1,0:T(8,128)(2,1)S(1)}, u32[]{:S(2)}, u32[]{:S(2)}) collective-permute-start(bf16[512,896]{1,0:T(8,128)(2,1)} %get-tuple-element.125), channel_id=1, source_target_pairs={{0,4},{4,0},{1,5},{5,1},{2,6},{6,2},{3,7},{7,3},{8,12},{12,8},{9,1... | collective-permute-start | bytes 2752520 | tf_op jit(solution)/shard_map/ppermute | solution.py:37
  199.6 12.2 %collective-permute-start.50 = (bf16[32,3456]{1,0:T(8,128)(2,1)S(1)}, bf16[32,3456]{1,0:T(8,128)(2,1)S(1)}, u32[]{:S(2)}, u32[]{:S(2)}) collective-permute-start(bf16[32,3456]{1,0:T(8,128)(2,1)S(1)} %get-tuple-element.137), channel_id=1, source_target_pairs={{0,8},{8,16},{16,24},{24,0},{1,9},{9,17},{17,25},{25,1},{2,10},{10... | collective-permute-start | bytes 663560 | tf_op jit(solution)/shard_map/ppermute | solution.py:37
  202.7 13.2 %collective-permute-start.52 = (bf16[32,3456]{1,0:T(8,128)(2,1)S(1)}, bf16[32,3456]{1,0:T(8,128)(2,1)S(1)}, u32[]{:S(2)}, u32[]{:S(2)}) collective-permute-start(bf16[32,3456]{1,0:T(8,128)(2,1)S(1)} %get-tuple-element.138), channel_id=1, source_target_pairs={{0,24},{8,0},{16,8},{24,16},{1,25},{9,1},{17,9},{25,17},{2,26},{10... | collective-permute-start | bytes 663560 | tf_op jit(solution)/shard_map/ppermute | solution.py:37
  205.8 11.9 %collective-permute-start.51 = (bf16[32,3456]{1,0:T(8,128)(2,1)S(1)}, bf16[32,3456]{1,0:T(8,128)(2,1)S(1)}, u32[]{:S(2)}, u32[]{:S(2)}) collective-permute-start(bf16[32,3456]{1,0:T(8,128)(2,1)S(1)} %get-tuple-element.139), channel_id=1, source_target_pairs={{0,16},{8,24},{16,0},{24,8},{1,17},{9,25},{17,1},{25,9},{2,18},{10... | collective-permute-start | bytes 663560 | tf_op jit(solution)/shard_map/ppermute | solution.py:37
  208.4 9.5 %collective-permute-start.41 = (bf16[128,896]{1,0:T(8,128)(2,1)S(1)}, bf16[128,896]{1,0:T(8,128)(2,1)S(1)}, u32[]{:S(2)}, u32[]{:S(2)}) collective-permute-start(bf16[128,896]{1,0:T(8,128)(2,1)S(1)} %get-tuple-element.130), channel_id=1, source_target_pairs={{0,32},{32,64},{64,96},{96,0},{1,33},{33,65},{65,97},{97,1},{2,34}... | collective-permute-start | bytes 688136 | tf_op jit(solution)/shard_map/ppermute | solution.py:37
  209.6 11.7 %collective-permute-start.43 = (bf16[128,896]{1,0:T(8,128)(2,1)S(1)}, bf16[128,896]{1,0:T(8,128)(2,1)S(1)}, u32[]{:S(2)}, u32[]{:S(2)}) collective-permute-start(bf16[128,896]{1,0:T(8,128)(2,1)S(1)} %get-tuple-element.131), channel_id=1, source_target_pairs={{0,96},{32,0},{64,32},{96,64},{1,97},{33,1},{65,33},{97,65},{2,98}... | collective-permute-start | bytes 688136 | tf_op jit(solution)/shard_map/ppermute | solution.py:37
  211.8 10.5 %collective-permute-start.42 = (bf16[128,896]{1,0:T(8,128)(2,1)S(1)}, bf16[128,896]{1,0:T(8,128)(2,1)S(1)}, u32[]{:S(2)}, u32[]{:S(2)}) collective-permute-start(bf16[128,896]{1,0:T(8,128)(2,1)S(1)} %get-tuple-element.132), channel_id=1, source_target_pairs={{0,64},{32,96},{64,0},{96,32},{1,65},{33,97},{65,1},{97,33},{2,66}... | collective-permute-start | bytes 688136 | tf_op jit(solution)/shard_map/ppermute | solution.py:37
  222.4 5.5 %collective-permute-start.44 = (bf16[32,896]{1,0:T(8,128)(2,1)S(1)}, bf16[32,896]{1,0:T(8,128)(2,1)S(1)}, u32[]{:S(2)}, u32[]{:S(2)}) collective-permute-start(bf16[32,896]{1,0:T(8,128)(2,1)S(1)} %get-tuple-element.143), channel_id=1, source_target_pairs={{0,8},{8,16},{16,24},{24,0},{1,9},{9,17},{17,25},{25,1},{2,10},{10... | collective-permute-start | bytes 172040 | tf_op jit(solution)/shard_map/ppermute | solution.py:37
  223.6 4.5 %collective-permute-start.46 = (bf16[32,896]{1,0:T(8,128)(2,1)S(1)}, bf16[32,896]{1,0:T(8,128)(2,1)S(1)}, u32[]{:S(2)}, u32[]{:S(2)}) collective-permute-start(bf16[32,896]{1,0:T(8,128)(2,1)S(1)} %get-tuple-element.144), channel_id=1, source_target_pairs={{0,24},{8,0},{16,8},{24,16},{1,25},{9,1},{17,9},{25,17},{2,26},{10... | collective-permute-start | bytes 172040 | tf_op jit(solution)/shard_map/ppermute | solution.py:37
  225.8 5.7 %collective-permute-start.45 = (bf16[32,896]{1,0:T(8,128)(2,1)S(1)}, bf16[32,896]{1,0:T(8,128)(2,1)S(1)}, u32[]{:S(2)}, u32[]{:S(2)}) collective-permute-start(bf16[32,896]{1,0:T(8,128)(2,1)S(1)} %get-tuple-element.145), channel_id=1, source_target_pairs={{0,16},{8,24},{16,0},{24,8},{1,17},{9,25},{17,1},{25,9},{2,18},{10... | collective-permute-start | bytes 172040 | tf_op jit(solution)/shard_map/ppermute | solution.py:37
  231.5 5.5 %collective-permute-start.48 = (f32[32,128]{1,0:T(8,128)S(1)}, f32[32,128]{1,0:T(8,128)S(1)}, u32[]{:S(2)}, u32[]{:S(2)}) collective-permute-start(f32[32,128]{1,0:T(8,128)S(1)} %slice.237), channel_id=1, source_target_pairs={{0,2},{1,3},{2,0},{3,1},{4,6},{5,7},{6,4},{7,5},{8,10},{9,11},{10,... | collective-permute-start | bytes 49160 | tf_op jit(solution)/shard_map/ppermute | solution.py:37
  233.2 3.9 %collective-permute-start.49 = (f32[32,128]{1,0:T(8,128)S(1)}, f32[32,128]{1,0:T(8,128)S(1)}, u32[]{:S(2)}, u32[]{:S(2)}) collective-permute-start(f32[32,128]{1,0:T(8,128)S(1)} %slice.237), channel_id=1, source_target_pairs={{0,3},{1,0},{2,1},{3,2},{4,7},{5,4},{6,5},{7,6},{8,11},{9,8},{10,9... | collective-permute-start | bytes 49160 | tf_op jit(solution)/shard_map/ppermute | solution.py:37
  235.7 4.9 %collective-permute-start.47 = (f32[32,128]{1,0:T(8,128)S(1)}, f32[32,128]{1,0:T(8,128)S(1)}, u32[]{:S(2)}, u32[]{:S(2)}) collective-permute-start(f32[32,128]{1,0:T(8,128)S(1)} %slice.237), channel_id=1, source_target_pairs={{0,1},{1,2},{2,3},{3,0},{4,5},{5,6},{6,7},{7,4},{8,9},{9,10},{10,1... | collective-permute-start | bytes 49160 | tf_op jit(solution)/shard_map/ppermute | solution.py:37
  (17 other events, 40.2 us)
Sparse Core Ops, SparseCore 0:
  10.3 59.4 all-gather.1
where the time goes:
time: 251 us; the launch traced here: 250 us
  starting transfers between devices  84.7 us (34%)
  waiting for transfers between devices  70.4 us (28%)
  Pallas kernels  46.6 us (19%)
  other arithmetic  23.5 us (9%)
  between operations  14.4 us (6%)
  local copies, waits for them, and re-layouts  10.7 us (4%)
    ppermute x53, starting transfers between devices, shift(): return lax.ppermute(x, axis, [(i, (i + k) % n) for i in range(n)])  84.7 us
    ppermute x53, waiting for transfers between devices, shift(): return lax.ppermute(x, axis, [(i, (i + k) % n) for i in range(n)])  70.3 us
    pallas_call x9, Pallas kernels, call(): pl.pallas_call(kernel, out_shape=outs, in_specs=in_specs or [pl.BlockSpec...  46.6 us
    convert_element_type x3, other arithmetic, core_sum(): (keep[k * step:(k + 1) * step].astype(f32) + got[k * step:(k + 1) * step]...  5.59 us
    unnamed x62, local copies, waits for them, and re-layouts  5.57 us
  transfers between devices with their start and end apart: 54, of which 30 were waited for; matrix products, arithmetic and copies ran while one was open for 10% of the time, Pallas kernels for 8%

commit v1 on v0

--- a/solution.py
+++ b/solution.py
@@ -86,12 +86,35 @@
         dst[:, ds(rot_index(idx[3], n - k, n), part)] = pieces[k][:, first : first + part]
 
 
-def cot_kernel(dims, own, idx, *refs):
+def cot_kernel(dims, idx, *refs):
     n = dims[3]
-    pieces, (full, rel, turned) = refs[:n], refs[n:]
+    pieces, (full, turned) = refs[:n], refs[n:]
     assemble(idx, n, pieces, full, full.shape[1] // n)
     turned[...] = full[...].T
-    store_relative(dims, idx, rel, turned, own)
+
+
+def head_columns(ref):
+    turned = jnp.broadcast_to(ref[...].astype(f32), (8, 2 * HD)).T
+    return turned[:HD, :1], turned[HD:, :1]
+
+
+def to_groups(dst, rows):
+    span = rows.shape[1]
+    group = dst.shape[1] // span
+    for h in range(rows.shape[0] // HD):
+        g, at = h // group, h % group
+        dst[g * HD : (g + 1) * HD, at * span : (at + 1) * span] = rows[h * HD : (h + 1) * HD]
+
+
+def from_groups(x, span):
+    group = x.shape[1] // span
+    return jnp.concatenate(
+        [
+            x[h // group * HD : (h // group + 1) * HD, h % group * span : (h % group + 1) * span]
+            for h in range(x.shape[0] // HD * group)
+        ],
+        axis=0,
+    )
 
 
 def turn_heads(raw, gain, cosine, sine, heads):
@@ -122,8 +145,9 @@
 def qkv_kernel(dims, own, qc, kc, oc, idx, *refs):
     nx, nz, nc, n = dims
     pieces = refs[:n]
-    w_own, w_partner, gq, gk, cosine, sine = refs[n : n + 6]
-    w, base, gains, q_t, raw_t, kv, rel, turned = refs[n + 6 :]
+    w_own, w_partner, head_gains, cosine, sine = refs[n : n + 5]
+    w, base, gains, q_t, raw_t, kv, rel, turned = refs[n + 5 :]
+    gq, gk = head_columns(head_gains)
     assemble(idx, n, pieces, base)
     for other, src in enumerate((w_own, w_partner)):
         core = idx[2] if other == 0 else 1 - idx[2]
@@ -144,48 +168,51 @@
     rt = raw[:, : qc + kc].T
     raw_t[...] = rt
     co, si = cosine[...], sine[...]
-    q_t[...] = turn_heads(rt[:qc], gq[...], co, si, qc // HD).astype(bf16)
-    kv[:, :kc] = turn_heads(rt[qc:], gk[...], co, si, kc // HD).T.astype(bf16)
-
-
-def attend_kernel(dims, qc, kc, oc, idx, q_t, kv_own, kv_partner, w_low, w_high, *refs):
+    q = (turn_heads(rt[:qc], gq, co, si, qc // HD) * SCALE).astype(bf16)
+    to_groups(q_t, q)
+    kv[:, :kc] = turn_heads(rt[qc:], gk, co, si, kc // HD).T.astype(bf16)
+
+
+def attend_kernel(dims, qc, kc, oc, idx, q_t, kv_own, kv_partner, kv, attn_t, attn_b, log_total, acc, tot):
     nx, nz, nc, n = dims
-    kv, attn_t, attn_b, log_total = refs[:4]
-    pieces = refs[4 : 4 + n]
-    acc, tot = refs[4 + n :]
-    span = q_t.shape[1]
+    span = attn_b.shape[0]
+    group = qc // kc
     me = idx[1] * nc + idx[2]
     for other, src in enumerate((kv_own, kv_partner)):
         core = idx[2] if other == 0 else 1 - idx[2]
         for zr in range(nz):
             block = rot_index(idx[1], nz - zr, nz) * nc + core
             kv[ds(block, span), :] = src[zr * span : (zr + 1) * span, :]
-    heads, kv_heads = qc // HD, kc // HD
-    group = heads // kv_heads
     acc[...] = jnp.zeros_like(acc)
     tot[...] = jnp.zeros_like(tot)
     keys_at = lax.broadcasted_iota(jnp.int32, (span, span), 0)
     query_at = lax.broadcasted_iota(jnp.int32, (span, span), 1)
+    ahead = keys_at - query_at
+    ahead = jnp.concatenate([ahead] * group, axis=1)
 
     def step(j, carry):
-        kb = kv[ds(j, span), :kc]
         vt = kv[ds(j, span), kc:].T
-        allowed = keys_at + j * span <= query_at + me * span
-        for h in range(heads):
-            g = h // group
-            s = dot(kb[:, g * HD : (g + 1) * HD], q_t[h * HD : (h + 1) * HD, :])
-            e = jnp.where(allowed, jnp.exp(s * SCALE), 0.0)
-            tot[h : h + 1, :] += jnp.sum(e, axis=0, keepdims=True)
-            acc[h * HD : (h + 1) * HD, :] += dot(vt[g * HD : (g + 1) * HD], e.astype(bf16))
+        allowed = ahead <= (me - j) * span
+        for g in range(kc // HD):
+            rows = slice(g * HD, (g + 1) * HD)
+            s = dot(kv[ds(j, span), rows], q_t[rows, :])
+            e = jnp.where(allowed, jnp.exp(s), 0.0)
+            tot[g : g + 1, :] += jnp.sum(e, axis=0, keepdims=True)
+            acc[rows, :] += dot(vt[rows], e.astype(bf16))
         return carry
 
     lax.fori_loop(0, me + 1, step, 0)
-    for h in range(heads):
-        rows = slice(h * HD, (h + 1) * HD)
-        attn_t[rows, :] = acc[rows, :] / tot[h : h + 1, :]
+    for g in range(kc // HD):
+        rows = slice(g * HD, (g + 1) * HD)
+        attn_t[rows, :] = acc[rows, :] / tot[g : g + 1, :]
     log_total[...] = jnp.log(jnp.maximum(tot[...], 1e-30))
-    attn = attn_t[...].T.astype(bf16)
+    attn = from_groups(attn_t[...], span).T.astype(bf16)
     attn_b[...] = attn
+
+
+def out_kernel(dims, idx, attn_b, w_low, w_high, *pieces):
+    n = dims[3]
+    attn = attn_b[...]
     part = w_low.shape[0] // n
     for k in range(n):
         rows = ds(rot_index(idx[3], k, n), part)
@@ -193,10 +220,14 @@
         pieces[k][...] = out.astype(bf16)
 
 
-def ffn_kernel(dims, own, idx, base, gains, cot, *refs):
+def hidden_grad_kernel(cot, wd, out):
+    out[...] = dot(cot[...], wd[...])
+
+
+def ffn_kernel(dims, own, idx, base, gains, *refs):
     n = dims[3]
     sums = refs[:n]
-    wg, wu, wd = refs[n : n + 3]
+    wg, wu, hgrad = refs[n : n + 3]
     middle, normed, big = refs[n + 3 : n + 6]
     pieces = refs[n + 6 : n + 6 + n]
     acc = refs[n + 6 + n]
@@ -219,7 +250,7 @@
     ff = big.shape[1] // 3
     gate = dot(v, wg[...])
     up = dot(v, wu[...])
-    hg = dot(cot[...], wd[...])
+    hg = hgrad[...]
     sig = 1.0 / (1.0 + jnp.exp(-gate))
     act = gate * sig
     hidden = (act * up).astype(bf16)
@@ -244,36 +275,31 @@
         refs[k][...] = dot(hidden[...], wd[rows, :], NT).astype(bf16)
 
 
-def ffn_grad_kernel(dims, own, idx, normed, cot_rel, big, keep, send, normed_rel, turned):
+def ffn_grad_kernel(normed, cot_t, big, out, turned):
     j = pl.program_id(0)
 
     @pl.when(j == 0)
     def _():
         turned[...] = normed[...].T
-        store_relative(dims, idx, normed_rel, turned, own)
-
-    half = keep.shape[0]
-    of_down = j * 3 >= pl.num_programs(0) * 2
-
-    def write(left):
-        out = dot(left[...], big[...]).astype(bf16)
-        keep[...] = out[:half]
-        send[...] = out[half:]
-
-    pl.when(jnp.logical_not(of_down))(lambda: write(normed_rel))
-    pl.when(of_down)(lambda: write(cot_rel))
+
+    @pl.when(j < 2)
+    def _():
+        out[...] = dot(turned[...], big[...]).astype(bf16)
+
+    @pl.when(j == 2)
+    def _():
+        out[...] = dot(cot_t[...], big[...]).astype(bf16)
 
 
 def attend_back_kernel(dims, own, qc, kc, oc, idx, middle, gains, cot, *refs):
     nx, nz, nc, n = dims
     grads = refs[:n]
-    w_low, w_high, attn_t, q_t, raw_t, kv, log_total, gq, cosine, sine = refs[n : n + 10]
+    w_low, w_high, attn_t, q_t, raw_t, kv, log_total, head_gains, cosine, sine = refs[n : n + 10]
     mine, rel, gain_two, q_gb, gq_grad, kv_keep, kv_send = refs[n + 10 : n + 17]
-    full, turned, dq, do_t, delta, mid_grad = refs[n + 17 :]
-    span = q_t.shape[1]
+    full, turned, dq, do_t, delta, mid_grad, do_f, q_n, do_n = refs[n + 17 :]
+    span = mine.shape[0]
+    group = qc // kc
     me = idx[1] * nc + idx[2]
-    heads, kv_heads = qc // HD, kc // HD
-    group = heads // kv_heads
     assemble(idx, n, grads, full)
     m = middle[...]
     r = lax.rsqrt(jnp.mean(m * m, axis=1, keepdims=True) + EPS)
@@ -289,16 +315,19 @@
     turned[...] = mgb.T
     store_relative(dims, idx, rel, turned, own)
     ag = jnp.concatenate([dot(mgb, w_low[...]), dot(mgb, w_high[...])], axis=1)
-    do = ag.astype(bf16)
-    ag_t = ag.T
-    do_t[...] = ag_t.astype(bf16)
-    prod = ag_t * attn_t[...]
-    for h in range(heads):
-        delta[h : h + 1, :] = jnp.sum(prod[h * HD : (h + 1) * HD], axis=0, keepdims=True)
-    q = q_t[...].T
+    to_groups(do_f, ag.T)
+    prod = do_f[...] * attn_t[...]
+    do_t[...] = do_f[...].astype(bf16)
+    for g in range(kc // HD):
+        rows = slice(g * HD, (g + 1) * HD)
+        delta[g : g + 1, :] = jnp.sum(prod[rows], axis=0, keepdims=True)
+        q_n[g * q_t.shape[1] : (g + 1) * q_t.shape[1], :] = q_t[rows, :].T
+        do_n[g * q_t.shape[1] : (g + 1) * q_t.shape[1], :] = do_t[rows, :].T
     dq[...] = jnp.zeros_like(dq)
     keys_at = lax.broadcasted_iota(jnp.int32, (span, span), 0)
     query_at = lax.broadcasted_iota(jnp.int32, (span, span), 1)
+    ahead = keys_at - query_at
+    ahead = jnp.concatenate([ahead] * group, axis=1)
     for other, out in enumerate((kv_keep, kv_send)):
         core = idx[2] if other == 0 else 1 - idx[2]
 
@@ -312,31 +341,26 @@
 
             @pl.when(j <= me)
             def _():
-                kb = kv[ds(j, span), :kc]
-                vb = kv[ds(j, span), kc:]
-                kt = kb.T
-                allowed = keys_at + j * span <= query_at + me * span
-                for g in range(kv_heads):
-                    cols = slice(g * HD, (g + 1) * HD)
-                    dk = jnp.zeros((span, HD), f32)
-                    dv = jnp.zeros((span, HD), f32)
-                    for h in range(g * group, (g + 1) * group):
-                        rows = slice(h * HD, (h + 1) * HD)
-                        s = dot(kb[:, cols], q_t[rows, :])
-                        p = jnp.where(allowed, jnp.exp(s * SCALE - log_total[h : h + 1, :]), 0.0)
-                        dp = dot(vb[:, cols], do_t[rows, :])
-                        sg = (p * (dp - delta[h : h + 1, :])).astype(bf16)
-                        dq[rows, :] += dot(kt[cols], sg)
-                        dk = dk + dot(sg, q[:, rows])
-                        dv = dv + dot(p.astype(bf16), do[:, rows])
-                    out[at, g * HD : (g + 1) * HD] = (dk * SCALE).astype(bf16)
+                kt = kv[ds(j, span), :kc].T
+                allowed = ahead <= (me - j) * span
+                wide = q_t.shape[1]
+                for g in range(kc // HD):
+                    rows = slice(g * HD, (g + 1) * HD)
+                    s = dot(kv[ds(j, span), rows], q_t[rows, :])
+                    p = jnp.where(allowed, jnp.exp(s - log_total[g : g + 1, :]), 0.0)
+                    dp = dot(kv[ds(j, span), kc + g * HD : kc + (g + 1) * HD], do_t[rows, :])
+                    sg = (p * (dp - delta[g : g + 1, :])).astype(bf16)
+                    dq[rows, :] += dot(kt[rows], sg)
+                    dk = dot(sg, q_n[g * wide : (g + 1) * wide, :])
+                    dv = dot(p.astype(bf16), do_n[g * wide : (g + 1) * wide, :])
+                    out[at, rows] = dk.astype(bf16)
                     out[at, kc + g * HD : kc + (g + 1) * HD] = dv.astype(bf16)
 
             return carry
 
         lax.fori_loop(0, nz, step, 0)
     raw_grad, gain_grad = turn_heads_back(
-        raw_t[:qc, :], dq[...] * SCALE, gq[...], cosine[...], sine[...], heads
+        raw_t[:qc, :], from_groups(dq[...], span) * SCALE, head_columns(head_gains)[0], cosine[...], sine[...], qc // HD
     )
     gq_grad[...] = gain_grad
     q_gb[...] = raw_grad.T.astype(bf16)
@@ -345,7 +369,7 @@
 def input_grad_kernel(dims, qc, kc, idx, *refs):
     n, nz = dims[3], dims[1]
     kv_parts = refs[:nz]
-    raw_t, gk, cosine, sine, q_gb, w, base, gains = refs[nz : nz + 8]
+    raw_t, head_gains, cosine, sine, q_gb, w, base, gains = refs[nz : nz + 8]
     qkv_gb, gain_one, gk_grad = refs[nz + 8 : nz + 11]
     pieces = refs[nz + 11 : nz + 11 + n]
     acc = refs[nz + 11 + n]
@@ -353,7 +377,7 @@
     for k in range(1, nz):
         total = total + kv_parts[k][...].astype(f32)
     raw_grad, gain_grad = turn_heads_back(
-        raw_t[qc:, :], total[:, :kc].T, gk[...], cosine[...], sine[...], kc // HD
+        raw_t[qc:, :], total[:, :kc].T, head_columns(head_gains)[1], cosine[...], sine[...], kc // HD
     )
     gk_grad[...] = gain_grad
     qkv_gb[:, :qc] = q_gb[...]
@@ -464,23 +488,23 @@
     by_z = jnp.concatenate(gathered(attn_local, "z"), axis=0)
     both = jnp.concatenate([block_input.reshape(span, part), cotangent.reshape(span, part)], axis=1)
     both_parts = gathered(both, "tensor")
-    w_own = jnp.concatenate(gathered(by_z, "dp"), axis=0)
-    cot, cot_rel = call(
-        functools.partial(cot_kernel, dims, own),
-        [sds((span, width), bf16), sds((width, span), bf16)],
-        [idx] + both_parts,
-        [pltpu.VMEM((width, span), bf16)],
-    )
-    w_own, (cot, cot_rel) = lax.optimization_barrier((w_own, (cot, cot_rel)))
-    w_partner = shift(w_own, "core", 1)
-
     my_first = (idx[1] * nc + idx[2]) * span
     positions = (my_first + jnp.arange(span, dtype=jnp.int32)).astype(f32)
     frequency = jnp.power(ROPE_BASE, -2.0 * jnp.arange(HALF, dtype=f32) / HD)
     angle = frequency[:, None] * positions[None, :]
     cosine, sine = jnp.cos(angle), jnp.sin(angle)
-    gq = query_gain.astype(f32)[:, None]
-    gk = key_gain.astype(f32)[:, None]
+    head_gains = jnp.concatenate([query_gain, key_gain])[None, :]
+    dp_parts = gathered(by_z, "dp")
+    dp_parts, both_parts, cosine, sine, head_gains = lax.optimization_barrier(
+        (dp_parts, both_parts, cosine, sine, head_gains)
+    )
+    w_own = jnp.concatenate(dp_parts, axis=0)
+    w_partner = shift(w_own, "core", 1)
+    cot, cot_t = call(
+        functools.partial(cot_kernel, dims),
+        [sds((span, width), bf16), sds((width, span), bf16)],
+        [idx] + both_parts,
+    )
 
     w, base, gains, q_t, raw_t, kv, one_rel = call(
         functools.partial(qkv_kernel, dims, own, qc, kc, oc),
@@ -488,12 +512,12 @@
             sds((width, qkv + PAD), bf16),
             sds((span, width), bf16),
             sds((8, width), f32),
-            sds((qc, span), bf16),
+            sds((kc, qc // kc * span), bf16),
             sds((qc + kc, span), f32),
             sds((span, 2 * kc), bf16),
             sds((width, span), bf16),
         ],
-        [idx] + both_parts + [w_own, w_partner, gq, gk, cosine, sine],
+        [idx] + both_parts + [w_own, w_partner, head_gains, cosine, sine],
         [pltpu.VMEM((width, span), bf16)],
         flops=2 * span * width * qkv,
     )
@@ -501,63 +525,71 @@
     kv_partner = shift(kv_own, "core", 1)
 
     length = span * nz * nc
+    (kv_own, kv_partner), (cot, cot_t) = lax.optimization_barrier(((kv_own, kv_partner), (cot, cot_t)))
     block = 384
     const = lambda s: pl.BlockSpec(s, lambda j: (0, 0))
     steps = ff // block
     out_blocks = [pl.BlockSpec((width, PAD), lambda j, o=o: (0, o)) for o in (3 * ff // PAD, 3 * ff // PAD + 1)]
+    kv_full, attn_t, attn_b, log_total = call(
+        functools.partial(attend_kernel, dims, qc, kc, oc),
+        [sds((length, 2 * kc), bf16), sds(q_t.shape, f32), sds((span, qc), bf16), sds((8, q_t.shape[1]), f32)],
+        [idx, q_t, kv_own, kv_partner],
+        [pltpu.VMEM(q_t.shape, f32), pltpu.VMEM((8, q_t.shape[1]), f32)],
+        flops=4 * span * length * qc,
+    )
     res = call(
-        functools.partial(attend_kernel, dims, qc, kc, oc),
-        [
-            sds((length, 2 * kc), bf16),
-            sds((qc, span), f32),
-            sds((span, qc), bf16),
-            sds((8, span), f32),
-        ]
-        + [sds((span, part), bf16)] * n,
-        [idx, q_t, kv_own, kv_partner, ffn_w, ffn_w],
-        [pltpu.VMEM((qc, span), f32), pltpu.VMEM((8, span), f32)],
+        functools.partial(out_kernel, dims),
+        [sds((span, part), bf16)] * n,
+        [idx, attn_b, ffn_w, ffn_w],
         grid=(1,),
-        in_specs=[pl.BlockSpec(memory_space=pltpu.SMEM), const((qc, span)), const((length // 2, 2 * kc)), const((length // 2, 2 * kc))]
-        + out_blocks,
-        out_specs=[const((length, 2 * kc)), const((qc, span)), const((span, qc)), const((8, span))]
-        + [const((span, part))] * n,
-        flops=4 * span * length * qc,
-    )
-    kv_full, attn_t, attn_b, log_total = res[:4]
-    attn_mine = summed(res[4:], "tensor").astype(bf16)
+        in_specs=[pl.BlockSpec(memory_space=pltpu.SMEM), const((span, qc))] + out_blocks,
+        out_specs=[const((span, part))] * n,
+        flops=2 * span * width * qc,
+    )
+    attn_mine = summed(res, "tensor").astype(bf16)
     attn_parts = gathered(attn_mine, "tensor")
 
+    hgrad = call(
+        hidden_grad_kernel,
+        [sds((span, ff), f32)],
+        [cot, ffn_w],
+        grid=(steps,),
+        in_specs=[const((span, width)), pl.BlockSpec((width, block), lambda j: (0, 2 * steps + j))],
+        out_specs=[pl.BlockSpec((span, block), lambda j: (0, j))],
+        flops=2 * span * width * ff,
+    )[0]
     res = call(
         functools.partial(ffn_kernel, dims, own),
         [sds((span, width), f32), sds((span, width), bf16), sds((span, 3 * ff), bf16)]
         + [sds((span, part), bf16)] * n,
-        [idx, base, gains, cot] + attn_parts + [ffn_w] * 3,
+        [idx, base, gains] + attn_parts + [ffn_w, ffn_w, hgrad],
         [pltpu.VMEM((span, width), f32)],
         grid=(steps,),
         in_specs=[pl.BlockSpec(memory_space=pltpu.SMEM)]
-        + [const((span, width)), const((8, width)), const((span, width))]
+        + [const((span, width)), const((8, width))]
         + [const((span, part))] * n
-        + [pl.BlockSpec((width, block), lambda j, o=o: (0, o + j)) for o in (0, steps, 2 * steps)],
+        + [pl.BlockSpec((width, block), lambda j, o=o: (0, o + j)) for o in (0, steps)]
+        + [pl.BlockSpec((span, block), lambda j: (0, j))],
         out_specs=[const((span, width)), const((span, width)), const((span, 3 * ff))]
         + [const((span, part))] * n,
-        flops=10 * span * width * ff,
+        flops=8 * span * width * ff,
     )
     middle, normed_two, big = res[:3]
-    grad_mine = summed(res[3:], "tensor").astype(bf16)
+    grad_got = [shift(res[3 + k], "tensor", k) for k in range(1, n)]
+    grad_mine = sum([g.astype(f32) for g in grad_got], res[3].astype(f32)).astype(bf16)
     grad_parts = gathered(grad_mine, "tensor")
 
-    ffn_keep, ffn_send = call(
-        functools.partial(ffn_grad_kernel, dims, own),
-        [sds((width // 2, 3 * ff), bf16)] * 2,
-        [idx, normed_two, cot_rel, big],
-        [pltpu.VMEM((width, span), bf16)] * 2,
-        grid=(3 * steps,),
-        in_specs=[pl.BlockSpec(memory_space=pltpu.SMEM), const((span, width)), const((width, span)), pl.BlockSpec((span, block), lambda j: (0, j))],
-        out_specs=[pl.BlockSpec((width // 2, block), lambda j: (0, j))] * 2,
+    ffn_grad = call(
+        ffn_grad_kernel,
+        [sds((width, 3 * ff), bf16)],
+        [normed_two, cot_t, big],
+        [pltpu.VMEM((width, span), bf16)],
+        grid=(3,),
+        in_specs=[const((span, width)), const((width, span)), pl.BlockSpec((span, ff), lambda j: (0, j))],
+        out_specs=[pl.BlockSpec((width, ff), lambda j: (0, j))],
         flops=6 * span * width * ff,
-    )
-    ffn_pieces = core_sum(ffn_keep, ffn_send, nx)
-    ffn_x = summed(ffn_pieces, "dp").astype(bf16)
+    )[0]
+    ffn_sum = lax.psum_scatter(ffn_grad, ("dp", "z", "core"), scatter_dimension=0, tiled=True).astype(f32)
 
     down_parts = call(
         functools.partial(down_kernel, dims),
@@ -572,9 +604,7 @@
         out_specs=[const((span, part))] * n,
         flops=2 * span * width * ff,
     )
-    me_t = idx[3]
-    middle_mine = lax.dynamic_slice_in_dim(middle, me_t * part, part, 1)
-    block_output = (middle_mine + summed(down_parts, "tensor")).astype(bf16)
+    grad_parts, down_parts = lax.optimization_barrier((grad_parts, down_parts))
 
     mine, mid_rel, gain_two, q_gb, gq_grad, kv_keep, kv_send = call(
         functools.partial(attend_back_kernel, dims, own, qc, kc, oc),
@@ -587,20 +617,23 @@
             sds((length // 2, 2 * kc), bf16),
             sds((length // 2, 2 * kc), bf16),
         ],
-        [idx, middle, gains, cot] + grad_parts + [ffn_w, ffn_w, attn_t, q_t, raw_t, kv_full, log_total, gq, cosine, sine],
+        [idx, middle, gains, cot] + grad_parts + [ffn_w, ffn_w, attn_t, q_t, raw_t, kv_full, log_total, head_gains, cosine, sine],
         [
             pltpu.VMEM((span, width), bf16),
             pltpu.VMEM((width, span), bf16),
-            pltpu.VMEM((qc, span), f32),
-            pltpu.VMEM((qc, span), bf16),
-            pltpu.VMEM((8, span), f32),
+            pltpu.VMEM(q_t.shape, f32),
+            pltpu.VMEM(q_t.shape, bf16),
+            pltpu.VMEM((8, q_t.shape[1]), f32),
             pltpu.VMEM((span, width), f32),
+            pltpu.VMEM(q_t.shape, f32),
+            pltpu.VMEM((kc // HD * q_t.shape[1], HD), bf16),
+            pltpu.VMEM((kc // HD * q_t.shape[1], HD), bf16),
         ],
         grid=(1,),
         in_specs=[pl.BlockSpec(memory_space=pltpu.SMEM), const((span, width)), const((8, width)), const((span, width))]
         + [const((span, part))] * n
         + out_blocks
-        + [const(v.shape) for v in (attn_t, q_t, raw_t, kv_full, log_total, gq, cosine, sine)],
+        + [const(v.shape) for v in (attn_t, q_t, raw_t, kv_full, log_total, head_gains, cosine, sine)],
         out_specs=[
             const((span, part)),
             const((width, span)),
@@ -614,18 +647,34 @@
     )
     kv_pieces = core_sum(kv_keep, kv_send, nz)
     kv_parts = [kv_pieces[0]] + [shift(kv_pieces[k], "z", k) for k in range(1, nz)]
-    kv_parts, ffn_x = lax.optimization_barrier((kv_parts, ffn_x))
+    kv_parts[1], down_parts = lax.optimization_barrier((kv_parts[1], down_parts))
+    me_t = idx[3]
+    middle_mine = lax.dynamic_slice_in_dim(middle, me_t * part, part, 1)
+    block_output = (middle_mine + summed(down_parts, "tensor")).astype(bf16)
 
     res = call(
         functools.partial(input_grad_kernel, dims, qc, kc),
         [sds((span, qkv), bf16), sds((8, width), f32), sds((HD, 1), f32)]
         + [sds((span + 16, part), bf16)] * n,
-        [idx] + kv_parts + [raw_t, gk, cosine, sine, q_gb, w, base, gains],
+        [idx] + kv_parts + [raw_t, head_gains, cosine, sine, q_gb, w, base, gains],
         [pltpu.VMEM((span, width), f32)],
         flops=2 * span * width * qkv,
     )
     qkv_gb, gain_one, gk_grad = res[:3]
-    norm_mine = summed(res[3:], "tensor")
+    norm_parts = res[3:]
+    keep, send = call(
+        functools.partial(attn_grad_kernel, dims, own, qc, kc, oc),
+        [sds((width // 2, aw), bf16)] * 2,
+        [idx, one_rel, mid_rel, qkv_gb, attn_b, gain_one, gain_two, gq_grad, gk_grad],
+        [pltpu.VMEM((width, PAD), bf16), pltpu.VMEM((width, PAD), bf16)],
+        flops=2 * span * width * (qkv + oc),
+    )
+    (keep, send), block_output = lax.optimization_barrier(((keep, send), block_output))
+    attn_pieces = core_sum(keep, send, nx)
+    attn_got = [shift(attn_pieces[k], "dp", k) for k in range(1, nx)]
+    attn_got[0], norm_parts = lax.optimization_barrier((attn_got[0], norm_parts))
+    attn_x = sum([v.astype(f32) for v in attn_got], attn_pieces[0].astype(f32)).astype(bf16)
+    norm_mine = summed(norm_parts, "tensor")
     along = (norm_mine[span] + norm_mine[span + 1])[:, None] * (1.0 / width)
     base_f = base.astype(f32)
     scale_one = lax.rsqrt(jnp.mean(base_f * base_f, axis=1, keepdims=True) + EPS)
@@ -633,16 +682,6 @@
     gain_mine = lax.dynamic_slice_in_dim(gains, me_t * part, part, 1)[0:1]
     input_grad = (mine + scale_one * (norm_mine[:span] * gain_mine - unit_mine * along)).astype(bf16)
 
-    keep, send = call(
-        functools.partial(attn_grad_kernel, dims, own, qc, kc, oc),
-        [sds((width // 2, aw), bf16)] * 2,
-        [idx, one_rel, mid_rel, qkv_gb, attn_b, gain_one, gain_two, gq_grad, gk_grad],
-        [pltpu.VMEM((width, PAD), bf16), pltpu.VMEM((width, PAD), bf16)],
-        flops=2 * span * width * (qkv + oc),
-    )
-    (keep, send), ffn_x = lax.optimization_barrier(((keep, send), ffn_x))
-    ffn_sum = row_sum(ffn_x, "z")
-    attn_x = summed(core_sum(keep, send, nx), "dp").astype(bf16)
     attn_sum = row_sum(attn_x, "z")
     small = attn_sum[:, qkv + oc :]
     small_all = sum(gathered(small, "tensor"))

time: 251 us -> 223 us (0.89)
  starting transfers between devices: 84.7 us -> 73.2 us
  waiting for transfers between devices: 70.4 us -> 59.4 us
  other arithmetic: 23.5 us -> 17.3 us
    ppermute x53 -> x46, waiting for transfers between devices: 70.3 us -> 56.3 us  [shift(): return lax.ppermute(x, axis, [(i, (i + k) % n) for i in range(n)])]
    ppermute x53 -> x46, starting transfers between devices: 84.7 us -> 73.1 us  [shift(): return lax.ppermute(x, axis, [(i, (i + k) % n) for i in range(n)])]
    all_gather x1, waiting for transfers between devices: 0.01 us -> 3.09 us  [body(): ffn_w = lax.all_gather(ffn_local, ('dp', 'z', 'core'), axis=0, tiled=True)]
    convert_element_type x3 -> x2, other arithmetic: 5.59 us -> 3.24 us  [core_sum(): (keep[k * step:(k + 1) * step].astype(f32) + got[k * step:(k + 1) * step]...]
    pallas_call x9 -> x11, Pallas kernels: 46.6 us -> 47.7 us  [call(): pl.pallas_call(kernel, out_shape=outs, in_specs=in_specs or [pl.BlockSpec...]
    unnamed x62 -> x78, local copies, waits for them, and re-layouts: 5.57 us -> 5.59 us
  transfers between devices with their start and end apart: 54 -> 48, of which waited for: 30 -> 28; matrix products, arithmetic and copies ran while one was open for 10% -> 8% of each run, Pallas kernels for 8% -> 14%
where the time goes in v1:
time: 223 us; the launch traced here: 222 us
  starting transfers between devices  73.2 us (33%)
  waiting for transfers between devices  59.4 us (27%)
  Pallas kernels  47.7 us (21%)
  other arithmetic  17.3 us (8%)
  between operations  14.5 us (7%)
  local copies, waits for them, and re-layouts  10.2 us (5%)
    ppermute x46, starting transfers between devices, shift(): return lax.ppermute(x, axis, [(i, (i + k) % n) for i in range(n)])  73.1 us
    ppermute x46, waiting for transfers between devices, shift(): return lax.ppermute(x, axis, [(i, (i + k) % n) for i in range(n)])  56.3 us
    pallas_call x11, Pallas kernels, call(): pl.pallas_call(kernel, out_shape=outs, in_specs=in_specs or [pl.BlockSpec...  47.7 us
    unnamed x78, local copies, waits for them, and re-layouts  5.59 us
  transfers between devices with their start and end apart: 48, of which 28 were waited for; matrix products, arithmetic and copies ran while one was open for 8% of the time, Pallas kernels for 14%

profile of v1, /device:TPU:0, one launch (start us, length us, event | category | flops | bytes accessed | tf_op | source)
XLA Modules:
  0.0 222.3 jit_solution(13337291544302747734)
XLA Ops:
  7.2 1.7 pad_maximum_fusion.1
  10.6 4.1 %collective-permute-start.2 = (bf16[32,640]{1,0:T(8,128)(2,1)S(1)}, bf16[32,640]{1,0:T(8,128)(2,1)S(1)}, u32[]{:S(2)}, u32[]{:S(2)}) collective-permute-start(bf16[32,640]{1,0:T(8,128)(2,1)S(1)} %pad_maximum_fusion.3), channel_id=1, source_target_pairs={{0,24},{8,0},{16,8},{24,16},{1,25},{9,1},{17,9},{25,17},{2,26},{10... | collective-permute-start | bytes 122888 | tf_op jit(solution)/shard_map/ppermute | solution.py:37
  14.7 1.3 collective-permute-start
  16.9 1.6 collective-permute-start.6
  18.6 2.9 %collective-permute-start.7 = (bf16[256,512]{1,0:T(8,128)(2,1)S(1)}, bf16[256,512]{1,0:T(8,128)(2,1)S(1)}, u32[]{:S(2)}, u32[]{:S(2)}) collective-permute-start(bf16[256,512]{1,0:T(8,128)(2,1)S(1)} %pad_maximum_fusion.refs_0_), channel_id=1, source_target_pairs={{0,2},{1,3},{2,0},{3,1},{4,6},{5,7},{6,4},{7,5},{8,10},{9,11},{10,... | collective-permute-start | bytes 786440 | tf_op jit(solution)/shard_map/ppermute | solution.py:37
  21.5 1.3 collective-permute-start.8
  23.6 1.6 collective-permute-start.3
  25.2 2.8 %collective-permute-start.4 = (bf16[128,640]{1,0:T(8,128)(2,1)S(1)}, bf16[128,640]{1,0:T(8,128)(2,1)S(1)}, u32[]{:S(2)}, u32[]{:S(2)}) collective-permute-start(bf16[128,640]{1,0:T(8,128)(2,1)S(1)} %pad_maximum_fusion.2), channel_id=1, source_target_pairs={{0,64},{32,96},{64,0},{96,32},{1,65},{33,97},{65,1},{97,33},{2,66}... | collective-permute-start | bytes 491528 | tf_op jit(solution)/shard_map/ppermute | solution.py:37
  28.0 3.4 %collective-permute-done.3 = bf16[128,640]{1,0:T(8,128)(2,1)S(1)} collective-permute-done((bf16[128,640]{1,0:T(8,128)(2,1)S(1)}, bf16[128,640]{1,0:T(8,128)(2,1)S(1)}, u32[]{:S(2)}, u32[]{:S(2)}) %collective-permute-start.3) | collective-permute-done | bytes 163872 | tf_op jit(solution)/shard_map/ppermute | solution.py:37
  31.4 3.8 %collective-permute-start.5 = (bf16[128,640]{1,0:T(8,128)(2,1)S(1)}, bf16[128,640]{1,0:T(8,128)(2,1)S(1)}, u32[]{:S(2)}, u32[]{:S(2)}) collective-permute-start(bf16[128,640]{1,0:T(8,128)(2,1)S(1)} %pad_maximum_fusion.2), channel_id=1, source_target_pairs={{0,96},{32,0},{64,32},{96,64},{1,97},{33,1},{65,33},{97,65},{2,98}... | collective-permute-start | bytes 491528 | tf_op jit(solution)/shard_map/ppermute | solution.py:37
  39.0 1.3 collective-permute-done.9.refs_5_
  41.2 4.0 %shard_map.228 = (bf16[1024,640]{1,0:T(8,128)(2,1)}, bf16[256,1024]{1,0:T(8,128)(2,1)}, f32[8,1024]{1,0:T(8,128)}, bf16[128,512]{1,0:T(8,128)(2,1)}, f32[384,256...) custom-call(s32[4]{0:T(128)} %pad_add_fusion.idx, bf16[256,512]{1,0:T(8,128)(2,1)} %copy-done.1, ...), custom_call_target="tpu_custom_call" | custom-call | flops 268435456 | bytes 5472528 | tf_op jit(solution)/shard_map/pallas_call | solution.py:55
  45.2 2.7 %collective-permute-start.10 = (bf16[256,256]{1,0:T(8,128)(2,1)}, bf16[256,256]{1,0:T(8,128)(2,1)S(1)}, u32[]{:S(2)}, u32[]{:S(2)}) collective-permute-start(bf16[256,256]{1,0:T(8,128)(2,1)} %get-tuple-element.108), channel_id=1, source_target_pairs={{0,8},{8,16},{16,24},{24,0},{1,9},{9,17},{17,25},{25,1},{2,10},{10... | collective-permute-start | bytes 393224 | tf_op jit(solution)/shard_map/ppermute | solution.py:37
  49.8 1.9 collective-permute-start.12
  51.7 3.9 %collective-permute-done.10 = bf16[256,256]{1,0:T(8,128)(2,1)S(1)} collective-permute-done((bf16[256,256]{1,0:T(8,128)(2,1)}, bf16[256,256]{1,0:T(8,128)(2,1)S(1)}, u32[]{:S(2)}, u32[]{:S(2)}) %collective-permute-start.10) | collective-permute-done | bytes 131104 | tf_op jit(solution)/shard_map/ppermute | solution.py:37
  55.5 5.8 %collective-permute-done.11 = bf16[256,256]{1,0:T(8,128)(2,1)S(1)} collective-permute-done((bf16[256,256]{1,0:T(8,128)(2,1)}, bf16[256,256]{1,0:T(8,128)(2,1)S(1)}, u32[]{:S(2)}, u32[]{:S(2)}) %collective-permute-start.11) | collective-permute-done | bytes 131104 | tf_op jit(solution)/shard_map/ppermute | solution.py:37
  62.0 2.4 %shard_map.229 = (bf16[256,1024]{1,0:T(8,128)(2,1)}, bf16[1024,256]{1,0:T(8,128)(2,1)}) custom-call(s32[4]{0:T(128)} %pad_add_fusion.idx, bf16[256,512]{1,0:T(8,128)(2,1)} %copy-done.1, bf16[256,512]{1,0:T(8,128)(2,1)} %copy-done.2, bf16[256,512]{1,0:T(8,128)(2,1)} %copy-done.3, bf16[256,512]{1,0:T(8,128)(2,1)} %copy-done.4), custom_call_target="tpu_custom_call" | custom-call | bytes 2097168 | tf_op jit(solution)/shard_map/pallas_call | solution.py:55
  65.2 3.1 %shard_map.230 = (bf16[2048,256]{1,0:T(8,128)(2,1)}, f32[128,512]{1,0:T(8,128)}, bf16[256,256]{1,0:T(8,128)(2,1)}, f32[8,512]{1,0:T(8,128)}) custom-call(s32[4]{0:T(128)} %pad_add_fusion.idx, bf16[128,512]{1,0:T(8,128)(2,1)} %get-tuple-element.107.q_t.refs_7_, bf16[1024,256]{1,0:T(8,128)(2,1)} %copy-done.23, bf16[1024,256]{1,0:T(8,128)(2,1)} %copy-done.24), custom_call_target="tpu_custom_call" | custom-call | flops 536870912 | bytes 2637840 | tf_op jit(solution)/shard_map/pallas_call | solution.py:55
  68.3 3.1 %all-gather.2.cloned.1.call-done.w_low.w_high.wd.refs_4_.refs_5_ = bf16[1024,3712]{1,0:T(8,128)(2,1)} async-done(((bf16[32,3712]{1,0:T(8,128)(2,1)}), bf16[1024,3712]{1,0:T(8,128)(2,1)}) %all-gather.2.cloned.1.call-update) | async-done | bytes 7602192 | tf_op jit(solution)/shard_map/all_gather | solution.py:484
  71.4 2.2 %shard_map.231 = (bf16[256,256]{1,0:T(8,128)(2,1)}, bf16[256,256]{1,0:T(8,128)(2,1)}, bf16[256,256]{1,0:T(8,128)(2,1)}, bf16[256,256]{1,0:T(8,128)(2,1)}) custom-call(s32[4]{0:T(128)} %pad_add_fusion.idx, bf16[256,256]{1,0:T(8,128)(2,1)} %get-tuple-element.113.attn_b, bf16[1024,3712]{1,0:T(8,128)(2,1)} %all-gather.2.cloned.1.call-done.w_low.w_high.wd.refs_4_.refs_5_, ...), custom_call_target="tpu_custom_call" | custom-call | flops 134217728 | bytes 15859728 | tf_op jit(solution)/shard_map/pallas_call | solution.py:55
  73.6 2.5 %collective-permute-start.16 = (bf16[256,256]{1,0:T(8,128)(2,1)}, bf16[256,256]{1,0:T(8,128)(2,1)S(1)}, u32[]{:S(2)}, u32[]{:S(2)}) collective-permute-start(bf16[256,256]{1,0:T(8,128)(2,1)} %get-tuple-element.117), channel_id=1, source_target_pairs={{0,3},{1,0},{2,1},{3,2},{4,7},{5,4},{6,5},{7,6},{8,11},{9,8},{10,9... | collective-permute-start | bytes 393224 | tf_op jit(solution)/shard_map/ppermute | solution.py:37
  77.8 4.7 %collective-permute-done.16 = bf16[256,256]{1,0:T(8,128)(2,1)S(1)} collective-permute-done((bf16[256,256]{1,0:T(8,128)(2,1)}, bf16[256,256]{1,0:T(8,128)(2,1)S(1)}, u32[]{:S(2)}, u32[]{:S(2)}) %collective-permute-start.16) | collective-permute-done | bytes 131104 | tf_op jit(solution)/shard_map/ppermute | solution.py:37
  82.5 1.7 collective-permute-done.15
  84.2 1.8 collective-permute-done.14
  87.1 2.0 collective-permute-start.18
  89.2 1.6 collective-permute-start.19
  90.8 4.2 %shard_map.232.refs_6_ = f32[256,1152]{1,0:T(8,128)} custom-call(bf16[256,1024]{1,0:T(8,128)(2,1)} %get-tuple-element.118.cot, bf16[1024,3712]{1,0:T(8,128)(2,1)} %all-gather.2.cloned.1.call-done.w_low.w_high.wd.refs_4_.refs_5_), custom_call_target="tpu_custom_call" | custom-call | flops 603979776 | bytes 9306112 | tf_op jit(solution)/shard_map/pallas_call | solution.py:55
  95.0 1.5 collective-permute-done.17.refs_1_
  97.8 8.4 %shard_map.233 = (f32[256,1024]{1,0:T(8,128)}, bf16[256,1024]{1,0:T(8,128)(2,1)}, bf16[256,3456]{1,0:T(8,128)(2,1)}, bf16[256,256]{1,0:T(8,128)(2,1)}, bf16[256,...) custom-call(s32[4]{0:T(128)} %pad_add_fusion.idx, ...), custom_call_target="tpu_custom_call" | custom-call | flops 2415919104 | bytes 21331984 | tf_op jit(solution)/shard_map/pallas_call | solution.py:55
  106.3 6.3 %shard_map.238 = bf16[1024,3456]{1,0:T(8,128)(2,1)} custom-call(bf16[256,1024]{1,0:T(8,128)(2,1)} %get-tuple-element.171.normed, bf16[1024,256]{1,0:T(8,128)(2,1)} %get-tuple-element.172.cot_t, bf16[256,3456]{1,0:T(8,128)(2,1)} %get-tuple-element.124.hidden.big), custom_call_target="tpu_custom_call" | custom-call | flops 1811939328 | bytes 9895936 | tf_op jit(solution)/shard_map/pallas_call | solution.py:55
  113.5 2.5 %collective-permute-start.22 = (bf16[256,256]{1,0:T(8,128)(2,1)S(1)}, bf16[256,256]{1,0:T(8,128)(2,1)S(1)}, u32[]{:S(2)}, u32[]{:S(2)}) collective-permute-start(bf16[256,256]{1,0:T(8,128)(2,1)S(1)} %copy-done.33), channel_id=1, source_target_pairs={{0,3},{1,0},{2,1},{3,2},{4,7},{5,4},{6,5},{7,6},{8,11},{9,8},{10,9... | collective-permute-start | bytes 393224 | tf_op jit(solution)/shard_map/ppermute | solution.py:37
  116.9 4.7 %collective-permute-done.22 = bf16[256,256]{1,0:T(8,128)(2,1)S(1)} collective-permute-done((bf16[256,256]{1,0:T(8,128)(2,1)S(1)}, bf16[256,256]{1,0:T(8,128)(2,1)S(1)}, u32[]{:S(2)}, u32[]{:S(2)}) %collective-permute-start.22) | collective-permute-done | bytes 131104 | tf_op jit(solution)/shard_map/ppermute | solution.py:37
  121.6 2.3 %collective-permute-done.21 = bf16[256,256]{1,0:T(8,128)(2,1)S(1)} collective-permute-done((bf16[256,256]{1,0:T(8,128)(2,1)S(1)}, bf16[256,256]{1,0:T(8,128)(2,1)S(1)}, u32[]{:S(2)}, u32[]{:S(2)}) %collective-permute-start.21) | collective-permute-done | bytes 131104 | tf_op jit(solution)/shard_map/ppermute | solution.py:37
  123.9 1.1 collective-permute-done.20
  125.2 2.3 %collective-permute-start.24 = (bf16[256,256]{1,0:T(8,128)(2,1)S(1)}, bf16[256,256]{1,0:T(8,128)(2,1)S(1)}, u32[]{:S(2)}, u32[]{:S(2)}) collective-permute-start(bf16[256,256]{1,0:T(8,128)(2,1)S(1)} %add_convert_fusion.10.refs_0_), channel_id=1, source_target_pairs={{0,2},{1,3},{2,0},{3,1},{4,6},{5,7},{6,4},{7,5},{8,10},{9,11},{10,... | collective-permute-start | bytes 393224 | tf_op jit(solution)/shard_map/ppermute | solution.py:37
  128.4 3.6 %shard_map.234 = (bf16[256,256]{1,0:T(8,128)(2,1)}, bf16[256,256]{1,0:T(8,128)(2,1)}, bf16[256,256]{1,0:T(8,128)(2,1)}, bf16[256,256]{1,0:T(8,128)(2,1)}) custom-call(s32[4]{0:T(128)} %pad_add_fusion.idx, bf16[256,3456]{1,0:T(8,128)(2,1)} %get-tuple-element.124.hidden.big, bf16[1024,3712]{1,0:T(8,128)(2,1)} %all-gather.2.cloned.1.call-done.w_low.w_high.wd.refs_4_.refs_5_), custom_call_target="tpu_custom_call" | custom-call | flops 603979776 | bytes 9895952 | tf_op jit(solution)/shard_map/pallas_call | solution.py:55
  132.0 2.4 %collective-permute-done.23.refs_1_ = bf16[256,256]{1,0:T(8,128)(2,1)S(1)} collective-permute-done((bf16[256,256]{1,0:T(8,128)(2,1)S(1)}, bf16[256,256]{1,0:T(8,128)(2,1)S(1)}, u32[]{:S(2)}, u32[]{:S(2)}) %collective-permute-start.23) | collective-permute-done | bytes 131104 | tf_op jit(solution)/shard_map/ppermute | solution.py:37
  135.7 6.5 %shard_map.235 = (f32[256,256]{1,0:T(8,128)}, bf16[1024,256]{1,0:T(8,128)(2,1)}, f32[8,1024]{1,0:T(8,128)}, bf16[256,256]{1,0:T(8,128)(2,1)}, f32[64,1]{1,0:T(8,...) custom-call(s32[4]{0:T(128)} %pad_add_fusion.idx, f32[256,1024]{1,0:T(8,128)} %get-tuple-element.119.middle, ...), custom_call_target="tpu_custom_call" | custom-call | flops 1342177280 | bytes 21250576 | tf_op jit(solution)/shard_map/pallas_call | solution.py:55
  142.3 2.1 collective-permute-done.26
  144.4 1.9 add_convert_fusion.6
  146.3 2.3 %collective-permute-start.27 = (bf16[256,256]{1,0:T(8,128)(2,1)S(1)}, bf16[256,256]{1,0:T(8,128)(2,1)S(1)}, u32[]{:S(2)}, u32[]{:S(2)}) collective-permute-start(bf16[256,256]{1,0:T(8,128)(2,1)S(1)} %get-tuple-element.178), channel_id=1, source_target_pairs={{0,8},{8,16},{16,24},{24,0},{1,9},{9,17},{17,25},{25,1},{2,10},{10... | collective-permute-start | bytes 393224 | tf_op jit(solution)/shard_map/ppermute | solution.py:37
  148.5 7.9 %collective-permute-start.28 = (bf16[256,256]{1,0:T(8,128)(2,1)S(1)}, bf16[256,256]{1,0:T(8,128)(2,1)S(1)}, u32[]{:S(2)}, u32[]{:S(2)}) collective-permute-start(bf16[256,256]{1,0:T(8,128)(2,1)S(1)} %get-tuple-element.177), channel_id=1, source_target_pairs={{0,16},{8,24},{16,0},{24,8},{1,17},{9,25},{17,1},{25,9},{2,18},{10... | collective-permute-start | bytes 393224 | tf_op jit(solution)/shard_map/ppermute | solution.py:37
  156.4 2.3 %collective-permute-done.27.refs_1_ = bf16[256,256]{1,0:T(8,128)(2,1)S(1)} collective-permute-done((bf16[256,256]{1,0:T(8,128)(2,1)S(1)}, bf16[256,256]{1,0:T(8,128)(2,1)S(1)}, u32[]{:S(2)}, u32[]{:S(2)}) %collective-permute-start.27) | collective-permute-done | bytes 131104 | tf_op jit(solution)/shard_map/ppermute | solution.py:37
  158.8 3.0 %collective-permute-start.32 = (bf16[256,256]{1,0:T(8,128)(2,1)S(1)}, bf16[256,256]{1,0:T(8,128)(2,1)S(1)}, u32[]{:S(2)}, u32[]{:S(2)}) collective-permute-start(bf16[256,256]{1,0:T(8,128)(2,1)S(1)} %copy-done.30), channel_id=1, source_target_pairs={{0,3},{1,0},{2,1},{3,2},{4,7},{5,4},{6,5},{7,6},{8,11},{9,8},{10,9... | collective-permute-start | bytes 393224 | tf_op jit(solution)/shard_map/ppermute | solution.py:37
  161.8 1.2 collective-permute-start.30
  163.7 3.7 %shard_map.236 = (bf16[256,512]{1,0:T(8,128)(2,1)}, f32[8,1024]{1,0:T(8,128)}, f32[64,1]{1,0:T(8,128)}, bf16[272,256]{1,0:T(8,128)(2,1)}, bf16[272,256]{1,0:T(8,...) custom-call(s32[4]{0:T(128)} %pad_add_fusion.idx, bf16[256,256]{1,0:T(8,128)(2,1)} %get-tuple-element.179.refs_0_, ...), custom_call_target="tpu_custom_call" | custom-call | flops 268435456 | bytes 3834384 | tf_op jit(solution)/shard_map/pallas_call | solution.py:55
  167.4 3.2 %shard_map.237 = (bf16[512,896]{1,0:T(8,128)(2,1)}, bf16[512,896]{1,0:T(8,128)(2,1)}) custom-call(s32[4]{0:T(128)} %pad_add_fusion.idx, bf16[1024,256]{1,0:T(8,128)(2,1)} %get-tuple-element.104.one_rel, bf16[1024,256]{1,0:T(8,128)(2,1)} %get-tuple-element.137.mid_rel, bf16[256,512]{1,0:T(8,128)(2,1)} %get-tuple-element.147.qkv_gb, ...), custom_call_target="tpu_custom_call" | custom-call | flops 402653184 | bytes 3342864 | tf_op jit(solution)/shard_map/pallas_call | solution.py:55
  170.8 1.7 add_convert_fusion.5
  172.5 2.7 %collective-permute-done.33 = bf16[512,896]{1,0:T(8,128)(2,1)S(1)} collective-permute-done((bf16[512,896]{1,0:T(8,128)(2,1)}, bf16[512,896]{1,0:T(8,128)(2,1)S(1)}, u32[]{:S(2)}, u32[]{:S(2)}) %collective-permute-start.33) | collective-permute-done | bytes 917536 | tf_op jit(solution)/shard_map/ppermute | solution.py:37
  175.2 1.4 add_convert_fusion.2
  176.6 1.1 collective-permute-start.34
  177.7 2.2 collective-permute-start.39
  179.9 1.8 collective-permute-start.38
  181.9 4.2 %collective-permute-done.34 = bf16[128,896]{1,0:T(8,128)(2,1)S(1)} collective-permute-done((bf16[128,896]{1,0:T(8,128)(2,1)S(1)}, bf16[128,896]{1,0:T(8,128)(2,1)S(1)}, u32[]{:S(2)}, u32[]{:S(2)}) %collective-permute-start.34) | collective-permute-done | bytes 229408 | tf_op jit(solution)/shard_map/ppermute | solution.py:37
  186.1 3.5 %collective-permute-done.39 = bf16[128,896]{1,0:T(8,128)(2,1)S(1)} collective-permute-done((bf16[128,896]{1,0:T(8,128)(2,1)S(1)}, bf16[128,896]{1,0:T(8,128)(2,1)S(1)}, u32[]{:S(2)}, u32[]{:S(2)}) %collective-permute-start.39) | collective-permute-done | bytes 229408 | tf_op jit(solution)/shard_map/ppermute | solution.py:37
  190.5 1.1 add_convert_fusion
  191.6 2.2 %collective-permute-start.42 = (bf16[32,896]{1,0:T(8,128)(2,1)S(1)}, bf16[32,896]{1,0:T(8,128)(2,1)S(1)}, u32[]{:S(2)}, u32[]{:S(2)}) collective-permute-start(bf16[32,896]{1,0:T(8,128)(2,1)S(1)} %get-tuple-element.181), channel_id=1, source_target_pairs={{0,24},{8,0},{16,8},{24,16},{1,25},{9,1},{17,9},{25,17},{2,26},{10... | collective-permute-start | bytes 172040 | tf_op jit(solution)/shard_map/ppermute | solution.py:37
  195.5 2.8 %collective-permute-start.37 = (bf16[272,256]{1,0:T(8,128)(2,1)S(1)}, bf16[272,256]{1,0:T(8,128)(2,1)S(1)}, u32[]{:S(2)}, u32[]{:S(2)}) collective-permute-start(bf16[272,256]{1,0:T(8,128)(2,1)S(1)} %copy-done.27), channel_id=1, source_target_pairs={{0,3},{1,0},{2,1},{3,2},{4,7},{5,4},{6,5},{7,6},{8,11},{9,8},{10,9... | collective-permute-start | bytes 417800 | tf_op jit(solution)/shard_map/ppermute | solution.py:37
  198.3 1.6 collective-permute-start.36
  200.6 2.8 %collective-permute-start.45 = (f32[32,128]{1,0:T(8,128)S(1)}, f32[32,128]{1,0:T(8,128)S(1)}, u32[]{:S(2)}, u32[]{:S(2)}) collective-permute-start(f32[32,128]{1,0:T(8,128)S(1)} %slice.185), channel_id=1, source_target_pairs={{0,3},{1,0},{2,1},{3,2},{4,7},{5,4},{6,5},{7,6},{8,11},{9,8},{10,9... | collective-permute-start | bytes 49160 | tf_op jit(solution)/shard_map/ppermute | solution.py:37
  203.4 1.6 collective-permute-start.44
  206.3 1.9 collective-permute-start.35
  208.7 1.2 collective-permute-done.43
  213.7 1.7 fusion.10
  (163 shorter events, 29.5 us)
Async XLA Ops:
  7.2 28.8 %copy-start.34 = (bf16[64]{0:T(256)(128)(2,1)S(1)}, bf16[64]{0:T(256)(128)(2,1)}, u32[]{:S(2)}) copy-start(bf16[64]{0:T(256)(128)(2,1)} %param.17) | copy-start | bytes 388
  7.2 28.8 %copy-start.35 = (bf16[64]{0:T(256)(128)(2,1)S(1)}, bf16[64]{0:T(256)(128)(2,1)}, u32[]{:S(2)}) copy-start(bf16[64]{0:T(256)(128)(2,1)} %param.16) | copy-start | bytes 388
  7.2 64.2 %all-gather.2.cloned.1.call-start = ((), (), s32[]{:S(2)}) async-start(), calls=%async_computation.1 | async-start | bytes 7839744 | tf_op jit(solution)/shard_map/all_gather | solution.py:484
  9.0 204.8 %reduce-scatter.2.cloned.1.call-start = ((), (), s32[]{:S(2)}) async-start(), calls=%async_computation.2 | async-start | bytes 7299072 | tf_op jit(solution)/shard_map/reduce_scatter | solution.py:592
  10.6 10.9 %collective-permute-start.2 = (bf16[32,640]{1,0:T(8,128)(2,1)S(1)}, bf16[32,640]{1,0:T(8,128)(2,1)S(1)}, u32[]{:S(2)}, u32[]{:S(2)}) collective-permute-start(bf16[32,640]{1,0:T(8,128)(2,1)S(1)} %pad_maximum_fusion.3), channel_id=1, source_target_pairs={{0,24},{8,0},{16,8},{24,16},{1,25},{9,1},{17,9},{25,17},{2,26},{10... | collective-permute-start | bytes 122888 | tf_op jit(solution)/shard_map/ppermute | solution.py:37
  14.7 8.2 %collective-permute-start.1 = (bf16[32,640]{1,0:T(8,128)(2,1)S(1)}, bf16[32,640]{1,0:T(8,128)(2,1)S(1)}, u32[]{:S(2)}, u32[]{:S(2)}) collective-permute-start(bf16[32,640]{1,0:T(8,128)(2,1)S(1)} %pad_maximum_fusion.3), channel_id=1, source_target_pairs={{0,16},{8,24},{16,0},{24,8},{1,17},{9,25},{17,1},{25,9},{2,18},{10... | collective-permute-start | bytes 122888 | tf_op jit(solution)/shard_map/ppermute | solution.py:37
  14.7 8.2 %collective-permute-start = (bf16[32,640]{1,0:T(8,128)(2,1)S(1)}, bf16[32,640]{1,0:T(8,128)(2,1)S(1)}, u32[]{:S(2)}, u32[]{:S(2)}) collective-permute-start(bf16[32,640]{1,0:T(8,128)(2,1)S(1)} %pad_maximum_fusion.3), channel_id=1, source_target_pairs={{0,8},{8,16},{16,24},{24,0},{1,9},{9,17},{17,25},{25,1},{2,10},{10... | collective-permute-start | bytes 122888 | tf_op jit(solution)/shard_map/ppermute | solution.py:37
  16.9 23.4 %copy-start.1 = (bf16[256,512]{1,0:T(8,128)(2,1)}, bf16[256,512]{1,0:T(8,128)(2,1)S(1)}, u32[]{:S(2)}) copy-start(bf16[256,512]{1,0:T(8,128)(2,1)S(1)} %pad_maximum_fusion.refs_0_) | copy-start | bytes 786436
  16.9 21.1 %collective-permute-start.6 = (bf16[256,512]{1,0:T(8,128)(2,1)S(1)}, bf16[256,512]{1,0:T(8,128)(2,1)S(1)}, u32[]{:S(2)}, u32[]{:S(2)}) collective-permute-start(bf16[256,512]{1,0:T(8,128)(2,1)S(1)} %pad_maximum_fusion.refs_0_), channel_id=1, source_target_pairs={{0,1},{1,2},{2,3},{3,0},{4,5},{5,6},{6,7},{7,4},{8,9},{9,10},{10,1... | collective-permute-start | bytes 786440 | tf_op jit(solution)/shard_map/ppermute | solution.py:37
  18.6 19.4 %collective-permute-start.7 = (bf16[256,512]{1,0:T(8,128)(2,1)S(1)}, bf16[256,512]{1,0:T(8,128)(2,1)S(1)}, u32[]{:S(2)}, u32[]{:S(2)}) collective-permute-start(bf16[256,512]{1,0:T(8,128)(2,1)S(1)} %pad_maximum_fusion.refs_0_), channel_id=1, source_target_pairs={{0,2},{1,3},{2,0},{3,1},{4,6},{5,7},{6,4},{7,5},{8,10},{9,11},{10,... | collective-permute-start | bytes 786440 | tf_op jit(solution)/shard_map/ppermute | solution.py:37
  21.5 16.5 %collective-permute-start.8 = (bf16[256,512]{1,0:T(8,128)(2,1)S(1)}, bf16[256,512]{1,0:T(8,128)(2,1)S(1)}, u32[]{:S(2)}, u32[]{:S(2)}) collective-permute-start(bf16[256,512]{1,0:T(8,128)(2,1)S(1)} %pad_maximum_fusion.refs_0_), channel_id=1, source_target_pairs={{0,3},{1,0},{2,1},{3,2},{4,7},{5,4},{6,5},{7,6},{8,11},{9,8},{10,9... | collective-permute-start | bytes 786440 | tf_op jit(solution)/shard_map/ppermute | solution.py:37
  23.6 7.8 %collective-permute-start.3 = (bf16[128,640]{1,0:T(8,128)(2,1)S(1)}, bf16[128,640]{1,0:T(8,128)(2,1)S(1)}, u32[]{:S(2)}, u32[]{:S(2)}) collective-permute-start(bf16[128,640]{1,0:T(8,128)(2,1)S(1)} %pad_maximum_fusion.2), channel_id=1, source_target_pairs={{0,32},{32,64},{64,96},{96,0},{1,33},{33,65},{65,97},{97,1},{2,34}... | collective-permute-start | bytes 491528 | tf_op jit(solution)/shard_map/ppermute | solution.py:37
  25.2 12.3 %collective-permute-start.4 = (bf16[128,640]{1,0:T(8,128)(2,1)S(1)}, bf16[128,640]{1,0:T(8,128)(2,1)S(1)}, u32[]{:S(2)}, u32[]{:S(2)}) collective-permute-start(bf16[128,640]{1,0:T(8,128)(2,1)S(1)} %pad_maximum_fusion.2), channel_id=1, source_target_pairs={{0,64},{32,96},{64,0},{96,32},{1,65},{33,97},{65,1},{97,33},{2,66}... | collective-permute-start | bytes 491528 | tf_op jit(solution)/shard_map/ppermute | solution.py:37
  31.4 6.6 %collective-permute-start.5 = (bf16[128,640]{1,0:T(8,128)(2,1)S(1)}, bf16[128,640]{1,0:T(8,128)(2,1)S(1)}, u32[]{:S(2)}, u32[]{:S(2)}) collective-permute-start(bf16[128,640]{1,0:T(8,128)(2,1)S(1)} %pad_maximum_fusion.2), channel_id=1, source_target_pairs={{0,96},{32,0},{64,32},{96,64},{1,97},{33,1},{65,33},{97,65},{2,98}... | collective-permute-start | bytes 491528 | tf_op jit(solution)/shard_map/ppermute | solution.py:37
  38.2 2.2 collective-permute-start.9
  45.2 10.3 %collective-permute-start.10 = (bf16[256,256]{1,0:T(8,128)(2,1)}, bf16[256,256]{1,0:T(8,128)(2,1)S(1)}, u32[]{:S(2)}, u32[]{:S(2)}) collective-permute-start(bf16[256,256]{1,0:T(8,128)(2,1)} %get-tuple-element.108), channel_id=1, source_target_pairs={{0,8},{8,16},{16,24},{24,0},{1,9},{9,17},{17,25},{25,1},{2,10},{10... | collective-permute-start | bytes 393224 | tf_op jit(solution)/shard_map/ppermute | solution.py:37
  47.9 13.5 %collective-permute-start.11 = (bf16[256,256]{1,0:T(8,128)(2,1)}, bf16[256,256]{1,0:T(8,128)(2,1)S(1)}, u32[]{:S(2)}, u32[]{:S(2)}) collective-permute-start(bf16[256,256]{1,0:T(8,128)(2,1)} %get-tuple-element.108), channel_id=1, source_target_pairs={{0,16},{8,24},{16,0},{24,8},{1,17},{9,25},{17,1},{25,9},{2,18},{10... | collective-permute-start | bytes 393224 | tf_op jit(solution)/shard_map/ppermute | solution.py:37
  49.8 12.1 %collective-permute-start.12 = (bf16[256,256]{1,0:T(8,128)(2,1)}, bf16[256,256]{1,0:T(8,128)(2,1)S(1)}, u32[]{:S(2)}, u32[]{:S(2)}) collective-permute-start(bf16[256,256]{1,0:T(8,128)(2,1)} %get-tuple-element.108), channel_id=1, source_target_pairs={{0,24},{8,0},{16,8},{24,16},{1,25},{9,1},{17,9},{25,17},{2,26},{10... | collective-permute-start | bytes 393224 | tf_op jit(solution)/shard_map/ppermute | solution.py:37
  61.9 2.5 %collective-permute-start.13 = (bf16[1024,256]{1,0:T(8,128)(2,1)S(1)}, bf16[1024,256]{1,0:T(8,128)(2,1)S(1)}, u32[]{:S(2)}, u32[]{:S(2)}) collective-permute-start(bf16[1024,256]{1,0:T(8,128)(2,1)S(1)} %constant_dynamic-update-slice_fusion.4.kv_own), channel_id=1, source_target_pairs={{0,4},{4,0},{1,5},{5,1},{2,6},{6,2},{3,7},{7,3},{8,12},{12,8},{9,1... | collective-permute-start | bytes 1572872 | tf_op jit(solution)/shard_map/ppermute | solution.py:37
  73.6 8.9 %collective-permute-start.16 = (bf16[256,256]{1,0:T(8,128)(2,1)}, bf16[256,256]{1,0:T(8,128)(2,1)S(1)}, u32[]{:S(2)}, u32[]{:S(2)}) collective-permute-start(bf16[256,256]{1,0:T(8,128)(2,1)} %get-tuple-element.117), channel_id=1, source_target_pairs={{0,3},{1,0},{2,1},{3,2},{4,7},{5,4},{6,5},{7,6},{8,11},{9,8},{10,9... | collective-permute-start | bytes 393224 | tf_op jit(solution)/shard_map/ppermute | solution.py:37
  76.2 8.1 %collective-permute-start.15 = (bf16[256,256]{1,0:T(8,128)(2,1)}, bf16[256,256]{1,0:T(8,128)(2,1)S(1)}, u32[]{:S(2)}, u32[]{:S(2)}) collective-permute-start(bf16[256,256]{1,0:T(8,128)(2,1)} %get-tuple-element.116), channel_id=1, source_target_pairs={{0,2},{1,3},{2,0},{3,1},{4,6},{5,7},{6,4},{7,5},{8,10},{9,11},{10,... | collective-permute-start | bytes 393224 | tf_op jit(solution)/shard_map/ppermute | solution.py:37
  77.2 8.9 %collective-permute-start.14 = (bf16[256,256]{1,0:T(8,128)(2,1)}, bf16[256,256]{1,0:T(8,128)(2,1)S(1)}, u32[]{:S(2)}, u32[]{:S(2)}) collective-permute-start(bf16[256,256]{1,0:T(8,128)(2,1)} %get-tuple-element.115), channel_id=1, source_target_pairs={{0,1},{1,2},{2,3},{3,0},{4,5},{5,6},{6,7},{7,4},{8,9},{9,10},{10,1... | collective-permute-start | bytes 393224 | tf_op jit(solution)/shard_map/ppermute | solution.py:37
  87.0 8.0 %copy-start.8 = (bf16[256,256]{1,0:T(8,128)(2,1)}, bf16[256,256]{1,0:T(8,128)(2,1)S(1)}, u32[]{:S(2)}) copy-start(bf16[256,256]{1,0:T(8,128)(2,1)S(1)} %add_convert_fusion.11.refs_0_) | copy-start | bytes 393220
  87.1 9.5 %collective-permute-start.17 = (bf16[256,256]{1,0:T(8,128)(2,1)S(1)}, bf16[256,256]{1,0:T(8,128)(2,1)S(1)}, u32[]{:S(2)}, u32[]{:S(2)}) collective-permute-start(bf16[256,256]{1,0:T(8,128)(2,1)S(1)} %add_convert_fusion.11.refs_0_), channel_id=1, source_target_pairs={{0,1},{1,2},{2,3},{3,0},{4,5},{5,6},{6,7},{7,4},{8,9},{9,10},{10,1... | collective-permute-start | bytes 393224 | tf_op jit(solution)/shard_map/ppermute | solution.py:37
  87.1 9.4 %collective-permute-start.18 = (bf16[256,256]{1,0:T(8,128)(2,1)S(1)}, bf16[256,256]{1,0:T(8,128)(2,1)S(1)}, u32[]{:S(2)}, u32[]{:S(2)}) collective-permute-start(bf16[256,256]{1,0:T(8,128)(2,1)S(1)} %add_convert_fusion.11.refs_0_), channel_id=1, source_target_pairs={{0,2},{1,3},{2,0},{3,1},{4,6},{5,7},{6,4},{7,5},{8,10},{9,11},{10,... | collective-permute-start | bytes 393224 | tf_op jit(solution)/shard_map/ppermute | solution.py:37
  89.2 8.0 %collective-permute-start.19 = (bf16[256,256]{1,0:T(8,128)(2,1)S(1)}, bf16[256,256]{1,0:T(8,128)(2,1)S(1)}, u32[]{:S(2)}, u32[]{:S(2)}) collective-permute-start(bf16[256,256]{1,0:T(8,128)(2,1)S(1)} %add_convert_fusion.11.refs_0_), channel_id=1, source_target_pairs={{0,3},{1,0},{2,1},{3,2},{4,7},{5,4},{6,5},{7,6},{8,11},{9,8},{10,9... | collective-permute-start | bytes 393224 | tf_op jit(solution)/shard_map/ppermute | solution.py:37
  112.6 12.4 %copy-start.22 = (bf16[256,256]{1,0:T(8,128)(2,1)S(1)}, bf16[256,256]{1,0:T(8,128)(2,1)}, u32[]{:S(2)}) copy-start(bf16[256,256]{1,0:T(8,128)(2,1)} %get-tuple-element.120) | copy-start | bytes 393220
  113.5 8.1 %collective-permute-start.22 = (bf16[256,256]{1,0:T(8,128)(2,1)S(1)}, bf16[256,256]{1,0:T(8,128)(2,1)S(1)}, u32[]{:S(2)}, u32[]{:S(2)}) collective-permute-start(bf16[256,256]{1,0:T(8,128)(2,1)S(1)} %copy-done.33), channel_id=1, source_target_pairs={{0,3},{1,0},{2,1},{3,2},{4,7},{5,4},{6,5},{7,6},{8,11},{9,8},{10,9... | collective-permute-start | bytes 393224 | tf_op jit(solution)/shard_map/ppermute | solution.py:37
  115.9 7.9 %collective-permute-start.21 = (bf16[256,256]{1,0:T(8,128)(2,1)S(1)}, bf16[256,256]{1,0:T(8,128)(2,1)S(1)}, u32[]{:S(2)}, u32[]{:S(2)}) collective-permute-start(bf16[256,256]{1,0:T(8,128)(2,1)S(1)} %copy-done.32), channel_id=1, source_target_pairs={{0,2},{1,3},{2,0},{3,1},{4,6},{5,7},{6,4},{7,5},{8,10},{9,11},{10,... | collective-permute-start | bytes 393224 | tf_op jit(solution)/shard_map/ppermute | solution.py:37
  116.0 9.1 %collective-permute-start.20 = (bf16[256,256]{1,0:T(8,128)(2,1)S(1)}, bf16[256,256]{1,0:T(8,128)(2,1)S(1)}, u32[]{:S(2)}, u32[]{:S(2)}) collective-permute-start(bf16[256,256]{1,0:T(8,128)(2,1)S(1)} %copy-done.31), channel_id=1, source_target_pairs={{0,1},{1,2},{2,3},{3,0},{4,5},{5,6},{6,7},{7,4},{8,9},{9,10},{10,1... | collective-permute-start | bytes 393224 | tf_op jit(solution)/shard_map/ppermute | solution.py:37
  125.1 9.3 %collective-permute-start.23 = (bf16[256,256]{1,0:T(8,128)(2,1)S(1)}, bf16[256,256]{1,0:T(8,128)(2,1)S(1)}, u32[]{:S(2)}, u32[]{:S(2)}) collective-permute-start(bf16[256,256]{1,0:T(8,128)(2,1)S(1)} %add_convert_fusion.10.refs_0_), channel_id=1, source_target_pairs={{0,1},{1,2},{2,3},{3,0},{4,5},{5,6},{6,7},{7,4},{8,9},{9,10},{10,1... | collective-permute-start | bytes 393224 | tf_op jit(solution)/shard_map/ppermute | solution.py:37
  125.2 9.2 %collective-permute-start.24 = (bf16[256,256]{1,0:T(8,128)(2,1)S(1)}, bf16[256,256]{1,0:T(8,128)(2,1)S(1)}, u32[]{:S(2)}, u32[]{:S(2)}) collective-permute-start(bf16[256,256]{1,0:T(8,128)(2,1)S(1)} %add_convert_fusion.10.refs_0_), channel_id=1, source_target_pairs={{0,2},{1,3},{2,0},{3,1},{4,6},{5,7},{6,4},{7,5},{8,10},{9,11},{10,... | collective-permute-start | bytes 393224 | tf_op jit(solution)/shard_map/ppermute | solution.py:37
  127.5 7.6 %collective-permute-start.25 = (bf16[256,256]{1,0:T(8,128)(2,1)S(1)}, bf16[256,256]{1,0:T(8,128)(2,1)S(1)}, u32[]{:S(2)}, u32[]{:S(2)}) collective-permute-start(bf16[256,256]{1,0:T(8,128)(2,1)S(1)} %add_convert_fusion.10.refs_0_), channel_id=1, source_target_pairs={{0,3},{1,0},{2,1},{3,2},{4,7},{5,4},{6,5},{7,6},{8,11},{9,8},{10,9... | collective-permute-start | bytes 393224 | tf_op jit(solution)/shard_map/ppermute | solution.py:37
  135.7 23.1 %copy-start.30 = (bf16[256,256]{1,0:T(8,128)(2,1)S(1)}, bf16[256,256]{1,0:T(8,128)(2,1)}, u32[]{:S(2)}) copy-start(bf16[256,256]{1,0:T(8,128)(2,1)} %get-tuple-element.157) | copy-start | bytes 393220
  135.7 26.2 %copy-start.29 = (bf16[256,256]{1,0:T(8,128)(2,1)S(1)}, bf16[256,256]{1,0:T(8,128)(2,1)}, u32[]{:S(2)}) copy-start(bf16[256,256]{1,0:T(8,128)(2,1)} %get-tuple-element.156) | copy-start | bytes 393220
  135.7 26.2 %copy-start.28 = (bf16[256,256]{1,0:T(8,128)(2,1)S(1)}, bf16[256,256]{1,0:T(8,128)(2,1)}, u32[]{:S(2)}) copy-start(bf16[256,256]{1,0:T(8,128)(2,1)} %get-tuple-element.155) | copy-start | bytes 393220
  142.2 2.2 collective-permute-start.26
  146.3 12.5 %collective-permute-start.27 = (bf16[256,256]{1,0:T(8,128)(2,1)S(1)}, bf16[256,256]{1,0:T(8,128)(2,1)S(1)}, u32[]{:S(2)}, u32[]{:S(2)}) collective-permute-start(bf16[256,256]{1,0:T(8,128)(2,1)S(1)} %get-tuple-element.178), channel_id=1, source_target_pairs={{0,8},{8,16},{16,24},{24,0},{1,9},{9,17},{17,25},{25,1},{2,10},{10... | collective-permute-start | bytes 393224 | tf_op jit(solution)/shard_map/ppermute | solution.py:37
  148.5 14.5 %collective-permute-start.28 = (bf16[256,256]{1,0:T(8,128)(2,1)S(1)}, bf16[256,256]{1,0:T(8,128)(2,1)S(1)}, u32[]{:S(2)}, u32[]{:S(2)}) collective-permute-start(bf16[256,256]{1,0:T(8,128)(2,1)S(1)} %get-tuple-element.177), channel_id=1, source_target_pairs={{0,16},{8,24},{16,0},{24,8},{1,17},{9,25},{17,1},{25,9},{2,18},{10... | collective-permute-start | bytes 393224 | tf_op jit(solution)/shard_map/ppermute | solution.py:37
  156.4 6.6 %collective-permute-start.29 = (bf16[256,256]{1,0:T(8,128)(2,1)S(1)}, bf16[256,256]{1,0:T(8,128)(2,1)S(1)}, u32[]{:S(2)}, u32[]{:S(2)}) collective-permute-start(bf16[256,256]{1,0:T(8,128)(2,1)S(1)} %get-tuple-element.176), channel_id=1, source_target_pairs={{0,24},{8,0},{16,8},{24,16},{1,25},{9,1},{17,9},{25,17},{2,26},{10... | collective-permute-start | bytes 393224 | tf_op jit(solution)/shard_map/ppermute | solution.py:37
  158.8 11.8 %collective-permute-start.32 = (bf16[256,256]{1,0:T(8,128)(2,1)S(1)}, bf16[256,256]{1,0:T(8,128)(2,1)S(1)}, u32[]{:S(2)}, u32[]{:S(2)}) collective-permute-start(bf16[256,256]{1,0:T(8,128)(2,1)S(1)} %copy-done.30), channel_id=1, source_target_pairs={{0,3},{1,0},{2,1},{3,2},{4,7},{5,4},{6,5},{7,6},{8,11},{9,8},{10,9... | collective-permute-start | bytes 393224 | tf_op jit(solution)/shard_map/ppermute | solution.py:37
  161.8 8.8 %collective-permute-start.31 = (bf16[256,256]{1,0:T(8,128)(2,1)S(1)}, bf16[256,256]{1,0:T(8,128)(2,1)S(1)}, u32[]{:S(2)}, u32[]{:S(2)}) collective-permute-start(bf16[256,256]{1,0:T(8,128)(2,1)S(1)} %copy-done.29), channel_id=1, source_target_pairs={{0,2},{1,3},{2,0},{3,1},{4,6},{5,7},{6,4},{7,5},{8,10},{9,11},{10,... | collective-permute-start | bytes 393224 | tf_op jit(solution)/shard_map/ppermute | solution.py:37
  161.8 9.0 %collective-permute-start.30 = (bf16[256,256]{1,0:T(8,128)(2,1)S(1)}, bf16[256,256]{1,0:T(8,128)(2,1)S(1)}, u32[]{:S(2)}, u32[]{:S(2)}) collective-permute-start(bf16[256,256]{1,0:T(8,128)(2,1)S(1)} %copy-done.28), channel_id=1, source_target_pairs={{0,1},{1,2},{2,3},{3,0},{4,5},{5,6},{6,7},{7,4},{8,9},{9,10},{10,1... | collective-permute-start | bytes 393224 | tf_op jit(solution)/shard_map/ppermute | solution.py:37
  163.7 7.1 %copy-start.18 = (bf16[256,256]{1,0:T(8,128)(2,1)S(1)}, bf16[256,256]{1,0:T(8,128)(2,1)}, u32[]{:S(2)}) copy-start(bf16[256,256]{1,0:T(8,128)(2,1)} %get-tuple-element.154) | copy-start | bytes 393220
  170.6 11.1 %copy-start = (bf16[256,1024]{1,0:T(8,128)(2,1)S(1)}, bf16[256,1024]{1,0:T(8,128)(2,1)}, u32[]{:S(2)}) copy-start(bf16[256,1024]{1,0:T(8,128)(2,1)} %get-tuple-element.105.base.refs_10_) | copy-start | bytes 1572868
  172.5 23.0 %copy-start.27 = (bf16[272,256]{1,0:T(8,128)(2,1)S(1)}, bf16[272,256]{1,0:T(8,128)(2,1)}, u32[]{:S(2)}) copy-start(bf16[272,256]{1,0:T(8,128)(2,1)} %get-tuple-element.169) | copy-start | bytes 417796
  172.5 25.8 %copy-start.26 = (bf16[272,256]{1,0:T(8,128)(2,1)S(1)}, bf16[272,256]{1,0:T(8,128)(2,1)}, u32[]{:S(2)}) copy-start(bf16[272,256]{1,0:T(8,128)(2,1)} %get-tuple-element.168) | copy-start | bytes 417796
  172.5 2.7 %collective-permute-start.33 = (bf16[512,896]{1,0:T(8,128)(2,1)}, bf16[512,896]{1,0:T(8,128)(2,1)S(1)}, u32[]{:S(2)}, u32[]{:S(2)}) collective-permute-start(bf16[512,896]{1,0:T(8,128)(2,1)} %get-tuple-element.161), channel_id=1, source_target_pairs={{0,4},{4,0},{1,5},{5,1},{2,6},{6,2},{3,7},{7,3},{8,12},{12,8},{9,1... | collective-permute-start | bytes 2752520 | tf_op jit(solution)/shard_map/ppermute | solution.py:37
  176.6 29.8 %copy-start.25 = (bf16[272,256]{1,0:T(8,128)(2,1)S(1)}, bf16[272,256]{1,0:T(8,128)(2,1)}, u32[]{:S(2)}) copy-start(bf16[272,256]{1,0:T(8,128)(2,1)} %get-tuple-element.167) | copy-start | bytes 417796
  176.6 36.2 %copy-start.11 = (bf16[272,256]{1,0:T(8,128)(2,1)S(1)}, bf16[272,256]{1,0:T(8,128)(2,1)}, u32[]{:S(2)}) copy-start(bf16[272,256]{1,0:T(8,128)(2,1)} %get-tuple-element.166) | copy-start | bytes 417796
  176.6 9.5 %collective-permute-start.34 = (bf16[128,896]{1,0:T(8,128)(2,1)S(1)}, bf16[128,896]{1,0:T(8,128)(2,1)S(1)}, u32[]{:S(2)}, u32[]{:S(2)}) collective-permute-start(bf16[128,896]{1,0:T(8,128)(2,1)S(1)} %get-tuple-element.175), channel_id=1, source_target_pairs={{0,32},{32,64},{64,96},{96,0},{1,33},{33,65},{65,97},{97,1},{2,34}... | collective-permute-start | bytes 688136 | tf_op jit(solution)/shard_map/ppermute | solution.py:37
  177.7 11.9 %collective-permute-start.39 = (bf16[128,896]{1,0:T(8,128)(2,1)S(1)}, bf16[128,896]{1,0:T(8,128)(2,1)S(1)}, u32[]{:S(2)}, u32[]{:S(2)}) collective-permute-start(bf16[128,896]{1,0:T(8,128)(2,1)S(1)} %get-tuple-element.174), channel_id=1, source_target_pairs={{0,96},{32,0},{64,32},{96,64},{1,97},{33,1},{65,33},{97,65},{2,98}... | collective-permute-start | bytes 688136 | tf_op jit(solution)/shard_map/ppermute | solution.py:37
  179.9 10.6 %collective-permute-start.38 = (bf16[128,896]{1,0:T(8,128)(2,1)S(1)}, bf16[128,896]{1,0:T(8,128)(2,1)S(1)}, u32[]{:S(2)}, u32[]{:S(2)}) collective-permute-start(bf16[128,896]{1,0:T(8,128)(2,1)S(1)} %get-tuple-element.173), channel_id=1, source_target_pairs={{0,64},{32,96},{64,0},{96,32},{1,65},{33,97},{65,1},{97,33},{2,66}... | collective-permute-start | bytes 688136 | tf_op jit(solution)/shard_map/ppermute | solution.py:37
  181.9 31.0 %copy-start.9 = (bf16[256,1,256]{2,0,1:T(8,128)(2,1)S(1)}, bf16[256,1,256]{2,0,1:T(8,128)(2,1)}, u32[]{:S(2)}) copy-start(bf16[256,1,256]{2,0,1:T(8,128)(2,1)} %param.13) | copy-start | bytes 393220
  181.9 31.0 %copy-start.10 = (f32[256,256]{1,0:T(8,128)S(1)}, f32[256,256]{1,0:T(8,128)}, u32[]{:S(2)}) copy-start(f32[256,256]{1,0:T(8,128)} %get-tuple-element.159) | copy-start | bytes 786436
  191.6 8.3 %collective-permute-start.42 = (bf16[32,896]{1,0:T(8,128)(2,1)S(1)}, bf16[32,896]{1,0:T(8,128)(2,1)S(1)}, u32[]{:S(2)}, u32[]{:S(2)}) collective-permute-start(bf16[32,896]{1,0:T(8,128)(2,1)S(1)} %get-tuple-element.181), channel_id=1, source_target_pairs={{0,24},{8,0},{16,8},{24,16},{1,25},{9,1},{17,9},{25,17},{2,26},{10... | collective-permute-start | bytes 172040 | tf_op jit(solution)/shard_map/ppermute | solution.py:37
  193.9 6.0 %collective-permute-start.41 = (bf16[32,896]{1,0:T(8,128)(2,1)S(1)}, bf16[32,896]{1,0:T(8,128)(2,1)S(1)}, u32[]{:S(2)}, u32[]{:S(2)}) collective-permute-start(bf16[32,896]{1,0:T(8,128)(2,1)S(1)} %get-tuple-element.182), channel_id=1, source_target_pairs={{0,16},{8,24},{16,0},{24,8},{1,17},{9,25},{17,1},{25,9},{2,18},{10... | collective-permute-start | bytes 172040 | tf_op jit(solution)/shard_map/ppermute | solution.py:37
  193.9 6.7 %collective-permute-start.40 = (bf16[32,896]{1,0:T(8,128)(2,1)S(1)}, bf16[32,896]{1,0:T(8,128)(2,1)S(1)}, u32[]{:S(2)}, u32[]{:S(2)}) collective-permute-start(bf16[32,896]{1,0:T(8,128)(2,1)S(1)} %get-tuple-element.180), channel_id=1, source_target_pairs={{0,8},{8,16},{16,24},{24,0},{1,9},{9,17},{17,25},{25,1},{2,10},{10... | collective-permute-start | bytes 172040 | tf_op jit(solution)/shard_map/ppermute | solution.py:37
  195.5 17.3 %collective-permute-start.37 = (bf16[272,256]{1,0:T(8,128)(2,1)S(1)}, bf16[272,256]{1,0:T(8,128)(2,1)S(1)}, u32[]{:S(2)}, u32[]{:S(2)}) collective-permute-start(bf16[272,256]{1,0:T(8,128)(2,1)S(1)} %copy-done.27), channel_id=1, source_target_pairs={{0,3},{1,0},{2,1},{3,2},{4,7},{5,4},{6,5},{7,6},{8,11},{9,8},{10,9... | collective-permute-start | bytes 417800 | tf_op jit(solution)/shard_map/ppermute | solution.py:37
  198.3 14.5 %collective-permute-start.36 = (bf16[272,256]{1,0:T(8,128)(2,1)S(1)}, bf16[272,256]{1,0:T(8,128)(2,1)S(1)}, u32[]{:S(2)}, u32[]{:S(2)}) collective-permute-start(bf16[272,256]{1,0:T(8,128)(2,1)S(1)} %copy-done.26), channel_id=1, source_target_pairs={{0,2},{1,3},{2,0},{3,1},{4,6},{5,7},{6,4},{7,5},{8,10},{9,11},{10,... | collective-permute-start | bytes 417800 | tf_op jit(solution)/shard_map/ppermute | solution.py:37
  200.6 5.7 %collective-permute-start.45 = (f32[32,128]{1,0:T(8,128)S(1)}, f32[32,128]{1,0:T(8,128)S(1)}, u32[]{:S(2)}, u32[]{:S(2)}) collective-permute-start(f32[32,128]{1,0:T(8,128)S(1)} %slice.185), channel_id=1, source_target_pairs={{0,3},{1,0},{2,1},{3,2},{4,7},{5,4},{6,5},{7,6},{8,11},{9,8},{10,9... | collective-permute-start | bytes 49160 | tf_op jit(solution)/shard_map/ppermute | solution.py:37
  203.4 5.3 %collective-permute-start.44 = (f32[32,128]{1,0:T(8,128)S(1)}, f32[32,128]{1,0:T(8,128)S(1)}, u32[]{:S(2)}, u32[]{:S(2)}) collective-permute-start(f32[32,128]{1,0:T(8,128)S(1)} %slice.185), channel_id=1, source_target_pairs={{0,2},{1,3},{2,0},{3,1},{4,6},{5,7},{6,4},{7,5},{8,10},{9,11},{10,... | collective-permute-start | bytes 49160 | tf_op jit(solution)/shard_map/ppermute | solution.py:37
  205.0 4.9 %collective-permute-start.43 = (f32[32,128]{1,0:T(8,128)S(1)}, f32[32,128]{1,0:T(8,128)S(1)}, u32[]{:S(2)}, u32[]{:S(2)}) collective-permute-start(f32[32,128]{1,0:T(8,128)S(1)} %slice.185), channel_id=1, source_target_pairs={{0,1},{1,2},{2,3},{3,0},{4,5},{5,6},{6,7},{7,4},{8,9},{9,10},{10,1... | collective-permute-start | bytes 49160 | tf_op jit(solution)/shard_map/ppermute | solution.py:37
  206.3 6.4 %collective-permute-start.35 = (bf16[272,256]{1,0:T(8,128)(2,1)S(1)}, bf16[272,256]{1,0:T(8,128)(2,1)S(1)}, u32[]{:S(2)}, u32[]{:S(2)}) collective-permute-start(bf16[272,256]{1,0:T(8,128)(2,1)S(1)} %copy-done.25), channel_id=1, source_target_pairs={{0,1},{1,2},{2,3},{3,0},{4,5},{5,6},{6,7},{7,4},{8,9},{9,10},{10,1... | collective-permute-start | bytes 417800 | tf_op jit(solution)/shard_map/ppermute | solution.py:37
  (20 other events, 37.5 us)
Sparse Core Ops, SparseCore 0:
  10.3 61.0 all-gather.1
  112.7 89.3 reduce-scatter.1

commit v2 on v1

--- a/solution.py
+++ b/solution.py
@@ -55,7 +55,7 @@
     return pl.pallas_call(
         kernel,
         out_shape=outs,
-        in_specs=in_specs or [pl.BlockSpec(memory_space=pltpu.SMEM)] + [vm] * (len(ins) - 1),
+        in_specs=in_specs or [pl.BlockSpec(memory_space=pltpu.SMEM) if x.dtype == jnp.int32 else vm for x in ins],
         out_specs=out_specs or [vm] * len(outs),
         scratch_shapes=list(scratch),
         cost_estimate=pl.CostEstimate(flops=flops, bytes_accessed=nbytes, transcendentals=0),
@@ -145,17 +145,17 @@
 def qkv_kernel(dims, own, qc, kc, oc, idx, *refs):
     nx, nz, nc, n = dims
     pieces = refs[:n]
-    w_own, w_partner, head_gains, cosine, sine = refs[n : n + 5]
-    w, base, gains, q_t, raw_t, kv, rel, turned = refs[n + 5 :]
+    w_parts = refs[n : n + 2 * nx]
+    head_gains, cosine, sine = refs[n + 2 * nx : n + 2 * nx + 3]
+    w, base, gains, q_t, raw_t, kv, rel, turned = refs[n + 2 * nx + 3 :]
     gq, gk = head_columns(head_gains)
     assemble(idx, n, pieces, base)
-    for other, src in enumerate((w_own, w_partner)):
+    for other in range(nc):
         core = idx[2] if other == 0 else 1 - idx[2]
         for zr in range(nz):
             for xr in range(nx):
                 row = (rot_index(idx[0], nx - xr, nx) * nz + rot_index(idx[1], nz - zr, nz)) * nc + core
-                at = xr * nz + zr
-                w[ds(row, own), :] = src[at * own : (at + 1) * own, :]
+                w[ds(row, own), :] = w_parts[other * nx + xr][zr * own : (zr + 1) * own, :]
     qkv = qc + 2 * kc
     gains[...] = w[:, qkv:].astype(f32).T[:8]
     b = base[...].astype(f32)
@@ -173,16 +173,18 @@
     kv[:, :kc] = turn_heads(rt[qc:], gk, co, si, kc // HD).T.astype(bf16)
 
 
-def attend_kernel(dims, qc, kc, oc, idx, q_t, kv_own, kv_partner, kv, attn_t, attn_b, log_total, acc, tot):
+def attend_kernel(dims, qc, kc, oc, idx, q_t, *refs):
     nx, nz, nc, n = dims
+    kv_parts = refs[: nz * nc]
+    kv, attn_t, attn_b, log_total, acc, tot = refs[nz * nc :]
     span = attn_b.shape[0]
     group = qc // kc
     me = idx[1] * nc + idx[2]
-    for other, src in enumerate((kv_own, kv_partner)):
+    for other in range(nc):
         core = idx[2] if other == 0 else 1 - idx[2]
         for zr in range(nz):
             block = rot_index(idx[1], nz - zr, nz) * nc + core
-            kv[ds(block, span), :] = src[zr * span : (zr + 1) * span, :]
+            kv[ds(block, span), :] = kv_parts[other * nz + zr][...]
     acc[...] = jnp.zeros_like(acc)
     tot[...] = jnp.zeros_like(tot)
     keys_at = lax.broadcasted_iota(jnp.int32, (span, span), 0)
@@ -295,8 +297,8 @@
     nx, nz, nc, n = dims
     grads = refs[:n]
     w_low, w_high, attn_t, q_t, raw_t, kv, log_total, head_gains, cosine, sine = refs[n : n + 10]
-    mine, rel, gain_two, q_gb, gq_grad, kv_keep, kv_send = refs[n + 10 : n + 17]
-    full, turned, dq, do_t, delta, mid_grad, do_f, q_n, do_n = refs[n + 17 :]
+    mine, mid, gain_two, q_gb, gq_grad, kv_keep, kv_send = refs[n + 10 : n + 17]
+    full, dq, do_t, delta, mid_grad, do_f, q_n, do_n = refs[n + 17 :]
     span = mine.shape[0]
     group = qc // kc
     me = idx[1] * nc + idx[2]
@@ -312,8 +314,7 @@
     part = grads[0].shape[1]
     mine[...] = mid_grad[:, ds(idx[3], part)]
     mgb = mg.astype(bf16)
-    turned[...] = mgb.T
-    store_relative(dims, idx, rel, turned, own)
+    mid[...] = mgb
     ag = jnp.concatenate([dot(mgb, w_low[...]), dot(mgb, w_high[...])], axis=1)
     to_groups(do_f, ag.T)
     prod = do_f[...] * attn_t[...]
@@ -401,7 +402,7 @@
         pieces[k][along.shape[1] :, :] = tail
 
 
-def attn_grad_kernel(dims, own, qc, kc, oc, idx, one_rel, mid_rel, qkv_gb, attn_b, gain_one, gain_two, gq_grad, gk_grad, keep, send, extra, extra_rel):
+def attn_grad_kernel(dims, own, qc, kc, oc, idx, one_rel, out_rel, qkv_gb, gain_one, gain_two, gq_grad, gk_grad, keep, send, extra, extra_rel):
     half = keep.shape[0]
     qkv = qc + 2 * kc
     width = one_rel.shape[0]
@@ -429,11 +430,45 @@
         extra[i * own : (i + 1) * own, :] = (cols[i * own : (i + 1) * own] + tile).astype(bf16)
     store_relative(dims, idx, extra_rel, extra, own)
     a = dot(one_rel[...], qkv_gb[...]).astype(bf16)
-    b = dot(mid_rel[...], attn_b[...]).astype(bf16)
     for out, at in ((keep, slice(0, half)), (send, slice(half, 2 * half))):
         out[:, :qkv] = a[at]
-        out[:, qkv : qkv + oc] = b[at]
+        out[:, qkv : qkv + oc] = out_rel[at, :]
         out[:, qkv + oc :] = extra_rel[at, :]
+
+
+def sum_kernel(cuts, *refs):
+    outs = refs[len(refs) - len(cuts) + 1 :]
+    ins = refs[: len(refs) - len(cuts) + 1]
+    for out, first, last in zip(outs, cuts[:-1], cuts[1:]):
+        total = ins[0][:, first:last].astype(f32)
+        for v in ins[1:]:
+            total = total + v[:, first:last].astype(f32)
+        out[...] = total
+
+
+def pack_kernel(q, k, v, o, g, u, d, gain_one, gain_two, x, c, attn, ffn, both, square):
+    at = 0
+    for w in (q, k, v):
+        attn[:, at : at + w.shape[1]] = w[...]
+        at += w.shape[1]
+    own = q.shape[0]
+    square[...] = jnp.zeros_like(square)
+    square[0:1, :own] = gain_one[...].astype(f32)
+    square[1:2, :own] = gain_two[...].astype(f32)
+    attn[:, at:] = square[...].T[:own].astype(bf16)
+    at = 0
+    for w in (g, u, d, o):
+        ffn[:, at : at + w.shape[1]] = w[...]
+        at += w.shape[1]
+    part = x.shape[1]
+    both[:, :part] = x[...]
+    both[:, part:] = c[...]
+
+
+def out_grad_kernel(dims, own, idx, mid, attn_b, out, turned, rel):
+    turned[...] = mid[...].T
+    store_relative(dims, idx, rel, turned, own)
+    out[...] = dot(rel[...], attn_b[...]).astype(bf16)
 
 
 def core_sum(keep, send, n):
@@ -480,13 +515,15 @@
     qkv = qc + 2 * kc
     aw = qkv + oc + PAD
 
-    ffn_local = jnp.concatenate([gate_weight, up_weight, down_weight, out_weight], axis=1)
+    attn_local, ffn_local, both = call(
+        pack_kernel,
+        [sds((own, qkv + PAD), bf16), sds((own, 3 * ff + oc), bf16), sds((span, 2 * part), bf16)],
+        [query_weight, key_weight, value_weight, out_weight, gate_weight, up_weight, down_weight]
+        + [attn_gain[None, :], ffn_gain[None, :], block_input.reshape(span, part), cotangent.reshape(span, part)],
+        [pltpu.VMEM((PAD, PAD), f32)],
+    )
     ffn_w = lax.all_gather(ffn_local, ("dp", "z", "core"), axis=0, tiled=True)
-
-    gains_local = jnp.pad(jnp.stack([attn_gain, ffn_gain], axis=1), ((0, 0), (0, PAD - 2)))
-    attn_local = jnp.concatenate([query_weight, key_weight, value_weight, gains_local], axis=1)
     by_z = jnp.concatenate(gathered(attn_local, "z"), axis=0)
-    both = jnp.concatenate([block_input.reshape(span, part), cotangent.reshape(span, part)], axis=1)
     both_parts = gathered(both, "tensor")
     my_first = (idx[1] * nc + idx[2]) * span
     positions = (my_first + jnp.arange(span, dtype=jnp.int32)).astype(f32)
@@ -498,8 +535,7 @@
     dp_parts, both_parts, cosine, sine, head_gains = lax.optimization_barrier(
         (dp_parts, both_parts, cosine, sine, head_gains)
     )
-    w_own = jnp.concatenate(dp_parts, axis=0)
-    w_partner = shift(w_own, "core", 1)
+    dp_partner = [shift(v, "core", 1) for v in dp_parts]
     cot, cot_t = call(
         functools.partial(cot_kernel, dims),
         [sds((span, width), bf16), sds((width, span), bf16)],
@@ -517,12 +553,12 @@
             sds((span, 2 * kc), bf16),
             sds((width, span), bf16),
         ],
-        [idx] + both_parts + [w_own, w_partner, head_gains, cosine, sine],
+        [idx] + both_parts + dp_parts + dp_partner + [head_gains, cosine, sine],
         [pltpu.VMEM((width, span), bf16)],
         flops=2 * span * width * qkv,
     )
-    kv_own = jnp.concatenate(gathered(kv, "z"), axis=0)
-    kv_partner = shift(kv_own, "core", 1)
+    kv_own = gathered(kv, "z")
+    kv_partner = [shift(v, "core", 1) for v in kv_own]
 
     length = span * nz * nc
     (kv_own, kv_partner), (cot, cot_t) = lax.optimization_barrier(((kv_own, kv_partner), (cot, cot_t)))
@@ -533,7 +569,7 @@
     kv_full, attn_t, attn_b, log_total = call(
         functools.partial(attend_kernel, dims, qc, kc, oc),
         [sds((length, 2 * kc), bf16), sds(q_t.shape, f32), sds((span, qc), bf16), sds((8, q_t.shape[1]), f32)],
-        [idx, q_t, kv_own, kv_partner],
+        [idx, q_t] + kv_own + kv_partner,
         [pltpu.VMEM(q_t.shape, f32), pltpu.VMEM((8, q_t.shape[1]), f32)],
         flops=4 * span * length * qc,
     )
@@ -576,8 +612,7 @@
     )
     middle, normed_two, big = res[:3]
     grad_got = [shift(res[3 + k], "tensor", k) for k in range(1, n)]
-    grad_mine = sum([g.astype(f32) for g in grad_got], res[3].astype(f32)).astype(bf16)
-    grad_parts = gathered(grad_mine, "tensor")
+    part_zero = res[3]
 
     ffn_grad = call(
         ffn_grad_kernel,
@@ -589,7 +624,10 @@
         out_specs=[pl.BlockSpec((width, ff), lambda j: (0, j))],
         flops=6 * span * width * ff,
     )[0]
-    ffn_sum = lax.psum_scatter(ffn_grad, ("dp", "z", "core"), scatter_dimension=0, tiled=True).astype(f32)
+    grad_got, ffn_grad = lax.optimization_barrier((grad_got, ffn_grad))
+    grad_mine = sum([g.astype(f32) for g in grad_got], part_zero.astype(f32)).astype(bf16)
+    grad_parts = gathered(grad_mine, "tensor")
+    ffn_sum = lax.psum_scatter(ffn_grad, ("dp", "z", "core"), scatter_dimension=0, tiled=True)
 
     down_parts = call(
         functools.partial(down_kernel, dims),
@@ -606,11 +644,11 @@
     )
     grad_parts, down_parts = lax.optimization_barrier((grad_parts, down_parts))
 
-    mine, mid_rel, gain_two, q_gb, gq_grad, kv_keep, kv_send = call(
+    mine, mid, gain_two, q_gb, gq_grad, kv_keep, kv_send = call(
         functools.partial(attend_back_kernel, dims, own, qc, kc, oc),
         [
             sds((span, part), f32),
-            sds((width, span), bf16),
+            sds((span, width), bf16),
             sds((8, width), f32),
             sds((span, qc), bf16),
             sds((HD, 1), f32),
@@ -620,7 +658,6 @@
         [idx, middle, gains, cot] + grad_parts + [ffn_w, ffn_w, attn_t, q_t, raw_t, kv_full, log_total, head_gains, cosine, sine],
         [
             pltpu.VMEM((span, width), bf16),
-            pltpu.VMEM((width, span), bf16),
             pltpu.VMEM(q_t.shape, f32),
             pltpu.VMEM(q_t.shape, bf16),
             pltpu.VMEM((8, q_t.shape[1]), f32),
@@ -636,7 +673,7 @@
         + [const(v.shape) for v in (attn_t, q_t, raw_t, kv_full, log_total, head_gains, cosine, sine)],
         out_specs=[
             const((span, part)),
-            const((width, span)),
+            const((span, width)),
             const((8, width)),
             const((span, qc)),
             const((HD, 1)),
@@ -648,9 +685,17 @@
     kv_pieces = core_sum(kv_keep, kv_send, nz)
     kv_parts = [kv_pieces[0]] + [shift(kv_pieces[k], "z", k) for k in range(1, nz)]
     kv_parts[1], down_parts = lax.optimization_barrier((kv_parts[1], down_parts))
+    out_rel = call(
+        functools.partial(out_grad_kernel, dims, own),
+        [sds((width, oc), bf16)],
+        [idx, mid, attn_b],
+        [pltpu.VMEM((width, span), bf16)] * 2,
+        flops=2 * span * width * oc,
+    )[0]
+    kv_parts[2], out_rel = lax.optimization_barrier((kv_parts[2], out_rel))
     me_t = idx[3]
     middle_mine = lax.dynamic_slice_in_dim(middle, me_t * part, part, 1)
-    block_output = (middle_mine + summed(down_parts, "tensor")).astype(bf16)
+    down_got = [down_parts[0]] + [shift(down_parts[k], "tensor", k) for k in range(1, n)]
 
     res = call(
         functools.partial(input_grad_kernel, dims, qc, kc),
@@ -665,16 +710,26 @@
     keep, send = call(
         functools.partial(attn_grad_kernel, dims, own, qc, kc, oc),
         [sds((width // 2, aw), bf16)] * 2,
-        [idx, one_rel, mid_rel, qkv_gb, attn_b, gain_one, gain_two, gq_grad, gk_grad],
+        [idx, one_rel, out_rel, qkv_gb, gain_one, gain_two, gq_grad, gk_grad],
         [pltpu.VMEM((width, PAD), bf16), pltpu.VMEM((width, PAD), bf16)],
         flops=2 * span * width * (qkv + oc),
     )
-    (keep, send), block_output = lax.optimization_barrier(((keep, send), block_output))
+    (keep, send), down_got = lax.optimization_barrier(((keep, send), down_got))
     attn_pieces = core_sum(keep, send, nx)
     attn_got = [shift(attn_pieces[k], "dp", k) for k in range(1, nx)]
     attn_got[0], norm_parts = lax.optimization_barrier((attn_got[0], norm_parts))
     attn_x = sum([v.astype(f32) for v in attn_got], attn_pieces[0].astype(f32)).astype(bf16)
-    norm_mine = summed(norm_parts, "tensor")
+    norm_got = [norm_parts[0]] + [shift(norm_parts[k], "tensor", k) for k in range(1, n)]
+    attn_x, norm_got = lax.optimization_barrier((attn_x, norm_got))
+    z_parts = [attn_x[:own]] + [shift(attn_x[k * own : (k + 1) * own], "z", k) for k in range(1, nz)]
+    wgrads = call(
+        functools.partial(sum_kernel, (0, qc, qc + kc, qkv, qkv + oc, aw)),
+        [sds((own, v), f32) for v in (qc, kc, kc, oc, PAD)],
+        z_parts,
+    )
+    small = wgrads[4]
+    block_output = (middle_mine + sum([v.astype(f32) for v in down_got[1:]], down_got[0].astype(f32))).astype(bf16)
+    norm_mine = sum([v.astype(f32) for v in norm_got[1:]], norm_got[0].astype(f32))
     along = (norm_mine[span] + norm_mine[span + 1])[:, None] * (1.0 / width)
     base_f = base.astype(f32)
     scale_one = lax.rsqrt(jnp.mean(base_f * base_f, axis=1, keepdims=True) + EPS)
@@ -682,8 +737,11 @@
     gain_mine = lax.dynamic_slice_in_dim(gains, me_t * part, part, 1)[0:1]
     input_grad = (mine + scale_one * (norm_mine[:span] * gain_mine - unit_mine * along)).astype(bf16)
 
-    attn_sum = row_sum(attn_x, "z")
-    small = attn_sum[:, qkv + oc :]
+    fgrads = call(
+        functools.partial(sum_kernel, (0, ff, 2 * ff, 3 * ff)),
+        [sds((own, ff), f32)] * 3,
+        [ffn_sum],
+    )
     small_all = sum(gathered(small, "tensor"))
     count = 2 * HD // own
     head_sum = (small_all[:, 4 : 4 + count] + small_all[:, 4 + count : 4 + 2 * count]).T.reshape(-1)
@@ -694,13 +752,8 @@
         small[:, 2] + small[:, 3],
         head_sum[:HD],
         head_sum[HD:],
-        attn_sum[:, :qc],
-        attn_sum[:, qc : qc + kc],
-        attn_sum[:, qc + kc : qkv],
-        attn_sum[:, qkv : qkv + oc],
-        ffn_sum[:, :ff],
-        ffn_sum[:, ff : 2 * ff],
-        ffn_sum[:, 2 * ff :],
+        *wgrads[:4],
+        *fgrads,
     )
 
 

time: 223 us -> 223 us (level)
  waiting for transfers between devices: 59.4 us -> 47.2 us
  starting transfers between devices: 73.2 us -> 82.2 us
  Pallas kernels: 47.7 us -> 55.1 us
  other arithmetic: 17.3 us -> 13.8 us
    ppermute x46 -> x52, waiting for transfers between devices: 56.3 us -> 43.8 us  [shift(): return lax.ppermute(x, axis, [(i, (i + k) % n) for i in range(n)])]
    ppermute x46 -> x52, starting transfers between devices: 73.1 us -> 82.2 us  [shift(): return lax.ppermute(x, axis, [(i, (i + k) % n) for i in range(n)])]
    pallas_call x11 -> x15, Pallas kernels: 47.7 us -> 55.1 us  [call(): pl.pallas_call(kernel, out_shape=outs, in_specs=in_specs or [pl.BlockSpec...]
    concatenate x4 -> x0, other arithmetic: 4.21 us -> none  [the longest x1 1.69 us: body(): jnp.concatenate([gate_weight, up_weight, down_weight, out_weight], axis=1)]
    unnamed x78 -> x91, local copies, waits for them, and re-layouts: 5.59 us -> 6.15 us
  transfers between devices with their start and end apart: 48 -> 54, of which waited for: 28 -> 22; matrix products, arithmetic and copies ran while one was open for 8% -> 8% of each run, Pallas kernels for 14% -> 18%
where the time goes in v2:
time: 223 us; the launch traced here: 222 us
  starting transfers between devices  82.2 us (37%)
  Pallas kernels  55.1 us (25%)
  waiting for transfers between devices  47.2 us (21%)
  between operations  14.5 us (7%)
  other arithmetic  13.8 us (6%)
  local copies, waits for them, and re-layouts  9.2 us (4%)
    ppermute x52, starting transfers between devices, shift(): return lax.ppermute(x, axis, [(i, (i + k) % n) for i in range(n)])  82.2 us
    pallas_call x15, Pallas kernels, call(): pl.pallas_call(kernel, out_shape=outs, in_specs=in_specs or [pl.BlockSpec...  55.1 us
    ppermute x52, waiting for transfers between devices, shift(): return lax.ppermute(x, axis, [(i, (i + k) % n) for i in range(n)])  43.8 us
    unnamed x91, local copies, waits for them, and re-layouts  6.15 us
  transfers between devices with their start and end apart: 54, of which 22 were waited for; matrix products, arithmetic and copies ran while one was open for 8% of the time, Pallas kernels for 18%

profile of v2, /device:TPU:0, one launch (start us, length us, event | category | flops | bytes accessed | tf_op | source)
XLA Modules:
  0.0 222.1 jit_solution(14139214132503030336)
XLA Ops:
  7.2 2.0 shard_map.228
  9.3 2.1 collective-permute-start
  11.4 3.6 %collective-permute-start.1 = (bf16[32,640]{1,0:T(8,128)(2,1)}, bf16[32,640]{1,0:T(8,128)(2,1)S(1)}, u32[]{:S(2)}, u32[]{:S(2)}) collective-permute-start(bf16[32,640]{1,0:T(8,128)(2,1)} %get-tuple-element.124), channel_id=1, source_target_pairs={{0,16},{8,24},{16,0},{24,8},{1,17},{9,25},{17,1},{25,9},{2,18},{10... | collective-permute-start | bytes 122888 | tf_op jit(solution)/shard_map/ppermute | solution.py:37
  15.9 1.6 collective-permute-start.6
  17.5 2.9 %collective-permute-start.7 = (bf16[256,512]{1,0:T(8,128)(2,1)}, bf16[256,512]{1,0:T(8,128)(2,1)S(1)}, u32[]{:S(2)}, u32[]{:S(2)}) collective-permute-start(bf16[256,512]{1,0:T(8,128)(2,1)} %get-tuple-element.126.refs_0_), channel_id=1, source_target_pairs={{0,2},{1,3},{2,0},{3,1},{4,6},{5,7},{6,4},{7,5},{8,10},{9,11},{10,... | collective-permute-start | bytes 786440 | tf_op jit(solution)/shard_map/ppermute | solution.py:37
  21.2 1.3 collective-permute-start.8
  22.6 1.6 collective-permute-start.3
  24.2 2.8 %collective-permute-start.4 = (bf16[128,640]{1,0:T(8,128)(2,1)S(1)}, bf16[128,640]{1,0:T(8,128)(2,1)S(1)}, u32[]{:S(2)}, u32[]{:S(2)}) collective-permute-start(bf16[128,640]{1,0:T(8,128)(2,1)S(1)} %constant_dynamic-update-slice_fusion.refs_4_), channel_id=1, source_target_pairs={{0,64},{32,96},{64,0},{96,32},{1,65},{33,97},{65,1},{97,33},{2,66}... | collective-permute-start | bytes 491528 | tf_op jit(solution)/shard_map/ppermute | solution.py:37
  27.0 3.8 %collective-permute-done.3.refs_5_ = bf16[128,640]{1,0:T(8,128)(2,1)S(1)} collective-permute-done((bf16[128,640]{1,0:T(8,128)(2,1)S(1)}, bf16[128,640]{1,0:T(8,128)(2,1)S(1)}, u32[]{:S(2)}, u32[]{:S(2)}) %collective-permute-start.3) | collective-permute-done | bytes 163872 | tf_op jit(solution)/shard_map/ppermute | solution.py:37
  30.8 2.9 %collective-permute-start.5 = (bf16[128,640]{1,0:T(8,128)(2,1)S(1)}, bf16[128,640]{1,0:T(8,128)(2,1)S(1)}, u32[]{:S(2)}, u32[]{:S(2)}) collective-permute-start(bf16[128,640]{1,0:T(8,128)(2,1)S(1)} %constant_dynamic-update-slice_fusion.refs_4_), channel_id=1, source_target_pairs={{0,96},{32,0},{64,32},{96,64},{1,97},{33,1},{65,33},{97,65},{2,98}... | collective-permute-start | bytes 491528 | tf_op jit(solution)/shard_map/ppermute | solution.py:37
  34.5 1.3 maximum_bitcast_fusion.refs_12_.refs_11_.refs_5_
  40.3 4.0 %shard_map.229 = (bf16[1024,640]{1,0:T(8,128)(2,1)}, bf16[256,1024]{1,0:T(8,128)(2,1)}, f32[8,1024]{1,0:T(8,128)}, bf16[128,512]{1,0:T(8,128)(2,1)}, f32[384,256...) custom-call(s32[4]{0:T(128)} %pad_add_fusion.idx, bf16[256,512]{1,0:T(8,128)(2,1)} %get-tuple-element.126.refs_0_, ...), custom_call_target="tpu_custom_call" | custom-call | flops 268435456 | bytes 5472528 | tf_op jit(solution)/shard_map/pallas_call | solution.py:55
  44.3 2.7 %collective-permute-start.13 = (bf16[256,256]{1,0:T(8,128)(2,1)}, bf16[256,256]{1,0:T(8,128)(2,1)S(1)}, u32[]{:S(2)}, u32[]{:S(2)}) collective-permute-start(bf16[256,256]{1,0:T(8,128)(2,1)} %get-tuple-element.143.refs_0_), channel_id=1, source_target_pairs={{0,8},{8,16},{16,24},{24,0},{1,9},{9,17},{17,25},{25,1},{2,10},{10... | collective-permute-start | bytes 393224 | tf_op jit(solution)/shard_map/ppermute | solution.py:37
  47.5 2.2 %collective-permute-start.15 = (bf16[256,256]{1,0:T(8,128)(2,1)}, bf16[256,256]{1,0:T(8,128)(2,1)S(1)}, u32[]{:S(2)}, u32[]{:S(2)}) collective-permute-start(bf16[256,256]{1,0:T(8,128)(2,1)} %get-tuple-element.143.refs_0_), channel_id=1, source_target_pairs={{0,24},{8,0},{16,8},{24,16},{1,25},{9,1},{17,9},{25,17},{2,26},{10... | collective-permute-start | bytes 393224 | tf_op jit(solution)/shard_map/ppermute | solution.py:37
  49.7 4.8 %collective-permute-done.13.refs_1_ = bf16[256,256]{1,0:T(8,128)(2,1)S(1)} collective-permute-done((bf16[256,256]{1,0:T(8,128)(2,1)}, bf16[256,256]{1,0:T(8,128)(2,1)S(1)}, u32[]{:S(2)}, u32[]{:S(2)}) %collective-permute-start.13) | collective-permute-done | bytes 131104 | tf_op jit(solution)/shard_map/ppermute | solution.py:37
  54.6 5.3 %collective-permute-done.14.refs_2_ = bf16[256,256]{1,0:T(8,128)(2,1)S(1)} collective-permute-done((bf16[256,256]{1,0:T(8,128)(2,1)}, bf16[256,256]{1,0:T(8,128)(2,1)S(1)}, u32[]{:S(2)}, u32[]{:S(2)}) %collective-permute-start.14) | collective-permute-done | bytes 131104 | tf_op jit(solution)/shard_map/ppermute | solution.py:37
  61.0 2.3 %shard_map.230 = (bf16[256,1024]{1,0:T(8,128)(2,1)}, bf16[1024,256]{1,0:T(8,128)(2,1)}) custom-call(s32[4]{0:T(128)} %pad_add_fusion.idx, bf16[256,512]{1,0:T(8,128)(2,1)} %get-tuple-element.126.refs_0_, bf16[256,512]{1,0:T(8,128)(2,1)} %copy-done.1, bf16[256,512]{1,0:T(8,128)(2,1)} %copy-done.2, bf16[256,512]{1,0:T(8,128)(2,1)} %copy-done.3), custom_call_target="tpu_custom_call" | custom-call | bytes 2097168 | tf_op jit(solution)/shard_map/pallas_call | solution.py:55
  64.1 3.3 %shard_map.231 = (bf16[2048,256]{1,0:T(8,128)(2,1)}, f32[128,512]{1,0:T(8,128)}, bf16[256,256]{1,0:T(8,128)(2,1)}, f32[8,512]{1,0:T(8,128)}) custom-call(s32[4]{0:T(128)} %pad_add_fusion.idx, bf16[128,512]{1,0:T(8,128)(2,1)} %get-tuple-element.139.q_t.refs_7_, bf16[256,256]{1,0:T(8,128)(2,1)} %get-tuple-element.143.refs_0_, bf16[256,256]{1,0:T(8,128)(2,1)} %copy-done.37, ...), custom_call_target="tpu_custom_call" | custom-call | flops 536870912 | bytes 2637840 | tf_op jit(solution)/shard_map/pallas_call | solution.py:55
  67.4 3.3 %all-gather.2.cloned.1.call-done.w_low.w_high.wd.refs_4_.refs_5_ = bf16[1024,3712]{1,0:T(8,128)(2,1)} async-done(((bf16[32,3712]{1,0:T(8,128)(2,1)}), bf16[1024,3712]{1,0:T(8,128)(2,1)}) %all-gather.2.cloned.1.call-update) | async-done | bytes 7602192 | tf_op jit(solution)/shard_map/all_gather | solution.py:525
  70.7 2.2 %shard_map.232 = (bf16[256,256]{1,0:T(8,128)(2,1)}, bf16[256,256]{1,0:T(8,128)(2,1)}, bf16[256,256]{1,0:T(8,128)(2,1)}, bf16[256,256]{1,0:T(8,128)(2,1)}) custom-call(s32[4]{0:T(128)} %pad_add_fusion.idx, bf16[256,256]{1,0:T(8,128)(2,1)} %get-tuple-element.151.attn_b, bf16[1024,3712]{1,0:T(8,128)(2,1)} %all-gather.2.cloned.1.call-done.w_low.w_high.wd.refs_4_.refs_5_, ...), custom_call_target="tpu_custom_call" | custom-call | flops 134217728 | bytes 15859728 | tf_op jit(solution)/shard_map/pallas_call | solution.py:55
  73.0 1.5 collective-permute-start.20
  74.4 2.3 %collective-permute-start.21 = (bf16[256,256]{1,0:T(8,128)(2,1)}, bf16[256,256]{1,0:T(8,128)(2,1)S(1)}, u32[]{:S(2)}, u32[]{:S(2)}) collective-permute-start(bf16[256,256]{1,0:T(8,128)(2,1)} %get-tuple-element.155), channel_id=1, source_target_pairs={{0,2},{1,3},{2,0},{3,1},{4,6},{5,7},{6,4},{7,5},{8,10},{9,11},{10,... | collective-permute-start | bytes 393224 | tf_op jit(solution)/shard_map/ppermute | solution.py:37
  76.7 1.5 collective-permute-start.22
  78.3 1.8 collective-permute-done.20
  80.1 3.3 %collective-permute-done.21 = bf16[256,256]{1,0:T(8,128)(2,1)S(1)} collective-permute-done((bf16[256,256]{1,0:T(8,128)(2,1)}, bf16[256,256]{1,0:T(8,128)(2,1)S(1)}, u32[]{:S(2)}, u32[]{:S(2)}) %collective-permute-start.21) | collective-permute-done | bytes 131104 | tf_op jit(solution)/shard_map/ppermute | solution.py:37
  84.4 1.8 collective-permute-start.23
  86.2 2.4 %collective-permute-start.24 = (bf16[256,256]{1,0:T(8,128)(2,1)S(1)}, bf16[256,256]{1,0:T(8,128)(2,1)S(1)}, u32[]{:S(2)}, u32[]{:S(2)}) collective-permute-start(bf16[256,256]{1,0:T(8,128)(2,1)S(1)} %add_convert_fusion.11.refs_0_), channel_id=1, source_target_pairs={{0,2},{1,3},{2,0},{3,1},{4,6},{5,7},{6,4},{7,5},{8,10},{9,11},{10,... | collective-permute-start | bytes 393224 | tf_op jit(solution)/shard_map/ppermute | solution.py:37
  89.9 4.2 %shard_map.233.refs_6_ = f32[256,1152]{1,0:T(8,128)} custom-call(bf16[256,1024]{1,0:T(8,128)(2,1)} %get-tuple-element.157.cot, bf16[1024,3712]{1,0:T(8,128)(2,1)} %all-gather.2.cloned.1.call-done.w_low.w_high.wd.refs_4_.refs_5_), custom_call_target="tpu_custom_call" | custom-call | flops 603979776 | bytes 9306112 | tf_op jit(solution)/shard_map/pallas_call | solution.py:55
  95.1 8.5 %shard_map.234 = (f32[256,1024]{1,0:T(8,128)}, bf16[256,1024]{1,0:T(8,128)(2,1)}, bf16[256,3456]{1,0:T(8,128)(2,1)}, bf16[256,256]{1,0:T(8,128)(2,1)}, bf16[256,...) custom-call(s32[4]{0:T(128)} %pad_add_fusion.idx, ...), custom_call_target="tpu_custom_call" | custom-call | flops 2415919104 | bytes 21331984 | tf_op jit(solution)/shard_map/pallas_call | solution.py:55
  103.5 1.3 collective-permute-start.26
  104.8 2.4 %collective-permute-start.27 = (bf16[256,256]{1,0:T(8,128)(2,1)}, bf16[256,256]{1,0:T(8,128)(2,1)S(1)}, u32[]{:S(2)}, u32[]{:S(2)}) collective-permute-start(bf16[256,256]{1,0:T(8,128)(2,1)} %get-tuple-element.162), channel_id=1, source_target_pairs={{0,2},{1,3},{2,0},{3,1},{4,6},{5,7},{6,4},{7,5},{8,10},{9,11},{10,... | collective-permute-start | bytes 393224 | tf_op jit(solution)/shard_map/ppermute | solution.py:37
  108.2 6.3 %shard_map.235 = bf16[1024,3456]{1,0:T(8,128)(2,1)} custom-call(bf16[256,1024]{1,0:T(8,128)(2,1)} %get-tuple-element.164.normed, bf16[1024,256]{1,0:T(8,128)(2,1)} %get-tuple-element.165.cot_t, bf16[256,3456]{1,0:T(8,128)(2,1)} %get-tuple-element.166.big.hidden), custom_call_target="tpu_custom_call" | custom-call | flops 1811939328 | bytes 9895936 | tf_op jit(solution)/shard_map/pallas_call | solution.py:55
  117.7 2.0 collective-permute-start.31
  119.7 3.5 %shard_map.236 = (bf16[256,256]{1,0:T(8,128)(2,1)}, bf16[256,256]{1,0:T(8,128)(2,1)}, bf16[256,256]{1,0:T(8,128)(2,1)}, bf16[256,256]{1,0:T(8,128)(2,1)}) custom-call(s32[4]{0:T(128)} %pad_add_fusion.idx, bf16[256,3456]{1,0:T(8,128)(2,1)} %get-tuple-element.166.big.hidden, bf16[1024,3712]{1,0:T(8,128)(2,1)} %all-gather.2.cloned.1.call-done.w_low.w_high.wd.refs_4_.refs_5_), custom_call_target="tpu_custom_call" | custom-call | flops 603979776 | bytes 9895952 | tf_op jit(solution)/shard_map/pallas_call | solution.py:55
  124.6 6.5 %shard_map.237 = (f32[256,256]{1,0:T(8,128)}, bf16[256,1024]{1,0:T(8,128)(2,1)}, f32[8,1024]{1,0:T(8,128)}, bf16[256,256]{1,0:T(8,128)(2,1)}, f32[64,1]{1,0:T(8,...) custom-call(s32[4]{0:T(128)} %pad_add_fusion.idx, f32[256,1024]{1,0:T(8,128)} %get-tuple-element.158.middle, ...), custom_call_target="tpu_custom_call" | custom-call | flops 1342177280 | bytes 21250576 | tf_op jit(solution)/shard_map/pallas_call | solution.py:55
  131.2 2.1 collective-permute-done.32
  133.3 1.9 add_convert_fusion.6
  135.2 2.5 %collective-permute-start.34 = (bf16[256,256]{1,0:T(8,128)(2,1)S(1)}, bf16[256,256]{1,0:T(8,128)(2,1)S(1)}, u32[]{:S(2)}, u32[]{:S(2)}) collective-permute-start(bf16[256,256]{1,0:T(8,128)(2,1)S(1)} %get-tuple-element.239), channel_id=1, source_target_pairs={{0,8},{8,16},{16,24},{24,0},{1,9},{9,17},{17,25},{25,1},{2,10},{10... | collective-permute-start | bytes 393224 | tf_op jit(solution)/shard_map/ppermute | solution.py:37
  137.7 8.4 %collective-permute-start.33 = (bf16[256,256]{1,0:T(8,128)(2,1)S(1)}, bf16[256,256]{1,0:T(8,128)(2,1)S(1)}, u32[]{:S(2)}, u32[]{:S(2)}) collective-permute-start(bf16[256,256]{1,0:T(8,128)(2,1)S(1)} %get-tuple-element.241), channel_id=1, source_target_pairs={{0,16},{8,24},{16,0},{24,8},{1,17},{9,25},{17,1},{25,9},{2,18},{10... | collective-permute-start | bytes 393224 | tf_op jit(solution)/shard_map/ppermute | solution.py:37
  146.1 2.3 %collective-permute-done.34.refs_1_ = bf16[256,256]{1,0:T(8,128)(2,1)S(1)} collective-permute-done((bf16[256,256]{1,0:T(8,128)(2,1)S(1)}, bf16[256,256]{1,0:T(8,128)(2,1)S(1)}, u32[]{:S(2)}, u32[]{:S(2)}) %collective-permute-start.34) | collective-permute-done | bytes 131104 | tf_op jit(solution)/shard_map/ppermute | solution.py:37
  148.4 1.8 collective-permute-start.36
  150.2 2.4 %collective-permute-start.37 = (bf16[256,256]{1,0:T(8,128)(2,1)S(1)}, bf16[256,256]{1,0:T(8,128)(2,1)S(1)}, u32[]{:S(2)}, u32[]{:S(2)}) collective-permute-start(bf16[256,256]{1,0:T(8,128)(2,1)S(1)} %copy-done.35), channel_id=1, source_target_pairs={{0,2},{1,3},{2,0},{3,1},{4,6},{5,7},{6,4},{7,5},{8,10},{9,11},{10,... | collective-permute-start | bytes 393224 | tf_op jit(solution)/shard_map/ppermute | solution.py:37
  153.3 2.3 %shard_map.238.out_rel = bf16[1024,256]{1,0:T(8,128)(2,1)} custom-call(s32[4]{0:T(128)} %pad_add_fusion.idx, bf16[256,1024]{1,0:T(8,128)(2,1)} %get-tuple-element.184.mid, bf16[256,256]{1,0:T(8,128)(2,1)} %get-tuple-element.151.attn_b), custom_call_target="tpu_custom_call" | custom-call | flops 134217728 | bytes 1179664 | tf_op jit(solution)/shard_map/pallas_call | solution.py:55
  156.3 3.7 %shard_map.239 = (bf16[256,512]{1,0:T(8,128)(2,1)}, f32[8,1024]{1,0:T(8,128)}, f32[64,1]{1,0:T(8,128)}, bf16[272,256]{1,0:T(8,128)(2,1)}, bf16[272,256]{1,0:T(8,...) custom-call(s32[4]{0:T(128)} %pad_add_fusion.idx, bf16[256,256]{1,0:T(8,128)(2,1)} %get-tuple-element.240.refs_0_, ...), custom_call_target="tpu_custom_call" | custom-call | flops 268435456 | bytes 3834384 | tf_op jit(solution)/shard_map/pallas_call | solution.py:55
  160.0 3.1 %shard_map.240 = (bf16[512,896]{1,0:T(8,128)(2,1)}, bf16[512,896]{1,0:T(8,128)(2,1)}) custom-call(s32[4]{0:T(128)} %pad_add_fusion.idx, bf16[1024,256]{1,0:T(8,128)(2,1)} %get-tuple-element.159.one_rel, bf16[1024,256]{1,0:T(8,128)(2,1)} %shard_map.238.out_rel, bf16[256,512]{1,0:T(8,128)(2,1)} %get-tuple-element.194.qkv_gb, ...), custom_call_target="tpu_custom_call" | custom-call | flops 402653184 | bytes 3211792 | tf_op jit(solution)/shard_map/pallas_call | solution.py:55
  164.4 1.5 collective-permute-done.39
  165.9 1.3 add_convert_fusion.3
  167.2 1.4 collective-permute-start.40
  168.7 2.3 %collective-permute-start.41 = (bf16[128,896]{1,0:T(8,128)(2,1)S(1)}, bf16[128,896]{1,0:T(8,128)(2,1)S(1)}, u32[]{:S(2)}, u32[]{:S(2)}) collective-permute-start(bf16[128,896]{1,0:T(8,128)(2,1)S(1)} %get-tuple-element.237), channel_id=1, source_target_pairs={{0,64},{32,96},{64,0},{96,32},{1,65},{33,97},{65,1},{97,33},{2,66}... | collective-permute-start | bytes 688136 | tf_op jit(solution)/shard_map/ppermute | solution.py:37
  171.0 2.0 collective-permute-start.42
  173.0 1.7 fusion.4
  174.7 6.5 %collective-permute-done.40 = bf16[128,896]{1,0:T(8,128)(2,1)S(1)} collective-permute-done((bf16[128,896]{1,0:T(8,128)(2,1)S(1)}, bf16[128,896]{1,0:T(8,128)(2,1)S(1)}, u32[]{:S(2)}, u32[]{:S(2)}) %collective-permute-start.40) | collective-permute-done | bytes 229408 | tf_op jit(solution)/shard_map/ppermute | solution.py:37
  181.2 1.3 collective-permute-start.43
  182.5 1.8 collective-permute-start.44
  184.3 1.5 collective-permute-start.45
  185.7 5.2 %collective-permute-done.41 = bf16[128,896]{1,0:T(8,128)(2,1)S(1)} collective-permute-done((bf16[128,896]{1,0:T(8,128)(2,1)S(1)}, bf16[128,896]{1,0:T(8,128)(2,1)S(1)}, u32[]{:S(2)}, u32[]{:S(2)}) %collective-permute-start.41) | collective-permute-done | bytes 229408 | tf_op jit(solution)/shard_map/ppermute | solution.py:37
  193.5 3.5 %collective-permute-start.47 = (bf16[32,896]{1,0:T(8,128)(2,1)S(1)}, bf16[32,896]{1,0:T(8,128)(2,1)S(1)}, u32[]{:S(2)}, u32[]{:S(2)}) collective-permute-start(bf16[32,896]{1,0:T(8,128)(2,1)S(1)} %get-tuple-element.243), channel_id=1, source_target_pairs={{0,16},{8,24},{16,0},{24,8},{1,17},{9,25},{17,1},{25,9},{2,18},{10... | collective-permute-start | bytes 172040 | tf_op jit(solution)/shard_map/ppermute | solution.py:37
  199.8 1.4 collective-permute-done.48.refs_3_
  201.8 1.5 shard_map.241
  203.3 1.5 collective-permute-start.49
  204.8 1.8 collective-permute-start.50
  206.6 1.5 collective-permute-start.51
  208.2 1.5 add_reduce_fusion
  213.5 1.7 shard_map.242
  (180 shorter events, 30.8 us)
Async XLA Ops:
  7.2 63.5 %all-gather.2.cloned.1.call-start = ((), (), s32[]{:S(2)}) async-start(), calls=%async_computation.1 | async-start | bytes 7839744 | tf_op jit(solution)/shard_map/all_gather | solution.py:525
  9.2 204.3 %reduce-scatter.2.cloned.1.call-start = ((), (), s32[]{:S(2)}) async-start(), calls=%async_computation.2 | async-start | bytes 7299072 | tf_op jit(solution)/shard_map/reduce_scatter | solution.py:630
  9.3 11.9 %collective-permute-start = (bf16[32,640]{1,0:T(8,128)(2,1)}, bf16[32,640]{1,0:T(8,128)(2,1)S(1)}, u32[]{:S(2)}, u32[]{:S(2)}) collective-permute-start(bf16[32,640]{1,0:T(8,128)(2,1)} %get-tuple-element.124), channel_id=1, source_target_pairs={{0,8},{8,16},{16,24},{24,0},{1,9},{9,17},{17,25},{25,1},{2,10},{10... | collective-permute-start | bytes 122888 | tf_op jit(solution)/shard_map/ppermute | solution.py:37
  11.4 11.2 %collective-permute-start.1 = (bf16[32,640]{1,0:T(8,128)(2,1)}, bf16[32,640]{1,0:T(8,128)(2,1)S(1)}, u32[]{:S(2)}, u32[]{:S(2)}) collective-permute-start(bf16[32,640]{1,0:T(8,128)(2,1)} %get-tuple-element.124), channel_id=1, source_target_pairs={{0,16},{8,24},{16,0},{24,8},{1,17},{9,25},{17,1},{25,9},{2,18},{10... | collective-permute-start | bytes 122888 | tf_op jit(solution)/shard_map/ppermute | solution.py:37
  14.9 7.7 %collective-permute-start.2 = (bf16[32,640]{1,0:T(8,128)(2,1)}, bf16[32,640]{1,0:T(8,128)(2,1)S(1)}, u32[]{:S(2)}, u32[]{:S(2)}) collective-permute-start(bf16[32,640]{1,0:T(8,128)(2,1)} %get-tuple-element.124), channel_id=1, source_target_pairs={{0,24},{8,0},{16,8},{24,16},{1,25},{9,1},{17,9},{25,17},{2,26},{10... | collective-permute-start | bytes 122888 | tf_op jit(solution)/shard_map/ppermute | solution.py:37
  15.9 21.0 %collective-permute-start.6 = (bf16[256,512]{1,0:T(8,128)(2,1)}, bf16[256,512]{1,0:T(8,128)(2,1)S(1)}, u32[]{:S(2)}, u32[]{:S(2)}) collective-permute-start(bf16[256,512]{1,0:T(8,128)(2,1)} %get-tuple-element.126.refs_0_), channel_id=1, source_target_pairs={{0,1},{1,2},{2,3},{3,0},{4,5},{5,6},{6,7},{7,4},{8,9},{9,10},{10,1... | collective-permute-start | bytes 786440 | tf_op jit(solution)/shard_map/ppermute | solution.py:37
  17.5 19.4 %collective-permute-start.7 = (bf16[256,512]{1,0:T(8,128)(2,1)}, bf16[256,512]{1,0:T(8,128)(2,1)S(1)}, u32[]{:S(2)}, u32[]{:S(2)}) collective-permute-start(bf16[256,512]{1,0:T(8,128)(2,1)} %get-tuple-element.126.refs_0_), channel_id=1, source_target_pairs={{0,2},{1,3},{2,0},{3,1},{4,6},{5,7},{6,4},{7,5},{8,10},{9,11},{10,... | collective-permute-start | bytes 786440 | tf_op jit(solution)/shard_map/ppermute | solution.py:37
  21.2 15.7 %collective-permute-start.8 = (bf16[256,512]{1,0:T(8,128)(2,1)}, bf16[256,512]{1,0:T(8,128)(2,1)S(1)}, u32[]{:S(2)}, u32[]{:S(2)}) collective-permute-start(bf16[256,512]{1,0:T(8,128)(2,1)} %get-tuple-element.126.refs_0_), channel_id=1, source_target_pairs={{0,3},{1,0},{2,1},{3,2},{4,7},{5,4},{6,5},{7,6},{8,11},{9,8},{10,9... | collective-permute-start | bytes 786440 | tf_op jit(solution)/shard_map/ppermute | solution.py:37
  22.6 16.6 %copy-start.8 = (bf16[128,640]{1,0:T(8,128)(2,1)}, bf16[128,640]{1,0:T(8,128)(2,1)S(1)}, u32[]{:S(2)}) copy-start(bf16[128,640]{1,0:T(8,128)(2,1)S(1)} %constant_dynamic-update-slice_fusion.refs_4_) | copy-start | bytes 491524
  22.6 8.2 %collective-permute-start.3 = (bf16[128,640]{1,0:T(8,128)(2,1)S(1)}, bf16[128,640]{1,0:T(8,128)(2,1)S(1)}, u32[]{:S(2)}, u32[]{:S(2)}) collective-permute-start(bf16[128,640]{1,0:T(8,128)(2,1)S(1)} %constant_dynamic-update-slice_fusion.refs_4_), channel_id=1, source_target_pairs={{0,32},{32,64},{64,96},{96,0},{1,33},{33,65},{65,97},{97,1},{2,34}... | collective-permute-start | bytes 491528 | tf_op jit(solution)/shard_map/ppermute | solution.py:37
  24.2 11.8 %collective-permute-start.4 = (bf16[128,640]{1,0:T(8,128)(2,1)S(1)}, bf16[128,640]{1,0:T(8,128)(2,1)S(1)}, u32[]{:S(2)}, u32[]{:S(2)}) collective-permute-start(bf16[128,640]{1,0:T(8,128)(2,1)S(1)} %constant_dynamic-update-slice_fusion.refs_4_), channel_id=1, source_target_pairs={{0,64},{32,96},{64,0},{96,32},{1,65},{33,97},{65,1},{97,33},{2,66}... | collective-permute-start | bytes 491528 | tf_op jit(solution)/shard_map/ppermute | solution.py:37
  30.8 6.1 %collective-permute-start.5 = (bf16[128,640]{1,0:T(8,128)(2,1)S(1)}, bf16[128,640]{1,0:T(8,128)(2,1)S(1)}, u32[]{:S(2)}, u32[]{:S(2)}) collective-permute-start(bf16[128,640]{1,0:T(8,128)(2,1)S(1)} %constant_dynamic-update-slice_fusion.refs_4_), channel_id=1, source_target_pairs={{0,96},{32,0},{64,32},{96,64},{1,97},{33,1},{65,33},{97,65},{2,98}... | collective-permute-start | bytes 491528 | tf_op jit(solution)/shard_map/ppermute | solution.py:37
  37.0 1.7 collective-permute-start.10
  37.0 1.6 collective-permute-start.11
  37.5 1.4 collective-permute-start.12
  37.6 1.5 collective-permute-start.9
  44.3 10.3 %collective-permute-start.13 = (bf16[256,256]{1,0:T(8,128)(2,1)}, bf16[256,256]{1,0:T(8,128)(2,1)S(1)}, u32[]{:S(2)}, u32[]{:S(2)}) collective-permute-start(bf16[256,256]{1,0:T(8,128)(2,1)} %get-tuple-element.143.refs_0_), channel_id=1, source_target_pairs={{0,8},{8,16},{16,24},{24,0},{1,9},{9,17},{17,25},{25,1},{2,10},{10... | collective-permute-start | bytes 393224 | tf_op jit(solution)/shard_map/ppermute | solution.py:37
  47.0 12.9 %collective-permute-start.14 = (bf16[256,256]{1,0:T(8,128)(2,1)}, bf16[256,256]{1,0:T(8,128)(2,1)S(1)}, u32[]{:S(2)}, u32[]{:S(2)}) collective-permute-start(bf16[256,256]{1,0:T(8,128)(2,1)} %get-tuple-element.143.refs_0_), channel_id=1, source_target_pairs={{0,16},{8,24},{16,0},{24,8},{1,17},{9,25},{17,1},{25,9},{2,18},{10... | collective-permute-start | bytes 393224 | tf_op jit(solution)/shard_map/ppermute | solution.py:37
  47.5 13.5 %collective-permute-start.15 = (bf16[256,256]{1,0:T(8,128)(2,1)}, bf16[256,256]{1,0:T(8,128)(2,1)S(1)}, u32[]{:S(2)}, u32[]{:S(2)}) collective-permute-start(bf16[256,256]{1,0:T(8,128)(2,1)} %get-tuple-element.143.refs_0_), channel_id=1, source_target_pairs={{0,24},{8,0},{16,8},{24,16},{1,25},{9,1},{17,9},{25,17},{2,26},{10... | collective-permute-start | bytes 393224 | tf_op jit(solution)/shard_map/ppermute | solution.py:37
  49.7 13.6 %collective-permute-start.16 = (bf16[256,256]{1,0:T(8,128)(2,1)}, bf16[256,256]{1,0:T(8,128)(2,1)S(1)}, u32[]{:S(2)}, u32[]{:S(2)}) collective-permute-start(bf16[256,256]{1,0:T(8,128)(2,1)} %get-tuple-element.143.refs_0_), channel_id=1, source_target_pairs={{0,4},{4,0},{1,5},{5,1},{2,6},{6,2},{3,7},{7,3},{8,12},{12,8},{9,1... | collective-permute-start | bytes 393224 | tf_op jit(solution)/shard_map/ppermute | solution.py:37
  54.6 8.7 %collective-permute-start.17 = (bf16[256,256]{1,0:T(8,128)(2,1)S(1)}, bf16[256,256]{1,0:T(8,128)(2,1)S(1)}, u32[]{:S(2)}, u32[]{:S(2)}) collective-permute-start(bf16[256,256]{1,0:T(8,128)(2,1)S(1)} %collective-permute-done.13.refs_1_), channel_id=1, source_target_pairs={{0,4},{4,0},{1,5},{5,1},{2,6},{6,2},{3,7},{7,3},{8,12},{12,8},{9,1... | collective-permute-start | bytes 393224 | tf_op jit(solution)/shard_map/ppermute | solution.py:37
  59.9 3.4 %collective-permute-start.18 = (bf16[256,256]{1,0:T(8,128)(2,1)S(1)}, bf16[256,256]{1,0:T(8,128)(2,1)S(1)}, u32[]{:S(2)}, u32[]{:S(2)}) collective-permute-start(bf16[256,256]{1,0:T(8,128)(2,1)S(1)} %collective-permute-done.14.refs_2_), channel_id=1, source_target_pairs={{0,4},{4,0},{1,5},{5,1},{2,6},{6,2},{3,7},{7,3},{8,12},{12,8},{9,1... | collective-permute-start | bytes 393224 | tf_op jit(solution)/shard_map/ppermute | solution.py:37
  61.0 2.4 %collective-permute-start.19 = (bf16[256,256]{1,0:T(8,128)(2,1)S(1)}, bf16[256,256]{1,0:T(8,128)(2,1)S(1)}, u32[]{:S(2)}, u32[]{:S(2)}) collective-permute-start(bf16[256,256]{1,0:T(8,128)(2,1)S(1)} %collective-permute-done.15.refs_3_), channel_id=1, source_target_pairs={{0,4},{4,0},{1,5},{5,1},{2,6},{6,2},{3,7},{7,3},{8,12},{12,8},{9,1... | collective-permute-start | bytes 393224 | tf_op jit(solution)/shard_map/ppermute | solution.py:37
  73.0 7.2 %collective-permute-start.20 = (bf16[256,256]{1,0:T(8,128)(2,1)}, bf16[256,256]{1,0:T(8,128)(2,1)S(1)}, u32[]{:S(2)}, u32[]{:S(2)}) collective-permute-start(bf16[256,256]{1,0:T(8,128)(2,1)} %get-tuple-element.154), channel_id=1, source_target_pairs={{0,1},{1,2},{2,3},{3,0},{4,5},{5,6},{6,7},{7,4},{8,9},{9,10},{10,1... | collective-permute-start | bytes 393224 | tf_op jit(solution)/shard_map/ppermute | solution.py:37
  74.4 9.0 %collective-permute-start.21 = (bf16[256,256]{1,0:T(8,128)(2,1)}, bf16[256,256]{1,0:T(8,128)(2,1)S(1)}, u32[]{:S(2)}, u32[]{:S(2)}) collective-permute-start(bf16[256,256]{1,0:T(8,128)(2,1)} %get-tuple-element.155), channel_id=1, source_target_pairs={{0,2},{1,3},{2,0},{3,1},{4,6},{5,7},{6,4},{7,5},{8,10},{9,11},{10,... | collective-permute-start | bytes 393224 | tf_op jit(solution)/shard_map/ppermute | solution.py:37
  76.7 6.7 %collective-permute-start.22 = (bf16[256,256]{1,0:T(8,128)(2,1)}, bf16[256,256]{1,0:T(8,128)(2,1)S(1)}, u32[]{:S(2)}, u32[]{:S(2)}) collective-permute-start(bf16[256,256]{1,0:T(8,128)(2,1)} %get-tuple-element.156), channel_id=1, source_target_pairs={{0,3},{1,0},{2,1},{3,2},{4,7},{5,4},{6,5},{7,6},{8,11},{9,8},{10,9... | collective-permute-start | bytes 393224 | tf_op jit(solution)/shard_map/ppermute | solution.py:37
  84.4 9.7 %collective-permute-start.23 = (bf16[256,256]{1,0:T(8,128)(2,1)S(1)}, bf16[256,256]{1,0:T(8,128)(2,1)S(1)}, u32[]{:S(2)}, u32[]{:S(2)}) collective-permute-start(bf16[256,256]{1,0:T(8,128)(2,1)S(1)} %add_convert_fusion.11.refs_0_), channel_id=1, source_target_pairs={{0,1},{1,2},{2,3},{3,0},{4,5},{5,6},{6,7},{7,4},{8,9},{9,10},{10,1... | collective-permute-start | bytes 393224 | tf_op jit(solution)/shard_map/ppermute | solution.py:37
  86.2 8.2 %collective-permute-start.24 = (bf16[256,256]{1,0:T(8,128)(2,1)S(1)}, bf16[256,256]{1,0:T(8,128)(2,1)S(1)}, u32[]{:S(2)}, u32[]{:S(2)}) collective-permute-start(bf16[256,256]{1,0:T(8,128)(2,1)S(1)} %add_convert_fusion.11.refs_0_), channel_id=1, source_target_pairs={{0,2},{1,3},{2,0},{3,1},{4,6},{5,7},{6,4},{7,5},{8,10},{9,11},{10,... | collective-permute-start | bytes 393224 | tf_op jit(solution)/shard_map/ppermute | solution.py:37
  88.6 5.8 %collective-permute-start.25 = (bf16[256,256]{1,0:T(8,128)(2,1)S(1)}, bf16[256,256]{1,0:T(8,128)(2,1)S(1)}, u32[]{:S(2)}, u32[]{:S(2)}) collective-permute-start(bf16[256,256]{1,0:T(8,128)(2,1)S(1)} %add_convert_fusion.11.refs_0_), channel_id=1, source_target_pairs={{0,3},{1,0},{2,1},{3,2},{4,7},{5,4},{6,5},{7,6},{8,11},{9,8},{10,9... | collective-permute-start | bytes 393224 | tf_op jit(solution)/shard_map/ppermute | solution.py:37
  103.5 10.9 %collective-permute-start.26 = (bf16[256,256]{1,0:T(8,128)(2,1)}, bf16[256,256]{1,0:T(8,128)(2,1)S(1)}, u32[]{:S(2)}, u32[]{:S(2)}) collective-permute-start(bf16[256,256]{1,0:T(8,128)(2,1)} %get-tuple-element.161), channel_id=1, source_target_pairs={{0,1},{1,2},{2,3},{3,0},{4,5},{5,6},{6,7},{7,4},{8,9},{9,10},{10,1... | collective-permute-start | bytes 393224 | tf_op jit(solution)/shard_map/ppermute | solution.py:37
  104.8 9.7 %collective-permute-start.27 = (bf16[256,256]{1,0:T(8,128)(2,1)}, bf16[256,256]{1,0:T(8,128)(2,1)S(1)}, u32[]{:S(2)}, u32[]{:S(2)}) collective-permute-start(bf16[256,256]{1,0:T(8,128)(2,1)} %get-tuple-element.162), channel_id=1, source_target_pairs={{0,2},{1,3},{2,0},{3,1},{4,6},{5,7},{6,4},{7,5},{8,10},{9,11},{10,... | collective-permute-start | bytes 393224 | tf_op jit(solution)/shard_map/ppermute | solution.py:37
  107.2 7.3 %collective-permute-start.28 = (bf16[256,256]{1,0:T(8,128)(2,1)}, bf16[256,256]{1,0:T(8,128)(2,1)S(1)}, u32[]{:S(2)}, u32[]{:S(2)}) collective-permute-start(bf16[256,256]{1,0:T(8,128)(2,1)} %get-tuple-element.163), channel_id=1, source_target_pairs={{0,3},{1,0},{2,1},{3,2},{4,7},{5,4},{6,5},{7,6},{8,11},{9,8},{10,9... | collective-permute-start | bytes 393224 | tf_op jit(solution)/shard_map/ppermute | solution.py:37
  115.5 7.7 %collective-permute-start.29 = (bf16[256,256]{1,0:T(8,128)(2,1)S(1)}, bf16[256,256]{1,0:T(8,128)(2,1)S(1)}, u32[]{:S(2)}, u32[]{:S(2)}) collective-permute-start(bf16[256,256]{1,0:T(8,128)(2,1)S(1)} %add_convert_fusion.10.refs_0_), channel_id=1, source_target_pairs={{0,1},{1,2},{2,3},{3,0},{4,5},{5,6},{6,7},{7,4},{8,9},{9,10},{10,1... | collective-permute-start | bytes 393224 | tf_op jit(solution)/shard_map/ppermute | solution.py:37
  116.6 6.6 %collective-permute-start.30 = (bf16[256,256]{1,0:T(8,128)(2,1)S(1)}, bf16[256,256]{1,0:T(8,128)(2,1)S(1)}, u32[]{:S(2)}, u32[]{:S(2)}) collective-permute-start(bf16[256,256]{1,0:T(8,128)(2,1)S(1)} %add_convert_fusion.10.refs_0_), channel_id=1, source_target_pairs={{0,2},{1,3},{2,0},{3,1},{4,6},{5,7},{6,4},{7,5},{8,10},{9,11},{10,... | collective-permute-start | bytes 393224 | tf_op jit(solution)/shard_map/ppermute | solution.py:37
  117.7 6.3 %collective-permute-start.31 = (bf16[256,256]{1,0:T(8,128)(2,1)S(1)}, bf16[256,256]{1,0:T(8,128)(2,1)S(1)}, u32[]{:S(2)}, u32[]{:S(2)}) collective-permute-start(bf16[256,256]{1,0:T(8,128)(2,1)S(1)} %add_convert_fusion.10.refs_0_), channel_id=1, source_target_pairs={{0,3},{1,0},{2,1},{3,2},{4,7},{5,4},{6,5},{7,6},{8,11},{9,8},{10,9... | collective-permute-start | bytes 393224 | tf_op jit(solution)/shard_map/ppermute | solution.py:37
  124.6 23.8 %copy-start.36 = (bf16[256,256]{1,0:T(8,128)(2,1)S(1)}, bf16[256,256]{1,0:T(8,128)(2,1)}, u32[]{:S(2)}) copy-start(bf16[256,256]{1,0:T(8,128)(2,1)} %get-tuple-element.202) | copy-start | bytes 393220
  124.6 25.6 %copy-start.35 = (bf16[256,256]{1,0:T(8,128)(2,1)S(1)}, bf16[256,256]{1,0:T(8,128)(2,1)}, u32[]{:S(2)}) copy-start(bf16[256,256]{1,0:T(8,128)(2,1)} %get-tuple-element.203) | copy-start | bytes 393220
  124.6 28.0 %copy-start.34 = (bf16[256,256]{1,0:T(8,128)(2,1)S(1)}, bf16[256,256]{1,0:T(8,128)(2,1)}, u32[]{:S(2)}) copy-start(bf16[256,256]{1,0:T(8,128)(2,1)} %get-tuple-element.204) | copy-start | bytes 393220
  131.1 2.2 collective-permute-start.32
  135.2 13.2 %collective-permute-start.34 = (bf16[256,256]{1,0:T(8,128)(2,1)S(1)}, bf16[256,256]{1,0:T(8,128)(2,1)S(1)}, u32[]{:S(2)}, u32[]{:S(2)}) collective-permute-start(bf16[256,256]{1,0:T(8,128)(2,1)S(1)} %get-tuple-element.239), channel_id=1, source_target_pairs={{0,8},{8,16},{16,24},{24,0},{1,9},{9,17},{17,25},{25,1},{2,10},{10... | collective-permute-start | bytes 393224 | tf_op jit(solution)/shard_map/ppermute | solution.py:37
  137.7 17.9 %collective-permute-start.33 = (bf16[256,256]{1,0:T(8,128)(2,1)S(1)}, bf16[256,256]{1,0:T(8,128)(2,1)S(1)}, u32[]{:S(2)}, u32[]{:S(2)}) collective-permute-start(bf16[256,256]{1,0:T(8,128)(2,1)S(1)} %get-tuple-element.241), channel_id=1, source_target_pairs={{0,16},{8,24},{16,0},{24,8},{1,17},{9,25},{17,1},{25,9},{2,18},{10... | collective-permute-start | bytes 393224 | tf_op jit(solution)/shard_map/ppermute | solution.py:37
  146.1 9.5 %collective-permute-start.35 = (bf16[256,256]{1,0:T(8,128)(2,1)S(1)}, bf16[256,256]{1,0:T(8,128)(2,1)S(1)}, u32[]{:S(2)}, u32[]{:S(2)}) collective-permute-start(bf16[256,256]{1,0:T(8,128)(2,1)S(1)} %get-tuple-element.238), channel_id=1, source_target_pairs={{0,24},{8,0},{16,8},{24,16},{1,25},{9,1},{17,9},{25,17},{2,26},{10... | collective-permute-start | bytes 393224 | tf_op jit(solution)/shard_map/ppermute | solution.py:37
  148.4 14.7 %collective-permute-start.36 = (bf16[256,256]{1,0:T(8,128)(2,1)S(1)}, bf16[256,256]{1,0:T(8,128)(2,1)S(1)}, u32[]{:S(2)}, u32[]{:S(2)}) collective-permute-start(bf16[256,256]{1,0:T(8,128)(2,1)S(1)} %copy-done.36), channel_id=1, source_target_pairs={{0,1},{1,2},{2,3},{3,0},{4,5},{5,6},{6,7},{7,4},{8,9},{9,10},{10,1... | collective-permute-start | bytes 393224 | tf_op jit(solution)/shard_map/ppermute | solution.py:37
  150.2 12.9 %collective-permute-start.37 = (bf16[256,256]{1,0:T(8,128)(2,1)S(1)}, bf16[256,256]{1,0:T(8,128)(2,1)S(1)}, u32[]{:S(2)}, u32[]{:S(2)}) collective-permute-start(bf16[256,256]{1,0:T(8,128)(2,1)S(1)} %copy-done.35), channel_id=1, source_target_pairs={{0,2},{1,3},{2,0},{3,1},{4,6},{5,7},{6,4},{7,5},{8,10},{9,11},{10,... | collective-permute-start | bytes 393224 | tf_op jit(solution)/shard_map/ppermute | solution.py:37
  152.6 10.5 %collective-permute-start.38 = (bf16[256,256]{1,0:T(8,128)(2,1)S(1)}, bf16[256,256]{1,0:T(8,128)(2,1)S(1)}, u32[]{:S(2)}, u32[]{:S(2)}) collective-permute-start(bf16[256,256]{1,0:T(8,128)(2,1)S(1)} %copy-done.34), channel_id=1, source_target_pairs={{0,3},{1,0},{2,1},{3,2},{4,7},{5,4},{6,5},{7,6},{8,11},{9,8},{10,9... | collective-permute-start | bytes 393224 | tf_op jit(solution)/shard_map/ppermute | solution.py:37
  163.1 18.1 %copy-start.33 = (bf16[272,256]{1,0:T(8,128)(2,1)S(1)}, bf16[272,256]{1,0:T(8,128)(2,1)}, u32[]{:S(2)}) copy-start(bf16[272,256]{1,0:T(8,128)(2,1)} %get-tuple-element.218) | copy-start | bytes 417796
  163.1 19.4 %copy-start.32 = (bf16[272,256]{1,0:T(8,128)(2,1)S(1)}, bf16[272,256]{1,0:T(8,128)(2,1)}, u32[]{:S(2)}) copy-start(bf16[272,256]{1,0:T(8,128)(2,1)} %get-tuple-element.219) | copy-start | bytes 417796
  163.1 21.2 %copy-start.31 = (bf16[272,256]{1,0:T(8,128)(2,1)S(1)}, bf16[272,256]{1,0:T(8,128)(2,1)}, u32[]{:S(2)}) copy-start(bf16[272,256]{1,0:T(8,128)(2,1)} %get-tuple-element.220) | copy-start | bytes 417796
  163.1 2.8 %collective-permute-start.39 = (bf16[512,896]{1,0:T(8,128)(2,1)}, bf16[512,896]{1,0:T(8,128)(2,1)S(1)}, u32[]{:S(2)}, u32[]{:S(2)}) collective-permute-start(bf16[512,896]{1,0:T(8,128)(2,1)} %get-tuple-element.211), channel_id=1, source_target_pairs={{0,4},{4,0},{1,5},{5,1},{2,6},{6,2},{3,7},{7,3},{8,12},{12,8},{9,1... | collective-permute-start | bytes 2752520 | tf_op jit(solution)/shard_map/ppermute | solution.py:37
  167.2 30.6 %copy-start.16 = (bf16[272,256]{1,0:T(8,128)(2,1)S(1)}, bf16[272,256]{1,0:T(8,128)(2,1)}, u32[]{:S(2)}) copy-start(bf16[272,256]{1,0:T(8,128)(2,1)} %get-tuple-element.221) | copy-start | bytes 417796
  167.2 13.9 %collective-permute-start.40 = (bf16[128,896]{1,0:T(8,128)(2,1)S(1)}, bf16[128,896]{1,0:T(8,128)(2,1)S(1)}, u32[]{:S(2)}, u32[]{:S(2)}) collective-permute-start(bf16[128,896]{1,0:T(8,128)(2,1)S(1)} %get-tuple-element.235), channel_id=1, source_target_pairs={{0,32},{32,64},{64,96},{96,0},{1,33},{33,65},{65,97},{97,1},{2,34}... | collective-permute-start | bytes 688136 | tf_op jit(solution)/shard_map/ppermute | solution.py:37
  168.7 22.2 %collective-permute-start.41 = (bf16[128,896]{1,0:T(8,128)(2,1)S(1)}, bf16[128,896]{1,0:T(8,128)(2,1)S(1)}, u32[]{:S(2)}, u32[]{:S(2)}) collective-permute-start(bf16[128,896]{1,0:T(8,128)(2,1)S(1)} %get-tuple-element.237), channel_id=1, source_target_pairs={{0,64},{32,96},{64,0},{96,32},{1,65},{33,97},{65,1},{97,33},{2,66}... | collective-permute-start | bytes 688136 | tf_op jit(solution)/shard_map/ppermute | solution.py:37
  171.0 27.0 %copy-start.6 = (bf16[256,1,256]{2,0,1:T(8,128)(2,1)S(1)}, bf16[256,1,256]{2,0,1:T(8,128)(2,1)}, u32[]{:S(2)}) copy-start(bf16[256,1,256]{2,0,1:T(8,128)(2,1)} %param.13) | copy-start | bytes 393220
  171.0 27.0 %copy-start.7 = (f32[256,256]{1,0:T(8,128)S(1)}, f32[256,256]{1,0:T(8,128)}, u32[]{:S(2)}) copy-start(f32[256,256]{1,0:T(8,128)} %get-tuple-element.209) | copy-start | bytes 786436
  171.0 19.9 %collective-permute-start.42 = (bf16[128,896]{1,0:T(8,128)(2,1)S(1)}, bf16[128,896]{1,0:T(8,128)(2,1)S(1)}, u32[]{:S(2)}, u32[]{:S(2)}) collective-permute-start(bf16[128,896]{1,0:T(8,128)(2,1)S(1)} %get-tuple-element.236), channel_id=1, source_target_pairs={{0,96},{32,0},{64,32},{96,64},{1,97},{33,1},{65,33},{97,65},{2,98}... | collective-permute-start | bytes 688136 | tf_op jit(solution)/shard_map/ppermute | solution.py:37
  181.2 10.9 %collective-permute-start.43 = (bf16[272,256]{1,0:T(8,128)(2,1)S(1)}, bf16[272,256]{1,0:T(8,128)(2,1)S(1)}, u32[]{:S(2)}, u32[]{:S(2)}) collective-permute-start(bf16[272,256]{1,0:T(8,128)(2,1)S(1)} %copy-done.33), channel_id=1, source_target_pairs={{0,1},{1,2},{2,3},{3,0},{4,5},{5,6},{6,7},{7,4},{8,9},{9,10},{10,1... | collective-permute-start | bytes 417800 | tf_op jit(solution)/shard_map/ppermute | solution.py:37
  182.5 9.5 %collective-permute-start.44 = (bf16[272,256]{1,0:T(8,128)(2,1)S(1)}, bf16[272,256]{1,0:T(8,128)(2,1)S(1)}, u32[]{:S(2)}, u32[]{:S(2)}) collective-permute-start(bf16[272,256]{1,0:T(8,128)(2,1)S(1)} %copy-done.32), channel_id=1, source_target_pairs={{0,2},{1,3},{2,0},{3,1},{4,6},{5,7},{6,4},{7,5},{8,10},{9,11},{10,... | collective-permute-start | bytes 417800 | tf_op jit(solution)/shard_map/ppermute | solution.py:37
  184.3 7.8 %collective-permute-start.45 = (bf16[272,256]{1,0:T(8,128)(2,1)S(1)}, bf16[272,256]{1,0:T(8,128)(2,1)S(1)}, u32[]{:S(2)}, u32[]{:S(2)}) collective-permute-start(bf16[272,256]{1,0:T(8,128)(2,1)S(1)} %copy-done.31), channel_id=1, source_target_pairs={{0,3},{1,0},{2,1},{3,2},{4,7},{5,4},{6,5},{7,6},{8,11},{9,8},{10,9... | collective-permute-start | bytes 417800 | tf_op jit(solution)/shard_map/ppermute | solution.py:37
  192.7 6.1 %collective-permute-start.46 = (bf16[32,896]{1,0:T(8,128)(2,1)S(1)}, bf16[32,896]{1,0:T(8,128)(2,1)S(1)}, u32[]{:S(2)}, u32[]{:S(2)}) collective-permute-start(bf16[32,896]{1,0:T(8,128)(2,1)S(1)} %get-tuple-element.244), channel_id=1, source_target_pairs={{0,8},{8,16},{16,24},{24,0},{1,9},{9,17},{17,25},{25,1},{2,10},{10... | collective-permute-start | bytes 172040 | tf_op jit(solution)/shard_map/ppermute | solution.py:37
  193.5 6.3 %collective-permute-start.47 = (bf16[32,896]{1,0:T(8,128)(2,1)S(1)}, bf16[32,896]{1,0:T(8,128)(2,1)S(1)}, u32[]{:S(2)}, u32[]{:S(2)}) collective-permute-start(bf16[32,896]{1,0:T(8,128)(2,1)S(1)} %get-tuple-element.243), channel_id=1, source_target_pairs={{0,16},{8,24},{16,0},{24,8},{1,17},{9,25},{17,1},{25,9},{2,18},{10... | collective-permute-start | bytes 172040 | tf_op jit(solution)/shard_map/ppermute | solution.py:37
  197.0 4.2 %collective-permute-start.48 = (bf16[32,896]{1,0:T(8,128)(2,1)S(1)}, bf16[32,896]{1,0:T(8,128)(2,1)S(1)}, u32[]{:S(2)}, u32[]{:S(2)}) collective-permute-start(bf16[32,896]{1,0:T(8,128)(2,1)S(1)} %get-tuple-element.242), channel_id=1, source_target_pairs={{0,24},{8,0},{16,8},{24,16},{1,25},{9,1},{17,9},{25,17},{2,26},{10... | collective-permute-start | bytes 172040 | tf_op jit(solution)/shard_map/ppermute | solution.py:37
  203.3 6.3 %collective-permute-start.49 = (f32[32,128]{1,0:T(8,128)}, f32[32,128]{1,0:T(8,128)S(1)}, u32[]{:S(2)}, u32[]{:S(2)}) collective-permute-start(f32[32,128]{1,0:T(8,128)} %get-tuple-element.226), channel_id=1, source_target_pairs={{0,1},{1,2},{2,3},{3,0},{4,5},{5,6},{6,7},{7,4},{8,9},{9,10},{10,1... | collective-permute-start | bytes 49160 | tf_op jit(solution)/shard_map/ppermute | solution.py:37
  204.8 5.5 %collective-permute-start.50 = (f32[32,128]{1,0:T(8,128)}, f32[32,128]{1,0:T(8,128)S(1)}, u32[]{:S(2)}, u32[]{:S(2)}) collective-permute-start(f32[32,128]{1,0:T(8,128)} %get-tuple-element.226), channel_id=1, source_target_pairs={{0,2},{1,3},{2,0},{3,1},{4,6},{5,7},{6,4},{7,5},{8,10},{9,11},{10,... | collective-permute-start | bytes 49160 | tf_op jit(solution)/shard_map/ppermute | solution.py:37
  206.6 3.9 %collective-permute-start.51 = (f32[32,128]{1,0:T(8,128)}, f32[32,128]{1,0:T(8,128)S(1)}, u32[]{:S(2)}, u32[]{:S(2)}) collective-permute-start(f32[32,128]{1,0:T(8,128)} %get-tuple-element.226), channel_id=1, source_target_pairs={{0,3},{1,0},{2,1},{3,2},{4,7},{5,4},{6,5},{7,6},{8,11},{9,8},{10,9... | collective-permute-start | bytes 49160 | tf_op jit(solution)/shard_map/ppermute | solution.py:37
  (34 other events, 97.2 us)
Sparse Core Ops, SparseCore 0:
  10.3 60.3 all-gather.1
  114.7 98.3 reduce-scatter.1

commit v3 on v2

--- a/solution.py
+++ b/solution.py
@@ -69,15 +69,16 @@
 
 def store_relative(dims, idx, dst, src, own):
     nx, nz, nc, _ = dims
-    x, z, c = idx[0], idx[1], idx[2]
-    at = 0
+    half = nx * nz
     for other in range(nc):
-        core = c if other == 0 else 1 - c
-        for xr in range(nx):
-            for zr in range(nz):
-                row = (rot_index(x, xr, nx) * nz + rot_index(z, zr, nz)) * nc + core
-                dst[at * own : (at + 1) * own, :] = src[ds(row, own), :]
-                at += 1
+        core = idx[2] if other == 0 else 1 - idx[2]
+
+        def step(i, carry, other=other, core=core):
+            row = (rot_index(idx[0], i // nz, nx) * nz + rot_index(idx[1], i % nz, nz)) * nc + core
+            dst[ds(other * half + i, own), :] = src[ds(row, own), :]
+            return carry
+
+        lax.fori_loop(0, half, step, 0)
 
 
 def assemble(idx, n, pieces, dst, first=0):
@@ -86,11 +87,12 @@
         dst[:, ds(rot_index(idx[3], n - k, n), part)] = pieces[k][:, first : first + part]
 
 
-def cot_kernel(dims, idx, *refs):
+def cot_kernel(dims, own, idx, *refs):
     n = dims[3]
-    pieces, (full, turned) = refs[:n], refs[n:]
+    pieces, (full, cot_t, turned) = refs[:n], refs[n:]
     assemble(idx, n, pieces, full, full.shape[1] // n)
     turned[...] = full[...].T
+    by_core(dims, idx, cot_t, turned, own)
 
 
 def head_columns(ref):
@@ -152,10 +154,15 @@
     assemble(idx, n, pieces, base)
     for other in range(nc):
         core = idx[2] if other == 0 else 1 - idx[2]
-        for zr in range(nz):
-            for xr in range(nx):
+        for xr in range(nx):
+            src = w_parts[other * nx + xr]
+
+            def step(zr, carry, src=src, xr=xr, core=core):
                 row = (rot_index(idx[0], nx - xr, nx) * nz + rot_index(idx[1], nz - zr, nz)) * nc + core
-                w[ds(row, own), :] = w_parts[other * nx + xr][zr * own : (zr + 1) * own, :]
+                w[ds(row, own), :] = src[ds(zr, own), :]
+                return carry
+
+            lax.fori_loop(0, nz, step, 0)
     qkv = qc + 2 * kc
     gains[...] = w[:, qkv:].astype(f32).T[:8]
     b = base[...].astype(f32)
@@ -277,20 +284,34 @@
         refs[k][...] = dot(hidden[...], wd[rows, :], NT).astype(bf16)
 
 
-def ffn_grad_kernel(normed, cot_t, big, out, turned):
+def by_core(dims, idx, dst, src, own):
+    nx, nz, nc, _ = dims
+    half = nx * nz
+    for other in range(nc):
+        core = idx[2] if other == 0 else 1 - idx[2]
+
+        def step(i, carry, other=other, core=core):
+            dst[ds(other * half + i, own), :] = src[ds(i * nc + core, own), :]
+            return carry
+
+        lax.fori_loop(0, half, step, 0)
+
+
+def ffn_grad_kernel(dims, own, idx, normed, cot_t, big, keep, send, turned, left):
     j = pl.program_id(0)
+    half = keep.shape[0]
 
     @pl.when(j == 0)
     def _():
         turned[...] = normed[...].T
-
-    @pl.when(j < 2)
-    def _():
-        out[...] = dot(turned[...], big[...]).astype(bf16)
+        by_core(dims, idx, left, turned, own)
 
     @pl.when(j == 2)
     def _():
-        out[...] = dot(cot_t[...], big[...]).astype(bf16)
+        left[...] = cot_t[...]
+
+    keep[...] = dot(left[:half, :], big[...]).astype(bf16)
+    send[...] = dot(left[half:, :], big[...]).astype(bf16)
 
 
 def attend_back_kernel(dims, own, qc, kc, oc, idx, middle, gains, cot, *refs):
@@ -298,7 +319,7 @@
     grads = refs[:n]
     w_low, w_high, attn_t, q_t, raw_t, kv, log_total, head_gains, cosine, sine = refs[n : n + 10]
     mine, mid, gain_two, q_gb, gq_grad, kv_keep, kv_send = refs[n + 10 : n + 17]
-    full, dq, do_t, delta, mid_grad, do_f, q_n, do_n = refs[n + 17 :]
+    full, dq, do_t, delta, mid_grad, do_f, q_n, do_n, out = refs[n + 17 :]
     span = mine.shape[0]
     group = qc // kc
     me = idx[1] * nc + idx[2]
@@ -329,37 +350,37 @@
     query_at = lax.broadcasted_iota(jnp.int32, (span, span), 1)
     ahead = keys_at - query_at
     ahead = jnp.concatenate([ahead] * group, axis=1)
-    for other, out in enumerate((kv_keep, kv_send)):
-        core = idx[2] if other == 0 else 1 - idx[2]
-
-        def step(zr, carry, out=out, core=core):
-            j = rot_index(idx[1], zr, nz) * nc + core
-            at = ds(zr, span)
-
-            @pl.when(j > me)
-            def _():
-                out[at, :] = jnp.zeros((span, 2 * kc), bf16)
-
-            @pl.when(j <= me)
-            def _():
-                kt = kv[ds(j, span), :kc].T
-                allowed = ahead <= (me - j) * span
-                wide = q_t.shape[1]
-                for g in range(kc // HD):
-                    rows = slice(g * HD, (g + 1) * HD)
-                    s = dot(kv[ds(j, span), rows], q_t[rows, :])
-                    p = jnp.where(allowed, jnp.exp(s - log_total[g : g + 1, :]), 0.0)
-                    dp = dot(kv[ds(j, span), kc + g * HD : kc + (g + 1) * HD], do_t[rows, :])
-                    sg = (p * (dp - delta[g : g + 1, :])).astype(bf16)
-                    dq[rows, :] += dot(kt[rows], sg)
-                    dk = dot(sg, q_n[g * wide : (g + 1) * wide, :])
-                    dv = dot(p.astype(bf16), do_n[g * wide : (g + 1) * wide, :])
-                    out[at, rows] = dk.astype(bf16)
-                    out[at, kc + g * HD : kc + (g + 1) * HD] = dv.astype(bf16)
-
-            return carry
-
-        lax.fori_loop(0, nz, step, 0)
+    def step(t, carry):
+        other = t // nz
+        j = rot_index(idx[1], t % nz, nz) * nc + lax.rem(idx[2] + other, nc)
+        at = ds(t, span)
+
+        @pl.when(j > me)
+        def _():
+            out[at, :] = jnp.zeros((span, 2 * kc), bf16)
+
+        @pl.when(j <= me)
+        def _():
+            kt = kv[ds(j, span), :kc].T
+            allowed = ahead <= (me - j) * span
+            wide = q_t.shape[1]
+            for g in range(kc // HD):
+                rows = slice(g * HD, (g + 1) * HD)
+                s = dot(kv[ds(j, span), rows], q_t[rows, :])
+                p = jnp.where(allowed, jnp.exp(s - log_total[g : g + 1, :]), 0.0)
+                dp = dot(kv[ds(j, span), kc + g * HD : kc + (g + 1) * HD], do_t[rows, :])
+                sg = (p * (dp - delta[g : g + 1, :])).astype(bf16)
+                dq[rows, :] += dot(kt[rows], sg)
+                dk = dot(sg, q_n[g * wide : (g + 1) * wide, :])
+                dv = dot(p.astype(bf16), do_n[g * wide : (g + 1) * wide, :])
+                out[at, rows] = dk.astype(bf16)
+                out[at, kc + g * HD : kc + (g + 1) * HD] = dv.astype(bf16)
+
+        return carry
+
+    lax.fori_loop(0, nz * nc, step, 0)
+    kv_keep[...] = out[: nz * span, :]
+    kv_send[...] = out[nz * span :, :]
     raw_grad, gain_grad = turn_heads_back(
         raw_t[:qc, :], from_groups(dq[...], span) * SCALE, head_columns(head_gains)[0], cosine[...], sine[...], qc // HD
     )
@@ -402,7 +423,7 @@
         pieces[k][along.shape[1] :, :] = tail
 
 
-def attn_grad_kernel(dims, own, qc, kc, oc, idx, one_rel, out_rel, qkv_gb, gain_one, gain_two, gq_grad, gk_grad, keep, send, extra, extra_rel):
+def attn_grad_kernel(dims, own, qc, kc, oc, idx, one_rel, out_rel, qkv_gb, gain_one, gain_two, gq_grad, gk_grad, keep, send, extra, extra_rel, lined, spread):
     half = keep.shape[0]
     qkv = qc + 2 * kc
     width = one_rel.shape[0]
@@ -426,8 +447,14 @@
         at = slice(i * own, (i + 1) * own)
         tile = tile + jnp.where(lane == 4 + i, high[at], 0.0)
         tile = tile + jnp.where(lane == 4 + count + i, low[at], 0.0)
-    for i in range(width // own):
-        extra[i * own : (i + 1) * own, :] = (cols[i * own : (i + 1) * own] + tile).astype(bf16)
+    lined[...] = cols
+    spread[...] = tile
+
+    def step(i, carry):
+        extra[ds(i, own), :] = (lined[ds(i, own), :] + spread[...]).astype(bf16)
+        return carry
+
+    lax.fori_loop(0, width // own, step, 0)
     store_relative(dims, idx, extra_rel, extra, own)
     a = dot(one_rel[...], qkv_gb[...]).astype(bf16)
     for out, at in ((keep, slice(0, half)), (send, slice(half, 2 * half))):
@@ -537,9 +564,10 @@
     )
     dp_partner = [shift(v, "core", 1) for v in dp_parts]
     cot, cot_t = call(
-        functools.partial(cot_kernel, dims),
+        functools.partial(cot_kernel, dims, own),
         [sds((span, width), bf16), sds((width, span), bf16)],
         [idx] + both_parts,
+        [pltpu.VMEM((width, span), bf16)],
     )
 
     w, base, gains, q_t, raw_t, kv, one_rel = call(
@@ -614,21 +642,20 @@
     grad_got = [shift(res[3 + k], "tensor", k) for k in range(1, n)]
     part_zero = res[3]
 
-    ffn_grad = call(
-        ffn_grad_kernel,
-        [sds((width, 3 * ff), bf16)],
-        [normed_two, cot_t, big],
-        [pltpu.VMEM((width, span), bf16)],
+    ffn_keep, ffn_send = call(
+        functools.partial(ffn_grad_kernel, dims, own),
+        [sds((width // nc, 3 * ff), bf16)] * 2,
+        [idx, normed_two, cot_t, big],
+        [pltpu.VMEM((width, span), bf16)] * 2,
         grid=(3,),
-        in_specs=[const((span, width)), const((width, span)), pl.BlockSpec((span, ff), lambda j: (0, j))],
-        out_specs=[pl.BlockSpec((width, ff), lambda j: (0, j))],
+        in_specs=[pl.BlockSpec(memory_space=pltpu.SMEM), const((span, width)), const((width, span))]
+        + [pl.BlockSpec((span, ff), lambda j: (0, j))],
+        out_specs=[pl.BlockSpec((width // nc, ff), lambda j: (0, j))] * 2,
         flops=6 * span * width * ff,
-    )[0]
-    grad_got, ffn_grad = lax.optimization_barrier((grad_got, ffn_grad))
+    )
+    grad_got, (ffn_keep, ffn_send) = lax.optimization_barrier((grad_got, (ffn_keep, ffn_send)))
     grad_mine = sum([g.astype(f32) for g in grad_got], part_zero.astype(f32)).astype(bf16)
     grad_parts = gathered(grad_mine, "tensor")
-    ffn_sum = lax.psum_scatter(ffn_grad, ("dp", "z", "core"), scatter_dimension=0, tiled=True)
-
     down_parts = call(
         functools.partial(down_kernel, dims),
         [sds((span, part), bf16)] * n,
@@ -642,7 +669,10 @@
         out_specs=[const((span, part))] * n,
         flops=2 * span * width * ff,
     )
-    grad_parts, down_parts = lax.optimization_barrier((grad_parts, down_parts))
+    ffn_got = shift(ffn_send, "core", 1)
+    grad_parts, ffn_got, down_parts = lax.optimization_barrier((grad_parts, ffn_got, down_parts))
+    ffn_half = (ffn_keep.astype(f32) + ffn_got.astype(f32)).astype(bf16)
+    ffn_x = lax.psum_scatter(ffn_half, "dp", scatter_dimension=0, tiled=True)
 
     mine, mid, gain_two, q_gb, gq_grad, kv_keep, kv_send = call(
         functools.partial(attend_back_kernel, dims, own, qc, kc, oc),
@@ -665,6 +695,7 @@
             pltpu.VMEM(q_t.shape, f32),
             pltpu.VMEM((kc // HD * q_t.shape[1], HD), bf16),
             pltpu.VMEM((kc // HD * q_t.shape[1], HD), bf16),
+            pltpu.VMEM((length, 2 * kc), bf16),
         ],
         grid=(1,),
         in_specs=[pl.BlockSpec(memory_space=pltpu.SMEM), const((span, width)), const((8, width)), const((span, width))]
@@ -711,13 +742,14 @@
         functools.partial(attn_grad_kernel, dims, own, qc, kc, oc),
         [sds((width // 2, aw), bf16)] * 2,
         [idx, one_rel, out_rel, qkv_gb, gain_one, gain_two, gq_grad, gk_grad],
-        [pltpu.VMEM((width, PAD), bf16), pltpu.VMEM((width, PAD), bf16)],
+        [pltpu.VMEM((width, PAD), bf16)] * 2 + [pltpu.VMEM((width, PAD), f32), pltpu.VMEM((own, PAD), f32)],
         flops=2 * span * width * (qkv + oc),
     )
     (keep, send), down_got = lax.optimization_barrier(((keep, send), down_got))
     attn_pieces = core_sum(keep, send, nx)
     attn_got = [shift(attn_pieces[k], "dp", k) for k in range(1, nx)]
-    attn_got[0], norm_parts = lax.optimization_barrier((attn_got[0], norm_parts))
+    attn_got[0], norm_parts, ffn_x = lax.optimization_barrier((attn_got[0], norm_parts, ffn_x))
+    ffn_sum = lax.psum_scatter(ffn_x, "z", scatter_dimension=0, tiled=True)
     attn_x = sum([v.astype(f32) for v in attn_got], attn_pieces[0].astype(f32)).astype(bf16)
     norm_got = [norm_parts[0]] + [shift(norm_parts[k], "tensor", k) for k in range(1, n)]
     attn_x, norm_got = lax.optimization_barrier((attn_x, norm_got))

time: 223 us -> 232 us (1.040)
  waiting for transfers between devices: 47.2 us -> 60.5 us
  starting transfers between devices: 82.2 us -> 71.3 us
  other arithmetic: 13.8 us -> 19.3 us
  Pallas kernels: 55.1 us -> 58 us
    ppermute x52 -> x53, waiting for transfers between devices: 43.8 us -> 58.5 us  [shift(): return lax.ppermute(x, axis, [(i, (i + k) % n) for i in range(n)])]
    ppermute x52 -> x53, starting transfers between devices: 82.2 us -> 71.1 us  [shift(): return lax.ppermute(x, axis, [(i, (i + k) % n) for i in range(n)])]
    convert_element_type x0 -> x1, other arithmetic: none -> 4.59 us  [body(): ffn_half = (ffn_keep.astype(f32) + ffn_got.astype(f32)).astype(bf16)]
    pallas_call x15, Pallas kernels: 55.1 us -> 58 us  [call(): pl.pallas_call(kernel, out_shape=outs, in_specs=in_specs or [pl.BlockSpec...]
    unnamed x91 -> x83, local copies, waits for them, and re-layouts: 6.15 us -> 4.65 us
  transfers between devices with their start and end apart: 54 -> 56, of which waited for: 22 -> 25; matrix products, arithmetic and copies ran while one was open for 8% -> 8% of each run, Pallas kernels for 18% -> 19%
where the time goes in v3:
time: 232 us; the launch traced here: 231 us
  starting transfers between devices  71.3 us (31%)
  waiting for transfers between devices  60.5 us (26%)
  Pallas kernels  58 us (25%)
  other arithmetic  19.3 us (8%)
  between operations  14.2 us (6%)
  local copies, waits for them, and re-layouts  7.44 us (3%)
    ppermute x53, starting transfers between devices, shift(): return lax.ppermute(x, axis, [(i, (i + k) % n) for i in range(n)])  71.1 us
    ppermute x53, waiting for transfers between devices, shift(): return lax.ppermute(x, axis, [(i, (i + k) % n) for i in range(n)])  58.5 us
    pallas_call x15, Pallas kernels, call(): pl.pallas_call(kernel, out_shape=outs, in_specs=in_specs or [pl.BlockSpec...  58 us
    unnamed x83, local copies, waits for them, and re-layouts  4.65 us
  transfers between devices with their start and end apart: 56, of which 25 were waited for; matrix products, arithmetic and copies ran while one was open for 8% of the time, Pallas kernels for 19%

profile of v3, /device:TPU:0, one launch (start us, length us, event | category | flops | bytes accessed | tf_op | source)
XLA Modules:
  0.0 230.8 jit_solution(417686744450905953)
XLA Ops:
  7.2 2.0 shard_map.228
  9.3 4.2 %collective-permute-start.2 = (bf16[32,640]{1,0:T(8,128)(2,1)}, bf16[32,640]{1,0:T(8,128)(2,1)S(1)}, u32[]{:S(2)}, u32[]{:S(2)}) collective-permute-start(bf16[32,640]{1,0:T(8,128)(2,1)} %get-tuple-element.129), channel_id=1, source_target_pairs={{0,24},{8,0},{16,8},{24,16},{1,25},{9,1},{17,9},{25,17},{2,26},{10... | collective-permute-start | bytes 122888 | tf_op jit(solution)/shard_map/ppermute | solution.py:37
  13.5 1.3 collective-permute-start
  14.7 3.0 %collective-permute-start.8 = (bf16[256,512]{1,0:T(8,128)(2,1)}, bf16[256,512]{1,0:T(8,128)(2,1)S(1)}, u32[]{:S(2)}, u32[]{:S(2)}) collective-permute-start(bf16[256,512]{1,0:T(8,128)(2,1)} %get-tuple-element.131.refs_0_), channel_id=1, source_target_pairs={{0,3},{1,0},{2,1},{3,2},{4,7},{5,4},{6,5},{7,6},{8,11},{9,8},{10,9... | collective-permute-start | bytes 786440 | tf_op jit(solution)/shard_map/ppermute | solution.py:37
  19.3 1.6 collective-permute-start.6
  21.0 2.8 %collective-permute-start.5 = (bf16[128,640]{1,0:T(8,128)(2,1)S(1)}, bf16[128,640]{1,0:T(8,128)(2,1)S(1)}, u32[]{:S(2)}, u32[]{:S(2)}) collective-permute-start(bf16[128,640]{1,0:T(8,128)(2,1)S(1)} %constant_dynamic-update-slice_fusion.refs_4_), channel_id=1, source_target_pairs={{0,96},{32,0},{64,32},{96,64},{1,97},{33,1},{65,33},{97,65},{2,98}... | collective-permute-start | bytes 491528 | tf_op jit(solution)/shard_map/ppermute | solution.py:37
  24.7 6.7 %collective-permute-done.5.refs_7_ = bf16[128,640]{1,0:T(8,128)(2,1)S(1)} collective-permute-done((bf16[128,640]{1,0:T(8,128)(2,1)S(1)}, bf16[128,640]{1,0:T(8,128)(2,1)S(1)}, u32[]{:S(2)}, u32[]{:S(2)}) %collective-permute-start.5) | collective-permute-done | bytes 163872 | tf_op jit(solution)/shard_map/ppermute | solution.py:37
  32.3 1.3 maximum_bitcast_fusion.refs_12_.refs_11_.refs_5_
  33.6 5.0 %collective-permute-done.3.refs_5_ = bf16[128,640]{1,0:T(8,128)(2,1)S(1)} collective-permute-done((bf16[128,640]{1,0:T(8,128)(2,1)S(1)}, bf16[128,640]{1,0:T(8,128)(2,1)S(1)}, u32[]{:S(2)}, u32[]{:S(2)}) %collective-permute-start.3) | collective-permute-done | bytes 163872 | tf_op jit(solution)/shard_map/ppermute | solution.py:37
  41.9 5.0 %shard_map.229 = (bf16[1024,640]{1,0:T(8,128)(2,1)}, bf16[256,1024]{1,0:T(8,128)(2,1)}, f32[8,1024]{1,0:T(8,128)}, bf16[128,512]{1,0:T(8,128)(2,1)}, f32[384,256...) custom-call(s32[4]{0:T(128)} %pad_add_fusion.idx, bf16[256,512]{1,0:T(8,128)(2,1)} %get-tuple-element.131.refs_0_, ...), custom_call_target="tpu_custom_call" | custom-call | flops 268435456 | bytes 5472528 | tf_op jit(solution)/shard_map/pallas_call | solution.py:55
  47.0 1.6 collective-permute-start.15
  48.6 2.0 collective-permute-start.14
  50.6 5.7 %collective-permute-done.15.refs_3_ = bf16[256,256]{1,0:T(8,128)(2,1)S(1)} collective-permute-done((bf16[256,256]{1,0:T(8,128)(2,1)}, bf16[256,256]{1,0:T(8,128)(2,1)S(1)}, u32[]{:S(2)}, u32[]{:S(2)}) %collective-permute-start.15) | collective-permute-done | bytes 131104 | tf_op jit(solution)/shard_map/ppermute | solution.py:37
  56.3 3.1 %collective-permute-done.14.refs_2_ = bf16[256,256]{1,0:T(8,128)(2,1)S(1)} collective-permute-done((bf16[256,256]{1,0:T(8,128)(2,1)}, bf16[256,256]{1,0:T(8,128)(2,1)S(1)}, u32[]{:S(2)}, u32[]{:S(2)}) %collective-permute-start.14) | collective-permute-done | bytes 131104 | tf_op jit(solution)/shard_map/ppermute | solution.py:37
  59.5 3.1 %collective-permute-done.13.refs_1_ = bf16[256,256]{1,0:T(8,128)(2,1)S(1)} collective-permute-done((bf16[256,256]{1,0:T(8,128)(2,1)}, bf16[256,256]{1,0:T(8,128)(2,1)S(1)}, u32[]{:S(2)}, u32[]{:S(2)}) %collective-permute-start.13) | collective-permute-done | bytes 131104 | tf_op jit(solution)/shard_map/ppermute | solution.py:37
  62.6 2.7 %shard_map.230 = (bf16[256,1024]{1,0:T(8,128)(2,1)}, bf16[1024,256]{1,0:T(8,128)(2,1)}) custom-call(s32[4]{0:T(128)} %pad_add_fusion.idx, bf16[256,512]{1,0:T(8,128)(2,1)} %get-tuple-element.131.refs_0_, bf16[256,512]{1,0:T(8,128)(2,1)} %copy-done.4, bf16[256,512]{1,0:T(8,128)(2,1)} %copy-done.3, bf16[256,512]{1,0:T(8,128)(2,1)} %copy-done.2), custom_call_target="tpu_custom_call" | custom-call | bytes 2097168 | tf_op jit(solution)/shard_map/pallas_call | solution.py:55
  66.1 3.2 %shard_map.231 = (bf16[2048,256]{1,0:T(8,128)(2,1)}, f32[128,512]{1,0:T(8,128)}, bf16[256,256]{1,0:T(8,128)(2,1)}, f32[8,512]{1,0:T(8,128)}) custom-call(s32[4]{0:T(128)} %pad_add_fusion.idx, bf16[128,512]{1,0:T(8,128)(2,1)} %get-tuple-element.144.q_t.refs_7_, bf16[256,256]{1,0:T(8,128)(2,1)} %get-tuple-element.148.refs_0_, bf16[256,256]{1,0:T(8,128)(2,1)} %copy-done.35, ...), custom_call_target="tpu_custom_call" | custom-call | flops 536870912 | bytes 2637840 | tf_op jit(solution)/shard_map/pallas_call | solution.py:55
  69.3 2.0 all-gather.2.cloned.1.call-done.w_low.w_high.wd.refs_4_.refs_5_
  71.3 2.2 shard_map.232
  73.5 1.5 collective-permute-start.20
  75.0 2.7 %collective-permute-start.21 = (bf16[256,256]{1,0:T(8,128)(2,1)}, bf16[256,256]{1,0:T(8,128)(2,1)S(1)}, u32[]{:S(2)}, u32[]{:S(2)}) collective-permute-start(bf16[256,256]{1,0:T(8,128)(2,1)} %get-tuple-element.160), channel_id=1, source_target_pairs={{0,2},{1,3},{2,0},{3,1},{4,6},{5,7},{6,4},{7,5},{8,10},{9,11},{10,... | collective-permute-start | bytes 393224 | tf_op jit(solution)/shard_map/ppermute | solution.py:37
  77.7 1.4 collective-permute-start.22
  79.2 1.4 collective-permute-done.20
  80.6 3.8 %collective-permute-done.21 = bf16[256,256]{1,0:T(8,128)(2,1)S(1)} collective-permute-done((bf16[256,256]{1,0:T(8,128)(2,1)}, bf16[256,256]{1,0:T(8,128)(2,1)S(1)}, u32[]{:S(2)}, u32[]{:S(2)}) %collective-permute-start.21) | collective-permute-done | bytes 131104 | tf_op jit(solution)/shard_map/ppermute | solution.py:37
  85.4 2.3 %collective-permute-start.25 = (bf16[256,256]{1,0:T(8,128)(2,1)S(1)}, bf16[256,256]{1,0:T(8,128)(2,1)S(1)}, u32[]{:S(2)}, u32[]{:S(2)}) collective-permute-start(bf16[256,256]{1,0:T(8,128)(2,1)S(1)} %add_convert_fusion.12.refs_0_), channel_id=1, source_target_pairs={{0,3},{1,0},{2,1},{3,2},{4,7},{5,4},{6,5},{7,6},{8,11},{9,8},{10,9... | collective-permute-start | bytes 393224 | tf_op jit(solution)/shard_map/ppermute | solution.py:37
  89.5 4.2 %shard_map.233.refs_6_ = f32[256,1152]{1,0:T(8,128)} custom-call(bf16[256,1024]{1,0:T(8,128)(2,1)} %get-tuple-element.162.cot, bf16[1024,3712]{1,0:T(8,128)(2,1)} %all-gather.2.cloned.1.call-done.w_low.w_high.wd.refs_4_.refs_5_), custom_call_target="tpu_custom_call" | custom-call | flops 603979776 | bytes 9306112 | tf_op jit(solution)/shard_map/pallas_call | solution.py:55
  93.8 1.4 collective-permute-done.24.refs_2_
  95.3 1.4 collective-permute-done.23.refs_1_
  97.3 8.5 %shard_map.234 = (f32[256,1024]{1,0:T(8,128)}, bf16[256,1024]{1,0:T(8,128)(2,1)}, bf16[256,3456]{1,0:T(8,128)(2,1)}, bf16[256,256]{1,0:T(8,128)(2,1)}, bf16[256,...) custom-call(s32[4]{0:T(128)} %pad_add_fusion.idx, ...), custom_call_target="tpu_custom_call" | custom-call | flops 2415919104 | bytes 21331984 | tf_op jit(solution)/shard_map/pallas_call | solution.py:55
  105.9 2.0 collective-permute-start.27
  107.9 1.6 collective-permute-start.28
  109.5 6.3 %shard_map.235 = (bf16[512,3456]{1,0:T(8,128)(2,1)}, bf16[512,3456]{1,0:T(8,128)(2,1)}) custom-call(s32[4]{0:T(128)} %pad_add_fusion.idx, bf16[256,1024]{1,0:T(8,128)(2,1)} %get-tuple-element.169.normed, bf16[1024,256]{1,0:T(8,128)(2,1)} %get-tuple-element.170.cot_t, bf16[256,3456]{1,0:T(8,128)(2,1)} %get-tuple-element.171.big.hidden), custom_call_target="tpu_custom_call" | custom-call | flops 1811939328 | bytes 9895952 | tf_op jit(solution)/shard_map/pallas_call | solution.py:55
  116.7 1.7 collective-permute-start.31
  119.2 1.4 collective-permute-start.29
  120.6 3.5 %shard_map.236 = (bf16[256,256]{1,0:T(8,128)(2,1)}, bf16[256,256]{1,0:T(8,128)(2,1)}, bf16[256,256]{1,0:T(8,128)(2,1)}, bf16[256,256]{1,0:T(8,128)(2,1)}) custom-call(s32[4]{0:T(128)} %pad_add_fusion.idx, bf16[256,3456]{1,0:T(8,128)(2,1)} %get-tuple-element.171.big.hidden, bf16[1024,3712]{1,0:T(8,128)(2,1)} %all-gather.2.cloned.1.call-done.w_low.w_high.wd.refs_4_.refs_5_), custom_call_target="tpu_custom_call" | custom-call | flops 603979776 | bytes 9895952 | tf_op jit(solution)/shard_map/pallas_call | solution.py:55
  124.1 2.4 %collective-permute-done.30.refs_2_ = bf16[256,256]{1,0:T(8,128)(2,1)} collective-permute-done((bf16[256,256]{1,0:T(8,128)(2,1)}, bf16[256,256]{1,0:T(8,128)(2,1)}, u32[]{:S(2)}, u32[]{:S(2)}) %collective-permute-start.30) | collective-permute-done | bytes 131104 | tf_op jit(solution)/shard_map/ppermute | solution.py:37
  126.5 2.1 collective-permute-done.29.refs_1_
  128.6 4.6 %add_convert_fusion = bf16[512,3456]{1,0:T(8,128)(2,1)} fusion(bf16[512,3456]{1,0:T(8,128)(2,1)} %collective-permute-done.32, bf16[512,3456]{1,0:T(8,128)(2,1)S(1)} %copy-done.1), kind=kLoop, calls=%fused_computation | loop fusion | flops 7077888 | bytes 10616832 | tf_op jit(solution)/shard_map/convert_element_type | solution.py:674
  133.3 6.4 %shard_map.237 = (f32[256,256]{1,0:T(8,128)}, bf16[256,1024]{1,0:T(8,128)(2,1)}, f32[8,1024]{1,0:T(8,128)}, bf16[256,256]{1,0:T(8,128)(2,1)}, f32[64,1]{1,0:T(8,...) custom-call(s32[4]{0:T(128)} %pad_add_fusion.idx, f32[256,1024]{1,0:T(8,128)} %get-tuple-element.163.middle, ...), custom_call_target="tpu_custom_call" | custom-call | flops 1342177280 | bytes 21250576 | tf_op jit(solution)/shard_map/pallas_call | solution.py:55
  140.9 1.7 collective-permute-done.33
  142.6 2.1 add_convert_fusion.7
  144.7 5.1 %collective-permute-start.35 = (bf16[256,256]{1,0:T(8,128)(2,1)S(1)}, bf16[256,256]{1,0:T(8,128)(2,1)S(1)}, u32[]{:S(2)}, u32[]{:S(2)}) collective-permute-start(bf16[256,256]{1,0:T(8,128)(2,1)S(1)} %get-tuple-element.249), channel_id=1, source_target_pairs={{0,8},{8,16},{16,24},{24,0},{1,9},{9,17},{17,25},{25,1},{2,10},{10... | collective-permute-start | bytes 393224 | tf_op jit(solution)/shard_map/ppermute | solution.py:37
  149.9 8.9 %collective-permute-start.34 = (bf16[256,256]{1,0:T(8,128)(2,1)S(1)}, bf16[256,256]{1,0:T(8,128)(2,1)S(1)}, u32[]{:S(2)}, u32[]{:S(2)}) collective-permute-start(bf16[256,256]{1,0:T(8,128)(2,1)S(1)} %get-tuple-element.251), channel_id=1, source_target_pairs={{0,16},{8,24},{16,0},{24,8},{1,17},{9,25},{17,1},{25,9},{2,18},{10... | collective-permute-start | bytes 393224 | tf_op jit(solution)/shard_map/ppermute | solution.py:37
  158.7 2.5 %collective-permute-done.35.refs_1_ = bf16[256,256]{1,0:T(8,128)(2,1)S(1)} collective-permute-done((bf16[256,256]{1,0:T(8,128)(2,1)S(1)}, bf16[256,256]{1,0:T(8,128)(2,1)S(1)}, u32[]{:S(2)}, u32[]{:S(2)}) %collective-permute-start.35) | collective-permute-done | bytes 131104 | tf_op jit(solution)/shard_map/ppermute | solution.py:37
  161.3 2.0 collective-permute-start.38
  163.3 1.5 collective-permute-start.39
  164.8 2.9 %shard_map.238.out_rel = bf16[1024,256]{1,0:T(8,128)(2,1)} custom-call(s32[4]{0:T(128)} %pad_add_fusion.idx, bf16[256,1024]{1,0:T(8,128)(2,1)} %get-tuple-element.192.mid, bf16[256,256]{1,0:T(8,128)(2,1)} %get-tuple-element.156.attn_b), custom_call_target="tpu_custom_call" | custom-call | flops 134217728 | bytes 1179664 | tf_op jit(solution)/shard_map/pallas_call | solution.py:55
  168.4 3.8 %shard_map.239 = (bf16[256,512]{1,0:T(8,128)(2,1)}, f32[8,1024]{1,0:T(8,128)}, f32[64,1]{1,0:T(8,128)}, bf16[272,256]{1,0:T(8,128)(2,1)}, bf16[272,256]{1,0:T(8,...) custom-call(s32[4]{0:T(128)} %pad_add_fusion.idx, bf16[256,256]{1,0:T(8,128)(2,1)} %get-tuple-element.250.refs_0_, ...), custom_call_target="tpu_custom_call" | custom-call | flops 268435456 | bytes 3834384 | tf_op jit(solution)/shard_map/pallas_call | solution.py:55
  172.2 4.0 %shard_map.240 = (bf16[512,896]{1,0:T(8,128)(2,1)}, bf16[512,896]{1,0:T(8,128)(2,1)}) custom-call(s32[4]{0:T(128)} %pad_add_fusion.idx, bf16[1024,256]{1,0:T(8,128)(2,1)} %get-tuple-element.164.one_rel, bf16[1024,256]{1,0:T(8,128)(2,1)} %shard_map.238.out_rel, bf16[256,512]{1,0:T(8,128)(2,1)} %get-tuple-element.202.qkv_gb, ...), custom_call_target="tpu_custom_call" | custom-call | flops 402653184 | bytes 3211792 | tf_op jit(solution)/shard_map/pallas_call | solution.py:55
  177.3 1.8 collective-permute-done.40
  179.0 1.3 add_convert_fusion.4
  180.4 3.2 %collective-permute-start.43 = (bf16[128,896]{1,0:T(8,128)(2,1)S(1)}, bf16[128,896]{1,0:T(8,128)(2,1)S(1)}, u32[]{:S(2)}, u32[]{:S(2)}) collective-permute-start(bf16[128,896]{1,0:T(8,128)(2,1)S(1)} %get-tuple-element.246), channel_id=1, source_target_pairs={{0,96},{32,0},{64,32},{96,64},{1,97},{33,1},{65,33},{97,65},{2,98}... | collective-permute-start | bytes 688136 | tf_op jit(solution)/shard_map/ppermute | solution.py:37
  184.0 1.7 fusion.4
  185.6 4.2 %collective-permute-done.41 = bf16[128,896]{1,0:T(8,128)(2,1)S(1)} collective-permute-done((bf16[128,896]{1,0:T(8,128)(2,1)S(1)}, bf16[128,896]{1,0:T(8,128)(2,1)S(1)}, u32[]{:S(2)}, u32[]{:S(2)}) %collective-permute-start.41) | collective-permute-done | bytes 229408 | tf_op jit(solution)/shard_map/ppermute | solution.py:37
  190.3 2.3 collective-permute-start.45
  192.6 2.5 %collective-permute-start.46 = (bf16[272,256]{1,0:T(8,128)(2,1)S(1)}, bf16[272,256]{1,0:T(8,128)(2,1)S(1)}, u32[]{:S(2)}, u32[]{:S(2)}) collective-permute-start(bf16[272,256]{1,0:T(8,128)(2,1)S(1)} %copy-done.28), channel_id=1, source_target_pairs={{0,3},{1,0},{2,1},{3,2},{4,7},{5,4},{6,5},{7,6},{8,11},{9,8},{10,9... | collective-permute-start | bytes 417800 | tf_op jit(solution)/shard_map/ppermute | solution.py:37
  196.2 2.4 %collective-permute-done.44 = bf16[272,256]{1,0:T(8,128)(2,1)S(1)} collective-permute-done((bf16[272,256]{1,0:T(8,128)(2,1)}, bf16[272,256]{1,0:T(8,128)(2,1)S(1)}, u32[]{:S(2)}, u32[]{:S(2)}) %collective-permute-start.44) | collective-permute-done | bytes 139296 | tf_op jit(solution)/shard_map/ppermute | solution.py:37
  199.7 2.3 collective-permute-start.49
  204.8 3.9 %collective-permute-done.48.refs_2_ = bf16[32,896]{1,0:T(8,128)(2,1)S(1)} collective-permute-done((bf16[32,896]{1,0:T(8,128)(2,1)S(1)}, bf16[32,896]{1,0:T(8,128)(2,1)S(1)}, u32[]{:S(2)}, u32[]{:S(2)}) %collective-permute-start.48) | collective-permute-done | bytes 57376 | tf_op jit(solution)/shard_map/ppermute | solution.py:37
  209.3 1.6 shard_map.241
  210.9 2.7 %collective-permute-start.52 = (f32[32,128]{1,0:T(8,128)}, f32[32,128]{1,0:T(8,128)S(1)}, u32[]{:S(2)}, u32[]{:S(2)}) collective-permute-start(f32[32,128]{1,0:T(8,128)} %get-tuple-element.236), channel_id=1, source_target_pairs={{0,3},{1,0},{2,1},{3,2},{4,7},{5,4},{6,5},{7,6},{8,11},{9,8},{10,9... | collective-permute-start | bytes 49160 | tf_op jit(solution)/shard_map/ppermute | solution.py:37
  214.6 1.5 add_reduce_fusion
  216.1 3.0 %collective-permute-done.51 = f32[32,128]{1,0:T(8,128)S(1)} collective-permute-done((f32[32,128]{1,0:T(8,128)}, f32[32,128]{1,0:T(8,128)S(1)}, u32[]{:S(2)}, u32[]{:S(2)}) %collective-permute-start.51) | collective-permute-done | bytes 16416 | tf_op jit(solution)/shard_map/ppermute | solution.py:37
  222.5 1.7 shard_map.242
  (178 shorter events, 26.6 us)
Async XLA Ops:
  7.2 64.1 %all-gather.2.cloned.1.call-start = ((), (), s32[]{:S(2)}) async-start(), calls=%async_computation.2 | async-start | bytes 7839744 | tf_op jit(solution)/shard_map/all_gather | solution.py:552
  9.2 180.6 %reduce-scatter.3.cloned.1.call-start = ((), (), s32[]{:S(2)}) async-start(), calls=%async_computation.3 | async-start | bytes 4423680 | tf_op jit(solution)/shard_map/reduce_scatter | solution.py:675
  9.3 11.7 %collective-permute-start.2 = (bf16[32,640]{1,0:T(8,128)(2,1)}, bf16[32,640]{1,0:T(8,128)(2,1)S(1)}, u32[]{:S(2)}, u32[]{:S(2)}) collective-permute-start(bf16[32,640]{1,0:T(8,128)(2,1)} %get-tuple-element.129), channel_id=1, source_target_pairs={{0,24},{8,0},{16,8},{24,16},{1,25},{9,1},{17,9},{25,17},{2,26},{10... | collective-permute-start | bytes 122888 | tf_op jit(solution)/shard_map/ppermute | solution.py:37
  13.5 7.5 %collective-permute-start.1 = (bf16[32,640]{1,0:T(8,128)(2,1)}, bf16[32,640]{1,0:T(8,128)(2,1)S(1)}, u32[]{:S(2)}, u32[]{:S(2)}) collective-permute-start(bf16[32,640]{1,0:T(8,128)(2,1)} %get-tuple-element.129), channel_id=1, source_target_pairs={{0,16},{8,24},{16,0},{24,8},{1,17},{9,25},{17,1},{25,9},{2,18},{10... | collective-permute-start | bytes 122888 | tf_op jit(solution)/shard_map/ppermute | solution.py:37
  13.5 5.9 %collective-permute-start = (bf16[32,640]{1,0:T(8,128)(2,1)}, bf16[32,640]{1,0:T(8,128)(2,1)S(1)}, u32[]{:S(2)}, u32[]{:S(2)}) collective-permute-start(bf16[32,640]{1,0:T(8,128)(2,1)} %get-tuple-element.129), channel_id=1, source_target_pairs={{0,8},{8,16},{16,24},{24,0},{1,9},{9,17},{17,25},{25,1},{2,10},{10... | collective-permute-start | bytes 122888 | tf_op jit(solution)/shard_map/ppermute | solution.py:37
  14.7 23.9 %collective-permute-start.8 = (bf16[256,512]{1,0:T(8,128)(2,1)}, bf16[256,512]{1,0:T(8,128)(2,1)S(1)}, u32[]{:S(2)}, u32[]{:S(2)}) collective-permute-start(bf16[256,512]{1,0:T(8,128)(2,1)} %get-tuple-element.131.refs_0_), channel_id=1, source_target_pairs={{0,3},{1,0},{2,1},{3,2},{4,7},{5,4},{6,5},{7,6},{8,11},{9,8},{10,9... | collective-permute-start | bytes 786440 | tf_op jit(solution)/shard_map/ppermute | solution.py:37
  17.7 20.9 %collective-permute-start.7 = (bf16[256,512]{1,0:T(8,128)(2,1)}, bf16[256,512]{1,0:T(8,128)(2,1)S(1)}, u32[]{:S(2)}, u32[]{:S(2)}) collective-permute-start(bf16[256,512]{1,0:T(8,128)(2,1)} %get-tuple-element.131.refs_0_), channel_id=1, source_target_pairs={{0,2},{1,3},{2,0},{3,1},{4,6},{5,7},{6,4},{7,5},{8,10},{9,11},{10,... | collective-permute-start | bytes 786440 | tf_op jit(solution)/shard_map/ppermute | solution.py:37
  19.3 19.3 %collective-permute-start.6 = (bf16[256,512]{1,0:T(8,128)(2,1)}, bf16[256,512]{1,0:T(8,128)(2,1)S(1)}, u32[]{:S(2)}, u32[]{:S(2)}) collective-permute-start(bf16[256,512]{1,0:T(8,128)(2,1)} %get-tuple-element.131.refs_0_), channel_id=1, source_target_pairs={{0,1},{1,2},{2,3},{3,0},{4,5},{5,6},{6,7},{7,4},{8,9},{9,10},{10,1... | collective-permute-start | bytes 786440 | tf_op jit(solution)/shard_map/ppermute | solution.py:37
  21.0 10.5 %collective-permute-start.5 = (bf16[128,640]{1,0:T(8,128)(2,1)S(1)}, bf16[128,640]{1,0:T(8,128)(2,1)S(1)}, u32[]{:S(2)}, u32[]{:S(2)}) collective-permute-start(bf16[128,640]{1,0:T(8,128)(2,1)S(1)} %constant_dynamic-update-slice_fusion.refs_4_), channel_id=1, source_target_pairs={{0,96},{32,0},{64,32},{96,64},{1,97},{33,1},{65,33},{97,65},{2,98}... | collective-permute-start | bytes 491528 | tf_op jit(solution)/shard_map/ppermute | solution.py:37
  23.8 9.8 %collective-permute-start.4 = (bf16[128,640]{1,0:T(8,128)(2,1)S(1)}, bf16[128,640]{1,0:T(8,128)(2,1)S(1)}, u32[]{:S(2)}, u32[]{:S(2)}) collective-permute-start(bf16[128,640]{1,0:T(8,128)(2,1)S(1)} %constant_dynamic-update-slice_fusion.refs_4_), channel_id=1, source_target_pairs={{0,64},{32,96},{64,0},{96,32},{1,65},{33,97},{65,1},{97,33},{2,66}... | collective-permute-start | bytes 491528 | tf_op jit(solution)/shard_map/ppermute | solution.py:37
  31.4 7.2 %collective-permute-start.3 = (bf16[128,640]{1,0:T(8,128)(2,1)S(1)}, bf16[128,640]{1,0:T(8,128)(2,1)S(1)}, u32[]{:S(2)}, u32[]{:S(2)}) collective-permute-start(bf16[128,640]{1,0:T(8,128)(2,1)S(1)} %constant_dynamic-update-slice_fusion.refs_4_), channel_id=1, source_target_pairs={{0,32},{32,64},{64,96},{96,0},{1,33},{33,65},{65,97},{97,1},{2,34}... | collective-permute-start | bytes 491528 | tf_op jit(solution)/shard_map/ppermute | solution.py:37
  38.6 1.7 collective-permute-start.9
  38.7 1.6 collective-permute-start.10
  39.2 1.4 collective-permute-start.11
  39.3 1.5 collective-permute-start.12
  47.0 9.3 %collective-permute-start.15 = (bf16[256,256]{1,0:T(8,128)(2,1)}, bf16[256,256]{1,0:T(8,128)(2,1)S(1)}, u32[]{:S(2)}, u32[]{:S(2)}) collective-permute-start(bf16[256,256]{1,0:T(8,128)(2,1)} %get-tuple-element.148.refs_0_), channel_id=1, source_target_pairs={{0,24},{8,0},{16,8},{24,16},{1,25},{9,1},{17,9},{25,17},{2,26},{10... | collective-permute-start | bytes 393224 | tf_op jit(solution)/shard_map/ppermute | solution.py:37
  48.6 10.9 %collective-permute-start.14 = (bf16[256,256]{1,0:T(8,128)(2,1)}, bf16[256,256]{1,0:T(8,128)(2,1)S(1)}, u32[]{:S(2)}, u32[]{:S(2)}) collective-permute-start(bf16[256,256]{1,0:T(8,128)(2,1)} %get-tuple-element.148.refs_0_), channel_id=1, source_target_pairs={{0,16},{8,24},{16,0},{24,8},{1,17},{9,25},{17,1},{25,9},{2,18},{10... | collective-permute-start | bytes 393224 | tf_op jit(solution)/shard_map/ppermute | solution.py:37
  50.6 12.0 %collective-permute-start.13 = (bf16[256,256]{1,0:T(8,128)(2,1)}, bf16[256,256]{1,0:T(8,128)(2,1)S(1)}, u32[]{:S(2)}, u32[]{:S(2)}) collective-permute-start(bf16[256,256]{1,0:T(8,128)(2,1)} %get-tuple-element.148.refs_0_), channel_id=1, source_target_pairs={{0,8},{8,16},{16,24},{24,0},{1,9},{9,17},{17,25},{25,1},{2,10},{10... | collective-permute-start | bytes 393224 | tf_op jit(solution)/shard_map/ppermute | solution.py:37
  50.6 14.7 %collective-permute-start.16 = (bf16[256,256]{1,0:T(8,128)(2,1)}, bf16[256,256]{1,0:T(8,128)(2,1)S(1)}, u32[]{:S(2)}, u32[]{:S(2)}) collective-permute-start(bf16[256,256]{1,0:T(8,128)(2,1)} %get-tuple-element.148.refs_0_), channel_id=1, source_target_pairs={{0,4},{4,0},{1,5},{5,1},{2,6},{6,2},{3,7},{7,3},{8,12},{12,8},{9,1... | collective-permute-start | bytes 393224 | tf_op jit(solution)/shard_map/ppermute | solution.py:37
  56.3 9.0 %collective-permute-start.19 = (bf16[256,256]{1,0:T(8,128)(2,1)S(1)}, bf16[256,256]{1,0:T(8,128)(2,1)S(1)}, u32[]{:S(2)}, u32[]{:S(2)}) collective-permute-start(bf16[256,256]{1,0:T(8,128)(2,1)S(1)} %collective-permute-done.15.refs_3_), channel_id=1, source_target_pairs={{0,4},{4,0},{1,5},{5,1},{2,6},{6,2},{3,7},{7,3},{8,12},{12,8},{9,1... | collective-permute-start | bytes 393224 | tf_op jit(solution)/shard_map/ppermute | solution.py:37
  59.5 5.8 %collective-permute-start.18 = (bf16[256,256]{1,0:T(8,128)(2,1)S(1)}, bf16[256,256]{1,0:T(8,128)(2,1)S(1)}, u32[]{:S(2)}, u32[]{:S(2)}) collective-permute-start(bf16[256,256]{1,0:T(8,128)(2,1)S(1)} %collective-permute-done.14.refs_2_), channel_id=1, source_target_pairs={{0,4},{4,0},{1,5},{5,1},{2,6},{6,2},{3,7},{7,3},{8,12},{12,8},{9,1... | collective-permute-start | bytes 393224 | tf_op jit(solution)/shard_map/ppermute | solution.py:37
  62.6 2.8 %collective-permute-start.17 = (bf16[256,256]{1,0:T(8,128)(2,1)S(1)}, bf16[256,256]{1,0:T(8,128)(2,1)S(1)}, u32[]{:S(2)}, u32[]{:S(2)}) collective-permute-start(bf16[256,256]{1,0:T(8,128)(2,1)S(1)} %collective-permute-done.13.refs_1_), channel_id=1, source_target_pairs={{0,4},{4,0},{1,5},{5,1},{2,6},{6,2},{3,7},{7,3},{8,12},{12,8},{9,1... | collective-permute-start | bytes 393224 | tf_op jit(solution)/shard_map/ppermute | solution.py:37
  73.5 7.1 %collective-permute-start.20 = (bf16[256,256]{1,0:T(8,128)(2,1)}, bf16[256,256]{1,0:T(8,128)(2,1)S(1)}, u32[]{:S(2)}, u32[]{:S(2)}) collective-permute-start(bf16[256,256]{1,0:T(8,128)(2,1)} %get-tuple-element.159), channel_id=1, source_target_pairs={{0,1},{1,2},{2,3},{3,0},{4,5},{5,6},{6,7},{7,4},{8,9},{9,10},{10,1... | collective-permute-start | bytes 393224 | tf_op jit(solution)/shard_map/ppermute | solution.py:37
  75.0 9.4 %collective-permute-start.21 = (bf16[256,256]{1,0:T(8,128)(2,1)}, bf16[256,256]{1,0:T(8,128)(2,1)S(1)}, u32[]{:S(2)}, u32[]{:S(2)}) collective-permute-start(bf16[256,256]{1,0:T(8,128)(2,1)} %get-tuple-element.160), channel_id=1, source_target_pairs={{0,2},{1,3},{2,0},{3,1},{4,6},{5,7},{6,4},{7,5},{8,10},{9,11},{10,... | collective-permute-start | bytes 393224 | tf_op jit(solution)/shard_map/ppermute | solution.py:37
  77.7 6.6 %collective-permute-start.22 = (bf16[256,256]{1,0:T(8,128)(2,1)}, bf16[256,256]{1,0:T(8,128)(2,1)S(1)}, u32[]{:S(2)}, u32[]{:S(2)}) collective-permute-start(bf16[256,256]{1,0:T(8,128)(2,1)} %get-tuple-element.161), channel_id=1, source_target_pairs={{0,3},{1,0},{2,1},{3,2},{4,7},{5,4},{6,5},{7,6},{8,11},{9,8},{10,9... | collective-permute-start | bytes 393224 | tf_op jit(solution)/shard_map/ppermute | solution.py:37
  85.4 8.4 %collective-permute-start.25 = (bf16[256,256]{1,0:T(8,128)(2,1)S(1)}, bf16[256,256]{1,0:T(8,128)(2,1)S(1)}, u32[]{:S(2)}, u32[]{:S(2)}) collective-permute-start(bf16[256,256]{1,0:T(8,128)(2,1)S(1)} %add_convert_fusion.12.refs_0_), channel_id=1, source_target_pairs={{0,3},{1,0},{2,1},{3,2},{4,7},{5,4},{6,5},{7,6},{8,11},{9,8},{10,9... | collective-permute-start | bytes 393224 | tf_op jit(solution)/shard_map/ppermute | solution.py:37
  87.7 7.5 %collective-permute-start.24 = (bf16[256,256]{1,0:T(8,128)(2,1)S(1)}, bf16[256,256]{1,0:T(8,128)(2,1)S(1)}, u32[]{:S(2)}, u32[]{:S(2)}) collective-permute-start(bf16[256,256]{1,0:T(8,128)(2,1)S(1)} %add_convert_fusion.12.refs_0_), channel_id=1, source_target_pairs={{0,2},{1,3},{2,0},{3,1},{4,6},{5,7},{6,4},{7,5},{8,10},{9,11},{10,... | collective-permute-start | bytes 393224 | tf_op jit(solution)/shard_map/ppermute | solution.py:37
  88.9 7.7 %collective-permute-start.23 = (bf16[256,256]{1,0:T(8,128)(2,1)S(1)}, bf16[256,256]{1,0:T(8,128)(2,1)S(1)}, u32[]{:S(2)}, u32[]{:S(2)}) collective-permute-start(bf16[256,256]{1,0:T(8,128)(2,1)S(1)} %add_convert_fusion.12.refs_0_), channel_id=1, source_target_pairs={{0,1},{1,2},{2,3},{3,0},{4,5},{5,6},{6,7},{7,4},{8,9},{9,10},{10,1... | collective-permute-start | bytes 393224 | tf_op jit(solution)/shard_map/ppermute | solution.py:37
  105.8 10.0 %collective-permute-start.26 = (bf16[256,256]{1,0:T(8,128)(2,1)}, bf16[256,256]{1,0:T(8,128)(2,1)S(1)}, u32[]{:S(2)}, u32[]{:S(2)}) collective-permute-start(bf16[256,256]{1,0:T(8,128)(2,1)} %get-tuple-element.166), channel_id=1, source_target_pairs={{0,1},{1,2},{2,3},{3,0},{4,5},{5,6},{6,7},{7,4},{8,9},{9,10},{10,1... | collective-permute-start | bytes 393224 | tf_op jit(solution)/shard_map/ppermute | solution.py:37
  105.9 10.0 %collective-permute-start.27 = (bf16[256,256]{1,0:T(8,128)(2,1)}, bf16[256,256]{1,0:T(8,128)(2,1)S(1)}, u32[]{:S(2)}, u32[]{:S(2)}) collective-permute-start(bf16[256,256]{1,0:T(8,128)(2,1)} %get-tuple-element.167), channel_id=1, source_target_pairs={{0,2},{1,3},{2,0},{3,1},{4,6},{5,7},{6,4},{7,5},{8,10},{9,11},{10,... | collective-permute-start | bytes 393224 | tf_op jit(solution)/shard_map/ppermute | solution.py:37
  107.9 8.0 %collective-permute-start.28 = (bf16[256,256]{1,0:T(8,128)(2,1)}, bf16[256,256]{1,0:T(8,128)(2,1)S(1)}, u32[]{:S(2)}, u32[]{:S(2)}) collective-permute-start(bf16[256,256]{1,0:T(8,128)(2,1)} %get-tuple-element.168), channel_id=1, source_target_pairs={{0,3},{1,0},{2,1},{3,2},{4,7},{5,4},{6,5},{7,6},{8,11},{9,8},{10,9... | collective-permute-start | bytes 393224 | tf_op jit(solution)/shard_map/ppermute | solution.py:37
  115.8 12.8 %collective-permute-start.32 = (bf16[512,3456]{1,0:T(8,128)(2,1)}, bf16[512,3456]{1,0:T(8,128)(2,1)}, u32[]{:S(2)}, u32[]{:S(2)}) collective-permute-start(bf16[512,3456]{1,0:T(8,128)(2,1)} %get-tuple-element.177), channel_id=1, source_target_pairs={{0,4},{4,0},{1,5},{5,1},{2,6},{6,2},{3,7},{7,3},{8,12},{12,8},{9,1... | collective-permute-start | bytes 10616840 | tf_op jit(solution)/shard_map/ppermute | solution.py:37
  116.7 7.4 %collective-permute-start.31 = (bf16[256,256]{1,0:T(8,128)(2,1)}, bf16[256,256]{1,0:T(8,128)(2,1)}, u32[]{:S(2)}, u32[]{:S(2)}) collective-permute-start(bf16[256,256]{1,0:T(8,128)(2,1)} %add_convert_fusion.11.refs_0_), channel_id=1, source_target_pairs={{0,3},{1,0},{2,1},{3,2},{4,7},{5,4},{6,5},{7,6},{8,11},{9,8},{10,9... | collective-permute-start | bytes 393224 | tf_op jit(solution)/shard_map/ppermute | solution.py:37
  118.3 8.2 %collective-permute-start.30 = (bf16[256,256]{1,0:T(8,128)(2,1)}, bf16[256,256]{1,0:T(8,128)(2,1)}, u32[]{:S(2)}, u32[]{:S(2)}) collective-permute-start(bf16[256,256]{1,0:T(8,128)(2,1)} %add_convert_fusion.11.refs_0_), channel_id=1, source_target_pairs={{0,2},{1,3},{2,0},{3,1},{4,6},{5,7},{6,4},{7,5},{8,10},{9,11},{10,... | collective-permute-start | bytes 393224 | tf_op jit(solution)/shard_map/ppermute | solution.py:37
  119.2 9.4 %collective-permute-start.29 = (bf16[256,256]{1,0:T(8,128)(2,1)}, bf16[256,256]{1,0:T(8,128)(2,1)}, u32[]{:S(2)}, u32[]{:S(2)}) collective-permute-start(bf16[256,256]{1,0:T(8,128)(2,1)} %add_convert_fusion.11.refs_0_), channel_id=1, source_target_pairs={{0,1},{1,2},{2,3},{3,0},{4,5},{5,6},{6,7},{7,4},{8,9},{9,10},{10,1... | collective-permute-start | bytes 393224 | tf_op jit(solution)/shard_map/ppermute | solution.py:37
  133.2 89.3 %reduce-scatter.5.cloned.1.call-start = ((), (), s32[]{:S(2)}) async-start(), calls=%async_computation.4 | async-start | bytes 1105920 | tf_op jit(solution)/shard_map/reduce_scatter | solution.py:752
  133.3 28.0 %copy-start.32 = (bf16[256,256]{1,0:T(8,128)(2,1)S(1)}, bf16[256,256]{1,0:T(8,128)(2,1)}, u32[]{:S(2)}) copy-start(bf16[256,256]{1,0:T(8,128)(2,1)} %get-tuple-element.210) | copy-start | bytes 393220
  133.3 28.0 %copy-start.31 = (bf16[256,256]{1,0:T(8,128)(2,1)S(1)}, bf16[256,256]{1,0:T(8,128)(2,1)}, u32[]{:S(2)}) copy-start(bf16[256,256]{1,0:T(8,128)(2,1)} %get-tuple-element.211) | copy-start | bytes 393220
  133.3 30.0 %copy-start.30 = (bf16[256,256]{1,0:T(8,128)(2,1)S(1)}, bf16[256,256]{1,0:T(8,128)(2,1)}, u32[]{:S(2)}) copy-start(bf16[256,256]{1,0:T(8,128)(2,1)} %get-tuple-element.212) | copy-start | bytes 393220
  139.7 2.9 %collective-permute-start.33 = (bf16[1024,256]{1,0:T(8,128)(2,1)}, bf16[1024,256]{1,0:T(8,128)(2,1)S(1)}, u32[]{:S(2)}, u32[]{:S(2)}) collective-permute-start(bf16[1024,256]{1,0:T(8,128)(2,1)} %get-tuple-element.191), channel_id=1, source_target_pairs={{0,4},{4,0},{1,5},{5,1},{2,6},{6,2},{3,7},{7,3},{8,12},{12,8},{9,1... | collective-permute-start | bytes 1572872 | tf_op jit(solution)/shard_map/ppermute | solution.py:37
  142.6 34.5 %copy-start = (bf16[256,1024]{1,0:T(8,128)(2,1)S(1)}, bf16[256,1024]{1,0:T(8,128)(2,1)}, u32[]{:S(2)}) copy-start(bf16[256,1024]{1,0:T(8,128)(2,1)} %get-tuple-element.142.base.refs_10_) | copy-start | bytes 1572868
  144.7 16.5 %collective-permute-start.35 = (bf16[256,256]{1,0:T(8,128)(2,1)S(1)}, bf16[256,256]{1,0:T(8,128)(2,1)S(1)}, u32[]{:S(2)}, u32[]{:S(2)}) collective-permute-start(bf16[256,256]{1,0:T(8,128)(2,1)S(1)} %get-tuple-element.249), channel_id=1, source_target_pairs={{0,8},{8,16},{16,24},{24,0},{1,9},{9,17},{17,25},{25,1},{2,10},{10... | collective-permute-start | bytes 393224 | tf_op jit(solution)/shard_map/ppermute | solution.py:37
  149.9 17.8 %collective-permute-start.34 = (bf16[256,256]{1,0:T(8,128)(2,1)S(1)}, bf16[256,256]{1,0:T(8,128)(2,1)S(1)}, u32[]{:S(2)}, u32[]{:S(2)}) collective-permute-start(bf16[256,256]{1,0:T(8,128)(2,1)S(1)} %get-tuple-element.251), channel_id=1, source_target_pairs={{0,16},{8,24},{16,0},{24,8},{1,17},{9,25},{17,1},{25,9},{2,18},{10... | collective-permute-start | bytes 393224 | tf_op jit(solution)/shard_map/ppermute | solution.py:37
  158.7 9.0 %collective-permute-start.36 = (bf16[256,256]{1,0:T(8,128)(2,1)S(1)}, bf16[256,256]{1,0:T(8,128)(2,1)S(1)}, u32[]{:S(2)}, u32[]{:S(2)}) collective-permute-start(bf16[256,256]{1,0:T(8,128)(2,1)S(1)} %get-tuple-element.248), channel_id=1, source_target_pairs={{0,24},{8,0},{16,8},{24,16},{1,25},{9,1},{17,9},{25,17},{2,26},{10... | collective-permute-start | bytes 393224 | tf_op jit(solution)/shard_map/ppermute | solution.py:37
  161.3 15.0 %collective-permute-start.37 = (bf16[256,256]{1,0:T(8,128)(2,1)S(1)}, bf16[256,256]{1,0:T(8,128)(2,1)S(1)}, u32[]{:S(2)}, u32[]{:S(2)}) collective-permute-start(bf16[256,256]{1,0:T(8,128)(2,1)S(1)} %copy-done.32), channel_id=1, source_target_pairs={{0,1},{1,2},{2,3},{3,0},{4,5},{5,6},{6,7},{7,4},{8,9},{9,10},{10,1... | collective-permute-start | bytes 393224 | tf_op jit(solution)/shard_map/ppermute | solution.py:37
  161.3 15.0 %collective-permute-start.38 = (bf16[256,256]{1,0:T(8,128)(2,1)S(1)}, bf16[256,256]{1,0:T(8,128)(2,1)S(1)}, u32[]{:S(2)}, u32[]{:S(2)}) collective-permute-start(bf16[256,256]{1,0:T(8,128)(2,1)S(1)} %copy-done.31), channel_id=1, source_target_pairs={{0,2},{1,3},{2,0},{3,1},{4,6},{5,7},{6,4},{7,5},{8,10},{9,11},{10,... | collective-permute-start | bytes 393224 | tf_op jit(solution)/shard_map/ppermute | solution.py:37
  163.3 13.0 %collective-permute-start.39 = (bf16[256,256]{1,0:T(8,128)(2,1)S(1)}, bf16[256,256]{1,0:T(8,128)(2,1)S(1)}, u32[]{:S(2)}, u32[]{:S(2)}) collective-permute-start(bf16[256,256]{1,0:T(8,128)(2,1)S(1)} %copy-done.30), channel_id=1, source_target_pairs={{0,3},{1,0},{2,1},{3,2},{4,7},{5,4},{6,5},{7,6},{8,11},{9,8},{10,9... | collective-permute-start | bytes 393224 | tf_op jit(solution)/shard_map/ppermute | solution.py:37
  172.2 20.4 %copy-start.28 = (bf16[272,256]{1,0:T(8,128)(2,1)S(1)}, bf16[272,256]{1,0:T(8,128)(2,1)}, u32[]{:S(2)}) copy-start(bf16[272,256]{1,0:T(8,128)(2,1)} %get-tuple-element.230) | copy-start | bytes 417796
  172.2 30.6 %copy-start.16 = (bf16[272,256]{1,0:T(8,128)(2,1)S(1)}, bf16[272,256]{1,0:T(8,128)(2,1)}, u32[]{:S(2)}) copy-start(bf16[272,256]{1,0:T(8,128)(2,1)} %get-tuple-element.231) | copy-start | bytes 417796
  176.3 2.8 %collective-permute-start.40 = (bf16[512,896]{1,0:T(8,128)(2,1)}, bf16[512,896]{1,0:T(8,128)(2,1)S(1)}, u32[]{:S(2)}, u32[]{:S(2)}) collective-permute-start(bf16[512,896]{1,0:T(8,128)(2,1)} %get-tuple-element.219), channel_id=1, source_target_pairs={{0,4},{4,0},{1,5},{5,1},{2,6},{6,2},{3,7},{7,3},{8,12},{12,8},{9,1... | collective-permute-start | bytes 2752520 | tf_op jit(solution)/shard_map/ppermute | solution.py:37
  177.1 25.8 %copy-start.6 = (bf16[256,1,256]{2,0,1:T(8,128)(2,1)S(1)}, bf16[256,1,256]{2,0,1:T(8,128)(2,1)}, u32[]{:S(2)}) copy-start(bf16[256,1,256]{2,0,1:T(8,128)(2,1)} %param.13) | copy-start | bytes 393220
  177.1 25.8 %copy-start.7 = (f32[256,256]{1,0:T(8,128)S(1)}, f32[256,256]{1,0:T(8,128)}, u32[]{:S(2)}) copy-start(f32[256,256]{1,0:T(8,128)} %get-tuple-element.217) | copy-start | bytes 786436
  180.4 9.4 %collective-permute-start.41 = (bf16[128,896]{1,0:T(8,128)(2,1)S(1)}, bf16[128,896]{1,0:T(8,128)(2,1)S(1)}, u32[]{:S(2)}, u32[]{:S(2)}) collective-permute-start(bf16[128,896]{1,0:T(8,128)(2,1)S(1)} %get-tuple-element.245), channel_id=1, source_target_pairs={{0,32},{32,64},{64,96},{96,0},{1,33},{33,65},{65,97},{97,1},{2,34}... | collective-permute-start | bytes 688136 | tf_op jit(solution)/shard_map/ppermute | solution.py:37
  180.4 14.7 %collective-permute-start.43 = (bf16[128,896]{1,0:T(8,128)(2,1)S(1)}, bf16[128,896]{1,0:T(8,128)(2,1)S(1)}, u32[]{:S(2)}, u32[]{:S(2)}) collective-permute-start(bf16[128,896]{1,0:T(8,128)(2,1)S(1)} %get-tuple-element.246), channel_id=1, source_target_pairs={{0,96},{32,0},{64,32},{96,64},{1,97},{33,1},{65,33},{97,65},{2,98}... | collective-permute-start | bytes 688136 | tf_op jit(solution)/shard_map/ppermute | solution.py:37
  183.7 11.5 %collective-permute-start.42 = (bf16[128,896]{1,0:T(8,128)(2,1)S(1)}, bf16[128,896]{1,0:T(8,128)(2,1)S(1)}, u32[]{:S(2)}, u32[]{:S(2)}) collective-permute-start(bf16[128,896]{1,0:T(8,128)(2,1)S(1)} %get-tuple-element.247), channel_id=1, source_target_pairs={{0,64},{32,96},{64,0},{96,32},{1,65},{33,97},{65,1},{97,33},{2,66}... | collective-permute-start | bytes 688136 | tf_op jit(solution)/shard_map/ppermute | solution.py:37
  189.8 8.9 %collective-permute-start.44 = (bf16[272,256]{1,0:T(8,128)(2,1)}, bf16[272,256]{1,0:T(8,128)(2,1)S(1)}, u32[]{:S(2)}, u32[]{:S(2)}) collective-permute-start(bf16[272,256]{1,0:T(8,128)(2,1)} %get-tuple-element.228), channel_id=1, source_target_pairs={{0,1},{1,2},{2,3},{3,0},{4,5},{5,6},{6,7},{7,4},{8,9},{9,10},{10,1... | collective-permute-start | bytes 417800 | tf_op jit(solution)/shard_map/ppermute | solution.py:37
  190.3 8.3 %collective-permute-start.45 = (bf16[272,256]{1,0:T(8,128)(2,1)S(1)}, bf16[272,256]{1,0:T(8,128)(2,1)S(1)}, u32[]{:S(2)}, u32[]{:S(2)}) collective-permute-start(bf16[272,256]{1,0:T(8,128)(2,1)S(1)} %copy-done.29), channel_id=1, source_target_pairs={{0,2},{1,3},{2,0},{3,1},{4,6},{5,7},{6,4},{7,5},{8,10},{9,11},{10,... | collective-permute-start | bytes 417800 | tf_op jit(solution)/shard_map/ppermute | solution.py:37
  192.6 6.4 %collective-permute-start.46 = (bf16[272,256]{1,0:T(8,128)(2,1)S(1)}, bf16[272,256]{1,0:T(8,128)(2,1)S(1)}, u32[]{:S(2)}, u32[]{:S(2)}) collective-permute-start(bf16[272,256]{1,0:T(8,128)(2,1)S(1)} %copy-done.28), channel_id=1, source_target_pairs={{0,3},{1,0},{2,1},{3,2},{4,7},{5,4},{6,5},{7,6},{8,11},{9,8},{10,9... | collective-permute-start | bytes 417800 | tf_op jit(solution)/shard_map/ppermute | solution.py:37
  199.7 5.1 %collective-permute-start.49 = (bf16[32,896]{1,0:T(8,128)(2,1)S(1)}, bf16[32,896]{1,0:T(8,128)(2,1)S(1)}, u32[]{:S(2)}, u32[]{:S(2)}) collective-permute-start(bf16[32,896]{1,0:T(8,128)(2,1)S(1)} %get-tuple-element.252), channel_id=1, source_target_pairs={{0,24},{8,0},{16,8},{24,16},{1,25},{9,1},{17,9},{25,17},{2,26},{10... | collective-permute-start | bytes 172040 | tf_op jit(solution)/shard_map/ppermute | solution.py:37
  202.0 6.7 %collective-permute-start.48 = (bf16[32,896]{1,0:T(8,128)(2,1)S(1)}, bf16[32,896]{1,0:T(8,128)(2,1)S(1)}, u32[]{:S(2)}, u32[]{:S(2)}) collective-permute-start(bf16[32,896]{1,0:T(8,128)(2,1)S(1)} %get-tuple-element.253), channel_id=1, source_target_pairs={{0,16},{8,24},{16,0},{24,8},{1,17},{9,25},{17,1},{25,9},{2,18},{10... | collective-permute-start | bytes 172040 | tf_op jit(solution)/shard_map/ppermute | solution.py:37
  202.0 6.7 %collective-permute-start.47 = (bf16[32,896]{1,0:T(8,128)(2,1)S(1)}, bf16[32,896]{1,0:T(8,128)(2,1)S(1)}, u32[]{:S(2)}, u32[]{:S(2)}) collective-permute-start(bf16[32,896]{1,0:T(8,128)(2,1)S(1)} %get-tuple-element.254), channel_id=1, source_target_pairs={{0,8},{8,16},{16,24},{24,0},{1,9},{9,17},{17,25},{25,1},{2,10},{10... | collective-permute-start | bytes 172040 | tf_op jit(solution)/shard_map/ppermute | solution.py:37
  210.9 5.2 %collective-permute-start.52 = (f32[32,128]{1,0:T(8,128)}, f32[32,128]{1,0:T(8,128)S(1)}, u32[]{:S(2)}, u32[]{:S(2)}) collective-permute-start(f32[32,128]{1,0:T(8,128)} %get-tuple-element.236), channel_id=1, source_target_pairs={{0,3},{1,0},{2,1},{3,2},{4,7},{5,4},{6,5},{7,6},{8,11},{9,8},{10,9... | collective-permute-start | bytes 49160 | tf_op jit(solution)/shard_map/ppermute | solution.py:37
  213.6 5.5 %collective-permute-start.51 = (f32[32,128]{1,0:T(8,128)}, f32[32,128]{1,0:T(8,128)S(1)}, u32[]{:S(2)}, u32[]{:S(2)}) collective-permute-start(f32[32,128]{1,0:T(8,128)} %get-tuple-element.236), channel_id=1, source_target_pairs={{0,2},{1,3},{2,0},{3,1},{4,6},{5,7},{6,4},{7,5},{8,10},{9,11},{10,... | collective-permute-start | bytes 49160 | tf_op jit(solution)/shard_map/ppermute | solution.py:37
  214.5 5.2 %collective-permute-start.50 = (f32[32,128]{1,0:T(8,128)}, f32[32,128]{1,0:T(8,128)S(1)}, u32[]{:S(2)}, u32[]{:S(2)}) collective-permute-start(f32[32,128]{1,0:T(8,128)} %get-tuple-element.236), channel_id=1, source_target_pairs={{0,1},{1,2},{2,3},{3,0},{4,5},{5,6},{6,7},{7,4},{8,9},{9,10},{10,1... | collective-permute-start | bytes 49160 | tf_op jit(solution)/shard_map/ppermute | solution.py:37
  (32 other events, 151.0 us)
Sparse Core Ops, SparseCore 0:
  10.3 60.9 all-gather.1
  133.3 42.9 reduce-scatter.2
  189.9 22.4 reduce-scatter.4

commit v4 on v3

--- a/solution.py
+++ b/solution.py
@@ -89,10 +89,8 @@
 
 def cot_kernel(dims, own, idx, *refs):
     n = dims[3]
-    pieces, (full, cot_t, turned) = refs[:n], refs[n:]
+    pieces, (full,) = refs[:n], refs[n:]
     assemble(idx, n, pieces, full, full.shape[1] // n)
-    turned[...] = full[...].T
-    by_core(dims, idx, cot_t, turned, own)
 
 
 def head_columns(ref):
@@ -284,34 +282,32 @@
         refs[k][...] = dot(hidden[...], wd[rows, :], NT).astype(bf16)
 
 
-def by_core(dims, idx, dst, src, own):
+def rows_kernel(dims, own, idx, mine, partner, out, turned):
     nx, nz, nc, _ = dims
-    half = nx * nz
-    for other in range(nc):
-        core = idx[2] if other == 0 else 1 - idx[2]
-
-        def step(i, carry, other=other, core=core):
-            dst[ds(other * half + i, own), :] = src[ds(i * nc + core, own), :]
+    span = mine.shape[0]
+    for k, src in enumerate((mine, partner)):
+        turned[...] = src[...].T
+
+        def step(i, carry, k=k):
+            out[ds(i, own), k * span : (k + 1) * span] = turned[ds(i * nc + idx[2], own), :]
             return carry
 
-        lax.fori_loop(0, half, step, 0)
-
-
-def ffn_grad_kernel(dims, own, idx, normed, cot_t, big, keep, send, turned, left):
+        lax.fori_loop(0, nx * nz, step, 0)
+
+
+def ffn_grad_kernel(normed_rows, cot_rows, big, partner_big, out, left):
     j = pl.program_id(0)
-    half = keep.shape[0]
 
     @pl.when(j == 0)
     def _():
-        turned[...] = normed[...].T
-        by_core(dims, idx, left, turned, own)
+        left[...] = normed_rows[...]
 
     @pl.when(j == 2)
     def _():
-        left[...] = cot_t[...]
-
-    keep[...] = dot(left[:half, :], big[...]).astype(bf16)
-    send[...] = dot(left[half:, :], big[...]).astype(bf16)
+        left[...] = cot_rows[...]
+
+    span = big.shape[0]
+    out[...] = (dot(left[:, :span], big[...]) + dot(left[:, span:], partner_big[...])).astype(bf16)
 
 
 def attend_back_kernel(dims, own, qc, kc, oc, idx, middle, gains, cot, *refs):
@@ -563,12 +559,21 @@
         (dp_parts, both_parts, cosine, sine, head_gains)
     )
     dp_partner = [shift(v, "core", 1) for v in dp_parts]
-    cot, cot_t = call(
+    cot = call(
         functools.partial(cot_kernel, dims, own),
-        [sds((span, width), bf16), sds((width, span), bf16)],
+        [sds((span, width), bf16)],
         [idx] + both_parts,
-        [pltpu.VMEM((width, span), bf16)],
-    )
+    )[0]
+
+    def core_rows(x):
+        return call(
+            functools.partial(rows_kernel, dims, own),
+            [sds((width // nc, nc * span), bf16)],
+            [idx, x, shift(x, "core", 1)],
+            [pltpu.VMEM((width, span), bf16)],
+        )[0]
+
+    cot_rows = core_rows(cot)
 
     w, base, gains, q_t, raw_t, kv, one_rel = call(
         functools.partial(qkv_kernel, dims, own, qc, kc, oc),
@@ -589,7 +594,6 @@
     kv_partner = [shift(v, "core", 1) for v in kv_own]
 
     length = span * nz * nc
-    (kv_own, kv_partner), (cot, cot_t) = lax.optimization_barrier(((kv_own, kv_partner), (cot, cot_t)))
     block = 384
     const = lambda s: pl.BlockSpec(s, lambda j: (0, 0))
     steps = ff // block
@@ -612,6 +616,7 @@
     )
     attn_mine = summed(res, "tensor").astype(bf16)
     attn_parts = gathered(attn_mine, "tensor")
+    attn_parts, cot_rows = lax.optimization_barrier((attn_parts, cot_rows))
 
     hgrad = call(
         hidden_grad_kernel,
@@ -642,18 +647,17 @@
     grad_got = [shift(res[3 + k], "tensor", k) for k in range(1, n)]
     part_zero = res[3]
 
-    ffn_keep, ffn_send = call(
-        functools.partial(ffn_grad_kernel, dims, own),
-        [sds((width // nc, 3 * ff), bf16)] * 2,
-        [idx, normed_two, cot_t, big],
-        [pltpu.VMEM((width, span), bf16)] * 2,
+    ffn_half = call(
+        ffn_grad_kernel,
+        [sds((width // nc, 3 * ff), bf16)],
+        [core_rows(normed_two), cot_rows, big, shift(big, "core", 1)],
+        [pltpu.VMEM((width // nc, nc * span), bf16)],
         grid=(3,),
-        in_specs=[pl.BlockSpec(memory_space=pltpu.SMEM), const((span, width)), const((width, span))]
-        + [pl.BlockSpec((span, ff), lambda j: (0, j))],
-        out_specs=[pl.BlockSpec((width // nc, ff), lambda j: (0, j))] * 2,
+        in_specs=[const((width // nc, nc * span))] * 2 + [pl.BlockSpec((span, ff), lambda j: (0, j))] * 2,
+        out_specs=[pl.BlockSpec((width // nc, ff), lambda j: (0, j))],
         flops=6 * span * width * ff,
-    )
-    grad_got, (ffn_keep, ffn_send) = lax.optimization_barrier((grad_got, (ffn_keep, ffn_send)))
+    )[0]
+    grad_got, ffn_half = lax.optimization_barrier((grad_got, ffn_half))
     grad_mine = sum([g.astype(f32) for g in grad_got], part_zero.astype(f32)).astype(bf16)
     grad_parts = gathered(grad_mine, "tensor")
     down_parts = call(
@@ -669,10 +673,8 @@
         out_specs=[const((span, part))] * n,
         flops=2 * span * width * ff,
     )
-    ffn_got = shift(ffn_send, "core", 1)
-    grad_parts, ffn_got, down_parts = lax.optimization_barrier((grad_parts, ffn_got, down_parts))
-    ffn_half = (ffn_keep.astype(f32) + ffn_got.astype(f32)).astype(bf16)
-    ffn_x = lax.psum_scatter(ffn_half, "dp", scatter_dimension=0, tiled=True)
+    grad_parts, down_parts = lax.optimization_barrier((grad_parts, down_parts))
+    ffn_sum = lax.psum_scatter(ffn_half, ("dp", "z"), scatter_dimension=0, tiled=True)
 
     mine, mid, gain_two, q_gb, gq_grad, kv_keep, kv_send = call(
         functools.partial(attend_back_kernel, dims, own, qc, kc, oc),
@@ -748,8 +750,7 @@
     (keep, send), down_got = lax.optimization_barrier(((keep, send), down_got))
     attn_pieces = core_sum(keep, send, nx)
     attn_got = [shift(attn_pieces[k], "dp", k) for k in range(1, nx)]
-    attn_got[0], norm_parts, ffn_x = lax.optimization_barrier((attn_got[0], norm_parts, ffn_x))
-    ffn_sum = lax.psum_scatter(ffn_x, "z", scatter_dimension=0, tiled=True)
+    attn_got[0], norm_parts = lax.optimization_barrier((attn_got[0], norm_parts))
     attn_x = sum([v.astype(f32) for v in attn_got], attn_pieces[0].astype(f32)).astype(bf16)
     norm_got = [norm_parts[0]] + [shift(norm_parts[k], "tensor", k) for k in range(1, n)]
     attn_x, norm_got = lax.optimization_barrier((attn_x, norm_got))

time: 232 us -> 232 us (level)
  waiting for transfers between devices: 60.5 us -> 46.3 us
  starting transfers between devices: 71.3 us -> 81.4 us
  other arithmetic: 19.3 us -> 13.8 us
  local copies, waits for them, and re-layouts: 7.44 us -> 11.9 us
  Pallas kernels: 58 us -> 62.4 us
    ppermute x53 -> x55, waiting for transfers between devices: 58.5 us -> 44.3 us  [shift(): return lax.ppermute(x, axis, [(i, (i + k) % n) for i in range(n)])]
    ppermute x53 -> x55, starting transfers between devices: 71.1 us -> 81.3 us  [shift(): return lax.ppermute(x, axis, [(i, (i + k) % n) for i in range(n)])]
    convert_element_type x1 -> x0, other arithmetic: 4.59 us -> none  [body(): ffn_half = (ffn_keep.astype(f32) + ffn_got.astype(f32)).astype(bf16)]
    unnamed x83 -> x97, local copies, waits for them, and re-layouts: 4.65 us -> 9.03 us
    pallas_call x15 -> x17, Pallas kernels: 58 us -> 62.4 us  [call(): pl.pallas_call(kernel, out_shape=outs, in_specs=in_specs or [pl.BlockSpec...]
  transfers between devices with their start and end apart: 56 -> 57, of which waited for: 25 -> 23; matrix products, arithmetic and copies ran while one was open for 8% -> 8% of each run, Pallas kernels for 19% -> 22%
where the time goes in v4:
time: 232 us; the launch traced here: 230 us
  starting transfers between devices  81.4 us (35%)
  Pallas kernels  62.4 us (27%)
  waiting for transfers between devices  46.3 us (20%)
  between operations  14.5 us (6%)
  other arithmetic  13.8 us (6%)
  local copies, waits for them, and re-layouts  11.9 us (5%)
    ppermute x55, starting transfers between devices, shift(): return lax.ppermute(x, axis, [(i, (i + k) % n) for i in range(n)])  81.3 us
    pallas_call x17, Pallas kernels, call(): pl.pallas_call(kernel, out_shape=outs, in_specs=in_specs or [pl.BlockSpec...  62.4 us
    ppermute x55, waiting for transfers between devices, shift(): return lax.ppermute(x, axis, [(i, (i + k) % n) for i in range(n)])  44.3 us
    unnamed x97, local copies, waits for them, and re-layouts  9.03 us
  transfers between devices with their start and end apart: 57, of which 23 were waited for; matrix products, arithmetic and copies ran while one was open for 8% of the time, Pallas kernels for 22%

profile of v4, /device:TPU:0, one launch (start us, length us, event | category | flops | bytes accessed | tf_op | source)
XLA Modules:
  0.0 230.2 jit_solution(17957619682002802222)
XLA Ops:
  7.2 2.0 shard_map.228
  9.3 2.1 collective-permute-start
  11.3 3.6 %collective-permute-start.1 = (bf16[32,640]{1,0:T(8,128)(2,1)}, bf16[32,640]{1,0:T(8,128)(2,1)S(1)}, u32[]{:S(2)}, u32[]{:S(2)}) collective-permute-start(bf16[32,640]{1,0:T(8,128)(2,1)} %get-tuple-element.117), channel_id=1, source_target_pairs={{0,16},{8,24},{16,0},{24,8},{1,17},{9,25},{17,1},{25,9},{2,18},{10... | collective-permute-start | bytes 122888 | tf_op jit(solution)/shard_map/ppermute | solution.py:37
  15.9 1.6 collective-permute-start.6
  17.5 2.9 %collective-permute-start.7 = (bf16[256,512]{1,0:T(8,128)(2,1)}, bf16[256,512]{1,0:T(8,128)(2,1)S(1)}, u32[]{:S(2)}, u32[]{:S(2)}) collective-permute-start(bf16[256,512]{1,0:T(8,128)(2,1)} %get-tuple-element.119.refs_0_), channel_id=1, source_target_pairs={{0,2},{1,3},{2,0},{3,1},{4,6},{5,7},{6,4},{7,5},{8,10},{9,11},{10,... | collective-permute-start | bytes 786440 | tf_op jit(solution)/shard_map/ppermute | solution.py:37
  21.2 1.3 collective-permute-start.8
  22.6 1.6 collective-permute-start.3
  24.2 2.8 %collective-permute-start.4 = (bf16[128,640]{1,0:T(8,128)(2,1)S(1)}, bf16[128,640]{1,0:T(8,128)(2,1)S(1)}, u32[]{:S(2)}, u32[]{:S(2)}) collective-permute-start(bf16[128,640]{1,0:T(8,128)(2,1)S(1)} %constant_dynamic-update-slice_fusion.refs_4_), channel_id=1, source_target_pairs={{0,64},{32,96},{64,0},{96,32},{1,65},{33,97},{65,1},{97,33},{2,66}... | collective-permute-start | bytes 491528 | tf_op jit(solution)/shard_map/ppermute | solution.py:37
  27.0 3.8 %collective-permute-done.3.refs_5_ = bf16[128,640]{1,0:T(8,128)(2,1)S(1)} collective-permute-done((bf16[128,640]{1,0:T(8,128)(2,1)S(1)}, bf16[128,640]{1,0:T(8,128)(2,1)S(1)}, u32[]{:S(2)}, u32[]{:S(2)}) %collective-permute-start.3) | collective-permute-done | bytes 163872 | tf_op jit(solution)/shard_map/ppermute | solution.py:37
  30.8 2.9 %collective-permute-start.5 = (bf16[128,640]{1,0:T(8,128)(2,1)S(1)}, bf16[128,640]{1,0:T(8,128)(2,1)S(1)}, u32[]{:S(2)}, u32[]{:S(2)}) collective-permute-start(bf16[128,640]{1,0:T(8,128)(2,1)S(1)} %constant_dynamic-update-slice_fusion.refs_4_), channel_id=1, source_target_pairs={{0,96},{32,0},{64,32},{96,64},{1,97},{33,1},{65,33},{97,65},{2,98}... | collective-permute-start | bytes 491528 | tf_op jit(solution)/shard_map/ppermute | solution.py:37
  40.2 5.0 %shard_map.229 = (bf16[1024,640]{1,0:T(8,128)(2,1)}, bf16[256,1024]{1,0:T(8,128)(2,1)}, f32[8,1024]{1,0:T(8,128)}, bf16[128,512]{1,0:T(8,128)(2,1)}, f32[384,256...) custom-call(s32[4]{0:T(128)} %pad_add_fusion.idx, bf16[256,512]{1,0:T(8,128)(2,1)} %get-tuple-element.119.refs_0_, ...), custom_call_target="tpu_custom_call" | custom-call | flops 268435456 | bytes 5472528 | tf_op jit(solution)/shard_map/pallas_call | solution.py:55
  45.2 2.8 %collective-permute-start.13 = (bf16[256,256]{1,0:T(8,128)(2,1)}, bf16[256,256]{1,0:T(8,128)(2,1)S(1)}, u32[]{:S(2)}, u32[]{:S(2)}) collective-permute-start(bf16[256,256]{1,0:T(8,128)(2,1)} %get-tuple-element.133.refs_0_), channel_id=1, source_target_pairs={{0,8},{8,16},{16,24},{24,0},{1,9},{9,17},{17,25},{25,1},{2,10},{10... | collective-permute-start | bytes 393224 | tf_op jit(solution)/shard_map/ppermute | solution.py:37
  48.5 2.3 collective-permute-start.15
  50.8 5.0 %collective-permute-done.13.refs_1_ = bf16[256,256]{1,0:T(8,128)(2,1)S(1)} collective-permute-done((bf16[256,256]{1,0:T(8,128)(2,1)}, bf16[256,256]{1,0:T(8,128)(2,1)S(1)}, u32[]{:S(2)}, u32[]{:S(2)}) %collective-permute-start.13) | collective-permute-done | bytes 131104 | tf_op jit(solution)/shard_map/ppermute | solution.py:37
  55.8 5.3 %collective-permute-done.14.refs_2_ = bf16[256,256]{1,0:T(8,128)(2,1)S(1)} collective-permute-done((bf16[256,256]{1,0:T(8,128)(2,1)}, bf16[256,256]{1,0:T(8,128)(2,1)S(1)}, u32[]{:S(2)}, u32[]{:S(2)}) %collective-permute-start.14) | collective-permute-done | bytes 131104 | tf_op jit(solution)/shard_map/ppermute | solution.py:37
  61.9 2.2 shard_map.232.mine.cot
  65.4 3.2 %shard_map.230 = (bf16[2048,256]{1,0:T(8,128)(2,1)}, f32[128,512]{1,0:T(8,128)}, bf16[256,256]{1,0:T(8,128)(2,1)}, f32[8,512]{1,0:T(8,128)}) custom-call(s32[4]{0:T(128)} %pad_add_fusion.idx, bf16[128,512]{1,0:T(8,128)(2,1)} %get-tuple-element.132.q_t.refs_7_, bf16[256,256]{1,0:T(8,128)(2,1)} %get-tuple-element.133.refs_0_, bf16[256,256]{1,0:T(8,128)(2,1)} %copy-done.40, ...), custom_call_target="tpu_custom_call" | custom-call | flops 536870912 | bytes 2637840 | tf_op jit(solution)/shard_map/pallas_call | solution.py:55
  68.7 2.0 all-gather.2.cloned.1.call-done.w_low.w_high.wd.refs_4_.refs_5_
  70.7 2.2 shard_map.231
  72.9 1.5 collective-permute-start.20
  74.4 2.5 %collective-permute-start.21 = (bf16[256,256]{1,0:T(8,128)(2,1)}, bf16[256,256]{1,0:T(8,128)(2,1)S(1)}, u32[]{:S(2)}, u32[]{:S(2)}) collective-permute-start(bf16[256,256]{1,0:T(8,128)(2,1)} %get-tuple-element.138), channel_id=1, source_target_pairs={{0,2},{1,3},{2,0},{3,1},{4,6},{5,7},{6,4},{7,5},{8,10},{9,11},{10,... | collective-permute-start | bytes 393224 | tf_op jit(solution)/shard_map/ppermute | solution.py:37
  76.9 1.4 collective-permute-start.22
  78.3 1.7 collective-permute-done.20
  80.0 3.6 %collective-permute-done.21 = bf16[256,256]{1,0:T(8,128)(2,1)S(1)} collective-permute-done((bf16[256,256]{1,0:T(8,128)(2,1)}, bf16[256,256]{1,0:T(8,128)(2,1)S(1)}, u32[]{:S(2)}, u32[]{:S(2)}) %collective-permute-start.21) | collective-permute-done | bytes 131104 | tf_op jit(solution)/shard_map/ppermute | solution.py:37
  84.5 1.6 collective-permute-start.23
  86.2 2.4 %collective-permute-start.24 = (bf16[256,256]{1,0:T(8,128)(2,1)S(1)}, bf16[256,256]{1,0:T(8,128)(2,1)S(1)}, u32[]{:S(2)}, u32[]{:S(2)}) collective-permute-start(bf16[256,256]{1,0:T(8,128)(2,1)S(1)} %add_convert_fusion.11.refs_0_), channel_id=1, source_target_pairs={{0,2},{1,3},{2,0},{3,1},{4,6},{5,7},{6,4},{7,5},{8,10},{9,11},{10,... | collective-permute-start | bytes 393224 | tf_op jit(solution)/shard_map/ppermute | solution.py:37
  88.6 1.3 collective-permute-start.25
  90.7 2.6 %shard_map.233.cot_rows = bf16[512,512]{1,0:T(8,128)(2,1)} custom-call(s32[4]{0:T(128)} %pad_add_fusion.idx, bf16[256,1024]{1,0:T(8,128)(2,1)} %shard_map.232.mine.cot, bf16[256,1024]{1,0:T(8,128)(2,1)} %copy-done.7), custom_call_target="tpu_custom_call" | custom-call | bytes 1572880 | tf_op jit(solution)/shard_map/pallas_call | solution.py:55
  93.3 4.3 %shard_map.234.refs_6_ = f32[256,1152]{1,0:T(8,128)} custom-call(bf16[256,1024]{1,0:T(8,128)(2,1)} %shard_map.232.mine.cot, bf16[1024,3712]{1,0:T(8,128)(2,1)} %all-gather.2.cloned.1.call-done.w_low.w_high.wd.refs_4_.refs_5_), custom_call_target="tpu_custom_call" | custom-call | flops 603979776 | bytes 9306112 | tf_op jit(solution)/shard_map/pallas_call | solution.py:55
  98.3 8.5 %shard_map.235 = (f32[256,1024]{1,0:T(8,128)}, bf16[256,1024]{1,0:T(8,128)(2,1)}, bf16[256,3456]{1,0:T(8,128)(2,1)}, bf16[256,256]{1,0:T(8,128)(2,1)}, bf16[256,...) custom-call(s32[4]{0:T(128)} %pad_add_fusion.idx, ...), custom_call_target="tpu_custom_call" | custom-call | flops 2415919104 | bytes 21331984 | tf_op jit(solution)/shard_map/pallas_call | solution.py:55
  109.3 1.7 collective-permute-start.29
  112.4 2.6 %shard_map.236.normed_rows = bf16[512,512]{1,0:T(8,128)(2,1)} custom-call(s32[4]{0:T(128)} %pad_add_fusion.idx, bf16[256,1024]{1,0:T(8,128)(2,1)} %get-tuple-element.150.mine, bf16[256,1024]{1,0:T(8,128)(2,1)} %copy-done.8), custom_call_target="tpu_custom_call" | custom-call | bytes 1572880 | tf_op jit(solution)/shard_map/pallas_call | solution.py:55
  116.2 6.1 %shard_map.237 = bf16[512,3456]{1,0:T(8,128)(2,1)} custom-call(bf16[512,512]{1,0:T(8,128)(2,1)} %shard_map.236.normed_rows, bf16[512,512]{1,0:T(8,128)(2,1)} %shard_map.233.cot_rows, bf16[256,3456]{1,0:T(8,128)(2,1)} %get-tuple-element.152.big.hidden, bf16[256,3456]{1,0:T(8,128)(2,1)} %copy-done.1), custom_call_target="tpu_custom_call" | custom-call | flops 1811939328 | bytes 8126464 | tf_op jit(solution)/shard_map/pallas_call | solution.py:55
  124.0 1.4 collective-permute-start.33
  125.4 2.5 %collective-permute-start.34 = (bf16[256,256]{1,0:T(8,128)(2,1)S(1)}, bf16[256,256]{1,0:T(8,128)(2,1)S(1)}, u32[]{:S(2)}, u32[]{:S(2)}) collective-permute-start(bf16[256,256]{1,0:T(8,128)(2,1)S(1)} %add_convert_fusion.10.refs_0_), channel_id=1, source_target_pairs={{0,3},{1,0},{2,1},{3,2},{4,7},{5,4},{6,5},{7,6},{8,11},{9,8},{10,9... | collective-permute-start | bytes 393224 | tf_op jit(solution)/shard_map/ppermute | solution.py:37
  128.0 3.5 %shard_map.238 = (bf16[256,256]{1,0:T(8,128)(2,1)}, bf16[256,256]{1,0:T(8,128)(2,1)}, bf16[256,256]{1,0:T(8,128)(2,1)}, bf16[256,256]{1,0:T(8,128)(2,1)}) custom-call(s32[4]{0:T(128)} %pad_add_fusion.idx, bf16[256,3456]{1,0:T(8,128)(2,1)} %get-tuple-element.152.big.hidden, bf16[1024,3712]{1,0:T(8,128)(2,1)} %all-gather.2.cloned.1.call-done.w_low.w_high.wd.refs_4_.refs_5_), custom_call_target="tpu_custom_call" | custom-call | flops 603979776 | bytes 9895952 | tf_op jit(solution)/shard_map/pallas_call | solution.py:55
  131.4 1.4 collective-permute-done.32.refs_1_
  134.2 6.3 %shard_map.239 = (f32[256,256]{1,0:T(8,128)}, bf16[256,1024]{1,0:T(8,128)(2,1)}, f32[8,1024]{1,0:T(8,128)}, bf16[256,256]{1,0:T(8,128)(2,1)}, f32[64,1]{1,0:T(8,...) custom-call(s32[4]{0:T(128)} %pad_add_fusion.idx, f32[256,1024]{1,0:T(8,128)} %get-tuple-element.144.middle, ...), custom_call_target="tpu_custom_call" | custom-call | flops 1342177280 | bytes 21250576 | tf_op jit(solution)/shard_map/pallas_call | solution.py:55
  140.7 2.0 collective-permute-done.35
  142.7 1.9 add_convert_fusion.6
  144.6 2.6 %collective-permute-start.37 = (bf16[256,256]{1,0:T(8,128)(2,1)S(1)}, bf16[256,256]{1,0:T(8,128)(2,1)S(1)}, u32[]{:S(2)}, u32[]{:S(2)}) collective-permute-start(bf16[256,256]{1,0:T(8,128)(2,1)S(1)} %get-tuple-element.225), channel_id=1, source_target_pairs={{0,8},{8,16},{16,24},{24,0},{1,9},{9,17},{17,25},{25,1},{2,10},{10... | collective-permute-start | bytes 393224 | tf_op jit(solution)/shard_map/ppermute | solution.py:37
  147.2 7.3 %collective-permute-start.36 = (bf16[256,256]{1,0:T(8,128)(2,1)S(1)}, bf16[256,256]{1,0:T(8,128)(2,1)S(1)}, u32[]{:S(2)}, u32[]{:S(2)}) collective-permute-start(bf16[256,256]{1,0:T(8,128)(2,1)S(1)} %get-tuple-element.227), channel_id=1, source_target_pairs={{0,16},{8,24},{16,0},{24,8},{1,17},{9,25},{17,1},{25,9},{2,18},{10... | collective-permute-start | bytes 393224 | tf_op jit(solution)/shard_map/ppermute | solution.py:37
  154.4 4.4 %collective-permute-done.37.refs_1_ = bf16[256,256]{1,0:T(8,128)(2,1)S(1)} collective-permute-done((bf16[256,256]{1,0:T(8,128)(2,1)S(1)}, bf16[256,256]{1,0:T(8,128)(2,1)S(1)}, u32[]{:S(2)}, u32[]{:S(2)}) %collective-permute-start.37) | collective-permute-done | bytes 131104 | tf_op jit(solution)/shard_map/ppermute | solution.py:37
  158.9 2.6 %collective-permute-start.39 = (bf16[256,256]{1,0:T(8,128)(2,1)S(1)}, bf16[256,256]{1,0:T(8,128)(2,1)S(1)}, u32[]{:S(2)}, u32[]{:S(2)}) collective-permute-start(bf16[256,256]{1,0:T(8,128)(2,1)S(1)} %copy-done.39), channel_id=1, source_target_pairs={{0,1},{1,2},{2,3},{3,0},{4,5},{5,6},{6,7},{7,4},{8,9},{9,10},{10,1... | collective-permute-start | bytes 393224 | tf_op jit(solution)/shard_map/ppermute | solution.py:37
  161.4 2.0 collective-permute-start.40
  164.2 2.9 %shard_map.240.out_rel = bf16[1024,256]{1,0:T(8,128)(2,1)} custom-call(s32[4]{0:T(128)} %pad_add_fusion.idx, bf16[256,1024]{1,0:T(8,128)(2,1)} %get-tuple-element.170.mid, bf16[256,256]{1,0:T(8,128)(2,1)} %get-tuple-element.134.attn_b), custom_call_target="tpu_custom_call" | custom-call | flops 134217728 | bytes 1179664 | tf_op jit(solution)/shard_map/pallas_call | solution.py:55
  167.8 3.8 %shard_map.241 = (bf16[256,512]{1,0:T(8,128)(2,1)}, f32[8,1024]{1,0:T(8,128)}, f32[64,1]{1,0:T(8,128)}, bf16[272,256]{1,0:T(8,128)(2,1)}, bf16[272,256]{1,0:T(8,...) custom-call(s32[4]{0:T(128)} %pad_add_fusion.idx, bf16[256,256]{1,0:T(8,128)(2,1)} %get-tuple-element.226.refs_0_, ...), custom_call_target="tpu_custom_call" | custom-call | flops 268435456 | bytes 3834384 | tf_op jit(solution)/shard_map/pallas_call | solution.py:55
  171.6 4.0 %shard_map.242 = (bf16[512,896]{1,0:T(8,128)(2,1)}, bf16[512,896]{1,0:T(8,128)(2,1)}) custom-call(s32[4]{0:T(128)} %pad_add_fusion.idx, bf16[1024,256]{1,0:T(8,128)(2,1)} %get-tuple-element.145.one_rel, bf16[1024,256]{1,0:T(8,128)(2,1)} %shard_map.240.out_rel, bf16[256,512]{1,0:T(8,128)(2,1)} %get-tuple-element.180.qkv_gb, ...), custom_call_target="tpu_custom_call" | custom-call | flops 402653184 | bytes 3211792 | tf_op jit(solution)/shard_map/pallas_call | solution.py:55
  176.7 1.7 collective-permute-done.42
  178.4 1.3 add_convert_fusion.3
  180.7 2.0 collective-permute-start.44
  182.7 2.5 %collective-permute-start.45 = (bf16[128,896]{1,0:T(8,128)(2,1)S(1)}, bf16[128,896]{1,0:T(8,128)(2,1)S(1)}, u32[]{:S(2)}, u32[]{:S(2)}) collective-permute-start(bf16[128,896]{1,0:T(8,128)(2,1)S(1)} %get-tuple-element.222), channel_id=1, source_target_pairs={{0,96},{32,0},{64,32},{96,64},{1,97},{33,1},{65,33},{97,65},{2,98}... | collective-permute-start | bytes 688136 | tf_op jit(solution)/shard_map/ppermute | solution.py:37
  185.2 1.7 fusion.4
  186.9 4.6 %collective-permute-done.43 = bf16[128,896]{1,0:T(8,128)(2,1)S(1)} collective-permute-done((bf16[128,896]{1,0:T(8,128)(2,1)S(1)}, bf16[128,896]{1,0:T(8,128)(2,1)S(1)}, u32[]{:S(2)}, u32[]{:S(2)}) %collective-permute-start.43) | collective-permute-done | bytes 229408 | tf_op jit(solution)/shard_map/ppermute | solution.py:37
  191.6 3.1 %collective-permute-start.46 = (bf16[272,256]{1,0:T(8,128)(2,1)S(1)}, bf16[272,256]{1,0:T(8,128)(2,1)S(1)}, u32[]{:S(2)}, u32[]{:S(2)}) collective-permute-start(bf16[272,256]{1,0:T(8,128)(2,1)S(1)} %copy-done.36), channel_id=1, source_target_pairs={{0,1},{1,2},{2,3},{3,0},{4,5},{5,6},{6,7},{7,4},{8,9},{9,10},{10,1... | collective-permute-start | bytes 417800 | tf_op jit(solution)/shard_map/ppermute | solution.py:37
  194.6 2.8 %collective-permute-start.48 = (bf16[272,256]{1,0:T(8,128)(2,1)S(1)}, bf16[272,256]{1,0:T(8,128)(2,1)S(1)}, u32[]{:S(2)}, u32[]{:S(2)}) collective-permute-start(bf16[272,256]{1,0:T(8,128)(2,1)S(1)} %copy-done.34), channel_id=1, source_target_pairs={{0,3},{1,0},{2,1},{3,2},{4,7},{5,4},{6,5},{7,6},{8,11},{9,8},{10,9... | collective-permute-start | bytes 417800 | tf_op jit(solution)/shard_map/ppermute | solution.py:37
  198.5 2.7 %collective-permute-done.47 = bf16[272,256]{1,0:T(8,128)(2,1)S(1)} collective-permute-done((bf16[272,256]{1,0:T(8,128)(2,1)S(1)}, bf16[272,256]{1,0:T(8,128)(2,1)S(1)}, u32[]{:S(2)}, u32[]{:S(2)}) %collective-permute-start.47) | collective-permute-done | bytes 139296 | tf_op jit(solution)/shard_map/ppermute | solution.py:37
  202.2 2.9 %collective-permute-start.51 = (bf16[32,896]{1,0:T(8,128)(2,1)S(1)}, bf16[32,896]{1,0:T(8,128)(2,1)S(1)}, u32[]{:S(2)}, u32[]{:S(2)}) collective-permute-start(bf16[32,896]{1,0:T(8,128)(2,1)S(1)} %get-tuple-element.228), channel_id=1, source_target_pairs={{0,24},{8,0},{16,8},{24,16},{1,25},{9,1},{17,9},{25,17},{2,26},{10... | collective-permute-start | bytes 172040 | tf_op jit(solution)/shard_map/ppermute | solution.py:37
  206.0 1.9 collective-permute-done.49.refs_1_
  209.3 1.5 shard_map.243
  210.9 1.5 collective-permute-start.52
  212.3 2.5 %collective-permute-start.53 = (f32[32,128]{1,0:T(8,128)}, f32[32,128]{1,0:T(8,128)S(1)}, u32[]{:S(2)}, u32[]{:S(2)}) collective-permute-start(f32[32,128]{1,0:T(8,128)} %get-tuple-element.212), channel_id=1, source_target_pairs={{0,2},{1,3},{2,0},{3,1},{4,6},{5,7},{6,4},{7,5},{8,10},{9,11},{10,... | collective-permute-start | bytes 49160 | tf_op jit(solution)/shard_map/ppermute | solution.py:37
  215.7 1.5 add_reduce_fusion
  221.7 1.7 shard_map.244
  (194 shorter events, 35.1 us)
Async XLA Ops:
  7.2 63.5 %all-gather.2.cloned.1.call-start = ((), (), s32[]{:S(2)}) async-start(), calls=%async_computation.1 | async-start | bytes 7839744 | tf_op jit(solution)/shard_map/all_gather | solution.py:548
  9.2 212.5 %reduce-scatter.2.cloned.1.call-start = ((), (), s32[]{:S(2)}) async-start(), calls=%async_computation.2 | async-start | bytes 3760128 | tf_op jit(solution)/shard_map/reduce_scatter | solution.py:677
  9.3 11.9 %collective-permute-start = (bf16[32,640]{1,0:T(8,128)(2,1)}, bf16[32,640]{1,0:T(8,128)(2,1)S(1)}, u32[]{:S(2)}, u32[]{:S(2)}) collective-permute-start(bf16[32,640]{1,0:T(8,128)(2,1)} %get-tuple-element.117), channel_id=1, source_target_pairs={{0,8},{8,16},{16,24},{24,0},{1,9},{9,17},{17,25},{25,1},{2,10},{10... | collective-permute-start | bytes 122888 | tf_op jit(solution)/shard_map/ppermute | solution.py:37
  11.3 11.2 %collective-permute-start.1 = (bf16[32,640]{1,0:T(8,128)(2,1)}, bf16[32,640]{1,0:T(8,128)(2,1)S(1)}, u32[]{:S(2)}, u32[]{:S(2)}) collective-permute-start(bf16[32,640]{1,0:T(8,128)(2,1)} %get-tuple-element.117), channel_id=1, source_target_pairs={{0,16},{8,24},{16,0},{24,8},{1,17},{9,25},{17,1},{25,9},{2,18},{10... | collective-permute-start | bytes 122888 | tf_op jit(solution)/shard_map/ppermute | solution.py:37
  14.9 7.7 %collective-permute-start.2 = (bf16[32,640]{1,0:T(8,128)(2,1)}, bf16[32,640]{1,0:T(8,128)(2,1)S(1)}, u32[]{:S(2)}, u32[]{:S(2)}) collective-permute-start(bf16[32,640]{1,0:T(8,128)(2,1)} %get-tuple-element.117), channel_id=1, source_target_pairs={{0,24},{8,0},{16,8},{24,16},{1,25},{9,1},{17,9},{25,17},{2,26},{10... | collective-permute-start | bytes 122888 | tf_op jit(solution)/shard_map/ppermute | solution.py:37
  15.9 20.9 %collective-permute-start.6 = (bf16[256,512]{1,0:T(8,128)(2,1)}, bf16[256,512]{1,0:T(8,128)(2,1)S(1)}, u32[]{:S(2)}, u32[]{:S(2)}) collective-permute-start(bf16[256,512]{1,0:T(8,128)(2,1)} %get-tuple-element.119.refs_0_), channel_id=1, source_target_pairs={{0,1},{1,2},{2,3},{3,0},{4,5},{5,6},{6,7},{7,4},{8,9},{9,10},{10,1... | collective-permute-start | bytes 786440 | tf_op jit(solution)/shard_map/ppermute | solution.py:37
  17.5 19.4 %collective-permute-start.7 = (bf16[256,512]{1,0:T(8,128)(2,1)}, bf16[256,512]{1,0:T(8,128)(2,1)S(1)}, u32[]{:S(2)}, u32[]{:S(2)}) collective-permute-start(bf16[256,512]{1,0:T(8,128)(2,1)} %get-tuple-element.119.refs_0_), channel_id=1, source_target_pairs={{0,2},{1,3},{2,0},{3,1},{4,6},{5,7},{6,4},{7,5},{8,10},{9,11},{10,... | collective-permute-start | bytes 786440 | tf_op jit(solution)/shard_map/ppermute | solution.py:37
  21.2 15.7 %collective-permute-start.8 = (bf16[256,512]{1,0:T(8,128)(2,1)}, bf16[256,512]{1,0:T(8,128)(2,1)S(1)}, u32[]{:S(2)}, u32[]{:S(2)}) collective-permute-start(bf16[256,512]{1,0:T(8,128)(2,1)} %get-tuple-element.119.refs_0_), channel_id=1, source_target_pairs={{0,3},{1,0},{2,1},{3,2},{4,7},{5,4},{6,5},{7,6},{8,11},{9,8},{10,9... | collective-permute-start | bytes 786440 | tf_op jit(solution)/shard_map/ppermute | solution.py:37
  22.6 8.2 %collective-permute-start.3 = (bf16[128,640]{1,0:T(8,128)(2,1)S(1)}, bf16[128,640]{1,0:T(8,128)(2,1)S(1)}, u32[]{:S(2)}, u32[]{:S(2)}) collective-permute-start(bf16[128,640]{1,0:T(8,128)(2,1)S(1)} %constant_dynamic-update-slice_fusion.refs_4_), channel_id=1, source_target_pairs={{0,32},{32,64},{64,96},{96,0},{1,33},{33,65},{65,97},{97,1},{2,34}... | collective-permute-start | bytes 491528 | tf_op jit(solution)/shard_map/ppermute | solution.py:37
  24.2 11.8 %collective-permute-start.4 = (bf16[128,640]{1,0:T(8,128)(2,1)S(1)}, bf16[128,640]{1,0:T(8,128)(2,1)S(1)}, u32[]{:S(2)}, u32[]{:S(2)}) collective-permute-start(bf16[128,640]{1,0:T(8,128)(2,1)S(1)} %constant_dynamic-update-slice_fusion.refs_4_), channel_id=1, source_target_pairs={{0,64},{32,96},{64,0},{96,32},{1,65},{33,97},{65,1},{97,33},{2,66}... | collective-permute-start | bytes 491528 | tf_op jit(solution)/shard_map/ppermute | solution.py:37
  30.8 6.1 %collective-permute-start.5 = (bf16[128,640]{1,0:T(8,128)(2,1)S(1)}, bf16[128,640]{1,0:T(8,128)(2,1)S(1)}, u32[]{:S(2)}, u32[]{:S(2)}) collective-permute-start(bf16[128,640]{1,0:T(8,128)(2,1)S(1)} %constant_dynamic-update-slice_fusion.refs_4_), channel_id=1, source_target_pairs={{0,96},{32,0},{64,32},{96,64},{1,97},{33,1},{65,33},{97,65},{2,98}... | collective-permute-start | bytes 491528 | tf_op jit(solution)/shard_map/ppermute | solution.py:37
  36.9 1.7 collective-permute-start.10
  37.0 1.6 collective-permute-start.11
  37.5 1.4 collective-permute-start.12
  37.6 1.5 collective-permute-start.9
  45.2 10.6 %collective-permute-start.13 = (bf16[256,256]{1,0:T(8,128)(2,1)}, bf16[256,256]{1,0:T(8,128)(2,1)S(1)}, u32[]{:S(2)}, u32[]{:S(2)}) collective-permute-start(bf16[256,256]{1,0:T(8,128)(2,1)} %get-tuple-element.133.refs_0_), channel_id=1, source_target_pairs={{0,8},{8,16},{16,24},{24,0},{1,9},{9,17},{17,25},{25,1},{2,10},{10... | collective-permute-start | bytes 393224 | tf_op jit(solution)/shard_map/ppermute | solution.py:37
  48.0 13.1 %collective-permute-start.14 = (bf16[256,256]{1,0:T(8,128)(2,1)}, bf16[256,256]{1,0:T(8,128)(2,1)S(1)}, u32[]{:S(2)}, u32[]{:S(2)}) collective-permute-start(bf16[256,256]{1,0:T(8,128)(2,1)} %get-tuple-element.133.refs_0_), channel_id=1, source_target_pairs={{0,16},{8,24},{16,0},{24,8},{1,17},{9,25},{17,1},{25,9},{2,18},{10... | collective-permute-start | bytes 393224 | tf_op jit(solution)/shard_map/ppermute | solution.py:37
  48.5 13.4 %collective-permute-start.15 = (bf16[256,256]{1,0:T(8,128)(2,1)}, bf16[256,256]{1,0:T(8,128)(2,1)S(1)}, u32[]{:S(2)}, u32[]{:S(2)}) collective-permute-start(bf16[256,256]{1,0:T(8,128)(2,1)} %get-tuple-element.133.refs_0_), channel_id=1, source_target_pairs={{0,24},{8,0},{16,8},{24,16},{1,25},{9,1},{17,9},{25,17},{2,26},{10... | collective-permute-start | bytes 393224 | tf_op jit(solution)/shard_map/ppermute | solution.py:37
  50.8 13.8 %collective-permute-start.16 = (bf16[256,256]{1,0:T(8,128)(2,1)}, bf16[256,256]{1,0:T(8,128)(2,1)S(1)}, u32[]{:S(2)}, u32[]{:S(2)}) collective-permute-start(bf16[256,256]{1,0:T(8,128)(2,1)} %get-tuple-element.133.refs_0_), channel_id=1, source_target_pairs={{0,4},{4,0},{1,5},{5,1},{2,6},{6,2},{3,7},{7,3},{8,12},{12,8},{9,1... | collective-permute-start | bytes 393224 | tf_op jit(solution)/shard_map/ppermute | solution.py:37
  55.8 8.8 %collective-permute-start.17 = (bf16[256,256]{1,0:T(8,128)(2,1)S(1)}, bf16[256,256]{1,0:T(8,128)(2,1)S(1)}, u32[]{:S(2)}, u32[]{:S(2)}) collective-permute-start(bf16[256,256]{1,0:T(8,128)(2,1)S(1)} %collective-permute-done.13.refs_1_), channel_id=1, source_target_pairs={{0,4},{4,0},{1,5},{5,1},{2,6},{6,2},{3,7},{7,3},{8,12},{12,8},{9,1... | collective-permute-start | bytes 393224 | tf_op jit(solution)/shard_map/ppermute | solution.py:37
  61.1 3.5 %collective-permute-start.18 = (bf16[256,256]{1,0:T(8,128)(2,1)S(1)}, bf16[256,256]{1,0:T(8,128)(2,1)S(1)}, u32[]{:S(2)}, u32[]{:S(2)}) collective-permute-start(bf16[256,256]{1,0:T(8,128)(2,1)S(1)} %collective-permute-done.14.refs_2_), channel_id=1, source_target_pairs={{0,4},{4,0},{1,5},{5,1},{2,6},{6,2},{3,7},{7,3},{8,12},{12,8},{9,1... | collective-permute-start | bytes 393224 | tf_op jit(solution)/shard_map/ppermute | solution.py:37
  61.9 2.7 %collective-permute-start.19 = (bf16[256,256]{1,0:T(8,128)(2,1)S(1)}, bf16[256,256]{1,0:T(8,128)(2,1)S(1)}, u32[]{:S(2)}, u32[]{:S(2)}) collective-permute-start(bf16[256,256]{1,0:T(8,128)(2,1)S(1)} %collective-permute-done.15.refs_3_), channel_id=1, source_target_pairs={{0,4},{4,0},{1,5},{5,1},{2,6},{6,2},{3,7},{7,3},{8,12},{12,8},{9,1... | collective-permute-start | bytes 393224 | tf_op jit(solution)/shard_map/ppermute | solution.py:37
  64.1 25.9 %collective-permute-start.26 = (bf16[256,1024]{1,0:T(8,128)(2,1)}, bf16[256,1024]{1,0:T(8,128)(2,1)S(1)}, u32[]{:S(2)}, u32[]{:S(2)}) collective-permute-start(bf16[256,1024]{1,0:T(8,128)(2,1)} %shard_map.232.mine.cot), channel_id=1, source_target_pairs={{0,4},{4,0},{1,5},{5,1},{2,6},{6,2},{3,7},{7,3},{8,12},{12,8},{9,1... | collective-permute-start | bytes 1572872 | tf_op jit(solution)/shard_map/ppermute | solution.py:37
  72.9 7.1 %collective-permute-start.20 = (bf16[256,256]{1,0:T(8,128)(2,1)}, bf16[256,256]{1,0:T(8,128)(2,1)S(1)}, u32[]{:S(2)}, u32[]{:S(2)}) collective-permute-start(bf16[256,256]{1,0:T(8,128)(2,1)} %get-tuple-element.137), channel_id=1, source_target_pairs={{0,1},{1,2},{2,3},{3,0},{4,5},{5,6},{6,7},{7,4},{8,9},{9,10},{10,1... | collective-permute-start | bytes 393224 | tf_op jit(solution)/shard_map/ppermute | solution.py:37
  74.4 9.2 %collective-permute-start.21 = (bf16[256,256]{1,0:T(8,128)(2,1)}, bf16[256,256]{1,0:T(8,128)(2,1)S(1)}, u32[]{:S(2)}, u32[]{:S(2)}) collective-permute-start(bf16[256,256]{1,0:T(8,128)(2,1)} %get-tuple-element.138), channel_id=1, source_target_pairs={{0,2},{1,3},{2,0},{3,1},{4,6},{5,7},{6,4},{7,5},{8,10},{9,11},{10,... | collective-permute-start | bytes 393224 | tf_op jit(solution)/shard_map/ppermute | solution.py:37
  76.9 6.7 %collective-permute-start.22 = (bf16[256,256]{1,0:T(8,128)(2,1)}, bf16[256,256]{1,0:T(8,128)(2,1)S(1)}, u32[]{:S(2)}, u32[]{:S(2)}) collective-permute-start(bf16[256,256]{1,0:T(8,128)(2,1)} %get-tuple-element.139), channel_id=1, source_target_pairs={{0,3},{1,0},{2,1},{3,2},{4,7},{5,4},{6,5},{7,6},{8,11},{9,8},{10,9... | collective-permute-start | bytes 393224 | tf_op jit(solution)/shard_map/ppermute | solution.py:37
  84.5 13.1 %collective-permute-start.23 = (bf16[256,256]{1,0:T(8,128)(2,1)S(1)}, bf16[256,256]{1,0:T(8,128)(2,1)S(1)}, u32[]{:S(2)}, u32[]{:S(2)}) collective-permute-start(bf16[256,256]{1,0:T(8,128)(2,1)S(1)} %add_convert_fusion.11.refs_0_), channel_id=1, source_target_pairs={{0,1},{1,2},{2,3},{3,0},{4,5},{5,6},{6,7},{7,4},{8,9},{9,10},{10,1... | collective-permute-start | bytes 393224 | tf_op jit(solution)/shard_map/ppermute | solution.py:37
  86.2 11.4 %collective-permute-start.24 = (bf16[256,256]{1,0:T(8,128)(2,1)S(1)}, bf16[256,256]{1,0:T(8,128)(2,1)S(1)}, u32[]{:S(2)}, u32[]{:S(2)}) collective-permute-start(bf16[256,256]{1,0:T(8,128)(2,1)S(1)} %add_convert_fusion.11.refs_0_), channel_id=1, source_target_pairs={{0,2},{1,3},{2,0},{3,1},{4,6},{5,7},{6,4},{7,5},{8,10},{9,11},{10,... | collective-permute-start | bytes 393224 | tf_op jit(solution)/shard_map/ppermute | solution.py:37
  88.6 9.1 %collective-permute-start.25 = (bf16[256,256]{1,0:T(8,128)(2,1)S(1)}, bf16[256,256]{1,0:T(8,128)(2,1)S(1)}, u32[]{:S(2)}, u32[]{:S(2)}) collective-permute-start(bf16[256,256]{1,0:T(8,128)(2,1)S(1)} %add_convert_fusion.11.refs_0_), channel_id=1, source_target_pairs={{0,3},{1,0},{2,1},{3,2},{4,7},{5,4},{6,5},{7,6},{8,11},{9,8},{10,9... | collective-permute-start | bytes 393224 | tf_op jit(solution)/shard_map/ppermute | solution.py:37
  106.9 8.1 %collective-permute-start.31 = (bf16[256,3456]{1,0:T(8,128)(2,1)}, bf16[256,3456]{1,0:T(8,128)(2,1)S(1)}, u32[]{:S(2)}, u32[]{:S(2)}) collective-permute-start(bf16[256,3456]{1,0:T(8,128)(2,1)} %get-tuple-element.152.big.hidden), channel_id=1, source_target_pairs={{0,4},{4,0},{1,5},{5,1},{2,6},{6,2},{3,7},{7,3},{8,12},{12,8},{9,1... | collective-permute-start | bytes 5308424 | tf_op jit(solution)/shard_map/ppermute | solution.py:37
  106.9 4.6 %collective-permute-start.30 = (bf16[256,1024]{1,0:T(8,128)(2,1)}, bf16[256,1024]{1,0:T(8,128)(2,1)S(1)}, u32[]{:S(2)}, u32[]{:S(2)}) collective-permute-start(bf16[256,1024]{1,0:T(8,128)(2,1)} %get-tuple-element.150.mine), channel_id=1, source_target_pairs={{0,4},{4,0},{1,5},{5,1},{2,6},{6,2},{3,7},{7,3},{8,12},{12,8},{9,1... | collective-permute-start | bytes 1572872 | tf_op jit(solution)/shard_map/ppermute | solution.py:37
  107.4 14.9 %collective-permute-start.27 = (bf16[256,256]{1,0:T(8,128)(2,1)}, bf16[256,256]{1,0:T(8,128)(2,1)S(1)}, u32[]{:S(2)}, u32[]{:S(2)}) collective-permute-start(bf16[256,256]{1,0:T(8,128)(2,1)} %get-tuple-element.147), channel_id=1, source_target_pairs={{0,1},{1,2},{2,3},{3,0},{4,5},{5,6},{6,7},{7,4},{8,9},{9,10},{10,1... | collective-permute-start | bytes 393224 | tf_op jit(solution)/shard_map/ppermute | solution.py:37
  108.1 14.2 %collective-permute-start.28 = (bf16[256,256]{1,0:T(8,128)(2,1)}, bf16[256,256]{1,0:T(8,128)(2,1)S(1)}, u32[]{:S(2)}, u32[]{:S(2)}) collective-permute-start(bf16[256,256]{1,0:T(8,128)(2,1)} %get-tuple-element.148), channel_id=1, source_target_pairs={{0,2},{1,3},{2,0},{3,1},{4,6},{5,7},{6,4},{7,5},{8,10},{9,11},{10,... | collective-permute-start | bytes 393224 | tf_op jit(solution)/shard_map/ppermute | solution.py:37
  109.3 13.0 %collective-permute-start.29 = (bf16[256,256]{1,0:T(8,128)(2,1)}, bf16[256,256]{1,0:T(8,128)(2,1)S(1)}, u32[]{:S(2)}, u32[]{:S(2)}) collective-permute-start(bf16[256,256]{1,0:T(8,128)(2,1)} %get-tuple-element.149), channel_id=1, source_target_pairs={{0,3},{1,0},{2,1},{3,2},{4,7},{5,4},{6,5},{7,6},{8,11},{9,8},{10,9... | collective-permute-start | bytes 393224 | tf_op jit(solution)/shard_map/ppermute | solution.py:37
  123.3 9.6 %collective-permute-start.32 = (bf16[256,256]{1,0:T(8,128)(2,1)S(1)}, bf16[256,256]{1,0:T(8,128)(2,1)S(1)}, u32[]{:S(2)}, u32[]{:S(2)}) collective-permute-start(bf16[256,256]{1,0:T(8,128)(2,1)S(1)} %add_convert_fusion.10.refs_0_), channel_id=1, source_target_pairs={{0,1},{1,2},{2,3},{3,0},{4,5},{5,6},{6,7},{7,4},{8,9},{9,10},{10,1... | collective-permute-start | bytes 393224 | tf_op jit(solution)/shard_map/ppermute | solution.py:37
  124.0 8.9 %collective-permute-start.33 = (bf16[256,256]{1,0:T(8,128)(2,1)S(1)}, bf16[256,256]{1,0:T(8,128)(2,1)S(1)}, u32[]{:S(2)}, u32[]{:S(2)}) collective-permute-start(bf16[256,256]{1,0:T(8,128)(2,1)S(1)} %add_convert_fusion.10.refs_0_), channel_id=1, source_target_pairs={{0,2},{1,3},{2,0},{3,1},{4,6},{5,7},{6,4},{7,5},{8,10},{9,11},{10,... | collective-permute-start | bytes 393224 | tf_op jit(solution)/shard_map/ppermute | solution.py:37
  125.4 8.1 %collective-permute-start.34 = (bf16[256,256]{1,0:T(8,128)(2,1)S(1)}, bf16[256,256]{1,0:T(8,128)(2,1)S(1)}, u32[]{:S(2)}, u32[]{:S(2)}) collective-permute-start(bf16[256,256]{1,0:T(8,128)(2,1)S(1)} %add_convert_fusion.10.refs_0_), channel_id=1, source_target_pairs={{0,3},{1,0},{2,1},{3,2},{4,7},{5,4},{6,5},{7,6},{8,11},{9,8},{10,9... | collective-permute-start | bytes 393224 | tf_op jit(solution)/shard_map/ppermute | solution.py:37
  134.2 24.7 %copy-start.39 = (bf16[256,256]{1,0:T(8,128)(2,1)S(1)}, bf16[256,256]{1,0:T(8,128)(2,1)}, u32[]{:S(2)}) copy-start(bf16[256,256]{1,0:T(8,128)(2,1)} %get-tuple-element.188) | copy-start | bytes 393220
  134.2 27.3 %copy-start.38 = (bf16[256,256]{1,0:T(8,128)(2,1)S(1)}, bf16[256,256]{1,0:T(8,128)(2,1)}, u32[]{:S(2)}) copy-start(bf16[256,256]{1,0:T(8,128)(2,1)} %get-tuple-element.189) | copy-start | bytes 393220
  134.2 29.3 %copy-start.37 = (bf16[256,256]{1,0:T(8,128)(2,1)S(1)}, bf16[256,256]{1,0:T(8,128)(2,1)}, u32[]{:S(2)}) copy-start(bf16[256,256]{1,0:T(8,128)(2,1)} %get-tuple-element.190) | copy-start | bytes 393220
  140.5 2.2 collective-permute-start.35
  144.6 14.3 %collective-permute-start.37 = (bf16[256,256]{1,0:T(8,128)(2,1)S(1)}, bf16[256,256]{1,0:T(8,128)(2,1)S(1)}, u32[]{:S(2)}, u32[]{:S(2)}) collective-permute-start(bf16[256,256]{1,0:T(8,128)(2,1)S(1)} %get-tuple-element.225), channel_id=1, source_target_pairs={{0,8},{8,16},{16,24},{24,0},{1,9},{9,17},{17,25},{25,1},{2,10},{10... | collective-permute-start | bytes 393224 | tf_op jit(solution)/shard_map/ppermute | solution.py:37
  147.2 19.9 %collective-permute-start.36 = (bf16[256,256]{1,0:T(8,128)(2,1)S(1)}, bf16[256,256]{1,0:T(8,128)(2,1)S(1)}, u32[]{:S(2)}, u32[]{:S(2)}) collective-permute-start(bf16[256,256]{1,0:T(8,128)(2,1)S(1)} %get-tuple-element.227), channel_id=1, source_target_pairs={{0,16},{8,24},{16,0},{24,8},{1,17},{9,25},{17,1},{25,9},{2,18},{10... | collective-permute-start | bytes 393224 | tf_op jit(solution)/shard_map/ppermute | solution.py:37
  154.4 12.6 %collective-permute-start.38 = (bf16[256,256]{1,0:T(8,128)(2,1)S(1)}, bf16[256,256]{1,0:T(8,128)(2,1)S(1)}, u32[]{:S(2)}, u32[]{:S(2)}) collective-permute-start(bf16[256,256]{1,0:T(8,128)(2,1)S(1)} %get-tuple-element.224), channel_id=1, source_target_pairs={{0,24},{8,0},{16,8},{24,16},{1,25},{9,1},{17,9},{25,17},{2,26},{10... | collective-permute-start | bytes 393224 | tf_op jit(solution)/shard_map/ppermute | solution.py:37
  158.9 16.7 %collective-permute-start.39 = (bf16[256,256]{1,0:T(8,128)(2,1)S(1)}, bf16[256,256]{1,0:T(8,128)(2,1)S(1)}, u32[]{:S(2)}, u32[]{:S(2)}) collective-permute-start(bf16[256,256]{1,0:T(8,128)(2,1)S(1)} %copy-done.39), channel_id=1, source_target_pairs={{0,1},{1,2},{2,3},{3,0},{4,5},{5,6},{6,7},{7,4},{8,9},{9,10},{10,1... | collective-permute-start | bytes 393224 | tf_op jit(solution)/shard_map/ppermute | solution.py:37
  161.4 14.2 %collective-permute-start.40 = (bf16[256,256]{1,0:T(8,128)(2,1)S(1)}, bf16[256,256]{1,0:T(8,128)(2,1)S(1)}, u32[]{:S(2)}, u32[]{:S(2)}) collective-permute-start(bf16[256,256]{1,0:T(8,128)(2,1)S(1)} %copy-done.38), channel_id=1, source_target_pairs={{0,2},{1,3},{2,0},{3,1},{4,6},{5,7},{6,4},{7,5},{8,10},{9,11},{10,... | collective-permute-start | bytes 393224 | tf_op jit(solution)/shard_map/ppermute | solution.py:37
  163.4 12.2 %collective-permute-start.41 = (bf16[256,256]{1,0:T(8,128)(2,1)S(1)}, bf16[256,256]{1,0:T(8,128)(2,1)S(1)}, u32[]{:S(2)}, u32[]{:S(2)}) collective-permute-start(bf16[256,256]{1,0:T(8,128)(2,1)S(1)} %copy-done.37), channel_id=1, source_target_pairs={{0,3},{1,0},{2,1},{3,2},{4,7},{5,4},{6,5},{7,6},{8,11},{9,8},{10,9... | collective-permute-start | bytes 393224 | tf_op jit(solution)/shard_map/ppermute | solution.py:37
  175.6 19.0 %copy-start.34 = (bf16[272,256]{1,0:T(8,128)(2,1)S(1)}, bf16[272,256]{1,0:T(8,128)(2,1)}, u32[]{:S(2)}) copy-start(bf16[272,256]{1,0:T(8,128)(2,1)} %get-tuple-element.206) | copy-start | bytes 417796
  175.6 2.8 %collective-permute-start.42 = (bf16[512,896]{1,0:T(8,128)(2,1)}, bf16[512,896]{1,0:T(8,128)(2,1)S(1)}, u32[]{:S(2)}, u32[]{:S(2)}) collective-permute-start(bf16[512,896]{1,0:T(8,128)(2,1)} %get-tuple-element.197), channel_id=1, source_target_pairs={{0,4},{4,0},{1,5},{5,1},{2,6},{6,2},{3,7},{7,3},{8,12},{12,8},{9,1... | collective-permute-start | bytes 2752520 | tf_op jit(solution)/shard_map/ppermute | solution.py:37
  179.7 25.4 %copy-start.19 = (bf16[272,256]{1,0:T(8,128)(2,1)S(1)}, bf16[272,256]{1,0:T(8,128)(2,1)}, u32[]{:S(2)}) copy-start(bf16[272,256]{1,0:T(8,128)(2,1)} %get-tuple-element.207) | copy-start | bytes 417796
  179.7 11.8 %collective-permute-start.43 = (bf16[128,896]{1,0:T(8,128)(2,1)S(1)}, bf16[128,896]{1,0:T(8,128)(2,1)S(1)}, u32[]{:S(2)}, u32[]{:S(2)}) collective-permute-start(bf16[128,896]{1,0:T(8,128)(2,1)S(1)} %get-tuple-element.221), channel_id=1, source_target_pairs={{0,32},{32,64},{64,96},{96,0},{1,33},{33,65},{65,97},{97,1},{2,34}... | collective-permute-start | bytes 688136 | tf_op jit(solution)/shard_map/ppermute | solution.py:37
  180.7 16.7 %collective-permute-start.44 = (bf16[128,896]{1,0:T(8,128)(2,1)S(1)}, bf16[128,896]{1,0:T(8,128)(2,1)S(1)}, u32[]{:S(2)}, u32[]{:S(2)}) collective-permute-start(bf16[128,896]{1,0:T(8,128)(2,1)S(1)} %get-tuple-element.223), channel_id=1, source_target_pairs={{0,64},{32,96},{64,0},{96,32},{1,65},{33,97},{65,1},{97,33},{2,66}... | collective-permute-start | bytes 688136 | tf_op jit(solution)/shard_map/ppermute | solution.py:37
  182.7 22.5 %copy-start.9 = (bf16[256,1,256]{2,0,1:T(8,128)(2,1)S(1)}, bf16[256,1,256]{2,0,1:T(8,128)(2,1)}, u32[]{:S(2)}) copy-start(bf16[256,1,256]{2,0,1:T(8,128)(2,1)} %param.13) | copy-start | bytes 393220
  182.7 22.5 %copy-start.10 = (f32[256,256]{1,0:T(8,128)S(1)}, f32[256,256]{1,0:T(8,128)}, u32[]{:S(2)}) copy-start(f32[256,256]{1,0:T(8,128)} %get-tuple-element.195) | copy-start | bytes 786436
  182.7 14.7 %collective-permute-start.45 = (bf16[128,896]{1,0:T(8,128)(2,1)S(1)}, bf16[128,896]{1,0:T(8,128)(2,1)S(1)}, u32[]{:S(2)}, u32[]{:S(2)}) collective-permute-start(bf16[128,896]{1,0:T(8,128)(2,1)S(1)} %get-tuple-element.222), channel_id=1, source_target_pairs={{0,96},{32,0},{64,32},{96,64},{1,97},{33,1},{65,33},{97,65},{2,98}... | collective-permute-start | bytes 688136 | tf_op jit(solution)/shard_map/ppermute | solution.py:37
  191.6 6.9 %collective-permute-start.46 = (bf16[272,256]{1,0:T(8,128)(2,1)S(1)}, bf16[272,256]{1,0:T(8,128)(2,1)S(1)}, u32[]{:S(2)}, u32[]{:S(2)}) collective-permute-start(bf16[272,256]{1,0:T(8,128)(2,1)S(1)} %copy-done.36), channel_id=1, source_target_pairs={{0,1},{1,2},{2,3},{3,0},{4,5},{5,6},{6,7},{7,4},{8,9},{9,10},{10,1... | collective-permute-start | bytes 417800 | tf_op jit(solution)/shard_map/ppermute | solution.py:37
  194.6 6.6 %collective-permute-start.47 = (bf16[272,256]{1,0:T(8,128)(2,1)S(1)}, bf16[272,256]{1,0:T(8,128)(2,1)S(1)}, u32[]{:S(2)}, u32[]{:S(2)}) collective-permute-start(bf16[272,256]{1,0:T(8,128)(2,1)S(1)} %copy-done.35), channel_id=1, source_target_pairs={{0,2},{1,3},{2,0},{3,1},{4,6},{5,7},{6,4},{7,5},{8,10},{9,11},{10,... | collective-permute-start | bytes 417800 | tf_op jit(solution)/shard_map/ppermute | solution.py:37
  194.6 6.6 %collective-permute-start.48 = (bf16[272,256]{1,0:T(8,128)(2,1)S(1)}, bf16[272,256]{1,0:T(8,128)(2,1)S(1)}, u32[]{:S(2)}, u32[]{:S(2)}) collective-permute-start(bf16[272,256]{1,0:T(8,128)(2,1)S(1)} %copy-done.34), channel_id=1, source_target_pairs={{0,3},{1,0},{2,1},{3,2},{4,7},{5,4},{6,5},{7,6},{8,11},{9,8},{10,9... | collective-permute-start | bytes 417800 | tf_op jit(solution)/shard_map/ppermute | solution.py:37
  201.8 6.0 %collective-permute-start.49 = (bf16[32,896]{1,0:T(8,128)(2,1)S(1)}, bf16[32,896]{1,0:T(8,128)(2,1)S(1)}, u32[]{:S(2)}, u32[]{:S(2)}) collective-permute-start(bf16[32,896]{1,0:T(8,128)(2,1)S(1)} %get-tuple-element.230), channel_id=1, source_target_pairs={{0,8},{8,16},{16,24},{24,0},{1,9},{9,17},{17,25},{25,1},{2,10},{10... | collective-permute-start | bytes 172040 | tf_op jit(solution)/shard_map/ppermute | solution.py:37
  201.8 6.0 %collective-permute-start.50 = (bf16[32,896]{1,0:T(8,128)(2,1)S(1)}, bf16[32,896]{1,0:T(8,128)(2,1)S(1)}, u32[]{:S(2)}, u32[]{:S(2)}) collective-permute-start(bf16[32,896]{1,0:T(8,128)(2,1)S(1)} %get-tuple-element.229), channel_id=1, source_target_pairs={{0,16},{8,24},{16,0},{24,8},{1,17},{9,25},{17,1},{25,9},{2,18},{10... | collective-permute-start | bytes 172040 | tf_op jit(solution)/shard_map/ppermute | solution.py:37
  202.2 6.5 %collective-permute-start.51 = (bf16[32,896]{1,0:T(8,128)(2,1)S(1)}, bf16[32,896]{1,0:T(8,128)(2,1)S(1)}, u32[]{:S(2)}, u32[]{:S(2)}) collective-permute-start(bf16[32,896]{1,0:T(8,128)(2,1)S(1)} %get-tuple-element.228), channel_id=1, source_target_pairs={{0,24},{8,0},{16,8},{24,16},{1,25},{9,1},{17,9},{25,17},{2,26},{10... | collective-permute-start | bytes 172040 | tf_op jit(solution)/shard_map/ppermute | solution.py:37
  210.9 6.3 %collective-permute-start.52 = (f32[32,128]{1,0:T(8,128)}, f32[32,128]{1,0:T(8,128)S(1)}, u32[]{:S(2)}, u32[]{:S(2)}) collective-permute-start(f32[32,128]{1,0:T(8,128)} %get-tuple-element.212), channel_id=1, source_target_pairs={{0,1},{1,2},{2,3},{3,0},{4,5},{5,6},{6,7},{7,4},{8,9},{9,10},{10,1... | collective-permute-start | bytes 49160 | tf_op jit(solution)/shard_map/ppermute | solution.py:37
  212.3 5.5 %collective-permute-start.53 = (f32[32,128]{1,0:T(8,128)}, f32[32,128]{1,0:T(8,128)S(1)}, u32[]{:S(2)}, u32[]{:S(2)}) collective-permute-start(f32[32,128]{1,0:T(8,128)} %get-tuple-element.212), channel_id=1, source_target_pairs={{0,2},{1,3},{2,0},{3,1},{4,6},{5,7},{6,4},{7,5},{8,10},{9,11},{10,... | collective-permute-start | bytes 49160 | tf_op jit(solution)/shard_map/ppermute | solution.py:37
  214.8 3.9 %collective-permute-start.54 = (f32[32,128]{1,0:T(8,128)}, f32[32,128]{1,0:T(8,128)S(1)}, u32[]{:S(2)}, u32[]{:S(2)}) collective-permute-start(f32[32,128]{1,0:T(8,128)} %get-tuple-element.212), channel_id=1, source_target_pairs={{0,3},{1,0},{2,1},{3,2},{4,7},{5,4},{6,5},{7,6},{8,11},{9,8},{10,9... | collective-permute-start | bytes 49160 | tf_op jit(solution)/shard_map/ppermute | solution.py:37
  (40 other events, 156.3 us)
Sparse Core Ops, SparseCore 0:
  10.3 60.3 all-gather.1
  122.5 80.6 reduce-scatter.1

commit v5 on v4

--- a/solution.py
+++ b/solution.py
@@ -29,6 +29,8 @@
 
 
 def ds(start, size):
+    if isinstance(start, int):
+        return pl.ds(start * size, size)
     return pl.ds(pl.multiple_of(start * size, size), size)
 
 
@@ -78,7 +80,8 @@
             dst[ds(other * half + i, own), :] = src[ds(row, own), :]
             return carry
 
-        lax.fori_loop(0, half, step, 0)
+        for i in range(half):
+            step(i, 0)
 
 
 def assemble(idx, n, pieces, dst, first=0):
@@ -160,7 +163,8 @@
                 w[ds(row, own), :] = src[ds(zr, own), :]
                 return carry
 
-            lax.fori_loop(0, nz, step, 0)
+            for zr in range(nz):
+                step(zr, 0)
     qkv = qc + 2 * kc
     gains[...] = w[:, qkv:].astype(f32).T[:8]
     b = base[...].astype(f32)
@@ -292,7 +296,8 @@
             out[ds(i, own), k * span : (k + 1) * span] = turned[ds(i * nc + idx[2], own), :]
             return carry
 
-        lax.fori_loop(0, nx * nz, step, 0)
+        for i in range(nx * nz):
+            step(i, 0)
 
 
 def ffn_grad_kernel(normed_rows, cot_rows, big, partner_big, out, left):
@@ -450,7 +455,8 @@
         extra[ds(i, own), :] = (lined[ds(i, own), :] + spread[...]).astype(bf16)
         return carry
 
-    lax.fori_loop(0, width // own, step, 0)
+    for i in range(width // own):
+        step(i, 0)
     store_relative(dims, idx, extra_rel, extra, own)
     a = dot(one_rel[...], qkv_gb[...]).astype(bf16)
     for out, at in ((keep, slice(0, half)), (send, slice(half, 2 * half))):
@@ -647,17 +653,18 @@
     grad_got = [shift(res[3 + k], "tensor", k) for k in range(1, n)]
     part_zero = res[3]
 
+    normed_rows = core_rows(normed_two)
+    grad_got, normed_rows = lax.optimization_barrier((grad_got, normed_rows))
     ffn_half = call(
         ffn_grad_kernel,
         [sds((width // nc, 3 * ff), bf16)],
-        [core_rows(normed_two), cot_rows, big, shift(big, "core", 1)],
+        [normed_rows, cot_rows, big, shift(big, "core", 1)],
         [pltpu.VMEM((width // nc, nc * span), bf16)],
         grid=(3,),
         in_specs=[const((width // nc, nc * span))] * 2 + [pl.BlockSpec((span, ff), lambda j: (0, j))] * 2,
         out_specs=[pl.BlockSpec((width // nc, ff), lambda j: (0, j))],
         flops=6 * span * width * ff,
     )[0]
-    grad_got, ffn_half = lax.optimization_barrier((grad_got, ffn_half))
     grad_mine = sum([g.astype(f32) for g in grad_got], part_zero.astype(f32)).astype(bf16)
     grad_parts = gathered(grad_mine, "tensor")
     down_parts = call(
@@ -673,7 +680,7 @@
         out_specs=[const((span, part))] * n,
         flops=2 * span * width * ff,
     )
-    grad_parts, down_parts = lax.optimization_barrier((grad_parts, down_parts))
+    grad_parts, ffn_half = lax.optimization_barrier((grad_parts, ffn_half))
     ffn_sum = lax.psum_scatter(ffn_half, ("dp", "z"), scatter_dimension=0, tiled=True)
 
     mine, mid, gain_two, q_gb, gq_grad, kv_keep, kv_send = call(

time: 232 us -> 233 us (level)
  waiting for transfers between devices: 46.3 us -> 55.9 us
  starting transfers between devices: 81.4 us -> 76.8 us
  Pallas kernels: 62.4 us -> 59.4 us
    ppermute x55, waiting for transfers between devices: 44.3 us -> 52.9 us  [shift(): return lax.ppermute(x, axis, [(i, (i + k) % n) for i in range(n)])]
    ppermute x55, starting transfers between devices: 81.3 us -> 76.7 us  [shift(): return lax.ppermute(x, axis, [(i, (i + k) % n) for i in range(n)])]
    pallas_call x17, Pallas kernels: 62.4 us -> 59.4 us  [call(): pl.pallas_call(kernel, out_shape=outs, in_specs=in_specs or [pl.BlockSpec...]
    unnamed x97 -> x89, local copies, waits for them, and re-layouts: 9.03 us -> 8.23 us
  transfers between devices with their start and end apart: 57 -> 57, of which waited for: 23 -> 24; matrix products, arithmetic and copies ran while one was open for 8% -> 8% of each run, Pallas kernels for 22% -> 20%
where the time goes in v5:
time: 233 us; the launch traced here: 232 us
  starting transfers between devices  76.8 us (33%)
  Pallas kernels  59.4 us (25%)
  waiting for transfers between devices  55.9 us (24%)
  other arithmetic  14.7 us (6%)
  between operations  14.5 us (6%)
  local copies, waits for them, and re-layouts  11.1 us (5%)
    ppermute x55, starting transfers between devices, shift(): return lax.ppermute(x, axis, [(i, (i + k) % n) for i in range(n)])  76.7 us
    pallas_call x17, Pallas kernels, call(): pl.pallas_call(kernel, out_shape=outs, in_specs=in_specs or [pl.BlockSpec...  59.4 us
    ppermute x55, waiting for transfers between devices, shift(): return lax.ppermute(x, axis, [(i, (i + k) % n) for i in range(n)])  52.9 us
    unnamed x89, local copies, waits for them, and re-layouts  8.23 us
  transfers between devices with their start and end apart: 57, of which 24 were waited for; matrix products, arithmetic and copies ran while one was open for 8% of the time, Pallas kernels for 20%

profile of v5, /device:TPU:0, one launch (start us, length us, event | category | flops | bytes accessed | tf_op | source)
XLA Modules:
  0.0 232.5 jit_solution(13288569387261821965)
XLA Ops:
  7.2 2.0 shard_map.228
  9.3 2.1 collective-permute-start
  11.4 3.6 %collective-permute-start.1 = (bf16[32,640]{1,0:T(8,128)(2,1)}, bf16[32,640]{1,0:T(8,128)(2,1)S(1)}, u32[]{:S(2)}, u32[]{:S(2)}) collective-permute-start(bf16[32,640]{1,0:T(8,128)(2,1)} %get-tuple-element.114), channel_id=1, source_target_pairs={{0,16},{8,24},{16,0},{24,8},{1,17},{9,25},{17,1},{25,9},{2,18},{10... | collective-permute-start | bytes 122888 | tf_op jit(solution)/shard_map/ppermute | solution.py:39
  16.0 1.6 collective-permute-start.6
  17.5 2.9 %collective-permute-start.7 = (bf16[256,512]{1,0:T(8,128)(2,1)}, bf16[256,512]{1,0:T(8,128)(2,1)S(1)}, u32[]{:S(2)}, u32[]{:S(2)}) collective-permute-start(bf16[256,512]{1,0:T(8,128)(2,1)} %get-tuple-element.116.refs_0_), channel_id=1, source_target_pairs={{0,2},{1,3},{2,0},{3,1},{4,6},{5,7},{6,4},{7,5},{8,10},{9,11},{10,... | collective-permute-start | bytes 786440 | tf_op jit(solution)/shard_map/ppermute | solution.py:39
  21.2 1.3 collective-permute-start.8
  22.6 1.6 collective-permute-start.3
  24.2 2.8 %collective-permute-start.4 = (bf16[128,640]{1,0:T(8,128)(2,1)S(1)}, bf16[128,640]{1,0:T(8,128)(2,1)S(1)}, u32[]{:S(2)}, u32[]{:S(2)}) collective-permute-start(bf16[128,640]{1,0:T(8,128)(2,1)S(1)} %constant_dynamic-update-slice_fusion.refs_4_), channel_id=1, source_target_pairs={{0,64},{32,96},{64,0},{96,32},{1,65},{33,97},{65,1},{97,33},{2,66}... | collective-permute-start | bytes 491528 | tf_op jit(solution)/shard_map/ppermute | solution.py:39
  27.0 3.8 %collective-permute-done.3.refs_5_ = bf16[128,640]{1,0:T(8,128)(2,1)S(1)} collective-permute-done((bf16[128,640]{1,0:T(8,128)(2,1)S(1)}, bf16[128,640]{1,0:T(8,128)(2,1)S(1)}, u32[]{:S(2)}, u32[]{:S(2)}) %collective-permute-start.3) | collective-permute-done | bytes 163872 | tf_op jit(solution)/shard_map/ppermute | solution.py:39
  30.8 2.9 %collective-permute-start.5 = (bf16[128,640]{1,0:T(8,128)(2,1)S(1)}, bf16[128,640]{1,0:T(8,128)(2,1)S(1)}, u32[]{:S(2)}, u32[]{:S(2)}) collective-permute-start(bf16[128,640]{1,0:T(8,128)(2,1)S(1)} %constant_dynamic-update-slice_fusion.refs_4_), channel_id=1, source_target_pairs={{0,96},{32,0},{64,32},{96,64},{1,97},{33,1},{65,33},{97,65},{2,98}... | collective-permute-start | bytes 491528 | tf_op jit(solution)/shard_map/ppermute | solution.py:39
  34.6 1.3 maximum_bitcast_fusion.refs_12_.refs_11_.refs_5_
  40.3 4.0 %shard_map.229 = (bf16[1024,640]{1,0:T(8,128)(2,1)}, bf16[256,1024]{1,0:T(8,128)(2,1)}, f32[8,1024]{1,0:T(8,128)}, bf16[128,512]{1,0:T(8,128)(2,1)}, f32[384,256...) custom-call(s32[4]{0:T(128)} %pad_add_fusion.idx, bf16[256,512]{1,0:T(8,128)(2,1)} %get-tuple-element.116.refs_0_, ...), custom_call_target="tpu_custom_call" | custom-call | flops 268435456 | bytes 5472528 | tf_op jit(solution)/shard_map/pallas_call | solution.py:57
  44.3 2.6 %collective-permute-start.13 = (bf16[256,256]{1,0:T(8,128)(2,1)}, bf16[256,256]{1,0:T(8,128)(2,1)S(1)}, u32[]{:S(2)}, u32[]{:S(2)}) collective-permute-start(bf16[256,256]{1,0:T(8,128)(2,1)} %get-tuple-element.130.refs_0_), channel_id=1, source_target_pairs={{0,8},{8,16},{16,24},{24,0},{1,9},{9,17},{17,25},{25,1},{2,10},{10... | collective-permute-start | bytes 393224 | tf_op jit(solution)/shard_map/ppermute | solution.py:39
  47.6 2.1 collective-permute-start.15
  49.7 5.0 %collective-permute-done.13.refs_1_ = bf16[256,256]{1,0:T(8,128)(2,1)S(1)} collective-permute-done((bf16[256,256]{1,0:T(8,128)(2,1)}, bf16[256,256]{1,0:T(8,128)(2,1)S(1)}, u32[]{:S(2)}, u32[]{:S(2)}) %collective-permute-start.13) | collective-permute-done | bytes 131104 | tf_op jit(solution)/shard_map/ppermute | solution.py:39
  54.7 5.2 %collective-permute-done.14.refs_2_ = bf16[256,256]{1,0:T(8,128)(2,1)S(1)} collective-permute-done((bf16[256,256]{1,0:T(8,128)(2,1)}, bf16[256,256]{1,0:T(8,128)(2,1)S(1)}, u32[]{:S(2)}, u32[]{:S(2)}) %collective-permute-start.14) | collective-permute-done | bytes 131104 | tf_op jit(solution)/shard_map/ppermute | solution.py:39
  61.0 2.1 shard_map.232.mine.cot
  64.5 3.2 %shard_map.230 = (bf16[2048,256]{1,0:T(8,128)(2,1)}, f32[128,512]{1,0:T(8,128)}, bf16[256,256]{1,0:T(8,128)(2,1)}, f32[8,512]{1,0:T(8,128)}) custom-call(s32[4]{0:T(128)} %pad_add_fusion.idx, bf16[128,512]{1,0:T(8,128)(2,1)} %get-tuple-element.129.q_t.refs_7_, bf16[256,256]{1,0:T(8,128)(2,1)} %get-tuple-element.130.refs_0_, bf16[256,256]{1,0:T(8,128)(2,1)} %copy-done.36, ...), custom_call_target="tpu_custom_call" | custom-call | flops 536870912 | bytes 2637840 | tf_op jit(solution)/shard_map/pallas_call | solution.py:57
  67.7 3.0 %all-gather.2.cloned.1.call-done.w_low.w_high.wd.refs_4_.refs_5_ = bf16[1024,3712]{1,0:T(8,128)(2,1)} async-done(((bf16[32,3712]{1,0:T(8,128)(2,1)}), bf16[1024,3712]{1,0:T(8,128)(2,1)}) %all-gather.2.cloned.1.call-update) | async-done | bytes 7602192 | tf_op jit(solution)/shard_map/all_gather | solution.py:554
  70.7 2.3 shard_map.231
  72.9 2.4 %collective-permute-start.22 = (bf16[256,256]{1,0:T(8,128)(2,1)}, bf16[256,256]{1,0:T(8,128)(2,1)S(1)}, u32[]{:S(2)}, u32[]{:S(2)}) collective-permute-start(bf16[256,256]{1,0:T(8,128)(2,1)} %get-tuple-element.136), channel_id=1, source_target_pairs={{0,3},{1,0},{2,1},{3,2},{4,7},{5,4},{6,5},{7,6},{8,11},{9,8},{10,9... | collective-permute-start | bytes 393224 | tf_op jit(solution)/shard_map/ppermute | solution.py:39
  77.1 4.5 %collective-permute-done.22 = bf16[256,256]{1,0:T(8,128)(2,1)S(1)} collective-permute-done((bf16[256,256]{1,0:T(8,128)(2,1)}, bf16[256,256]{1,0:T(8,128)(2,1)S(1)}, u32[]{:S(2)}, u32[]{:S(2)}) %collective-permute-start.22) | collective-permute-done | bytes 131104 | tf_op jit(solution)/shard_map/ppermute | solution.py:39
  81.7 1.7 collective-permute-done.21
  83.4 1.8 collective-permute-done.20
  86.3 2.0 collective-permute-start.24
  88.3 1.7 collective-permute-start.25
  90.9 2.4 %shard_map.233.cot_rows = bf16[512,512]{1,0:T(8,128)(2,1)} custom-call(s32[4]{0:T(128)} %pad_add_fusion.idx, bf16[256,1024]{1,0:T(8,128)(2,1)} %shard_map.232.mine.cot, bf16[256,1024]{1,0:T(8,128)(2,1)} %copy-done.7), custom_call_target="tpu_custom_call" | custom-call | bytes 1572880 | tf_op jit(solution)/shard_map/pallas_call | solution.py:57
  93.3 4.2 %shard_map.234.refs_6_ = f32[256,1152]{1,0:T(8,128)} custom-call(bf16[256,1024]{1,0:T(8,128)(2,1)} %shard_map.232.mine.cot, bf16[1024,3712]{1,0:T(8,128)(2,1)} %all-gather.2.cloned.1.call-done.w_low.w_high.wd.refs_4_.refs_5_), custom_call_target="tpu_custom_call" | custom-call | flops 603979776 | bytes 9306112 | tf_op jit(solution)/shard_map/pallas_call | solution.py:57
  98.2 8.5 %shard_map.235 = (f32[256,1024]{1,0:T(8,128)}, bf16[256,1024]{1,0:T(8,128)(2,1)}, bf16[256,3456]{1,0:T(8,128)(2,1)}, bf16[256,256]{1,0:T(8,128)(2,1)}, bf16[256,...) custom-call(s32[4]{0:T(128)} %pad_add_fusion.idx, ...), custom_call_target="tpu_custom_call" | custom-call | flops 2415919104 | bytes 21331984 | tf_op jit(solution)/shard_map/pallas_call | solution.py:57
  107.6 2.5 %collective-permute-start.28 = (bf16[256,256]{1,0:T(8,128)(2,1)}, bf16[256,256]{1,0:T(8,128)(2,1)S(1)}, u32[]{:S(2)}, u32[]{:S(2)}) collective-permute-start(bf16[256,256]{1,0:T(8,128)(2,1)} %get-tuple-element.145), channel_id=1, source_target_pairs={{0,2},{1,3},{2,0},{3,1},{4,6},{5,7},{6,4},{7,5},{8,10},{9,11},{10,... | collective-permute-start | bytes 393224 | tf_op jit(solution)/shard_map/ppermute | solution.py:39
  110.1 2.2 collective-permute-start.29
  113.2 2.4 %shard_map.236.normed_rows = bf16[512,512]{1,0:T(8,128)(2,1)} custom-call(s32[4]{0:T(128)} %pad_add_fusion.idx, bf16[256,1024]{1,0:T(8,128)(2,1)} %get-tuple-element.147.mine, bf16[256,1024]{1,0:T(8,128)(2,1)} %copy-done.8), custom_call_target="tpu_custom_call" | custom-call | bytes 1572880 | tf_op jit(solution)/shard_map/pallas_call | solution.py:57
  115.5 1.5 collective-permute-done.27
  118.6 1.8 collective-permute-start.31
  120.4 2.4 %collective-permute-start.32 = (bf16[256,256]{1,0:T(8,128)(2,1)S(1)}, bf16[256,256]{1,0:T(8,128)(2,1)S(1)}, u32[]{:S(2)}, u32[]{:S(2)}) collective-permute-start(bf16[256,256]{1,0:T(8,128)(2,1)S(1)} %add_convert_fusion.10.refs_0_), channel_id=1, source_target_pairs={{0,2},{1,3},{2,0},{3,1},{4,6},{5,7},{6,4},{7,5},{8,10},{9,11},{10,... | collective-permute-start | bytes 393224 | tf_op jit(solution)/shard_map/ppermute | solution.py:39
  123.7 1.2 copy-done.1
  125.0 6.1 %shard_map.237 = bf16[512,3456]{1,0:T(8,128)(2,1)} custom-call(bf16[512,512]{1,0:T(8,128)(2,1)} %shard_map.236.normed_rows, bf16[512,512]{1,0:T(8,128)(2,1)} %shard_map.233.cot_rows, bf16[256,3456]{1,0:T(8,128)(2,1)} %get-tuple-element.153.big.hidden, bf16[256,3456]{1,0:T(8,128)(2,1)} %copy-done.1), custom_call_target="tpu_custom_call" | custom-call | flops 1811939328 | bytes 8126464 | tf_op jit(solution)/shard_map/pallas_call | solution.py:57
  131.8 6.3 %shard_map.238 = (f32[256,256]{1,0:T(8,128)}, bf16[256,1024]{1,0:T(8,128)(2,1)}, f32[8,1024]{1,0:T(8,128)}, bf16[256,256]{1,0:T(8,128)(2,1)}, f32[64,1]{1,0:T(8,...) custom-call(s32[4]{0:T(128)} %pad_add_fusion.idx, f32[256,1024]{1,0:T(8,128)} %get-tuple-element.141.middle, ...), custom_call_target="tpu_custom_call" | custom-call | flops 1342177280 | bytes 21250576 | tf_op jit(solution)/shard_map/pallas_call | solution.py:57
  138.2 2.1 collective-permute-done.35
  140.3 1.9 add_convert_fusion.6
  142.2 2.6 %collective-permute-start.37 = (bf16[256,256]{1,0:T(8,128)(2,1)S(1)}, bf16[256,256]{1,0:T(8,128)(2,1)S(1)}, u32[]{:S(2)}, u32[]{:S(2)}) collective-permute-start(bf16[256,256]{1,0:T(8,128)(2,1)S(1)} %get-tuple-element.219), channel_id=1, source_target_pairs={{0,8},{8,16},{16,24},{24,0},{1,9},{9,17},{17,25},{25,1},{2,10},{10... | collective-permute-start | bytes 393224 | tf_op jit(solution)/shard_map/ppermute | solution.py:39
  144.8 6.1 %collective-permute-start.36 = (bf16[256,256]{1,0:T(8,128)(2,1)S(1)}, bf16[256,256]{1,0:T(8,128)(2,1)S(1)}, u32[]{:S(2)}, u32[]{:S(2)}) collective-permute-start(bf16[256,256]{1,0:T(8,128)(2,1)S(1)} %get-tuple-element.221), channel_id=1, source_target_pairs={{0,16},{8,24},{16,0},{24,8},{1,17},{9,25},{17,1},{25,9},{2,18},{10... | collective-permute-start | bytes 393224 | tf_op jit(solution)/shard_map/ppermute | solution.py:39
  150.9 3.6 %shard_map.240 = (bf16[256,256]{1,0:T(8,128)(2,1)}, bf16[256,256]{1,0:T(8,128)(2,1)}, bf16[256,256]{1,0:T(8,128)(2,1)}, bf16[256,256]{1,0:T(8,128)(2,1)}) custom-call(s32[4]{0:T(128)} %pad_add_fusion.idx, bf16[256,3456]{1,0:T(8,128)(2,1)} %get-tuple-element.153.big.hidden, bf16[1024,3712]{1,0:T(8,128)(2,1)} %all-gather.2.cloned.1.call-done.w_low.w_high.wd.refs_4_.refs_5_), custom_call_target="tpu_custom_call" | custom-call | flops 603979776 | bytes 9895952 | tf_op jit(solution)/shard_map/pallas_call | solution.py:57
  154.5 1.7 collective-permute-start.39
  157.0 2.0 collective-permute-start.41
  159.0 2.3 shard_map.239.out_rel
  162.0 3.7 %shard_map.241 = (bf16[256,512]{1,0:T(8,128)(2,1)}, f32[8,1024]{1,0:T(8,128)}, f32[64,1]{1,0:T(8,128)}, bf16[272,256]{1,0:T(8,128)(2,1)}, bf16[272,256]{1,0:T(8,...) custom-call(s32[4]{0:T(128)} %pad_add_fusion.idx, bf16[256,256]{1,0:T(8,128)(2,1)} %get-tuple-element.220.refs_0_, ...), custom_call_target="tpu_custom_call" | custom-call | flops 268435456 | bytes 3834384 | tf_op jit(solution)/shard_map/pallas_call | solution.py:57
  165.7 3.1 %shard_map.242 = (bf16[512,896]{1,0:T(8,128)(2,1)}, bf16[512,896]{1,0:T(8,128)(2,1)}) custom-call(s32[4]{0:T(128)} %pad_add_fusion.idx, bf16[1024,256]{1,0:T(8,128)(2,1)} %get-tuple-element.142.one_rel, bf16[1024,256]{1,0:T(8,128)(2,1)} %shard_map.239.out_rel, bf16[256,512]{1,0:T(8,128)(2,1)} %get-tuple-element.174.qkv_gb, ...), custom_call_target="tpu_custom_call" | custom-call | flops 402653184 | bytes 3211792 | tf_op jit(solution)/shard_map/pallas_call | solution.py:57
  170.0 1.7 collective-permute-done.42
  171.7 1.3 add_convert_fusion.3
  173.0 3.2 %collective-permute-start.45 = (bf16[128,896]{1,0:T(8,128)(2,1)S(1)}, bf16[128,896]{1,0:T(8,128)(2,1)S(1)}, u32[]{:S(2)}, u32[]{:S(2)}) collective-permute-start(bf16[128,896]{1,0:T(8,128)(2,1)S(1)} %get-tuple-element.216), channel_id=1, source_target_pairs={{0,96},{32,0},{64,32},{96,64},{1,97},{33,1},{65,33},{97,65},{2,98}... | collective-permute-start | bytes 688136 | tf_op jit(solution)/shard_map/ppermute | solution.py:39
  177.1 1.3 collective-permute-start.43
  178.3 1.7 fusion.4
  180.0 11.2 %collective-permute-done.43 = bf16[128,896]{1,0:T(8,128)(2,1)S(1)} collective-permute-done((bf16[128,896]{1,0:T(8,128)(2,1)S(1)}, bf16[128,896]{1,0:T(8,128)(2,1)S(1)}, u32[]{:S(2)}, u32[]{:S(2)}) %collective-permute-start.43) | collective-permute-done | bytes 229408 | tf_op jit(solution)/shard_map/ppermute | solution.py:39
  191.4 3.0 %collective-permute-start.47 = (bf16[272,256]{1,0:T(8,128)(2,1)S(1)}, bf16[272,256]{1,0:T(8,128)(2,1)S(1)}, u32[]{:S(2)}, u32[]{:S(2)}) collective-permute-start(bf16[272,256]{1,0:T(8,128)(2,1)S(1)} %copy-done.34), channel_id=1, source_target_pairs={{0,2},{1,3},{2,0},{3,1},{4,6},{5,7},{6,4},{7,5},{8,10},{9,11},{10,... | collective-permute-start | bytes 417800 | tf_op jit(solution)/shard_map/ppermute | solution.py:39
  194.4 1.6 collective-permute-start.48
  197.1 3.8 %collective-permute-done.46 = bf16[272,256]{1,0:T(8,128)(2,1)S(1)} collective-permute-done((bf16[272,256]{1,0:T(8,128)(2,1)S(1)}, bf16[272,256]{1,0:T(8,128)(2,1)S(1)}, u32[]{:S(2)}, u32[]{:S(2)}) %collective-permute-start.46) | collective-permute-done | bytes 139296 | tf_op jit(solution)/shard_map/ppermute | solution.py:39
  203.3 2.4 %collective-permute-start.50 = (bf16[32,896]{1,0:T(8,128)(2,1)S(1)}, bf16[32,896]{1,0:T(8,128)(2,1)S(1)}, u32[]{:S(2)}, u32[]{:S(2)}) collective-permute-start(bf16[32,896]{1,0:T(8,128)(2,1)S(1)} %get-tuple-element.223), channel_id=1, source_target_pairs={{0,16},{8,24},{16,0},{24,8},{1,17},{9,25},{17,1},{25,9},{2,18},{10... | collective-permute-start | bytes 172040 | tf_op jit(solution)/shard_map/ppermute | solution.py:39
  207.8 1.6 collective-permute-done.50.refs_2_
  210.6 1.5 shard_map.243
  212.1 2.9 %collective-permute-start.54 = (f32[32,128]{1,0:T(8,128)}, f32[32,128]{1,0:T(8,128)S(1)}, u32[]{:S(2)}, u32[]{:S(2)}) collective-permute-start(f32[32,128]{1,0:T(8,128)} %get-tuple-element.206), channel_id=1, source_target_pairs={{0,3},{1,0},{2,1},{3,2},{4,7},{5,4},{6,5},{7,6},{8,11},{9,8},{10,9... | collective-permute-start | bytes 49160 | tf_op jit(solution)/shard_map/ppermute | solution.py:39
  216.0 1.5 add_reduce_fusion
  217.5 3.0 %collective-permute-done.53 = f32[32,128]{1,0:T(8,128)S(1)} collective-permute-done((f32[32,128]{1,0:T(8,128)}, f32[32,128]{1,0:T(8,128)S(1)}, u32[]{:S(2)}, u32[]{:S(2)}) %collective-permute-start.53) | collective-permute-done | bytes 16416 | tf_op jit(solution)/shard_map/ppermute | solution.py:39
  223.9 1.7 shard_map.244
  (186 shorter events, 34.1 us)
Async XLA Ops:
  7.2 63.5 %all-gather.2.cloned.1.call-start = ((), (), s32[]{:S(2)}) async-start(), calls=%async_computation.1 | async-start | bytes 7839744 | tf_op jit(solution)/shard_map/all_gather | solution.py:554
  9.3 214.7 %reduce-scatter.2.cloned.1.call-start = ((), (), s32[]{:S(2)}) async-start(), calls=%async_computation.2 | async-start | bytes 3760128 | tf_op jit(solution)/shard_map/reduce_scatter | solution.py:684
  9.3 11.9 %collective-permute-start = (bf16[32,640]{1,0:T(8,128)(2,1)}, bf16[32,640]{1,0:T(8,128)(2,1)S(1)}, u32[]{:S(2)}, u32[]{:S(2)}) collective-permute-start(bf16[32,640]{1,0:T(8,128)(2,1)} %get-tuple-element.114), channel_id=1, source_target_pairs={{0,8},{8,16},{16,24},{24,0},{1,9},{9,17},{17,25},{25,1},{2,10},{10... | collective-permute-start | bytes 122888 | tf_op jit(solution)/shard_map/ppermute | solution.py:39
  11.4 11.2 %collective-permute-start.1 = (bf16[32,640]{1,0:T(8,128)(2,1)}, bf16[32,640]{1,0:T(8,128)(2,1)S(1)}, u32[]{:S(2)}, u32[]{:S(2)}) collective-permute-start(bf16[32,640]{1,0:T(8,128)(2,1)} %get-tuple-element.114), channel_id=1, source_target_pairs={{0,16},{8,24},{16,0},{24,8},{1,17},{9,25},{17,1},{25,9},{2,18},{10... | collective-permute-start | bytes 122888 | tf_op jit(solution)/shard_map/ppermute | solution.py:39
  15.0 7.7 %collective-permute-start.2 = (bf16[32,640]{1,0:T(8,128)(2,1)}, bf16[32,640]{1,0:T(8,128)(2,1)S(1)}, u32[]{:S(2)}, u32[]{:S(2)}) collective-permute-start(bf16[32,640]{1,0:T(8,128)(2,1)} %get-tuple-element.114), channel_id=1, source_target_pairs={{0,24},{8,0},{16,8},{24,16},{1,25},{9,1},{17,9},{25,17},{2,26},{10... | collective-permute-start | bytes 122888 | tf_op jit(solution)/shard_map/ppermute | solution.py:39
  16.0 21.0 %collective-permute-start.6 = (bf16[256,512]{1,0:T(8,128)(2,1)}, bf16[256,512]{1,0:T(8,128)(2,1)S(1)}, u32[]{:S(2)}, u32[]{:S(2)}) collective-permute-start(bf16[256,512]{1,0:T(8,128)(2,1)} %get-tuple-element.116.refs_0_), channel_id=1, source_target_pairs={{0,1},{1,2},{2,3},{3,0},{4,5},{5,6},{6,7},{7,4},{8,9},{9,10},{10,1... | collective-permute-start | bytes 786440 | tf_op jit(solution)/shard_map/ppermute | solution.py:39
  17.5 19.4 %collective-permute-start.7 = (bf16[256,512]{1,0:T(8,128)(2,1)}, bf16[256,512]{1,0:T(8,128)(2,1)S(1)}, u32[]{:S(2)}, u32[]{:S(2)}) collective-permute-start(bf16[256,512]{1,0:T(8,128)(2,1)} %get-tuple-element.116.refs_0_), channel_id=1, source_target_pairs={{0,2},{1,3},{2,0},{3,1},{4,6},{5,7},{6,4},{7,5},{8,10},{9,11},{10,... | collective-permute-start | bytes 786440 | tf_op jit(solution)/shard_map/ppermute | solution.py:39
  21.2 15.7 %collective-permute-start.8 = (bf16[256,512]{1,0:T(8,128)(2,1)}, bf16[256,512]{1,0:T(8,128)(2,1)S(1)}, u32[]{:S(2)}, u32[]{:S(2)}) collective-permute-start(bf16[256,512]{1,0:T(8,128)(2,1)} %get-tuple-element.116.refs_0_), channel_id=1, source_target_pairs={{0,3},{1,0},{2,1},{3,2},{4,7},{5,4},{6,5},{7,6},{8,11},{9,8},{10,9... | collective-permute-start | bytes 786440 | tf_op jit(solution)/shard_map/ppermute | solution.py:39
  22.6 16.6 %copy-start.11 = (bf16[128,640]{1,0:T(8,128)(2,1)}, bf16[128,640]{1,0:T(8,128)(2,1)S(1)}, u32[]{:S(2)}) copy-start(bf16[128,640]{1,0:T(8,128)(2,1)S(1)} %constant_dynamic-update-slice_fusion.refs_4_) | copy-start | bytes 491524
  22.6 8.2 %collective-permute-start.3 = (bf16[128,640]{1,0:T(8,128)(2,1)S(1)}, bf16[128,640]{1,0:T(8,128)(2,1)S(1)}, u32[]{:S(2)}, u32[]{:S(2)}) collective-permute-start(bf16[128,640]{1,0:T(8,128)(2,1)S(1)} %constant_dynamic-update-slice_fusion.refs_4_), channel_id=1, source_target_pairs={{0,32},{32,64},{64,96},{96,0},{1,33},{33,65},{65,97},{97,1},{2,34}... | collective-permute-start | bytes 491528 | tf_op jit(solution)/shard_map/ppermute | solution.py:39
  24.2 11.9 %collective-permute-start.4 = (bf16[128,640]{1,0:T(8,128)(2,1)S(1)}, bf16[128,640]{1,0:T(8,128)(2,1)S(1)}, u32[]{:S(2)}, u32[]{:S(2)}) collective-permute-start(bf16[128,640]{1,0:T(8,128)(2,1)S(1)} %constant_dynamic-update-slice_fusion.refs_4_), channel_id=1, source_target_pairs={{0,64},{32,96},{64,0},{96,32},{1,65},{33,97},{65,1},{97,33},{2,66}... | collective-permute-start | bytes 491528 | tf_op jit(solution)/shard_map/ppermute | solution.py:39
  30.8 6.1 %collective-permute-start.5 = (bf16[128,640]{1,0:T(8,128)(2,1)S(1)}, bf16[128,640]{1,0:T(8,128)(2,1)S(1)}, u32[]{:S(2)}, u32[]{:S(2)}) collective-permute-start(bf16[128,640]{1,0:T(8,128)(2,1)S(1)} %constant_dynamic-update-slice_fusion.refs_4_), channel_id=1, source_target_pairs={{0,96},{32,0},{64,32},{96,64},{1,97},{33,1},{65,33},{97,65},{2,98}... | collective-permute-start | bytes 491528 | tf_op jit(solution)/shard_map/ppermute | solution.py:39
  37.0 1.7 collective-permute-start.9
  37.1 1.6 collective-permute-start.10
  37.6 1.4 collective-permute-start.11
  37.7 1.5 collective-permute-start.12
  44.3 10.4 %collective-permute-start.13 = (bf16[256,256]{1,0:T(8,128)(2,1)}, bf16[256,256]{1,0:T(8,128)(2,1)S(1)}, u32[]{:S(2)}, u32[]{:S(2)}) collective-permute-start(bf16[256,256]{1,0:T(8,128)(2,1)} %get-tuple-element.130.refs_0_), channel_id=1, source_target_pairs={{0,8},{8,16},{16,24},{24,0},{1,9},{9,17},{17,25},{25,1},{2,10},{10... | collective-permute-start | bytes 393224 | tf_op jit(solution)/shard_map/ppermute | solution.py:39
  46.9 13.0 %collective-permute-start.14 = (bf16[256,256]{1,0:T(8,128)(2,1)}, bf16[256,256]{1,0:T(8,128)(2,1)S(1)}, u32[]{:S(2)}, u32[]{:S(2)}) collective-permute-start(bf16[256,256]{1,0:T(8,128)(2,1)} %get-tuple-element.130.refs_0_), channel_id=1, source_target_pairs={{0,16},{8,24},{16,0},{24,8},{1,17},{9,25},{17,1},{25,9},{2,18},{10... | collective-permute-start | bytes 393224 | tf_op jit(solution)/shard_map/ppermute | solution.py:39
  47.6 13.5 %collective-permute-start.15 = (bf16[256,256]{1,0:T(8,128)(2,1)}, bf16[256,256]{1,0:T(8,128)(2,1)S(1)}, u32[]{:S(2)}, u32[]{:S(2)}) collective-permute-start(bf16[256,256]{1,0:T(8,128)(2,1)} %get-tuple-element.130.refs_0_), channel_id=1, source_target_pairs={{0,24},{8,0},{16,8},{24,16},{1,25},{9,1},{17,9},{25,17},{2,26},{10... | collective-permute-start | bytes 393224 | tf_op jit(solution)/shard_map/ppermute | solution.py:39
  49.7 13.9 %collective-permute-start.16 = (bf16[256,256]{1,0:T(8,128)(2,1)}, bf16[256,256]{1,0:T(8,128)(2,1)S(1)}, u32[]{:S(2)}, u32[]{:S(2)}) collective-permute-start(bf16[256,256]{1,0:T(8,128)(2,1)} %get-tuple-element.130.refs_0_), channel_id=1, source_target_pairs={{0,4},{4,0},{1,5},{5,1},{2,6},{6,2},{3,7},{7,3},{8,12},{12,8},{9,1... | collective-permute-start | bytes 393224 | tf_op jit(solution)/shard_map/ppermute | solution.py:39
  54.7 8.9 %collective-permute-start.17 = (bf16[256,256]{1,0:T(8,128)(2,1)S(1)}, bf16[256,256]{1,0:T(8,128)(2,1)S(1)}, u32[]{:S(2)}, u32[]{:S(2)}) collective-permute-start(bf16[256,256]{1,0:T(8,128)(2,1)S(1)} %collective-permute-done.13.refs_1_), channel_id=1, source_target_pairs={{0,4},{4,0},{1,5},{5,1},{2,6},{6,2},{3,7},{7,3},{8,12},{12,8},{9,1... | collective-permute-start | bytes 393224 | tf_op jit(solution)/shard_map/ppermute | solution.py:39
  60.0 3.7 %collective-permute-start.18 = (bf16[256,256]{1,0:T(8,128)(2,1)S(1)}, bf16[256,256]{1,0:T(8,128)(2,1)S(1)}, u32[]{:S(2)}, u32[]{:S(2)}) collective-permute-start(bf16[256,256]{1,0:T(8,128)(2,1)S(1)} %collective-permute-done.14.refs_2_), channel_id=1, source_target_pairs={{0,4},{4,0},{1,5},{5,1},{2,6},{6,2},{3,7},{7,3},{8,12},{12,8},{9,1... | collective-permute-start | bytes 393224 | tf_op jit(solution)/shard_map/ppermute | solution.py:39
  61.0 2.7 %collective-permute-start.19 = (bf16[256,256]{1,0:T(8,128)(2,1)S(1)}, bf16[256,256]{1,0:T(8,128)(2,1)S(1)}, u32[]{:S(2)}, u32[]{:S(2)}) collective-permute-start(bf16[256,256]{1,0:T(8,128)(2,1)S(1)} %collective-permute-done.15.refs_3_), channel_id=1, source_target_pairs={{0,4},{4,0},{1,5},{5,1},{2,6},{6,2},{3,7},{7,3},{8,12},{12,8},{9,1... | collective-permute-start | bytes 393224 | tf_op jit(solution)/shard_map/ppermute | solution.py:39
  63.1 26.9 %collective-permute-start.26 = (bf16[256,1024]{1,0:T(8,128)(2,1)}, bf16[256,1024]{1,0:T(8,128)(2,1)S(1)}, u32[]{:S(2)}, u32[]{:S(2)}) collective-permute-start(bf16[256,1024]{1,0:T(8,128)(2,1)} %shard_map.232.mine.cot), channel_id=1, source_target_pairs={{0,4},{4,0},{1,5},{5,1},{2,6},{6,2},{3,7},{7,3},{8,12},{12,8},{9,1... | collective-permute-start | bytes 1572872 | tf_op jit(solution)/shard_map/ppermute | solution.py:39
  72.9 8.8 %collective-permute-start.22 = (bf16[256,256]{1,0:T(8,128)(2,1)}, bf16[256,256]{1,0:T(8,128)(2,1)S(1)}, u32[]{:S(2)}, u32[]{:S(2)}) collective-permute-start(bf16[256,256]{1,0:T(8,128)(2,1)} %get-tuple-element.136), channel_id=1, source_target_pairs={{0,3},{1,0},{2,1},{3,2},{4,7},{5,4},{6,5},{7,6},{8,11},{9,8},{10,9... | collective-permute-start | bytes 393224 | tf_op jit(solution)/shard_map/ppermute | solution.py:39
  75.3 8.1 %collective-permute-start.21 = (bf16[256,256]{1,0:T(8,128)(2,1)}, bf16[256,256]{1,0:T(8,128)(2,1)S(1)}, u32[]{:S(2)}, u32[]{:S(2)}) collective-permute-start(bf16[256,256]{1,0:T(8,128)(2,1)} %get-tuple-element.135), channel_id=1, source_target_pairs={{0,2},{1,3},{2,0},{3,1},{4,6},{5,7},{6,4},{7,5},{8,10},{9,11},{10,... | collective-permute-start | bytes 393224 | tf_op jit(solution)/shard_map/ppermute | solution.py:39
  76.5 8.8 %collective-permute-start.20 = (bf16[256,256]{1,0:T(8,128)(2,1)}, bf16[256,256]{1,0:T(8,128)(2,1)S(1)}, u32[]{:S(2)}, u32[]{:S(2)}) collective-permute-start(bf16[256,256]{1,0:T(8,128)(2,1)} %get-tuple-element.134), channel_id=1, source_target_pairs={{0,1},{1,2},{2,3},{3,0},{4,5},{5,6},{6,7},{7,4},{8,9},{9,10},{10,1... | collective-permute-start | bytes 393224 | tf_op jit(solution)/shard_map/ppermute | solution.py:39
  86.2 11.3 %collective-permute-start.23 = (bf16[256,256]{1,0:T(8,128)(2,1)S(1)}, bf16[256,256]{1,0:T(8,128)(2,1)S(1)}, u32[]{:S(2)}, u32[]{:S(2)}) collective-permute-start(bf16[256,256]{1,0:T(8,128)(2,1)S(1)} %add_convert_fusion.11.refs_0_), channel_id=1, source_target_pairs={{0,1},{1,2},{2,3},{3,0},{4,5},{5,6},{6,7},{7,4},{8,9},{9,10},{10,1... | collective-permute-start | bytes 393224 | tf_op jit(solution)/shard_map/ppermute | solution.py:39
  86.3 11.2 %collective-permute-start.24 = (bf16[256,256]{1,0:T(8,128)(2,1)S(1)}, bf16[256,256]{1,0:T(8,128)(2,1)S(1)}, u32[]{:S(2)}, u32[]{:S(2)}) collective-permute-start(bf16[256,256]{1,0:T(8,128)(2,1)S(1)} %add_convert_fusion.11.refs_0_), channel_id=1, source_target_pairs={{0,2},{1,3},{2,0},{3,1},{4,6},{5,7},{6,4},{7,5},{8,10},{9,11},{10,... | collective-permute-start | bytes 393224 | tf_op jit(solution)/shard_map/ppermute | solution.py:39
  88.3 9.2 %collective-permute-start.25 = (bf16[256,256]{1,0:T(8,128)(2,1)S(1)}, bf16[256,256]{1,0:T(8,128)(2,1)S(1)}, u32[]{:S(2)}, u32[]{:S(2)}) collective-permute-start(bf16[256,256]{1,0:T(8,128)(2,1)S(1)} %add_convert_fusion.11.refs_0_), channel_id=1, source_target_pairs={{0,3},{1,0},{2,1},{3,2},{4,7},{5,4},{6,5},{7,6},{8,11},{9,8},{10,9... | collective-permute-start | bytes 393224 | tf_op jit(solution)/shard_map/ppermute | solution.py:39
  106.7 17.0 %collective-permute-start.34 = (bf16[256,3456]{1,0:T(8,128)(2,1)}, bf16[256,3456]{1,0:T(8,128)(2,1)S(1)}, u32[]{:S(2)}, u32[]{:S(2)}) collective-permute-start(bf16[256,3456]{1,0:T(8,128)(2,1)} %get-tuple-element.153.big.hidden), channel_id=1, source_target_pairs={{0,4},{4,0},{1,5},{5,1},{2,6},{6,2},{3,7},{7,3},{8,12},{12,8},{9,1... | collective-permute-start | bytes 5308424 | tf_op jit(solution)/shard_map/ppermute | solution.py:39
  106.8 5.5 %collective-permute-start.30 = (bf16[256,1024]{1,0:T(8,128)(2,1)}, bf16[256,1024]{1,0:T(8,128)(2,1)S(1)}, u32[]{:S(2)}, u32[]{:S(2)}) collective-permute-start(bf16[256,1024]{1,0:T(8,128)(2,1)} %get-tuple-element.147.mine), channel_id=1, source_target_pairs={{0,4},{4,0},{1,5},{5,1},{2,6},{6,2},{3,7},{7,3},{8,12},{12,8},{9,1... | collective-permute-start | bytes 1572872 | tf_op jit(solution)/shard_map/ppermute | solution.py:39
  107.3 9.7 %collective-permute-start.27 = (bf16[256,256]{1,0:T(8,128)(2,1)}, bf16[256,256]{1,0:T(8,128)(2,1)S(1)}, u32[]{:S(2)}, u32[]{:S(2)}) collective-permute-start(bf16[256,256]{1,0:T(8,128)(2,1)} %get-tuple-element.144), channel_id=1, source_target_pairs={{0,1},{1,2},{2,3},{3,0},{4,5},{5,6},{6,7},{7,4},{8,9},{9,10},{10,1... | collective-permute-start | bytes 393224 | tf_op jit(solution)/shard_map/ppermute | solution.py:39
  107.6 9.4 %collective-permute-start.28 = (bf16[256,256]{1,0:T(8,128)(2,1)}, bf16[256,256]{1,0:T(8,128)(2,1)S(1)}, u32[]{:S(2)}, u32[]{:S(2)}) collective-permute-start(bf16[256,256]{1,0:T(8,128)(2,1)} %get-tuple-element.145), channel_id=1, source_target_pairs={{0,2},{1,3},{2,0},{3,1},{4,6},{5,7},{6,4},{7,5},{8,10},{9,11},{10,... | collective-permute-start | bytes 393224 | tf_op jit(solution)/shard_map/ppermute | solution.py:39
  110.1 7.5 %collective-permute-start.29 = (bf16[256,256]{1,0:T(8,128)(2,1)}, bf16[256,256]{1,0:T(8,128)(2,1)S(1)}, u32[]{:S(2)}, u32[]{:S(2)}) collective-permute-start(bf16[256,256]{1,0:T(8,128)(2,1)} %get-tuple-element.146), channel_id=1, source_target_pairs={{0,3},{1,0},{2,1},{3,2},{4,7},{5,4},{6,5},{7,6},{8,11},{9,8},{10,9... | collective-permute-start | bytes 393224 | tf_op jit(solution)/shard_map/ppermute | solution.py:39
  118.6 12.5 %collective-permute-start.31 = (bf16[256,256]{1,0:T(8,128)(2,1)S(1)}, bf16[256,256]{1,0:T(8,128)(2,1)S(1)}, u32[]{:S(2)}, u32[]{:S(2)}) collective-permute-start(bf16[256,256]{1,0:T(8,128)(2,1)S(1)} %add_convert_fusion.10.refs_0_), channel_id=1, source_target_pairs={{0,1},{1,2},{2,3},{3,0},{4,5},{5,6},{6,7},{7,4},{8,9},{9,10},{10,1... | collective-permute-start | bytes 393224 | tf_op jit(solution)/shard_map/ppermute | solution.py:39
  120.4 10.7 %collective-permute-start.32 = (bf16[256,256]{1,0:T(8,128)(2,1)S(1)}, bf16[256,256]{1,0:T(8,128)(2,1)S(1)}, u32[]{:S(2)}, u32[]{:S(2)}) collective-permute-start(bf16[256,256]{1,0:T(8,128)(2,1)S(1)} %add_convert_fusion.10.refs_0_), channel_id=1, source_target_pairs={{0,2},{1,3},{2,0},{3,1},{4,6},{5,7},{6,4},{7,5},{8,10},{9,11},{10,... | collective-permute-start | bytes 393224 | tf_op jit(solution)/shard_map/ppermute | solution.py:39
  122.8 8.3 %collective-permute-start.33 = (bf16[256,256]{1,0:T(8,128)(2,1)S(1)}, bf16[256,256]{1,0:T(8,128)(2,1)S(1)}, u32[]{:S(2)}, u32[]{:S(2)}) collective-permute-start(bf16[256,256]{1,0:T(8,128)(2,1)S(1)} %add_convert_fusion.10.refs_0_), channel_id=1, source_target_pairs={{0,3},{1,0},{2,1},{3,2},{4,7},{5,4},{6,5},{7,6},{8,11},{9,8},{10,9... | collective-permute-start | bytes 393224 | tf_op jit(solution)/shard_map/ppermute | solution.py:39
  138.1 2.2 collective-permute-start.35
  142.2 12.3 %collective-permute-start.37 = (bf16[256,256]{1,0:T(8,128)(2,1)S(1)}, bf16[256,256]{1,0:T(8,128)(2,1)S(1)}, u32[]{:S(2)}, u32[]{:S(2)}) collective-permute-start(bf16[256,256]{1,0:T(8,128)(2,1)S(1)} %get-tuple-element.219), channel_id=1, source_target_pairs={{0,8},{8,16},{16,24},{24,0},{1,9},{9,17},{17,25},{25,1},{2,10},{10... | collective-permute-start | bytes 393224 | tf_op jit(solution)/shard_map/ppermute | solution.py:39
  144.8 16.5 %collective-permute-start.36 = (bf16[256,256]{1,0:T(8,128)(2,1)S(1)}, bf16[256,256]{1,0:T(8,128)(2,1)S(1)}, u32[]{:S(2)}, u32[]{:S(2)}) collective-permute-start(bf16[256,256]{1,0:T(8,128)(2,1)S(1)} %get-tuple-element.221), channel_id=1, source_target_pairs={{0,16},{8,24},{16,0},{24,8},{1,17},{9,25},{17,1},{25,9},{2,18},{10... | collective-permute-start | bytes 393224 | tf_op jit(solution)/shard_map/ppermute | solution.py:39
  150.9 10.4 %collective-permute-start.38 = (bf16[256,256]{1,0:T(8,128)(2,1)S(1)}, bf16[256,256]{1,0:T(8,128)(2,1)S(1)}, u32[]{:S(2)}, u32[]{:S(2)}) collective-permute-start(bf16[256,256]{1,0:T(8,128)(2,1)S(1)} %get-tuple-element.218), channel_id=1, source_target_pairs={{0,24},{8,0},{16,8},{24,16},{1,25},{9,1},{17,9},{25,17},{2,26},{10... | collective-permute-start | bytes 393224 | tf_op jit(solution)/shard_map/ppermute | solution.py:39
  154.5 14.4 %collective-permute-start.39 = (bf16[256,256]{1,0:T(8,128)(2,1)}, bf16[256,256]{1,0:T(8,128)(2,1)S(1)}, u32[]{:S(2)}, u32[]{:S(2)}) collective-permute-start(bf16[256,256]{1,0:T(8,128)(2,1)} %get-tuple-element.182), channel_id=1, source_target_pairs={{0,1},{1,2},{2,3},{3,0},{4,5},{5,6},{6,7},{7,4},{8,9},{9,10},{10,1... | collective-permute-start | bytes 393224 | tf_op jit(solution)/shard_map/ppermute | solution.py:39
  156.2 12.7 %collective-permute-start.40 = (bf16[256,256]{1,0:T(8,128)(2,1)}, bf16[256,256]{1,0:T(8,128)(2,1)S(1)}, u32[]{:S(2)}, u32[]{:S(2)}) collective-permute-start(bf16[256,256]{1,0:T(8,128)(2,1)} %get-tuple-element.183), channel_id=1, source_target_pairs={{0,2},{1,3},{2,0},{3,1},{4,6},{5,7},{6,4},{7,5},{8,10},{9,11},{10,... | collective-permute-start | bytes 393224 | tf_op jit(solution)/shard_map/ppermute | solution.py:39
  157.0 11.9 %collective-permute-start.41 = (bf16[256,256]{1,0:T(8,128)(2,1)}, bf16[256,256]{1,0:T(8,128)(2,1)S(1)}, u32[]{:S(2)}, u32[]{:S(2)}) collective-permute-start(bf16[256,256]{1,0:T(8,128)(2,1)} %get-tuple-element.184), channel_id=1, source_target_pairs={{0,3},{1,0},{2,1},{3,2},{4,7},{5,4},{6,5},{7,6},{8,11},{9,8},{10,9... | collective-permute-start | bytes 393224 | tf_op jit(solution)/shard_map/ppermute | solution.py:39
  168.9 22.4 %copy-start.35 = (bf16[272,256]{1,0:T(8,128)(2,1)S(1)}, bf16[272,256]{1,0:T(8,128)(2,1)}, u32[]{:S(2)}) copy-start(bf16[272,256]{1,0:T(8,128)(2,1)} %get-tuple-element.198) | copy-start | bytes 417796
  168.9 22.5 %copy-start.34 = (bf16[272,256]{1,0:T(8,128)(2,1)S(1)}, bf16[272,256]{1,0:T(8,128)(2,1)}, u32[]{:S(2)}) copy-start(bf16[272,256]{1,0:T(8,128)(2,1)} %get-tuple-element.199) | copy-start | bytes 417796
  168.9 25.5 %copy-start.33 = (bf16[272,256]{1,0:T(8,128)(2,1)S(1)}, bf16[272,256]{1,0:T(8,128)(2,1)}, u32[]{:S(2)}) copy-start(bf16[272,256]{1,0:T(8,128)(2,1)} %get-tuple-element.200) | copy-start | bytes 417796
  168.9 2.8 %collective-permute-start.42 = (bf16[512,896]{1,0:T(8,128)(2,1)}, bf16[512,896]{1,0:T(8,128)(2,1)S(1)}, u32[]{:S(2)}, u32[]{:S(2)}) collective-permute-start(bf16[512,896]{1,0:T(8,128)(2,1)} %get-tuple-element.191), channel_id=1, source_target_pairs={{0,4},{4,0},{1,5},{5,1},{2,6},{6,2},{3,7},{7,3},{8,12},{12,8},{9,1... | collective-permute-start | bytes 2752520 | tf_op jit(solution)/shard_map/ppermute | solution.py:39
  173.0 33.0 %copy-start.19 = (bf16[272,256]{1,0:T(8,128)(2,1)S(1)}, bf16[272,256]{1,0:T(8,128)(2,1)}, u32[]{:S(2)}) copy-start(bf16[272,256]{1,0:T(8,128)(2,1)} %get-tuple-element.201) | copy-start | bytes 417796
  173.0 23.0 %collective-permute-start.45 = (bf16[128,896]{1,0:T(8,128)(2,1)S(1)}, bf16[128,896]{1,0:T(8,128)(2,1)S(1)}, u32[]{:S(2)}, u32[]{:S(2)}) collective-permute-start(bf16[128,896]{1,0:T(8,128)(2,1)S(1)} %get-tuple-element.216), channel_id=1, source_target_pairs={{0,96},{32,0},{64,32},{96,64},{1,97},{33,1},{65,33},{97,65},{2,98}... | collective-permute-start | bytes 688136 | tf_op jit(solution)/shard_map/ppermute | solution.py:39
  176.2 19.8 %collective-permute-start.44 = (bf16[128,896]{1,0:T(8,128)(2,1)S(1)}, bf16[128,896]{1,0:T(8,128)(2,1)S(1)}, u32[]{:S(2)}, u32[]{:S(2)}) collective-permute-start(bf16[128,896]{1,0:T(8,128)(2,1)S(1)} %get-tuple-element.217), channel_id=1, source_target_pairs={{0,64},{32,96},{64,0},{96,32},{1,65},{33,97},{65,1},{97,33},{2,66}... | collective-permute-start | bytes 688136 | tf_op jit(solution)/shard_map/ppermute | solution.py:39
  177.1 29.0 %copy-start.9 = (bf16[256,1,256]{2,0,1:T(8,128)(2,1)S(1)}, bf16[256,1,256]{2,0,1:T(8,128)(2,1)}, u32[]{:S(2)}) copy-start(bf16[256,1,256]{2,0,1:T(8,128)(2,1)} %param.13) | copy-start | bytes 393220
  177.1 29.0 %copy-start.10 = (f32[256,256]{1,0:T(8,128)S(1)}, f32[256,256]{1,0:T(8,128)}, u32[]{:S(2)}) copy-start(f32[256,256]{1,0:T(8,128)} %get-tuple-element.189) | copy-start | bytes 786436
  177.1 14.2 %collective-permute-start.43 = (bf16[128,896]{1,0:T(8,128)(2,1)S(1)}, bf16[128,896]{1,0:T(8,128)(2,1)S(1)}, u32[]{:S(2)}, u32[]{:S(2)}) collective-permute-start(bf16[128,896]{1,0:T(8,128)(2,1)S(1)} %get-tuple-element.215), channel_id=1, source_target_pairs={{0,32},{32,64},{64,96},{96,0},{1,33},{33,65},{65,97},{97,1},{2,34}... | collective-permute-start | bytes 688136 | tf_op jit(solution)/shard_map/ppermute | solution.py:39
  191.2 9.7 %collective-permute-start.46 = (bf16[272,256]{1,0:T(8,128)(2,1)S(1)}, bf16[272,256]{1,0:T(8,128)(2,1)S(1)}, u32[]{:S(2)}, u32[]{:S(2)}) collective-permute-start(bf16[272,256]{1,0:T(8,128)(2,1)S(1)} %copy-done.35), channel_id=1, source_target_pairs={{0,1},{1,2},{2,3},{3,0},{4,5},{5,6},{6,7},{7,4},{8,9},{9,10},{10,1... | collective-permute-start | bytes 417800 | tf_op jit(solution)/shard_map/ppermute | solution.py:39
  191.4 9.5 %collective-permute-start.47 = (bf16[272,256]{1,0:T(8,128)(2,1)S(1)}, bf16[272,256]{1,0:T(8,128)(2,1)S(1)}, u32[]{:S(2)}, u32[]{:S(2)}) collective-permute-start(bf16[272,256]{1,0:T(8,128)(2,1)S(1)} %copy-done.34), channel_id=1, source_target_pairs={{0,2},{1,3},{2,0},{3,1},{4,6},{5,7},{6,4},{7,5},{8,10},{9,11},{10,... | collective-permute-start | bytes 417800 | tf_op jit(solution)/shard_map/ppermute | solution.py:39
  194.4 7.1 %collective-permute-start.48 = (bf16[272,256]{1,0:T(8,128)(2,1)S(1)}, bf16[272,256]{1,0:T(8,128)(2,1)S(1)}, u32[]{:S(2)}, u32[]{:S(2)}) collective-permute-start(bf16[272,256]{1,0:T(8,128)(2,1)S(1)} %copy-done.33), channel_id=1, source_target_pairs={{0,3},{1,0},{2,1},{3,2},{4,7},{5,4},{6,5},{7,6},{8,11},{9,8},{10,9... | collective-permute-start | bytes 417800 | tf_op jit(solution)/shard_map/ppermute | solution.py:39
  202.1 5.7 %collective-permute-start.49 = (bf16[32,896]{1,0:T(8,128)(2,1)S(1)}, bf16[32,896]{1,0:T(8,128)(2,1)S(1)}, u32[]{:S(2)}, u32[]{:S(2)}) collective-permute-start(bf16[32,896]{1,0:T(8,128)(2,1)S(1)} %get-tuple-element.224), channel_id=1, source_target_pairs={{0,8},{8,16},{16,24},{24,0},{1,9},{9,17},{17,25},{25,1},{2,10},{10... | collective-permute-start | bytes 172040 | tf_op jit(solution)/shard_map/ppermute | solution.py:39
  203.3 6.1 %collective-permute-start.50 = (bf16[32,896]{1,0:T(8,128)(2,1)S(1)}, bf16[32,896]{1,0:T(8,128)(2,1)S(1)}, u32[]{:S(2)}, u32[]{:S(2)}) collective-permute-start(bf16[32,896]{1,0:T(8,128)(2,1)S(1)} %get-tuple-element.223), channel_id=1, source_target_pairs={{0,16},{8,24},{16,0},{24,8},{1,17},{9,25},{17,1},{25,9},{2,18},{10... | collective-permute-start | bytes 172040 | tf_op jit(solution)/shard_map/ppermute | solution.py:39
  205.8 4.2 %collective-permute-start.51 = (bf16[32,896]{1,0:T(8,128)(2,1)S(1)}, bf16[32,896]{1,0:T(8,128)(2,1)S(1)}, u32[]{:S(2)}, u32[]{:S(2)}) collective-permute-start(bf16[32,896]{1,0:T(8,128)(2,1)S(1)} %get-tuple-element.222), channel_id=1, source_target_pairs={{0,24},{8,0},{16,8},{24,16},{1,25},{9,1},{17,9},{25,17},{2,26},{10... | collective-permute-start | bytes 172040 | tf_op jit(solution)/shard_map/ppermute | solution.py:39
  212.1 5.3 %collective-permute-start.54 = (f32[32,128]{1,0:T(8,128)}, f32[32,128]{1,0:T(8,128)S(1)}, u32[]{:S(2)}, u32[]{:S(2)}) collective-permute-start(f32[32,128]{1,0:T(8,128)} %get-tuple-element.206), channel_id=1, source_target_pairs={{0,3},{1,0},{2,1},{3,2},{4,7},{5,4},{6,5},{7,6},{8,11},{9,8},{10,9... | collective-permute-start | bytes 49160 | tf_op jit(solution)/shard_map/ppermute | solution.py:39
  215.1 5.5 %collective-permute-start.53 = (f32[32,128]{1,0:T(8,128)}, f32[32,128]{1,0:T(8,128)S(1)}, u32[]{:S(2)}, u32[]{:S(2)}) collective-permute-start(f32[32,128]{1,0:T(8,128)} %get-tuple-element.206), channel_id=1, source_target_pairs={{0,2},{1,3},{2,0},{3,1},{4,6},{5,7},{6,4},{7,5},{8,10},{9,11},{10,... | collective-permute-start | bytes 49160 | tf_op jit(solution)/shard_map/ppermute | solution.py:39
  215.8 5.2 %collective-permute-start.52 = (f32[32,128]{1,0:T(8,128)}, f32[32,128]{1,0:T(8,128)S(1)}, u32[]{:S(2)}, u32[]{:S(2)}) collective-permute-start(f32[32,128]{1,0:T(8,128)} %get-tuple-element.206), channel_id=1, source_target_pairs={{0,1},{1,2},{2,3},{3,0},{4,5},{5,6},{6,7},{7,4},{8,9},{9,10},{10,1... | collective-permute-start | bytes 49160 | tf_op jit(solution)/shard_map/ppermute | solution.py:39
  (36 other events, 104.4 us)
Sparse Core Ops, SparseCore 0:
  10.3 60.3 all-gather.1
  131.2 82.0 reduce-scatter.1

commit v6 on v2

--- a/solution.py
+++ b/solution.py
@@ -73,8 +73,8 @@
     at = 0
     for other in range(nc):
         core = c if other == 0 else 1 - c
-        for xr in range(nx):
-            for zr in range(nz):
+        for zr in range(nz):
+            for xr in range(nx):
                 row = (rot_index(x, xr, nx) * nz + rot_index(z, zr, nz)) * nc + core
                 dst[at * own : (at + 1) * own, :] = src[ds(row, own), :]
                 at += 1
@@ -715,13 +715,13 @@
         flops=2 * span * width * (qkv + oc),
     )
     (keep, send), down_got = lax.optimization_barrier(((keep, send), down_got))
-    attn_pieces = core_sum(keep, send, nx)
-    attn_got = [shift(attn_pieces[k], "dp", k) for k in range(1, nx)]
+    attn_pieces = core_sum(keep, send, nz)
+    attn_got = [shift(attn_pieces[k], "z", k) for k in range(1, nz)]
     attn_got[0], norm_parts = lax.optimization_barrier((attn_got[0], norm_parts))
     attn_x = sum([v.astype(f32) for v in attn_got], attn_pieces[0].astype(f32)).astype(bf16)
     norm_got = [norm_parts[0]] + [shift(norm_parts[k], "tensor", k) for k in range(1, n)]
     attn_x, norm_got = lax.optimization_barrier((attn_x, norm_got))
-    z_parts = [attn_x[:own]] + [shift(attn_x[k * own : (k + 1) * own], "z", k) for k in range(1, nz)]
+    z_parts = [attn_x[:own]] + [shift(attn_x[k * own : (k + 1) * own], "dp", k) for k in range(1, nx)]
     wgrads = call(
         functools.partial(sum_kernel, (0, qc, qc + kc, qkv, qkv + oc, aw)),
         [sds((own, v), f32) for v in (qc, kc, kc, oc, PAD)],

time: 223 us -> 223 us (level)
  no operation moved by 1% of the time
where the time goes in v6:
time: 223 us; the launch traced here: 222 us
  starting transfers between devices  80.9 us (36%)
  Pallas kernels  55.1 us (25%)
  waiting for transfers between devices  48.5 us (22%)
  between operations  14.5 us (7%)
  other arithmetic  13.8 us (6%)
  local copies, waits for them, and re-layouts  9.2 us (4%)
    ppermute x52, starting transfers between devices, shift(): return lax.ppermute(x, axis, [(i, (i + k) % n) for i in range(n)])  80.8 us
    pallas_call x15, Pallas kernels, call(): pl.pallas_call(kernel, out_shape=outs, in_specs=in_specs or [pl.BlockSpec...  55.1 us
    ppermute x52, waiting for transfers between devices, shift(): return lax.ppermute(x, axis, [(i, (i + k) % n) for i in range(n)])  45.1 us
    unnamed x91, local copies, waits for them, and re-layouts  6.15 us
  transfers between devices with their start and end apart: 54, of which 22 were waited for; matrix products, arithmetic and copies ran while one was open for 8% of the time, Pallas kernels for 18%

profile of v6, /device:TPU:0, one launch (start us, length us, event | category | flops | bytes accessed | tf_op | source)
XLA Modules:
  0.0 222.1 jit_solution(674516107983747537)
XLA Ops:
  7.2 2.0 shard_map.228
  9.3 2.1 collective-permute-start
  11.4 3.6 %collective-permute-start.1 = (bf16[32,640]{1,0:T(8,128)(2,1)}, bf16[32,640]{1,0:T(8,128)(2,1)S(1)}, u32[]{:S(2)}, u32[]{:S(2)}) collective-permute-start(bf16[32,640]{1,0:T(8,128)(2,1)} %get-tuple-element.124), channel_id=1, source_target_pairs={{0,16},{8,24},{16,0},{24,8},{1,17},{9,25},{17,1},{25,9},{2,18},{10... | collective-permute-start | bytes 122888 | tf_op jit(solution)/shard_map/ppermute | solution.py:37
  15.9 1.6 collective-permute-start.6
  17.5 2.9 %collective-permute-start.7 = (bf16[256,512]{1,0:T(8,128)(2,1)}, bf16[256,512]{1,0:T(8,128)(2,1)S(1)}, u32[]{:S(2)}, u32[]{:S(2)}) collective-permute-start(bf16[256,512]{1,0:T(8,128)(2,1)} %get-tuple-element.126.refs_0_), channel_id=1, source_target_pairs={{0,2},{1,3},{2,0},{3,1},{4,6},{5,7},{6,4},{7,5},{8,10},{9,11},{10,... | collective-permute-start | bytes 786440 | tf_op jit(solution)/shard_map/ppermute | solution.py:37
  21.2 1.3 collective-permute-start.8
  22.6 1.6 collective-permute-start.3
  24.2 2.8 %collective-permute-start.4 = (bf16[128,640]{1,0:T(8,128)(2,1)S(1)}, bf16[128,640]{1,0:T(8,128)(2,1)S(1)}, u32[]{:S(2)}, u32[]{:S(2)}) collective-permute-start(bf16[128,640]{1,0:T(8,128)(2,1)S(1)} %constant_dynamic-update-slice_fusion.refs_4_), channel_id=1, source_target_pairs={{0,64},{32,96},{64,0},{96,32},{1,65},{33,97},{65,1},{97,33},{2,66}... | collective-permute-start | bytes 491528 | tf_op jit(solution)/shard_map/ppermute | solution.py:37
  27.0 3.8 %collective-permute-done.3.refs_5_ = bf16[128,640]{1,0:T(8,128)(2,1)S(1)} collective-permute-done((bf16[128,640]{1,0:T(8,128)(2,1)S(1)}, bf16[128,640]{1,0:T(8,128)(2,1)S(1)}, u32[]{:S(2)}, u32[]{:S(2)}) %collective-permute-start.3) | collective-permute-done | bytes 163872 | tf_op jit(solution)/shard_map/ppermute | solution.py:37
  30.8 2.9 %collective-permute-start.5 = (bf16[128,640]{1,0:T(8,128)(2,1)S(1)}, bf16[128,640]{1,0:T(8,128)(2,1)S(1)}, u32[]{:S(2)}, u32[]{:S(2)}) collective-permute-start(bf16[128,640]{1,0:T(8,128)(2,1)S(1)} %constant_dynamic-update-slice_fusion.refs_4_), channel_id=1, source_target_pairs={{0,96},{32,0},{64,32},{96,64},{1,97},{33,1},{65,33},{97,65},{2,98}... | collective-permute-start | bytes 491528 | tf_op jit(solution)/shard_map/ppermute | solution.py:37
  34.5 1.3 maximum_bitcast_fusion.refs_12_.refs_11_.refs_5_
  40.3 4.0 %shard_map.229 = (bf16[1024,640]{1,0:T(8,128)(2,1)}, bf16[256,1024]{1,0:T(8,128)(2,1)}, f32[8,1024]{1,0:T(8,128)}, bf16[128,512]{1,0:T(8,128)(2,1)}, f32[384,256...) custom-call(s32[4]{0:T(128)} %pad_add_fusion.idx, bf16[256,512]{1,0:T(8,128)(2,1)} %get-tuple-element.126.refs_0_, ...), custom_call_target="tpu_custom_call" | custom-call | flops 268435456 | bytes 5472528 | tf_op jit(solution)/shard_map/pallas_call | solution.py:55
  44.3 2.7 %collective-permute-start.13 = (bf16[256,256]{1,0:T(8,128)(2,1)}, bf16[256,256]{1,0:T(8,128)(2,1)S(1)}, u32[]{:S(2)}, u32[]{:S(2)}) collective-permute-start(bf16[256,256]{1,0:T(8,128)(2,1)} %get-tuple-element.143.refs_0_), channel_id=1, source_target_pairs={{0,8},{8,16},{16,24},{24,0},{1,9},{9,17},{17,25},{25,1},{2,10},{10... | collective-permute-start | bytes 393224 | tf_op jit(solution)/shard_map/ppermute | solution.py:37
  47.5 2.2 %collective-permute-start.15 = (bf16[256,256]{1,0:T(8,128)(2,1)}, bf16[256,256]{1,0:T(8,128)(2,1)S(1)}, u32[]{:S(2)}, u32[]{:S(2)}) collective-permute-start(bf16[256,256]{1,0:T(8,128)(2,1)} %get-tuple-element.143.refs_0_), channel_id=1, source_target_pairs={{0,24},{8,0},{16,8},{24,16},{1,25},{9,1},{17,9},{25,17},{2,26},{10... | collective-permute-start | bytes 393224 | tf_op jit(solution)/shard_map/ppermute | solution.py:37
  49.7 4.8 %collective-permute-done.13.refs_1_ = bf16[256,256]{1,0:T(8,128)(2,1)S(1)} collective-permute-done((bf16[256,256]{1,0:T(8,128)(2,1)}, bf16[256,256]{1,0:T(8,128)(2,1)S(1)}, u32[]{:S(2)}, u32[]{:S(2)}) %collective-permute-start.13) | collective-permute-done | bytes 131104 | tf_op jit(solution)/shard_map/ppermute | solution.py:37
  54.6 5.3 %collective-permute-done.14.refs_2_ = bf16[256,256]{1,0:T(8,128)(2,1)S(1)} collective-permute-done((bf16[256,256]{1,0:T(8,128)(2,1)}, bf16[256,256]{1,0:T(8,128)(2,1)S(1)}, u32[]{:S(2)}, u32[]{:S(2)}) %collective-permute-start.14) | collective-permute-done | bytes 131104 | tf_op jit(solution)/shard_map/ppermute | solution.py:37
  61.0 2.3 %shard_map.230 = (bf16[256,1024]{1,0:T(8,128)(2,1)}, bf16[1024,256]{1,0:T(8,128)(2,1)}) custom-call(s32[4]{0:T(128)} %pad_add_fusion.idx, bf16[256,512]{1,0:T(8,128)(2,1)} %get-tuple-element.126.refs_0_, bf16[256,512]{1,0:T(8,128)(2,1)} %copy-done.1, bf16[256,512]{1,0:T(8,128)(2,1)} %copy-done.2, bf16[256,512]{1,0:T(8,128)(2,1)} %copy-done.3), custom_call_target="tpu_custom_call" | custom-call | bytes 2097168 | tf_op jit(solution)/shard_map/pallas_call | solution.py:55
  64.1 3.3 %shard_map.231 = (bf16[2048,256]{1,0:T(8,128)(2,1)}, f32[128,512]{1,0:T(8,128)}, bf16[256,256]{1,0:T(8,128)(2,1)}, f32[8,512]{1,0:T(8,128)}) custom-call(s32[4]{0:T(128)} %pad_add_fusion.idx, bf16[128,512]{1,0:T(8,128)(2,1)} %get-tuple-element.139.q_t.refs_7_, bf16[256,256]{1,0:T(8,128)(2,1)} %get-tuple-element.143.refs_0_, bf16[256,256]{1,0:T(8,128)(2,1)} %copy-done.37, ...), custom_call_target="tpu_custom_call" | custom-call | flops 536870912 | bytes 2637840 | tf_op jit(solution)/shard_map/pallas_call | solution.py:55
  67.4 3.3 %all-gather.2.cloned.1.call-done.w_low.w_high.wd.refs_4_.refs_5_ = bf16[1024,3712]{1,0:T(8,128)(2,1)} async-done(((bf16[32,3712]{1,0:T(8,128)(2,1)}), bf16[1024,3712]{1,0:T(8,128)(2,1)}) %all-gather.2.cloned.1.call-update) | async-done | bytes 7602192 | tf_op jit(solution)/shard_map/all_gather | solution.py:525
  70.7 2.2 %shard_map.232 = (bf16[256,256]{1,0:T(8,128)(2,1)}, bf16[256,256]{1,0:T(8,128)(2,1)}, bf16[256,256]{1,0:T(8,128)(2,1)}, bf16[256,256]{1,0:T(8,128)(2,1)}) custom-call(s32[4]{0:T(128)} %pad_add_fusion.idx, bf16[256,256]{1,0:T(8,128)(2,1)} %get-tuple-element.151.attn_b, bf16[1024,3712]{1,0:T(8,128)(2,1)} %all-gather.2.cloned.1.call-done.w_low.w_high.wd.refs_4_.refs_5_, ...), custom_call_target="tpu_custom_call" | custom-call | flops 134217728 | bytes 15859728 | tf_op jit(solution)/shard_map/pallas_call | solution.py:55
  73.0 1.5 collective-permute-start.20
  74.4 2.3 %collective-permute-start.21 = (bf16[256,256]{1,0:T(8,128)(2,1)}, bf16[256,256]{1,0:T(8,128)(2,1)S(1)}, u32[]{:S(2)}, u32[]{:S(2)}) collective-permute-start(bf16[256,256]{1,0:T(8,128)(2,1)} %get-tuple-element.155), channel_id=1, source_target_pairs={{0,2},{1,3},{2,0},{3,1},{4,6},{5,7},{6,4},{7,5},{8,10},{9,11},{10,... | collective-permute-start | bytes 393224 | tf_op jit(solution)/shard_map/ppermute | solution.py:37
  76.7 1.5 collective-permute-start.22
  78.3 1.8 collective-permute-done.20
  80.1 3.3 %collective-permute-done.21 = bf16[256,256]{1,0:T(8,128)(2,1)S(1)} collective-permute-done((bf16[256,256]{1,0:T(8,128)(2,1)}, bf16[256,256]{1,0:T(8,128)(2,1)S(1)}, u32[]{:S(2)}, u32[]{:S(2)}) %collective-permute-start.21) | collective-permute-done | bytes 131104 | tf_op jit(solution)/shard_map/ppermute | solution.py:37
  84.4 1.8 collective-permute-start.23
  86.2 2.4 %collective-permute-start.24 = (bf16[256,256]{1,0:T(8,128)(2,1)S(1)}, bf16[256,256]{1,0:T(8,128)(2,1)S(1)}, u32[]{:S(2)}, u32[]{:S(2)}) collective-permute-start(bf16[256,256]{1,0:T(8,128)(2,1)S(1)} %add_convert_fusion.11.refs_0_), channel_id=1, source_target_pairs={{0,2},{1,3},{2,0},{3,1},{4,6},{5,7},{6,4},{7,5},{8,10},{9,11},{10,... | collective-permute-start | bytes 393224 | tf_op jit(solution)/shard_map/ppermute | solution.py:37
  88.6 1.3 collective-permute-start.25
  89.9 4.2 %shard_map.233.refs_6_ = f32[256,1152]{1,0:T(8,128)} custom-call(bf16[256,1024]{1,0:T(8,128)(2,1)} %get-tuple-element.157.cot, bf16[1024,3712]{1,0:T(8,128)(2,1)} %all-gather.2.cloned.1.call-done.w_low.w_high.wd.refs_4_.refs_5_), custom_call_target="tpu_custom_call" | custom-call | flops 603979776 | bytes 9306112 | tf_op jit(solution)/shard_map/pallas_call | solution.py:55
  95.1 8.5 %shard_map.234 = (f32[256,1024]{1,0:T(8,128)}, bf16[256,1024]{1,0:T(8,128)(2,1)}, bf16[256,3456]{1,0:T(8,128)(2,1)}, bf16[256,256]{1,0:T(8,128)(2,1)}, bf16[256,...) custom-call(s32[4]{0:T(128)} %pad_add_fusion.idx, ...), custom_call_target="tpu_custom_call" | custom-call | flops 2415919104 | bytes 21331984 | tf_op jit(solution)/shard_map/pallas_call | solution.py:55
  103.5 1.3 collective-permute-start.26
  104.8 2.4 %collective-permute-start.27 = (bf16[256,256]{1,0:T(8,128)(2,1)}, bf16[256,256]{1,0:T(8,128)(2,1)S(1)}, u32[]{:S(2)}, u32[]{:S(2)}) collective-permute-start(bf16[256,256]{1,0:T(8,128)(2,1)} %get-tuple-element.162), channel_id=1, source_target_pairs={{0,2},{1,3},{2,0},{3,1},{4,6},{5,7},{6,4},{7,5},{8,10},{9,11},{10,... | collective-permute-start | bytes 393224 | tf_op jit(solution)/shard_map/ppermute | solution.py:37
  108.2 6.3 %shard_map.235 = bf16[1024,3456]{1,0:T(8,128)(2,1)} custom-call(bf16[256,1024]{1,0:T(8,128)(2,1)} %get-tuple-element.164.normed, bf16[1024,256]{1,0:T(8,128)(2,1)} %get-tuple-element.165.cot_t, bf16[256,3456]{1,0:T(8,128)(2,1)} %get-tuple-element.166.big.hidden), custom_call_target="tpu_custom_call" | custom-call | flops 1811939328 | bytes 9895936 | tf_op jit(solution)/shard_map/pallas_call | solution.py:55
  117.7 2.0 collective-permute-start.31
  119.7 3.5 %shard_map.236 = (bf16[256,256]{1,0:T(8,128)(2,1)}, bf16[256,256]{1,0:T(8,128)(2,1)}, bf16[256,256]{1,0:T(8,128)(2,1)}, bf16[256,256]{1,0:T(8,128)(2,1)}) custom-call(s32[4]{0:T(128)} %pad_add_fusion.idx, bf16[256,3456]{1,0:T(8,128)(2,1)} %get-tuple-element.166.big.hidden, bf16[1024,3712]{1,0:T(8,128)(2,1)} %all-gather.2.cloned.1.call-done.w_low.w_high.wd.refs_4_.refs_5_), custom_call_target="tpu_custom_call" | custom-call | flops 603979776 | bytes 9895952 | tf_op jit(solution)/shard_map/pallas_call | solution.py:55
  124.6 6.5 %shard_map.237 = (f32[256,256]{1,0:T(8,128)}, bf16[256,1024]{1,0:T(8,128)(2,1)}, f32[8,1024]{1,0:T(8,128)}, bf16[256,256]{1,0:T(8,128)(2,1)}, f32[64,1]{1,0:T(8,...) custom-call(s32[4]{0:T(128)} %pad_add_fusion.idx, f32[256,1024]{1,0:T(8,128)} %get-tuple-element.158.middle, ...), custom_call_target="tpu_custom_call" | custom-call | flops 1342177280 | bytes 21250576 | tf_op jit(solution)/shard_map/pallas_call | solution.py:55
  131.2 2.1 collective-permute-done.32
  133.3 1.9 add_convert_fusion.6
  135.2 2.5 %collective-permute-start.34 = (bf16[256,256]{1,0:T(8,128)(2,1)S(1)}, bf16[256,256]{1,0:T(8,128)(2,1)S(1)}, u32[]{:S(2)}, u32[]{:S(2)}) collective-permute-start(bf16[256,256]{1,0:T(8,128)(2,1)S(1)} %get-tuple-element.239), channel_id=1, source_target_pairs={{0,8},{8,16},{16,24},{24,0},{1,9},{9,17},{17,25},{25,1},{2,10},{10... | collective-permute-start | bytes 393224 | tf_op jit(solution)/shard_map/ppermute | solution.py:37
  137.7 8.4 %collective-permute-start.33 = (bf16[256,256]{1,0:T(8,128)(2,1)S(1)}, bf16[256,256]{1,0:T(8,128)(2,1)S(1)}, u32[]{:S(2)}, u32[]{:S(2)}) collective-permute-start(bf16[256,256]{1,0:T(8,128)(2,1)S(1)} %get-tuple-element.241), channel_id=1, source_target_pairs={{0,16},{8,24},{16,0},{24,8},{1,17},{9,25},{17,1},{25,9},{2,18},{10... | collective-permute-start | bytes 393224 | tf_op jit(solution)/shard_map/ppermute | solution.py:37
  146.1 2.3 %collective-permute-done.34.refs_1_ = bf16[256,256]{1,0:T(8,128)(2,1)S(1)} collective-permute-done((bf16[256,256]{1,0:T(8,128)(2,1)S(1)}, bf16[256,256]{1,0:T(8,128)(2,1)S(1)}, u32[]{:S(2)}, u32[]{:S(2)}) %collective-permute-start.34) | collective-permute-done | bytes 131104 | tf_op jit(solution)/shard_map/ppermute | solution.py:37
  148.4 1.8 collective-permute-start.36
  150.2 2.4 %collective-permute-start.37 = (bf16[256,256]{1,0:T(8,128)(2,1)S(1)}, bf16[256,256]{1,0:T(8,128)(2,1)S(1)}, u32[]{:S(2)}, u32[]{:S(2)}) collective-permute-start(bf16[256,256]{1,0:T(8,128)(2,1)S(1)} %copy-done.35), channel_id=1, source_target_pairs={{0,2},{1,3},{2,0},{3,1},{4,6},{5,7},{6,4},{7,5},{8,10},{9,11},{10,... | collective-permute-start | bytes 393224 | tf_op jit(solution)/shard_map/ppermute | solution.py:37
  153.3 2.3 %shard_map.238.out_rel = bf16[1024,256]{1,0:T(8,128)(2,1)} custom-call(s32[4]{0:T(128)} %pad_add_fusion.idx, bf16[256,1024]{1,0:T(8,128)(2,1)} %get-tuple-element.184.mid, bf16[256,256]{1,0:T(8,128)(2,1)} %get-tuple-element.151.attn_b), custom_call_target="tpu_custom_call" | custom-call | flops 134217728 | bytes 1179664 | tf_op jit(solution)/shard_map/pallas_call | solution.py:55
  156.3 3.7 %shard_map.239 = (bf16[256,512]{1,0:T(8,128)(2,1)}, f32[8,1024]{1,0:T(8,128)}, f32[64,1]{1,0:T(8,128)}, bf16[272,256]{1,0:T(8,128)(2,1)}, bf16[272,256]{1,0:T(8,...) custom-call(s32[4]{0:T(128)} %pad_add_fusion.idx, bf16[256,256]{1,0:T(8,128)(2,1)} %get-tuple-element.240.refs_0_, ...), custom_call_target="tpu_custom_call" | custom-call | flops 268435456 | bytes 3834384 | tf_op jit(solution)/shard_map/pallas_call | solution.py:55
  160.0 3.1 %shard_map.240 = (bf16[512,896]{1,0:T(8,128)(2,1)}, bf16[512,896]{1,0:T(8,128)(2,1)}) custom-call(s32[4]{0:T(128)} %pad_add_fusion.idx, bf16[1024,256]{1,0:T(8,128)(2,1)} %get-tuple-element.159.one_rel, bf16[1024,256]{1,0:T(8,128)(2,1)} %shard_map.238.out_rel, bf16[256,512]{1,0:T(8,128)(2,1)} %get-tuple-element.194.qkv_gb, ...), custom_call_target="tpu_custom_call" | custom-call | flops 402653184 | bytes 3211792 | tf_op jit(solution)/shard_map/pallas_call | solution.py:55
  164.4 1.5 collective-permute-done.39
  165.9 1.3 add_convert_fusion.3
  167.3 4.0 %collective-permute-start.41 = (bf16[128,896]{1,0:T(8,128)(2,1)S(1)}, bf16[128,896]{1,0:T(8,128)(2,1)S(1)}, u32[]{:S(2)}, u32[]{:S(2)}) collective-permute-start(bf16[128,896]{1,0:T(8,128)(2,1)S(1)} %get-tuple-element.237), channel_id=1, source_target_pairs={{0,16},{8,24},{16,0},{24,8},{1,17},{9,25},{17,1},{25,9},{2,18},{10... | collective-permute-start | bytes 688136 | tf_op jit(solution)/shard_map/ppermute | solution.py:37
  171.5 1.7 fusion.4
  173.2 8.0 %collective-permute-done.40 = bf16[128,896]{1,0:T(8,128)(2,1)S(1)} collective-permute-done((bf16[128,896]{1,0:T(8,128)(2,1)S(1)}, bf16[128,896]{1,0:T(8,128)(2,1)S(1)}, u32[]{:S(2)}, u32[]{:S(2)}) %collective-permute-start.40) | collective-permute-done | bytes 229408 | tf_op jit(solution)/shard_map/ppermute | solution.py:37
  181.2 1.3 collective-permute-start.43
  182.5 1.7 collective-permute-start.44
  184.2 1.4 collective-permute-start.45
  185.6 5.6 %collective-permute-done.41 = bf16[128,896]{1,0:T(8,128)(2,1)S(1)} collective-permute-done((bf16[128,896]{1,0:T(8,128)(2,1)S(1)}, bf16[128,896]{1,0:T(8,128)(2,1)S(1)}, u32[]{:S(2)}, u32[]{:S(2)}) %collective-permute-start.41) | collective-permute-done | bytes 229408 | tf_op jit(solution)/shard_map/ppermute | solution.py:37
  193.0 1.2 collective-permute-start.46
  194.2 2.7 %collective-permute-start.47 = (bf16[32,896]{1,0:T(8,128)(2,1)S(1)}, bf16[32,896]{1,0:T(8,128)(2,1)S(1)}, u32[]{:S(2)}, u32[]{:S(2)}) collective-permute-start(bf16[32,896]{1,0:T(8,128)(2,1)S(1)} %get-tuple-element.243), channel_id=1, source_target_pairs={{0,64},{32,96},{64,0},{96,32},{1,65},{33,97},{65,1},{97,33},{2,66}... | collective-permute-start | bytes 172040 | tf_op jit(solution)/shard_map/ppermute | solution.py:37
  196.9 1.4 collective-permute-start.48
  201.7 1.5 shard_map.241
  203.3 1.5 collective-permute-start.49
  204.8 1.9 collective-permute-start.50
  206.6 1.5 collective-permute-start.51
  208.2 1.5 add_reduce_fusion
  213.5 1.7 shard_map.242
  (180 shorter events, 28.9 us)
Async XLA Ops:
  7.2 63.5 %all-gather.2.cloned.1.call-start = ((), (), s32[]{:S(2)}) async-start(), calls=%async_computation.1 | async-start | bytes 7839744 | tf_op jit(solution)/shard_map/all_gather | solution.py:525
  9.2 204.3 %reduce-scatter.2.cloned.1.call-start = ((), (), s32[]{:S(2)}) async-start(), calls=%async_computation.2 | async-start | bytes 7299072 | tf_op jit(solution)/shard_map/reduce_scatter | solution.py:630
  9.3 11.9 %collective-permute-start = (bf16[32,640]{1,0:T(8,128)(2,1)}, bf16[32,640]{1,0:T(8,128)(2,1)S(1)}, u32[]{:S(2)}, u32[]{:S(2)}) collective-permute-start(bf16[32,640]{1,0:T(8,128)(2,1)} %get-tuple-element.124), channel_id=1, source_target_pairs={{0,8},{8,16},{16,24},{24,0},{1,9},{9,17},{17,25},{25,1},{2,10},{10... | collective-permute-start | bytes 122888 | tf_op jit(solution)/shard_map/ppermute | solution.py:37
  11.4 11.2 %collective-permute-start.1 = (bf16[32,640]{1,0:T(8,128)(2,1)}, bf16[32,640]{1,0:T(8,128)(2,1)S(1)}, u32[]{:S(2)}, u32[]{:S(2)}) collective-permute-start(bf16[32,640]{1,0:T(8,128)(2,1)} %get-tuple-element.124), channel_id=1, source_target_pairs={{0,16},{8,24},{16,0},{24,8},{1,17},{9,25},{17,1},{25,9},{2,18},{10... | collective-permute-start | bytes 122888 | tf_op jit(solution)/shard_map/ppermute | solution.py:37
  14.9 7.7 %collective-permute-start.2 = (bf16[32,640]{1,0:T(8,128)(2,1)}, bf16[32,640]{1,0:T(8,128)(2,1)S(1)}, u32[]{:S(2)}, u32[]{:S(2)}) collective-permute-start(bf16[32,640]{1,0:T(8,128)(2,1)} %get-tuple-element.124), channel_id=1, source_target_pairs={{0,24},{8,0},{16,8},{24,16},{1,25},{9,1},{17,9},{25,17},{2,26},{10... | collective-permute-start | bytes 122888 | tf_op jit(solution)/shard_map/ppermute | solution.py:37
  15.9 21.0 %collective-permute-start.6 = (bf16[256,512]{1,0:T(8,128)(2,1)}, bf16[256,512]{1,0:T(8,128)(2,1)S(1)}, u32[]{:S(2)}, u32[]{:S(2)}) collective-permute-start(bf16[256,512]{1,0:T(8,128)(2,1)} %get-tuple-element.126.refs_0_), channel_id=1, source_target_pairs={{0,1},{1,2},{2,3},{3,0},{4,5},{5,6},{6,7},{7,4},{8,9},{9,10},{10,1... | collective-permute-start | bytes 786440 | tf_op jit(solution)/shard_map/ppermute | solution.py:37
  17.5 19.4 %collective-permute-start.7 = (bf16[256,512]{1,0:T(8,128)(2,1)}, bf16[256,512]{1,0:T(8,128)(2,1)S(1)}, u32[]{:S(2)}, u32[]{:S(2)}) collective-permute-start(bf16[256,512]{1,0:T(8,128)(2,1)} %get-tuple-element.126.refs_0_), channel_id=1, source_target_pairs={{0,2},{1,3},{2,0},{3,1},{4,6},{5,7},{6,4},{7,5},{8,10},{9,11},{10,... | collective-permute-start | bytes 786440 | tf_op jit(solution)/shard_map/ppermute | solution.py:37
  21.2 15.7 %collective-permute-start.8 = (bf16[256,512]{1,0:T(8,128)(2,1)}, bf16[256,512]{1,0:T(8,128)(2,1)S(1)}, u32[]{:S(2)}, u32[]{:S(2)}) collective-permute-start(bf16[256,512]{1,0:T(8,128)(2,1)} %get-tuple-element.126.refs_0_), channel_id=1, source_target_pairs={{0,3},{1,0},{2,1},{3,2},{4,7},{5,4},{6,5},{7,6},{8,11},{9,8},{10,9... | collective-permute-start | bytes 786440 | tf_op jit(solution)/shard_map/ppermute | solution.py:37
  22.6 16.6 %copy-start.8 = (bf16[128,640]{1,0:T(8,128)(2,1)}, bf16[128,640]{1,0:T(8,128)(2,1)S(1)}, u32[]{:S(2)}) copy-start(bf16[128,640]{1,0:T(8,128)(2,1)S(1)} %constant_dynamic-update-slice_fusion.refs_4_) | copy-start | bytes 491524
  22.6 8.2 %collective-permute-start.3 = (bf16[128,640]{1,0:T(8,128)(2,1)S(1)}, bf16[128,640]{1,0:T(8,128)(2,1)S(1)}, u32[]{:S(2)}, u32[]{:S(2)}) collective-permute-start(bf16[128,640]{1,0:T(8,128)(2,1)S(1)} %constant_dynamic-update-slice_fusion.refs_4_), channel_id=1, source_target_pairs={{0,32},{32,64},{64,96},{96,0},{1,33},{33,65},{65,97},{97,1},{2,34}... | collective-permute-start | bytes 491528 | tf_op jit(solution)/shard_map/ppermute | solution.py:37
  24.2 11.8 %collective-permute-start.4 = (bf16[128,640]{1,0:T(8,128)(2,1)S(1)}, bf16[128,640]{1,0:T(8,128)(2,1)S(1)}, u32[]{:S(2)}, u32[]{:S(2)}) collective-permute-start(bf16[128,640]{1,0:T(8,128)(2,1)S(1)} %constant_dynamic-update-slice_fusion.refs_4_), channel_id=1, source_target_pairs={{0,64},{32,96},{64,0},{96,32},{1,65},{33,97},{65,1},{97,33},{2,66}... | collective-permute-start | bytes 491528 | tf_op jit(solution)/shard_map/ppermute | solution.py:37
  30.8 6.1 %collective-permute-start.5 = (bf16[128,640]{1,0:T(8,128)(2,1)S(1)}, bf16[128,640]{1,0:T(8,128)(2,1)S(1)}, u32[]{:S(2)}, u32[]{:S(2)}) collective-permute-start(bf16[128,640]{1,0:T(8,128)(2,1)S(1)} %constant_dynamic-update-slice_fusion.refs_4_), channel_id=1, source_target_pairs={{0,96},{32,0},{64,32},{96,64},{1,97},{33,1},{65,33},{97,65},{2,98}... | collective-permute-start | bytes 491528 | tf_op jit(solution)/shard_map/ppermute | solution.py:37
  37.0 1.7 collective-permute-start.10
  37.0 1.6 collective-permute-start.11
  37.5 1.4 collective-permute-start.12
  37.6 1.5 collective-permute-start.9
  44.3 10.3 %collective-permute-start.13 = (bf16[256,256]{1,0:T(8,128)(2,1)}, bf16[256,256]{1,0:T(8,128)(2,1)S(1)}, u32[]{:S(2)}, u32[]{:S(2)}) collective-permute-start(bf16[256,256]{1,0:T(8,128)(2,1)} %get-tuple-element.143.refs_0_), channel_id=1, source_target_pairs={{0,8},{8,16},{16,24},{24,0},{1,9},{9,17},{17,25},{25,1},{2,10},{10... | collective-permute-start | bytes 393224 | tf_op jit(solution)/shard_map/ppermute | solution.py:37
  47.0 12.9 %collective-permute-start.14 = (bf16[256,256]{1,0:T(8,128)(2,1)}, bf16[256,256]{1,0:T(8,128)(2,1)S(1)}, u32[]{:S(2)}, u32[]{:S(2)}) collective-permute-start(bf16[256,256]{1,0:T(8,128)(2,1)} %get-tuple-element.143.refs_0_), channel_id=1, source_target_pairs={{0,16},{8,24},{16,0},{24,8},{1,17},{9,25},{17,1},{25,9},{2,18},{10... | collective-permute-start | bytes 393224 | tf_op jit(solution)/shard_map/ppermute | solution.py:37
  47.5 13.5 %collective-permute-start.15 = (bf16[256,256]{1,0:T(8,128)(2,1)}, bf16[256,256]{1,0:T(8,128)(2,1)S(1)}, u32[]{:S(2)}, u32[]{:S(2)}) collective-permute-start(bf16[256,256]{1,0:T(8,128)(2,1)} %get-tuple-element.143.refs_0_), channel_id=1, source_target_pairs={{0,24},{8,0},{16,8},{24,16},{1,25},{9,1},{17,9},{25,17},{2,26},{10... | collective-permute-start | bytes 393224 | tf_op jit(solution)/shard_map/ppermute | solution.py:37
  49.7 13.6 %collective-permute-start.16 = (bf16[256,256]{1,0:T(8,128)(2,1)}, bf16[256,256]{1,0:T(8,128)(2,1)S(1)}, u32[]{:S(2)}, u32[]{:S(2)}) collective-permute-start(bf16[256,256]{1,0:T(8,128)(2,1)} %get-tuple-element.143.refs_0_), channel_id=1, source_target_pairs={{0,4},{4,0},{1,5},{5,1},{2,6},{6,2},{3,7},{7,3},{8,12},{12,8},{9,1... | collective-permute-start | bytes 393224 | tf_op jit(solution)/shard_map/ppermute | solution.py:37
  54.6 8.7 %collective-permute-start.17 = (bf16[256,256]{1,0:T(8,128)(2,1)S(1)}, bf16[256,256]{1,0:T(8,128)(2,1)S(1)}, u32[]{:S(2)}, u32[]{:S(2)}) collective-permute-start(bf16[256,256]{1,0:T(8,128)(2,1)S(1)} %collective-permute-done.13.refs_1_), channel_id=1, source_target_pairs={{0,4},{4,0},{1,5},{5,1},{2,6},{6,2},{3,7},{7,3},{8,12},{12,8},{9,1... | collective-permute-start | bytes 393224 | tf_op jit(solution)/shard_map/ppermute | solution.py:37
  59.9 3.4 %collective-permute-start.18 = (bf16[256,256]{1,0:T(8,128)(2,1)S(1)}, bf16[256,256]{1,0:T(8,128)(2,1)S(1)}, u32[]{:S(2)}, u32[]{:S(2)}) collective-permute-start(bf16[256,256]{1,0:T(8,128)(2,1)S(1)} %collective-permute-done.14.refs_2_), channel_id=1, source_target_pairs={{0,4},{4,0},{1,5},{5,1},{2,6},{6,2},{3,7},{7,3},{8,12},{12,8},{9,1... | collective-permute-start | bytes 393224 | tf_op jit(solution)/shard_map/ppermute | solution.py:37
  61.0 2.4 %collective-permute-start.19 = (bf16[256,256]{1,0:T(8,128)(2,1)S(1)}, bf16[256,256]{1,0:T(8,128)(2,1)S(1)}, u32[]{:S(2)}, u32[]{:S(2)}) collective-permute-start(bf16[256,256]{1,0:T(8,128)(2,1)S(1)} %collective-permute-done.15.refs_3_), channel_id=1, source_target_pairs={{0,4},{4,0},{1,5},{5,1},{2,6},{6,2},{3,7},{7,3},{8,12},{12,8},{9,1... | collective-permute-start | bytes 393224 | tf_op jit(solution)/shard_map/ppermute | solution.py:37
  73.0 7.2 %collective-permute-start.20 = (bf16[256,256]{1,0:T(8,128)(2,1)}, bf16[256,256]{1,0:T(8,128)(2,1)S(1)}, u32[]{:S(2)}, u32[]{:S(2)}) collective-permute-start(bf16[256,256]{1,0:T(8,128)(2,1)} %get-tuple-element.154), channel_id=1, source_target_pairs={{0,1},{1,2},{2,3},{3,0},{4,5},{5,6},{6,7},{7,4},{8,9},{9,10},{10,1... | collective-permute-start | bytes 393224 | tf_op jit(solution)/shard_map/ppermute | solution.py:37
  74.4 9.0 %collective-permute-start.21 = (bf16[256,256]{1,0:T(8,128)(2,1)}, bf16[256,256]{1,0:T(8,128)(2,1)S(1)}, u32[]{:S(2)}, u32[]{:S(2)}) collective-permute-start(bf16[256,256]{1,0:T(8,128)(2,1)} %get-tuple-element.155), channel_id=1, source_target_pairs={{0,2},{1,3},{2,0},{3,1},{4,6},{5,7},{6,4},{7,5},{8,10},{9,11},{10,... | collective-permute-start | bytes 393224 | tf_op jit(solution)/shard_map/ppermute | solution.py:37
  76.7 6.7 %collective-permute-start.22 = (bf16[256,256]{1,0:T(8,128)(2,1)}, bf16[256,256]{1,0:T(8,128)(2,1)S(1)}, u32[]{:S(2)}, u32[]{:S(2)}) collective-permute-start(bf16[256,256]{1,0:T(8,128)(2,1)} %get-tuple-element.156), channel_id=1, source_target_pairs={{0,3},{1,0},{2,1},{3,2},{4,7},{5,4},{6,5},{7,6},{8,11},{9,8},{10,9... | collective-permute-start | bytes 393224 | tf_op jit(solution)/shard_map/ppermute | solution.py:37
  84.4 9.7 %collective-permute-start.23 = (bf16[256,256]{1,0:T(8,128)(2,1)S(1)}, bf16[256,256]{1,0:T(8,128)(2,1)S(1)}, u32[]{:S(2)}, u32[]{:S(2)}) collective-permute-start(bf16[256,256]{1,0:T(8,128)(2,1)S(1)} %add_convert_fusion.11.refs_0_), channel_id=1, source_target_pairs={{0,1},{1,2},{2,3},{3,0},{4,5},{5,6},{6,7},{7,4},{8,9},{9,10},{10,1... | collective-permute-start | bytes 393224 | tf_op jit(solution)/shard_map/ppermute | solution.py:37
  86.2 8.2 %collective-permute-start.24 = (bf16[256,256]{1,0:T(8,128)(2,1)S(1)}, bf16[256,256]{1,0:T(8,128)(2,1)S(1)}, u32[]{:S(2)}, u32[]{:S(2)}) collective-permute-start(bf16[256,256]{1,0:T(8,128)(2,1)S(1)} %add_convert_fusion.11.refs_0_), channel_id=1, source_target_pairs={{0,2},{1,3},{2,0},{3,1},{4,6},{5,7},{6,4},{7,5},{8,10},{9,11},{10,... | collective-permute-start | bytes 393224 | tf_op jit(solution)/shard_map/ppermute | solution.py:37
  88.6 5.8 %collective-permute-start.25 = (bf16[256,256]{1,0:T(8,128)(2,1)S(1)}, bf16[256,256]{1,0:T(8,128)(2,1)S(1)}, u32[]{:S(2)}, u32[]{:S(2)}) collective-permute-start(bf16[256,256]{1,0:T(8,128)(2,1)S(1)} %add_convert_fusion.11.refs_0_), channel_id=1, source_target_pairs={{0,3},{1,0},{2,1},{3,2},{4,7},{5,4},{6,5},{7,6},{8,11},{9,8},{10,9... | collective-permute-start | bytes 393224 | tf_op jit(solution)/shard_map/ppermute | solution.py:37
  103.5 11.0 %collective-permute-start.26 = (bf16[256,256]{1,0:T(8,128)(2,1)}, bf16[256,256]{1,0:T(8,128)(2,1)S(1)}, u32[]{:S(2)}, u32[]{:S(2)}) collective-permute-start(bf16[256,256]{1,0:T(8,128)(2,1)} %get-tuple-element.161), channel_id=1, source_target_pairs={{0,1},{1,2},{2,3},{3,0},{4,5},{5,6},{6,7},{7,4},{8,9},{9,10},{10,1... | collective-permute-start | bytes 393224 | tf_op jit(solution)/shard_map/ppermute | solution.py:37
  104.8 9.7 %collective-permute-start.27 = (bf16[256,256]{1,0:T(8,128)(2,1)}, bf16[256,256]{1,0:T(8,128)(2,1)S(1)}, u32[]{:S(2)}, u32[]{:S(2)}) collective-permute-start(bf16[256,256]{1,0:T(8,128)(2,1)} %get-tuple-element.162), channel_id=1, source_target_pairs={{0,2},{1,3},{2,0},{3,1},{4,6},{5,7},{6,4},{7,5},{8,10},{9,11},{10,... | collective-permute-start | bytes 393224 | tf_op jit(solution)/shard_map/ppermute | solution.py:37
  107.2 7.3 %collective-permute-start.28 = (bf16[256,256]{1,0:T(8,128)(2,1)}, bf16[256,256]{1,0:T(8,128)(2,1)S(1)}, u32[]{:S(2)}, u32[]{:S(2)}) collective-permute-start(bf16[256,256]{1,0:T(8,128)(2,1)} %get-tuple-element.163), channel_id=1, source_target_pairs={{0,3},{1,0},{2,1},{3,2},{4,7},{5,4},{6,5},{7,6},{8,11},{9,8},{10,9... | collective-permute-start | bytes 393224 | tf_op jit(solution)/shard_map/ppermute | solution.py:37
  115.5 7.7 %collective-permute-start.29 = (bf16[256,256]{1,0:T(8,128)(2,1)S(1)}, bf16[256,256]{1,0:T(8,128)(2,1)S(1)}, u32[]{:S(2)}, u32[]{:S(2)}) collective-permute-start(bf16[256,256]{1,0:T(8,128)(2,1)S(1)} %add_convert_fusion.10.refs_0_), channel_id=1, source_target_pairs={{0,1},{1,2},{2,3},{3,0},{4,5},{5,6},{6,7},{7,4},{8,9},{9,10},{10,1... | collective-permute-start | bytes 393224 | tf_op jit(solution)/shard_map/ppermute | solution.py:37
  116.6 6.6 %collective-permute-start.30 = (bf16[256,256]{1,0:T(8,128)(2,1)S(1)}, bf16[256,256]{1,0:T(8,128)(2,1)S(1)}, u32[]{:S(2)}, u32[]{:S(2)}) collective-permute-start(bf16[256,256]{1,0:T(8,128)(2,1)S(1)} %add_convert_fusion.10.refs_0_), channel_id=1, source_target_pairs={{0,2},{1,3},{2,0},{3,1},{4,6},{5,7},{6,4},{7,5},{8,10},{9,11},{10,... | collective-permute-start | bytes 393224 | tf_op jit(solution)/shard_map/ppermute | solution.py:37
  117.7 6.3 %collective-permute-start.31 = (bf16[256,256]{1,0:T(8,128)(2,1)S(1)}, bf16[256,256]{1,0:T(8,128)(2,1)S(1)}, u32[]{:S(2)}, u32[]{:S(2)}) collective-permute-start(bf16[256,256]{1,0:T(8,128)(2,1)S(1)} %add_convert_fusion.10.refs_0_), channel_id=1, source_target_pairs={{0,3},{1,0},{2,1},{3,2},{4,7},{5,4},{6,5},{7,6},{8,11},{9,8},{10,9... | collective-permute-start | bytes 393224 | tf_op jit(solution)/shard_map/ppermute | solution.py:37
  124.6 23.8 %copy-start.36 = (bf16[256,256]{1,0:T(8,128)(2,1)S(1)}, bf16[256,256]{1,0:T(8,128)(2,1)}, u32[]{:S(2)}) copy-start(bf16[256,256]{1,0:T(8,128)(2,1)} %get-tuple-element.202) | copy-start | bytes 393220
  124.6 25.6 %copy-start.35 = (bf16[256,256]{1,0:T(8,128)(2,1)S(1)}, bf16[256,256]{1,0:T(8,128)(2,1)}, u32[]{:S(2)}) copy-start(bf16[256,256]{1,0:T(8,128)(2,1)} %get-tuple-element.203) | copy-start | bytes 393220
  124.6 28.0 %copy-start.34 = (bf16[256,256]{1,0:T(8,128)(2,1)S(1)}, bf16[256,256]{1,0:T(8,128)(2,1)}, u32[]{:S(2)}) copy-start(bf16[256,256]{1,0:T(8,128)(2,1)} %get-tuple-element.204) | copy-start | bytes 393220
  131.1 2.2 collective-permute-start.32
  135.2 13.2 %collective-permute-start.34 = (bf16[256,256]{1,0:T(8,128)(2,1)S(1)}, bf16[256,256]{1,0:T(8,128)(2,1)S(1)}, u32[]{:S(2)}, u32[]{:S(2)}) collective-permute-start(bf16[256,256]{1,0:T(8,128)(2,1)S(1)} %get-tuple-element.239), channel_id=1, source_target_pairs={{0,8},{8,16},{16,24},{24,0},{1,9},{9,17},{17,25},{25,1},{2,10},{10... | collective-permute-start | bytes 393224 | tf_op jit(solution)/shard_map/ppermute | solution.py:37
  137.7 17.9 %collective-permute-start.33 = (bf16[256,256]{1,0:T(8,128)(2,1)S(1)}, bf16[256,256]{1,0:T(8,128)(2,1)S(1)}, u32[]{:S(2)}, u32[]{:S(2)}) collective-permute-start(bf16[256,256]{1,0:T(8,128)(2,1)S(1)} %get-tuple-element.241), channel_id=1, source_target_pairs={{0,16},{8,24},{16,0},{24,8},{1,17},{9,25},{17,1},{25,9},{2,18},{10... | collective-permute-start | bytes 393224 | tf_op jit(solution)/shard_map/ppermute | solution.py:37
  146.1 9.5 %collective-permute-start.35 = (bf16[256,256]{1,0:T(8,128)(2,1)S(1)}, bf16[256,256]{1,0:T(8,128)(2,1)S(1)}, u32[]{:S(2)}, u32[]{:S(2)}) collective-permute-start(bf16[256,256]{1,0:T(8,128)(2,1)S(1)} %get-tuple-element.238), channel_id=1, source_target_pairs={{0,24},{8,0},{16,8},{24,16},{1,25},{9,1},{17,9},{25,17},{2,26},{10... | collective-permute-start | bytes 393224 | tf_op jit(solution)/shard_map/ppermute | solution.py:37
  148.4 14.7 %collective-permute-start.36 = (bf16[256,256]{1,0:T(8,128)(2,1)S(1)}, bf16[256,256]{1,0:T(8,128)(2,1)S(1)}, u32[]{:S(2)}, u32[]{:S(2)}) collective-permute-start(bf16[256,256]{1,0:T(8,128)(2,1)S(1)} %copy-done.36), channel_id=1, source_target_pairs={{0,1},{1,2},{2,3},{3,0},{4,5},{5,6},{6,7},{7,4},{8,9},{9,10},{10,1... | collective-permute-start | bytes 393224 | tf_op jit(solution)/shard_map/ppermute | solution.py:37
  150.2 12.9 %collective-permute-start.37 = (bf16[256,256]{1,0:T(8,128)(2,1)S(1)}, bf16[256,256]{1,0:T(8,128)(2,1)S(1)}, u32[]{:S(2)}, u32[]{:S(2)}) collective-permute-start(bf16[256,256]{1,0:T(8,128)(2,1)S(1)} %copy-done.35), channel_id=1, source_target_pairs={{0,2},{1,3},{2,0},{3,1},{4,6},{5,7},{6,4},{7,5},{8,10},{9,11},{10,... | collective-permute-start | bytes 393224 | tf_op jit(solution)/shard_map/ppermute | solution.py:37
  152.6 10.5 %collective-permute-start.38 = (bf16[256,256]{1,0:T(8,128)(2,1)S(1)}, bf16[256,256]{1,0:T(8,128)(2,1)S(1)}, u32[]{:S(2)}, u32[]{:S(2)}) collective-permute-start(bf16[256,256]{1,0:T(8,128)(2,1)S(1)} %copy-done.34), channel_id=1, source_target_pairs={{0,3},{1,0},{2,1},{3,2},{4,7},{5,4},{6,5},{7,6},{8,11},{9,8},{10,9... | collective-permute-start | bytes 393224 | tf_op jit(solution)/shard_map/ppermute | solution.py:37
  163.1 18.1 %copy-start.33 = (bf16[272,256]{1,0:T(8,128)(2,1)S(1)}, bf16[272,256]{1,0:T(8,128)(2,1)}, u32[]{:S(2)}) copy-start(bf16[272,256]{1,0:T(8,128)(2,1)} %get-tuple-element.218) | copy-start | bytes 417796
  163.1 19.4 %copy-start.32 = (bf16[272,256]{1,0:T(8,128)(2,1)S(1)}, bf16[272,256]{1,0:T(8,128)(2,1)}, u32[]{:S(2)}) copy-start(bf16[272,256]{1,0:T(8,128)(2,1)} %get-tuple-element.219) | copy-start | bytes 417796
  163.1 21.1 %copy-start.31 = (bf16[272,256]{1,0:T(8,128)(2,1)S(1)}, bf16[272,256]{1,0:T(8,128)(2,1)}, u32[]{:S(2)}) copy-start(bf16[272,256]{1,0:T(8,128)(2,1)} %get-tuple-element.220) | copy-start | bytes 417796
  163.1 2.8 %collective-permute-start.39 = (bf16[512,896]{1,0:T(8,128)(2,1)}, bf16[512,896]{1,0:T(8,128)(2,1)S(1)}, u32[]{:S(2)}, u32[]{:S(2)}) collective-permute-start(bf16[512,896]{1,0:T(8,128)(2,1)} %get-tuple-element.211), channel_id=1, source_target_pairs={{0,4},{4,0},{1,5},{5,1},{2,6},{6,2},{3,7},{7,3},{8,12},{12,8},{9,1... | collective-permute-start | bytes 2752520 | tf_op jit(solution)/shard_map/ppermute | solution.py:37
  167.2 31.1 %copy-start.16 = (bf16[272,256]{1,0:T(8,128)(2,1)S(1)}, bf16[272,256]{1,0:T(8,128)(2,1)}, u32[]{:S(2)}) copy-start(bf16[272,256]{1,0:T(8,128)(2,1)} %get-tuple-element.221) | copy-start | bytes 417796
  167.2 14.0 %collective-permute-start.40 = (bf16[128,896]{1,0:T(8,128)(2,1)S(1)}, bf16[128,896]{1,0:T(8,128)(2,1)S(1)}, u32[]{:S(2)}, u32[]{:S(2)}) collective-permute-start(bf16[128,896]{1,0:T(8,128)(2,1)S(1)} %get-tuple-element.235), channel_id=1, source_target_pairs={{0,8},{8,16},{16,24},{24,0},{1,9},{9,17},{17,25},{25,1},{2,10},{10... | collective-permute-start | bytes 688136 | tf_op jit(solution)/shard_map/ppermute | solution.py:37
  167.3 23.9 %collective-permute-start.41 = (bf16[128,896]{1,0:T(8,128)(2,1)S(1)}, bf16[128,896]{1,0:T(8,128)(2,1)S(1)}, u32[]{:S(2)}, u32[]{:S(2)}) collective-permute-start(bf16[128,896]{1,0:T(8,128)(2,1)S(1)} %get-tuple-element.237), channel_id=1, source_target_pairs={{0,16},{8,24},{16,0},{24,8},{1,17},{9,25},{17,1},{25,9},{2,18},{10... | collective-permute-start | bytes 688136 | tf_op jit(solution)/shard_map/ppermute | solution.py:37
  171.3 27.1 %copy-start.6 = (bf16[256,1,256]{2,0,1:T(8,128)(2,1)S(1)}, bf16[256,1,256]{2,0,1:T(8,128)(2,1)}, u32[]{:S(2)}) copy-start(bf16[256,1,256]{2,0,1:T(8,128)(2,1)} %param.13) | copy-start | bytes 393220
  171.3 27.1 %copy-start.7 = (f32[256,256]{1,0:T(8,128)S(1)}, f32[256,256]{1,0:T(8,128)}, u32[]{:S(2)}) copy-start(f32[256,256]{1,0:T(8,128)} %get-tuple-element.209) | copy-start | bytes 786436
  171.3 19.9 %collective-permute-start.42 = (bf16[128,896]{1,0:T(8,128)(2,1)S(1)}, bf16[128,896]{1,0:T(8,128)(2,1)S(1)}, u32[]{:S(2)}, u32[]{:S(2)}) collective-permute-start(bf16[128,896]{1,0:T(8,128)(2,1)S(1)} %get-tuple-element.236), channel_id=1, source_target_pairs={{0,24},{8,0},{16,8},{24,16},{1,25},{9,1},{17,9},{25,17},{2,26},{10... | collective-permute-start | bytes 688136 | tf_op jit(solution)/shard_map/ppermute | solution.py:37
  181.2 11.1 %collective-permute-start.43 = (bf16[272,256]{1,0:T(8,128)(2,1)S(1)}, bf16[272,256]{1,0:T(8,128)(2,1)S(1)}, u32[]{:S(2)}, u32[]{:S(2)}) collective-permute-start(bf16[272,256]{1,0:T(8,128)(2,1)S(1)} %copy-done.33), channel_id=1, source_target_pairs={{0,1},{1,2},{2,3},{3,0},{4,5},{5,6},{6,7},{7,4},{8,9},{9,10},{10,1... | collective-permute-start | bytes 417800 | tf_op jit(solution)/shard_map/ppermute | solution.py:37
  182.5 9.8 %collective-permute-start.44 = (bf16[272,256]{1,0:T(8,128)(2,1)S(1)}, bf16[272,256]{1,0:T(8,128)(2,1)S(1)}, u32[]{:S(2)}, u32[]{:S(2)}) collective-permute-start(bf16[272,256]{1,0:T(8,128)(2,1)S(1)} %copy-done.32), channel_id=1, source_target_pairs={{0,2},{1,3},{2,0},{3,1},{4,6},{5,7},{6,4},{7,5},{8,10},{9,11},{10,... | collective-permute-start | bytes 417800 | tf_op jit(solution)/shard_map/ppermute | solution.py:37
  184.2 8.1 %collective-permute-start.45 = (bf16[272,256]{1,0:T(8,128)(2,1)S(1)}, bf16[272,256]{1,0:T(8,128)(2,1)S(1)}, u32[]{:S(2)}, u32[]{:S(2)}) collective-permute-start(bf16[272,256]{1,0:T(8,128)(2,1)S(1)} %copy-done.31), channel_id=1, source_target_pairs={{0,3},{1,0},{2,1},{3,2},{4,7},{5,4},{6,5},{7,6},{8,11},{9,8},{10,9... | collective-permute-start | bytes 417800 | tf_op jit(solution)/shard_map/ppermute | solution.py:37
  193.0 6.3 %collective-permute-start.46 = (bf16[32,896]{1,0:T(8,128)(2,1)S(1)}, bf16[32,896]{1,0:T(8,128)(2,1)S(1)}, u32[]{:S(2)}, u32[]{:S(2)}) collective-permute-start(bf16[32,896]{1,0:T(8,128)(2,1)S(1)} %get-tuple-element.244), channel_id=1, source_target_pairs={{0,32},{32,64},{64,96},{96,0},{1,33},{33,65},{65,97},{97,1},{2,34}... | collective-permute-start | bytes 172040 | tf_op jit(solution)/shard_map/ppermute | solution.py:37
  194.2 5.7 %collective-permute-start.47 = (bf16[32,896]{1,0:T(8,128)(2,1)S(1)}, bf16[32,896]{1,0:T(8,128)(2,1)S(1)}, u32[]{:S(2)}, u32[]{:S(2)}) collective-permute-start(bf16[32,896]{1,0:T(8,128)(2,1)S(1)} %get-tuple-element.243), channel_id=1, source_target_pairs={{0,64},{32,96},{64,0},{96,32},{1,65},{33,97},{65,1},{97,33},{2,66}... | collective-permute-start | bytes 172040 | tf_op jit(solution)/shard_map/ppermute | solution.py:37
  196.9 4.2 %collective-permute-start.48 = (bf16[32,896]{1,0:T(8,128)(2,1)S(1)}, bf16[32,896]{1,0:T(8,128)(2,1)S(1)}, u32[]{:S(2)}, u32[]{:S(2)}) collective-permute-start(bf16[32,896]{1,0:T(8,128)(2,1)S(1)} %get-tuple-element.242), channel_id=1, source_target_pairs={{0,96},{32,0},{64,32},{96,64},{1,97},{33,1},{65,33},{97,65},{2,98}... | collective-permute-start | bytes 172040 | tf_op jit(solution)/shard_map/ppermute | solution.py:37
  203.3 6.4 %collective-permute-start.49 = (f32[32,128]{1,0:T(8,128)}, f32[32,128]{1,0:T(8,128)S(1)}, u32[]{:S(2)}, u32[]{:S(2)}) collective-permute-start(f32[32,128]{1,0:T(8,128)} %get-tuple-element.226), channel_id=1, source_target_pairs={{0,1},{1,2},{2,3},{3,0},{4,5},{5,6},{6,7},{7,4},{8,9},{9,10},{10,1... | collective-permute-start | bytes 49160 | tf_op jit(solution)/shard_map/ppermute | solution.py:37
  204.8 5.5 %collective-permute-start.50 = (f32[32,128]{1,0:T(8,128)}, f32[32,128]{1,0:T(8,128)S(1)}, u32[]{:S(2)}, u32[]{:S(2)}) collective-permute-start(f32[32,128]{1,0:T(8,128)} %get-tuple-element.226), channel_id=1, source_target_pairs={{0,2},{1,3},{2,0},{3,1},{4,6},{5,7},{6,4},{7,5},{8,10},{9,11},{10,... | collective-permute-start | bytes 49160 | tf_op jit(solution)/shard_map/ppermute | solution.py:37
  206.6 3.9 %collective-permute-start.51 = (f32[32,128]{1,0:T(8,128)}, f32[32,128]{1,0:T(8,128)S(1)}, u32[]{:S(2)}, u32[]{:S(2)}) collective-permute-start(f32[32,128]{1,0:T(8,128)} %get-tuple-element.226), channel_id=1, source_target_pairs={{0,3},{1,0},{2,1},{3,2},{4,7},{5,4},{6,5},{7,6},{8,11},{9,8},{10,9... | collective-permute-start | bytes 49160 | tf_op jit(solution)/shard_map/ppermute | solution.py:37
  (34 other events, 95.0 us)
Sparse Core Ops, SparseCore 0:
  10.3 60.3 all-gather.1
  114.7 98.4 reduce-scatter.1
